TPU v7x, 32 devices: a whole 2x2x4 slice. The times are simulated.
32 devices in a mesh: pix: 8 (over y, x, core), tm: 4 (over z).
Axes of the slice: x: 2, y: 2, z: 4, core: 2. Of those that a mesh axis runs over, the one named last changes fastest.
Arguments:
- raw_movie: float32 [64, 256, 2048], P('pix', None, 'tm'), may hold values from 0.05 to 2
- footprints: float32 [256, 16384], P('tm', 'pix'), may hold values from 0.05 to 1
- traces: float32 [256, 2048], P('pix', 'tm'), may hold values from 0.05 to 1
Outputs:
- denoised: float32 [64, 256, 2048], P('pix', None, 'tm')
- new_footprints: float32 [256, 16384], P('tm', 'pix')
- new_traces: float32 [256, 2048], P('pix', 'tm')
All inputs are finite; a program needn't handle non-finite values.
Results may differ from a plain program's by a relative error of at most 0.00013.
Values sent between devices are 32-bit elements; how exact they have to be, the bound alone decides.
No kernel may reach another device: no remote copies, remote signals or barrier semaphores. Data moves between devices by JAX's collectives and lax.ppermute only.
A program may use at most 64 MiB of HBM per device.

v0:
```python
import jax
import jax.numpy as jnp
from jax import lax
from jax.sharding import PartitionSpec as P

edge_scale = 0.5
step_size = 0.24


def with_halo(cells, sides, width):
    for axis, dim in sides:
        count = lax.axis_size(axis)
        ends = count - 1
        head = lax.slice_in_dim(cells, 0, width, axis=dim)
        tail = lax.slice_in_dim(cells, cells.shape[dim] - width, cells.shape[dim], axis=dim)
        cells = jnp.concatenate(
            [
                lax.ppermute(tail, axis, [(i, (i + 1) % count) for i in range(ends)]),
                cells,
                lax.ppermute(head, axis, [((i + 1) % count, i) for i in range(ends)]),
            ],
            axis=dim,
        )
    return cells


def flux_term(change):
    return change / (1.0 + change / edge_scale * (change / edge_scale))


def substep(extended):
    middle = extended[1:-1]
    padded = jnp.pad(middle, ((0, 0), (1, 1), (0, 0)))
    summed = flux_term(extended[:-2] - middle) + flux_term(extended[2:] - middle)
    summed = summed + flux_term(padded[:, :-2] - middle) + flux_term(padded[:, 2:] - middle)
    return middle + step_size * summed


def matmul_hi(left, right):
    return jnp.dot(left, right, precision=lax.Precision.HIGHEST, preferred_element_type=jnp.float32)


def contract_last(left, right):
    return lax.dot_general(
        left,
        right,
        (((1,), (1,)), ((), ())),
        precision=lax.Precision.HIGHEST,
        preferred_element_type=jnp.float32,
    )


def body(raw_movie, footprints, traces):
    row_count = raw_movie.shape[0]
    col_count = raw_movie.shape[1]
    frame_count = raw_movie.shape[2]
    current = raw_movie
    for repeat in range(4):
        extended = with_halo(current, (("pix", 0),), 1)
        current = substep(extended)
    pixels = current.reshape(row_count * col_count, frame_count)
    foot_full = lax.all_gather(footprints, "tm", axis=0, tiled=True)
    trace_full = lax.all_gather(traces, "pix", axis=0, tiled=True)
    part = foot_full
    merged = lax.psum_scatter(
        jnp.concatenate([matmul_hi(part, pixels), contract_last(part, foot_full)], axis=1),
        "pix",
        scatter_dimension=0,
        tiled=True,
    )
    numerator = merged[:, :frame_count]
    gram_rows = merged[:, frame_count:]
    new_traces = traces * numerator / matmul_hi(gram_rows, trace_full)
    new_full = lax.all_gather(new_traces, "pix", axis=0, tiled=True)
    part = new_full
    joined = lax.psum_scatter(
        jnp.concatenate([contract_last(part, pixels), contract_last(part, new_full)], axis=1),
        "tm",
        scatter_dimension=0,
        tiled=True,
    )
    foot_numerator = joined[:, : row_count * col_count]
    trace_rows = joined[:, row_count * col_count :]
    new_footprints = footprints * foot_numerator / matmul_hi(trace_rows, foot_full)
    return (current, new_footprints, new_traces)


def solution(mesh):
    placed = (P("pix", None, "tm"), P("tm", "pix"), P("pix", "tm"))
    return jax.shard_map(
        body,
        mesh=mesh,
        in_specs=placed,
        out_specs=(P("pix", None, "tm"), P("tm", "pix"), P("pix", "tm")),
        check_vma=False,
    )
```

profile of v0, /device:TPU:0, one launch (start us, length us, event | category | flops | bytes accessed | tf_op | source)
XLA Modules:
  0.0 233.4 jit_solution(9281021780774878681)
XLA Ops:
  7.2 0.0 all-gather.2.cloned.1.call-start
  7.2 1.3 fusion.13
  8.5 2.4 %collective-permute-start = (f32[1,256,512]{2,1,0:T(8,128)S(1)}, f32[1,256,512]{2,1,0:T(8,128)S(1)}, u32[]{:S(2)}, u32[]{:S(2)}) collective-permute-start(f32[1,256,512]{2,1,0:T(8,128)S(1)} %get-tuple-element.12), channel_id=1, source_target_pairs={{0,4},{4,8},{8,12},{12,16},{16,20},{20,24},{24,28},{1,5},{5,9},{9,... | collective-permute-start | bytes 1572872 | tf_op jit(solution)/shard_map/ppermute | solution.py:18
  10.9 1.3 collective-permute-start.1
  12.2 0.2 collective-permute-done
  12.4 4.4 %collective-permute-done.1 = f32[1,256,512]{2,1,0:T(8,128)S(1)} collective-permute-done((f32[1,256,512]{2,1,0:T(8,128)S(1)}, f32[1,256,512]{2,1,0:T(8,128)S(1)}, u32[]{:S(2)}, u32[]{:S(2)}) %collective-permute-start.1) | collective-permute-done | bytes 524320 | tf_op jit(solution)/shard_map/ppermute | solution.py:20
  16.8 9.8 %multiply_add_fusion.3 = f32[8,256,512]{2,1,0:T(8,128)S(1)} fusion(f32[8,256,512]{2,1,0:T(8,128)} %param.3, f32[1,256,512]{2,1,0:T(8,128)S(1)} %collective-permute-done.1, f32[1,256,512]{2,1,0:T(8,128)S(1)} %collective-permute-done), kind=kLoop, calls=%fused_computation.19 | loop fusion | flops 28311552 | bytes 9437184 | tf_op jit(solution)/shard_map/add | solution.py:36
  26.6 0.1 fusion.12
  26.7 12.0 %collective-permute-start.2 = (f32[1,256,512]{2,1,0:T(8,128)S(1)}, f32[1,256,512]{2,1,0:T(8,128)S(1)}, u32[]{:S(2)}, u32[]{:S(2)}) collective-permute-start(f32[1,256,512]{2,1,0:T(8,128)S(1)} %get-tuple-element.10), channel_id=1, source_target_pairs={{0,4},{4,8},{8,12},{12,16},{16,20},{20,24},{24,28},{1,5},{5,9},{9,... | collective-permute-start | bytes 1572872 | tf_op jit(solution)/shard_map/ppermute | solution.py:18
  38.7 1.3 collective-permute-start.3
  40.0 0.2 collective-permute-done.2
  40.2 2.3 collective-permute-done.3
  42.5 4.5 %multiply_add_fusion.2 = f32[8,256,512]{2,1,0:T(8,128)S(1)} fusion(f32[8,256,512]{2,1,0:T(8,128)S(1)} %multiply_add_fusion.3, f32[1,256,512]{2,1,0:T(8,128)S(1)} %collective-permute-done.3, f32[1,256,512]{2,1,0:T(8,128)S(1)} %collective-permute-done.2), kind=kLoop, calls=%fused_computation.18 | loop fusion | flops 28311552 | bytes 9437184 | tf_op jit(solution)/shard_map/add | solution.py:36
  47.0 0.0 copy-start.2
  47.1 2.0 copy-done.2
  49.1 0.1 fusion.11
  49.1 11.5 %collective-permute-start.4 = (f32[1,256,512]{2,1,0:T(8,128)S(1)}, f32[1,256,512]{2,1,0:T(8,128)S(1)}, u32[]{:S(2)}, u32[]{:S(2)}) collective-permute-start(f32[1,256,512]{2,1,0:T(8,128)S(1)} %get-tuple-element.8), channel_id=1, source_target_pairs={{0,4},{4,8},{8,12},{12,16},{16,20},{20,24},{24,28},{1,5},{5,9},{9,... | collective-permute-start | bytes 1572872 | tf_op jit(solution)/shard_map/ppermute | solution.py:18
  60.6 1.3 collective-permute-start.5
  61.9 0.0 all-gather.2.cloned.1.call-update
  62.0 0.0 reduce-scatter.7.cloned.1.call-start
  62.0 0.1 collective-permute-done.4
  62.1 2.3 collective-permute-done.5
  64.4 10.0 %multiply_add_fusion.1 = f32[8,256,512]{2,1,0:T(8,128)S(1)} fusion(f32[8,256,512]{2,1,0:T(8,128)} %copy-done.2, f32[1,256,512]{2,1,0:T(8,128)S(1)} %collective-permute-done.5, f32[1,256,512]{2,1,0:T(8,128)S(1)} %collective-permute-done.4), kind=kLoop, calls=%fused_computation.17 | loop fusion | flops 28311552 | bytes 9437184 | tf_op jit(solution)/shard_map/add | solution.py:36
  74.4 0.1 fusion.10
  74.5 10.5 %collective-permute-start.6 = (f32[1,256,512]{2,1,0:T(8,128)S(1)}, f32[1,256,512]{2,1,0:T(8,128)S(1)}, u32[]{:S(2)}, u32[]{:S(2)}) collective-permute-start(f32[1,256,512]{2,1,0:T(8,128)S(1)} %get-tuple-element.6), channel_id=1, source_target_pairs={{0,4},{4,8},{8,12},{12,16},{16,20},{20,24},{24,28},{1,5},{5,9},{9,... | collective-permute-start | bytes 1572872 | tf_op jit(solution)/shard_map/ppermute | solution.py:18
  85.0 1.5 collective-permute-start.7
  86.5 0.0 collective-permute-done.6
  86.5 2.3 collective-permute-done.7
  88.8 5.5 %multiply_add_fusion = f32[8,256,512]{2,1,0:T(8,128)} fusion(f32[8,256,512]{2,1,0:T(8,128)S(1)} %multiply_add_fusion.1, f32[1,256,512]{2,1,0:T(8,128)S(1)} %collective-permute-done.7, f32[1,256,512]{2,1,0:T(8,128)S(1)} %collective-permute-done.6), kind=kLoop, calls=%fused_computation.16 | loop fusion | flops 28311552 | bytes 9437184 | tf_op jit(solution)/shard_map/add | solution.py:36
  94.3 14.5 %all-gather.2.cloned.1.call-done = f32[256,2048]{1,0:T(8,128)} async-done(((f32[64,2048]{1,0:T(8,128)}), f32[256,2048]{1,0:T(8,128)}) %all-gather.2.cloned.1.call-update) | async-done | bytes 2097168 | tf_op jit(solution)/shard_map/all_gather | solution.py:62
  108.8 4.2 %fusion.14 = f32[256,256]{0,1:T(8,128)S(1)} fusion(f32[256,2048]{1,0:T(8,128)} %all-gather.2.cloned.1.call-done), kind=kOutput, calls=%fused_computation.33 | convolution fusion | flops 1610612736 | bytes 2359296 | tf_op jit(solution)/shard_map/dot_general | solution.py:44
  113.0 0.0 copy-start.4
  113.1 8.4 %convolution_bitcast_fusion = f32[256,512]{0,1:T(8,128)S(1)} fusion(f32[2048,512]{1,0:T(8,128)S(1)} %bitcast.15, f32[256,2048]{1,0:T(8,128)} %all-gather.2.cloned.1.call-done), kind=kOutput, calls=%fused_computation.22 | convolution fusion | flops 3221225472 | bytes 6815744 | tf_op jit(solution)/shard_map/dot_general | solution.py:40
  121.5 0.1 pad_maximum_fusion.9
  121.6 1.1 copy.13
  122.7 0.0 reduce-scatter.7.cloned.1.call-update
  122.7 0.0 reduce-scatter.5.cloned.1.call-start
  122.8 9.8 %all_gather.10 = f32[256,512]{1,0:T(8,128)S(1)} all-gather(f32[32,512]{1,0:T(8,128)S(1)} %copy-done.4), channel_id=1, replica_groups=mesh['pix'=8,'tm'=4] {'pix'}, dimensions={0}, use_global_device_ids=true | all-gather | bytes 589824 | tf_op jit(solution)/shard_map/all_gather | solution.py:63
  132.6 24.0 %reduce-scatter.7.cloned.1.call-done = f32[32,768]{1,0:T(8,128)} async-done(((f32[256,768]{1,0:T(8,128)}), f32[32,768]{1,0:T(8,128)}) %reduce-scatter.7.cloned.1.call-update) | async-done | bytes 98320 | tf_op jit(solution)/shard_map/reduce_scatter | solution.py:65
  156.7 1.3 convolution_divide_fusion.1
  157.9 0.0 copy-start.5
  157.9 10.0 %all_gather.11 = f32[256,512]{1,0:T(8,128)S(1)} all-gather(f32[32,512]{1,0:T(8,128)S(1)} %convolution_divide_fusion.1), channel_id=1, replica_groups=mesh['pix'=8,'tm'=4] {'pix'}, dimensions={0}, use_global_device_ids=true | all-gather | bytes 589824 | tf_op jit(solution)/shard_map/all_gather | solution.py:74
  168.0 5.5 %fusion.15 = f32[256,2048]{1,0:T(8,128)S(1)} fusion(f32[256,512]{1,0:T(8,128)S(1)} %all_gather.11, f32[2048,512]{1,0:T(8,128)} %bitcast.14), kind=kOutput, calls=%fused_computation.34 | convolution fusion | flops 3221225472 | bytes 6815744 | tf_op jit(solution)/shard_map/dot_general | solution.py:44
  173.5 0.6 fusion.16
  174.1 1.6 pad_maximum_fusion.8
  175.7 0.0 reduce-scatter.5.cloned.1.call-update
  175.8 47.9 %reduce-scatter.5.cloned.1.call-done = f32[64,2304]{1,0:T(8,128)} async-done(((f32[256,2304]{1,0:T(8,128)}), f32[64,2304]{1,0:T(8,128)}) %reduce-scatter.5.cloned.1.call-update) | async-done | bytes 589840 | tf_op jit(solution)/shard_map/reduce_scatter | solution.py:76
  223.6 3.3 %convolution_divide_fusion = f32[64,2048]{1,0:T(8,128)} fusion(f32[256,2048]{1,0:T(8,128)S(1)} %copy-done.1, f32[64,2048]{1,0:T(8,128)S(1)} %copy-done.3, f32[64,2304]{1,0:T(8,128)} %reduce-scatter.5.cloned.1.call-done), kind=kOutput, calls=%fused_computation.21 | convolution fusion | flops 402915328 | bytes 3735552 | tf_op jit(solution)/shard_map/dot_general | solution.py:40
  (8 shorter events, 0.0 us)
Async XLA Ops:
  7.2 101.6 %all-gather.2.cloned.1.call-start = ((), (), s32[]{:S(2)}) async-start(), calls=%async_computation.2 | async-start | bytes 2621440 | tf_op jit(solution)/shard_map/all_gather | solution.py:62
  8.5 3.9 %collective-permute-start = (f32[1,256,512]{2,1,0:T(8,128)S(1)}, f32[1,256,512]{2,1,0:T(8,128)S(1)}, u32[]{:S(2)}, u32[]{:S(2)}) collective-permute-start(f32[1,256,512]{2,1,0:T(8,128)S(1)} %get-tuple-element.12), channel_id=1, source_target_pairs={{0,4},{4,8},{8,12},{12,16},{16,20},{20,24},{24,28},{1,5},{5,9},{9,... | collective-permute-start | bytes 1572872 | tf_op jit(solution)/shard_map/ppermute | solution.py:18
  10.9 5.9 %collective-permute-start.1 = (f32[1,256,512]{2,1,0:T(8,128)S(1)}, f32[1,256,512]{2,1,0:T(8,128)S(1)}, u32[]{:S(2)}, u32[]{:S(2)}) collective-permute-start(f32[1,256,512]{2,1,0:T(8,128)S(1)} %get-tuple-element.13), channel_id=1, source_target_pairs={{4,0},{8,4},{12,8},{16,12},{20,16},{24,20},{28,24},{5,1},{9,5},{13... | collective-permute-start | bytes 1572872 | tf_op jit(solution)/shard_map/ppermute | solution.py:20
  26.7 13.5 %collective-permute-start.2 = (f32[1,256,512]{2,1,0:T(8,128)S(1)}, f32[1,256,512]{2,1,0:T(8,128)S(1)}, u32[]{:S(2)}, u32[]{:S(2)}) collective-permute-start(f32[1,256,512]{2,1,0:T(8,128)S(1)} %get-tuple-element.10), channel_id=1, source_target_pairs={{0,4},{4,8},{8,12},{12,16},{16,20},{20,24},{24,28},{1,5},{5,9},{9,... | collective-permute-start | bytes 1572872 | tf_op jit(solution)/shard_map/ppermute | solution.py:18
  38.7 3.8 %collective-permute-start.3 = (f32[1,256,512]{2,1,0:T(8,128)S(1)}, f32[1,256,512]{2,1,0:T(8,128)S(1)}, u32[]{:S(2)}, u32[]{:S(2)}) collective-permute-start(f32[1,256,512]{2,1,0:T(8,128)S(1)} %get-tuple-element.11), channel_id=1, source_target_pairs={{4,0},{8,4},{12,8},{16,12},{20,16},{24,20},{28,24},{5,1},{9,5},{13... | collective-permute-start | bytes 1572872 | tf_op jit(solution)/shard_map/ppermute | solution.py:20
  47.0 2.0 copy-start.2
  49.1 13.0 %collective-permute-start.4 = (f32[1,256,512]{2,1,0:T(8,128)S(1)}, f32[1,256,512]{2,1,0:T(8,128)S(1)}, u32[]{:S(2)}, u32[]{:S(2)}) collective-permute-start(f32[1,256,512]{2,1,0:T(8,128)S(1)} %get-tuple-element.8), channel_id=1, source_target_pairs={{0,4},{4,8},{8,12},{12,16},{16,20},{20,24},{24,28},{1,5},{5,9},{9,... | collective-permute-start | bytes 1572872 | tf_op jit(solution)/shard_map/ppermute | solution.py:18
  60.6 3.8 %collective-permute-start.5 = (f32[1,256,512]{2,1,0:T(8,128)S(1)}, f32[1,256,512]{2,1,0:T(8,128)S(1)}, u32[]{:S(2)}, u32[]{:S(2)}) collective-permute-start(f32[1,256,512]{2,1,0:T(8,128)S(1)} %get-tuple-element.9), channel_id=1, source_target_pairs={{4,0},{8,4},{12,8},{16,12},{20,16},{24,20},{28,24},{5,1},{9,5},{13... | collective-permute-start | bytes 1572872 | tf_op jit(solution)/shard_map/ppermute | solution.py:20
  62.0 94.7 %reduce-scatter.7.cloned.1.call-start = ((), (), s32[]{:S(2)}) async-start(), calls=%async_computation.4 | async-start | bytes 884736 | tf_op jit(solution)/shard_map/reduce_scatter | solution.py:65
  74.5 12.0 %collective-permute-start.6 = (f32[1,256,512]{2,1,0:T(8,128)S(1)}, f32[1,256,512]{2,1,0:T(8,128)S(1)}, u32[]{:S(2)}, u32[]{:S(2)}) collective-permute-start(f32[1,256,512]{2,1,0:T(8,128)S(1)} %get-tuple-element.6), channel_id=1, source_target_pairs={{0,4},{4,8},{8,12},{12,16},{16,20},{20,24},{24,28},{1,5},{5,9},{9,... | collective-permute-start | bytes 1572872 | tf_op jit(solution)/shard_map/ppermute | solution.py:18
  85.0 3.8 %collective-permute-start.7 = (f32[1,256,512]{2,1,0:T(8,128)S(1)}, f32[1,256,512]{2,1,0:T(8,128)S(1)}, u32[]{:S(2)}, u32[]{:S(2)}) collective-permute-start(f32[1,256,512]{2,1,0:T(8,128)S(1)} %get-tuple-element.7), channel_id=1, source_target_pairs={{4,0},{8,4},{12,8},{16,12},{20,16},{24,20},{28,24},{5,1},{9,5},{13... | collective-permute-start | bytes 1572872 | tf_op jit(solution)/shard_map/ppermute | solution.py:20
  108.8 4.2 %copy-start = (f32[8,256,512]{2,1,0:T(8,128)S(1)}, f32[8,256,512]{2,1,0:T(8,128)}, u32[]{:S(2)}) copy-start(f32[8,256,512]{2,1,0:T(8,128)} %multiply_add_fusion) | copy-start | bytes 12582916
  113.0 9.7 %copy-start.4 = (f32[32,512]{1,0:T(8,128)S(1)}, f32[32,512]{1,0:T(8,128)}, u32[]{:S(2)}) copy-start(f32[32,512]{1,0:T(8,128)} %param.5) | copy-start | bytes 196612
  122.7 100.9 %reduce-scatter.5.cloned.1.call-start = ((), (), s32[]{:S(2)}) async-start(), calls=%async_computation.3 | async-start | bytes 2949120 | tf_op jit(solution)/shard_map/reduce_scatter | solution.py:76
  157.9 16.2 %copy-start.5 = (f32[32,512]{1,0:T(8,128)}, f32[32,512]{1,0:T(8,128)S(1)}, u32[]{:S(2)}) copy-start(f32[32,512]{1,0:T(8,128)S(1)} %convolution_divide_fusion.1) | copy-start | bytes 196612
  173.5 50.1 %copy-start.1 = (f32[256,2048]{1,0:T(8,128)S(1)}, f32[256,2048]{1,0:T(8,128)}, u32[]{:S(2)}) copy-start(f32[256,2048]{1,0:T(8,128)} %all-gather.2.cloned.1.call-done) | copy-start | bytes 6291460
  173.5 50.1 %copy-start.3 = (f32[64,2048]{1,0:T(8,128)S(1)}, f32[64,2048]{1,0:T(8,128)}, u32[]{:S(2)}) copy-start(f32[64,2048]{1,0:T(8,128)} %param.4) | copy-start | bytes 1572868
Sparse Core Ops, SparseCore 0:
  62.1 46.6 all-gather.1
  122.9 33.7 reduce-scatter.6
  175.9 47.6 reduce-scatter.4
where the time goes:
time: 234 us; the launch traced here: 233 us
  waiting for transfers between devices  98.3 us (42%)
  starting transfers between devices  41.9 us (18%)
  other arithmetic  31.5 us (13%)
  matrix products  23.3 us (10%)
  blocking collectives  19.8 us (8%)
  between operations  14 us (6%)
  local copies, waits for them, and re-layouts  4.67 us (2%)
    reduce_scatter x1, waiting for transfers between devices, body(): lax.psum_scatter(jnp.concatenate([contract_last(part, pixels), contract_l...  47.9 us
    ppermute x4, starting transfers between devices, with_halo(): lax.ppermute(tail, axis, [(i, (i + 1) % count) for i in range(ends)])  36.4 us
    add x4, other arithmetic, substep(): return middle + step_size * summed  29.8 us
    reduce_scatter x1, waiting for transfers between devices, body(): lax.psum_scatter(jnp.concatenate([matmul_hi(part, pixels), contract_last(...  24 us
    all_gather x1, waiting for transfers between devices, body(): foot_full = lax.all_gather(footprints, 'tm', axis=0, tiled=True)  14.5 us
    dot_general x3, matrix products, matmul_hi(): jnp.dot(left, right, precision=lax.Precision.HIGHEST, preferred_element_t...  13 us
    ppermute x4, waiting for transfers between devices, with_halo(): lax.ppermute(head, axis, [((i + 1) % count, i) for i in range(ends)])  11.3 us
    dot_general x3, matrix products, contract_last(): lax.dot_general(left, right, (((1,), (1,)), ((), ())), precision=lax.Prec...  10.3 us
  transfers between devices with their start and end apart: 11, of which 10 were waited for; matrix products, arithmetic and copies ran while one was open for 7% of the time, Pallas kernels for 0%

commit v1 on v0

v1 whole, which is shorter than its diff:
```python
import jax
import jax.numpy as jnp
from jax import lax
from jax.experimental import pallas as pl
from jax.experimental.pallas import tpu as pltpu
from jax.sharding import PartitionSpec as P


edge_square = 0.25
step_scale = 0.06
SUBSTEPS = 4
LANES = 128
GROUP = 4
HALVES = 2
CHUNKS = 2

NN = ((1,), (0,))
NT = ((1,), (1,))


def flux_quarter(change):
    return change / (change * change + edge_square)


def split(value):
    high = value.astype(jnp.bfloat16)
    low = (value - high.astype(jnp.float32)).astype(jnp.bfloat16)
    return high, low


def stacked(value):
    return jnp.concatenate(split(value), axis=0)


def dot(left, right, dims):
    return lax.dot_general(left, right, (dims, ((), ())), preferred_element_type=jnp.float32)


def fold(value):
    half = value.shape[0] // 2
    return value[:half] + value[half:]


def cost(flops, moved):
    return pl.CostEstimate(flops=flops, bytes_accessed=moved, transcendentals=0)


def shaped(*shape, dtype=jnp.float32):
    return jax.ShapeDtypeStruct(shape, dtype)


def edges_call(flags, raw, halo, chunk, frames, with_corner):
    rows, cols, _ = raw.shape
    shift = rows - halo

    def kernel(flags, head_ref, tail_ref, head_out, tail_out, *corner_out):
        head_out[...] = head_ref[...]
        tail_out[...] = tail_ref[...]
        if with_corner:
            corner_out[0][...] = jnp.where(flags[4] == 1, tail_ref[...], head_ref[...])

    block = (1, cols, frames)
    outs = 3 if with_corner else 2
    return pl.pallas_call(
        kernel,
        grid_spec=pltpu.PrefetchScalarGridSpec(
            num_scalar_prefetch=1,
            grid=(halo,),
            in_specs=[
                pl.BlockSpec(block, lambda i, flags: (i, 0, chunk)),
                pl.BlockSpec(block, lambda i, flags: (shift + i, 0, chunk)),
            ],
            out_specs=[pl.BlockSpec(block, lambda i, flags: (i, 0, 0))] * outs,
        ),
        out_shape=[shaped(halo, cols, frames)] * outs,
        cost_estimate=cost(1, 4 * halo * cols * frames * 4),
        name="edges",
    )(flags, raw, raw)


def diffuse_call(flags, raw, halo_up, halo_down, detour, carried, chunk):
    rows, cols, total = raw.shape
    halo, _, frames = halo_up.shape
    groups = frames // LANES
    width = 64
    pad = 8
    extended = rows + 2 * halo

    def kernel(flags, *refs):
        if detour is None:
            raw_ref, up_ref, down_ref = refs[:3]
            refs = refs[3:]
        else:
            raw_ref, up_ref, down_ref, detour_ref = refs[:4]
            refs = refs[4:]
        if carried is not None:
            refs = refs[1:]
        out_ref, pair_ref, first_buf, second_buf = refs
        zero = jnp.zeros((extended, pad, LANES), jnp.float32)
        for buf in (first_buf, second_buf):
            buf[:, 0:pad, :] = zero
            buf[:, pad + cols :, :] = zero
        inside = slice(pad, pad + cols)
        first_buf[0:halo, inside, :] = up_ref[...]
        first_buf[halo : halo + rows, inside, :] = raw_ref[...]
        first_buf[halo + rows :, inside, :] = down_ref[...]
        if detour is not None:

            @pl.when(flags[2] == 1)
            def _():
                first_buf[0:halo, inside, :] = detour_ref[...]

            @pl.when(flags[3] == 1)
            def _():
                first_buf[halo + rows :, inside, :] = detour_ref[...]

        scale_up = step_scale * flags[0].astype(jnp.float32)
        scale_down = step_scale * flags[1].astype(jnp.float32)
        head = lax.broadcasted_iota(jnp.int32, (width, LANES), 0) == 0
        bufs = (first_buf, second_buf)
        for step in range(SUBSTEPS):
            src, dst = bufs[step % 2], bufs[1 - step % 2]
            top = step
            middle = range(step + 1, extended - step - 1)

            def tile(j, left_flux):
                base = pl.multiple_of(pad + j * width, 8)
                col = pl.multiple_of(j * width, width)
                kept = []
                current = src[top + 1, pl.ds(base, width), :]
                flux_up = flux_quarter(current - src[top, pl.ds(base, width), :])
                for k, row in enumerate(middle):
                    below = src[row + 1, pl.ds(base, width), :]
                    flux_down = flux_quarter(below - current)
                    flux_right = flux_quarter(src[row, pl.ds(base + 1, width), :] - current)
                    rolled = pltpu.roll(flux_right, 1, 0)
                    flux_left = jnp.where(head, left_flux[k], rolled)
                    scale = step_scale
                    if row < halo:
                        scale = scale_up
                    if row >= halo + rows:
                        scale = scale_down
                    value = current + scale * ((flux_down - flux_up) + (flux_right - flux_left))
                    kept.append(rolled)
                    if step + 1 < SUBSTEPS:
                        dst[row, pl.ds(base, width), :] = value
                    else:
                        out_ref[row - halo, pl.ds(col, width), :] = value
                        high, low = split(value)
                        pair_ref[row - halo, pl.ds(col, width), 0:LANES] = high
                        pair_ref[row - halo, pl.ds(col, width), LANES:] = low
                    current, flux_up = below, flux_down
                return tuple(kept)

            edge = tuple(flux_quarter(src[row, pl.ds(pad, width), :]) for row in middle)
            lax.fori_loop(0, cols // width, tile, edge)

    def spec(count, at):
        return pl.BlockSpec((count, cols, LANES), lambda i, flags: (0, 0, at + i))

    operands = [flags, raw, halo_up, halo_down]
    in_specs = [spec(rows, chunk * groups), spec(halo, 0), spec(halo, 0)]
    if detour is not None:
        operands.append(detour)
        in_specs.append(spec(halo, 0))
    aliases = {}
    if carried is not None:
        operands.append(carried)
        in_specs.append(pl.BlockSpec(memory_space=pl.ANY))
        aliases = {len(operands) - 1: 0}
    return pl.pallas_call(
        kernel,
        grid_spec=pltpu.PrefetchScalarGridSpec(
            num_scalar_prefetch=1,
            grid=(groups,),
            in_specs=in_specs,
            out_specs=[
                spec(rows, chunk * groups),
                pl.BlockSpec((rows, cols, 2 * LANES), lambda i, flags: (0, 0, i)),
            ],
            scratch_shapes=[pltpu.VMEM((extended, cols + 2 * pad, LANES), jnp.float32)] * 2,
        ),
        out_shape=[shaped(rows, cols, total), shaped(rows, cols, 2 * frames, dtype=jnp.bfloat16)],
        input_output_aliases=aliases,
        cost_estimate=cost(rows * cols * frames * 200, rows * cols * frames * 16),
        name="diffuse",
    )(*operands)


def footprints_call(scalars, own, pairs):
    count = len(pairs) + 1
    share, pixel_count = own.shape
    rank = share * count
    block = 512
    steps = pixel_count // block

    def kernel(scalars, *refs):
        own_ref = refs[0]
        pair_refs = [(refs[1 + 2 * k], refs[2 + 2 * k]) for k in range(count - 1)]
        out_ref, gram_ref, total = refs[2 * count - 1 :]
        here = scalars[0]
        step = pl.program_id(0)

        def put(slot, value):
            at = pl.multiple_of(lax.rem(here + slot, count) * share, share)
            high, low = split(value)
            out_ref[pl.ds(at, share), :] = high
            out_ref[pl.ds(rank + at, share), :] = low

        put(0, own_ref[...])
        for s, (from_above, from_below) in enumerate(pair_refs, 1):
            put(s, jnp.where(here + s < count, from_above[...], from_below[...]))

        @pl.when(step == 0)
        def _():
            total[...] = jnp.zeros_like(total)

        total[...] += dot(out_ref[...], out_ref[0:rank, :], NT)

        @pl.when(step == steps - 1)
        def _():
            cross = total[rank:, :]
            gram_ref[...] = total[0:rank, :] + (cross + cross.T)

    foot_spec = pl.BlockSpec((share, block), lambda k, s: (0, k))
    flat = [array for pair in pairs for array in pair]
    return pl.pallas_call(
        kernel,
        grid_spec=pltpu.PrefetchScalarGridSpec(
            num_scalar_prefetch=1,
            grid=(steps,),
            in_specs=[foot_spec] * (1 + len(flat)),
            out_specs=[
                pl.BlockSpec((2 * rank, block), lambda k, s: (0, k)),
                pl.BlockSpec((rank, rank), lambda k, s: (0, 0)),
            ],
            scratch_shapes=[pltpu.VMEM((2 * rank, rank), jnp.float32)],
        ),
        out_shape=[shaped(2 * rank, pixel_count, dtype=jnp.bfloat16), shaped(rank, rank)],
        cost_estimate=cost(4 * rank * rank * pixel_count, 8 * rank * pixel_count),
        name="footprints",
    )(scalars, own, *flat)


def numerator_call(scalars, foot, movies, gram, trace_rows):
    rank = foot.shape[0] // 2
    pixel_count, pair = movies[0].shape
    frames = pair // 2
    columns = frames * len(movies) + rank
    block = 512
    steps = pixel_count // block
    chips = rank // (2 * trace_rows)

    def kernel(scalars, foot_ref, gram_ref, *refs):
        movie_refs = refs[: len(movies)]
        keep_ref, send_ref, total = refs[len(movies) :]
        step = pl.program_id(0)

        @pl.when(step == 0)
        def _():
            total[...] = jnp.zeros_like(total)

        for k, movie_ref in enumerate(movie_refs):
            part = fold(dot(foot_ref[...], movie_ref[...], NN))
            for g in range(frames // LANES):
                at = k * frames + g * LANES
                both = part[:, 2 * g * LANES : 2 * (g + 1) * LANES]
                total[:, at : at + LANES] += both[:, 0:LANES] + both[:, LANES:]

        @pl.when(step == steps - 1)
        def _():
            total[:, frames * len(movies) :] = gram_ref[...]
            core = scalars[1]
            for k in range(chips):
                chip = scalars[2] ^ k
                mine = pl.multiple_of((2 * chip + core) * trace_rows, trace_rows)
                other = pl.multiple_of((2 * chip + 1 - core) * trace_rows, trace_rows)
                keep_ref[k] = total[pl.ds(mine, trace_rows), :]
                send_ref[k] = total[pl.ds(other, trace_rows), :]

    out_spec = pl.BlockSpec((chips, trace_rows, columns), lambda k, s: (0, 0, 0))
    return pl.pallas_call(
        kernel,
        grid_spec=pltpu.PrefetchScalarGridSpec(
            num_scalar_prefetch=1,
            grid=(steps,),
            in_specs=[
                pl.BlockSpec((2 * rank, block), lambda k, s: (0, k)),
                pl.BlockSpec((rank, rank), lambda k, s: (0, 0)),
            ]
            + [pl.BlockSpec((block, pair), lambda k, s: (k, 0))] * len(movies),
            out_specs=[out_spec, out_spec],
            scratch_shapes=[pltpu.VMEM((rank, columns), jnp.float32)],
        ),
        out_shape=[shaped(chips, trace_rows, columns)] * 2,
        cost_estimate=cost(8 * rank * pixel_count * columns, 4 * pixel_count * (rank + columns)),
        name="numerator",
    )(scalars, foot, gram, *movies)


def traces_call(scalars, keep, arrived, parts, near, far):
    _, trace_rows, columns = keep.shape
    frames = near.shape[2]
    rank = columns - frames
    chips = near.shape[0]

    def kernel(scalars, near_ref, far_ref, *refs):
        part_refs, (out_ref, full) = refs[:-2], refs[-2:]
        for k in range(chips):
            device = 2 * (scalars[2] ^ k) + scalars[1]
            full[pl.ds(pl.multiple_of(device * trace_rows, trace_rows), trace_rows), :] = near_ref[k]
            device = 2 * (scalars[2] ^ k) + 1 - scalars[1]
            full[pl.ds(pl.multiple_of(device * trace_rows, trace_rows), trace_rows), :] = far_ref[k]
        total = part_refs[0][0] + part_refs[1][0]
        for part_ref in part_refs[2:]:
            total = total + part_ref[...]
        gram = stacked(total[:, frames:])
        high, low = split(full[...])
        below = fold(dot(gram, high, NN)) + dot(gram[0:trace_rows], low, NN)
        out_ref[...] = near_ref[0] * total[:, 0:frames] / below

    whole = pl.BlockSpec(near.shape, lambda k, s: (0, 0, 0))
    return pl.pallas_call(
        kernel,
        grid_spec=pltpu.PrefetchScalarGridSpec(
            num_scalar_prefetch=1,
            grid=(1,),
            in_specs=[whole, whole]
            + [pl.BlockSpec((1, trace_rows, columns), lambda k, s: (0, 0, 0))] * 2
            + [pl.BlockSpec((trace_rows, columns), lambda k, s: (0, 0))] * len(parts),
            out_specs=pl.BlockSpec((trace_rows, frames), lambda k, s: (0, 0)),
            scratch_shapes=[pltpu.VMEM((rank, frames), jnp.float32)],
        ),
        out_shape=shaped(trace_rows, frames),
        cost_estimate=cost(6 * trace_rows * rank * frames, 8 * rank * frames),
        name="traces",
    )(scalars, near, far, keep, arrived, *parts)


def products_call(scalars, near, far, movies, half, count, with_gram):
    chips = len(near)
    trace_rows, frames = near[0].shape
    rank = 2 * chips * trace_rows
    share = rank // count
    pixel_count, pair = movies[0].shape
    part = pixel_count // HALVES
    block = rank
    steps = part // block
    columns = part + (rank if with_gram else 0)
    groups = frames // LANES
    outs = count + 1

    def kernel(scalars, *refs):
        near_refs, far_refs, refs = refs[:chips], refs[chips : 2 * chips], refs[2 * chips :]
        movie_refs = refs[: len(movies)]
        refs = refs[len(movies) :]
        out_refs = refs[:outs]
        full, left, result = refs[outs:]
        step = pl.program_id(0)
        here = scalars[0]

        @pl.when(step == 0)
        def _():
            for k in range(chips):
                device = 2 * (scalars[2] ^ k) + scalars[1]
                full[pl.ds(pl.multiple_of(device * trace_rows, trace_rows), trace_rows), :] = near_refs[k][...]
                device = 2 * (scalars[2] ^ k) + 1 - scalars[1]
                full[pl.ds(pl.multiple_of(device * trace_rows, trace_rows), trace_rows), :] = far_refs[k][...]
            high, low = split(full[...])
            for g in range(groups):
                cut = slice(g * LANES, (g + 1) * LANES)
                at = 2 * g * LANES
                left[0:rank, at : at + LANES] = high[:, cut]
                left[0:rank, at + LANES : at + 2 * LANES] = high[:, cut]
                left[rank:, at : at + LANES] = low[:, cut]
                left[rank:, at + LANES : at + 2 * LANES] = jnp.zeros_like(low[:, cut])

        def emit(total, at):
            result[...] = total
            for k, out_ref in enumerate(out_refs):
                slot = lax.rem(here + k, count) if k < count else scalars[3]
                row = pl.multiple_of(slot * share, share)
                out_ref[:, pl.ds(at, block)] = result[pl.ds(row, share), :]

        total = dot(left[:, 0:pair], movie_refs[0][...], NT)
        for k in range(1, len(movies)):
            total += dot(left[:, k * pair : (k + 1) * pair], movie_refs[k][...], NT)
        emit(fold(total), pl.multiple_of(step * block, block))
        if with_gram:

            @pl.when(step == steps - 1)
            def _():
                high, low = split(full[...])
                both = dot(jnp.concatenate([high, low], axis=0), high, NT)
                cross = both[rank:]
                emit(both[0:rank] + (cross + cross.T), part)

    piece = pl.BlockSpec((trace_rows, frames), lambda j, s: (0, 0))
    return pl.pallas_call(
        kernel,
        grid_spec=pltpu.PrefetchScalarGridSpec(
            num_scalar_prefetch=1,
            grid=(steps,),
            in_specs=[piece] * (2 * chips)
            + [pl.BlockSpec((block, pair), lambda j, s: (half * steps + j, 0))] * len(movies),
            out_specs=[pl.BlockSpec((share, columns), lambda j, s: (0, 0))] * outs,
            scratch_shapes=[
                pltpu.VMEM((rank, frames), jnp.float32),
                pltpu.VMEM((2 * rank, 2 * frames), jnp.bfloat16),
                pltpu.VMEM((rank, block), jnp.float32),
            ],
        ),
        out_shape=[shaped(share, columns)] * outs,
        cost_estimate=cost(8 * rank * part * frames, 4 * part * (frames + rank)),
        name="products",
    )(scalars, *near, *far, *movies)


def final_call(scalars, own, foot, parts, grams, carried, half):
    share, pixel_count = own.shape
    rank = foot.shape[0] // 2
    part = pixel_count // HALVES
    block = 512
    steps = part // block

    def kernel(scalars, own_ref, foot_ref, *refs):
        part_refs = refs[: len(parts)]
        gram_refs = refs[len(parts) : len(parts) + len(grams)]
        out_ref = refs[-1]
        above = part_refs[0][...]
        for part_ref in part_refs[1:]:
            above = above + part_ref[...]
        gram = gram_refs[0][...]
        for gram_ref in gram_refs[1:]:
            gram = gram + gram_ref[...]
        both = stacked(gram)
        below = fold(dot(both, foot_ref[0:rank, :], NN)) + dot(both[0:share], foot_ref[rank:, :], NN)
        out_ref[...] = own_ref[...] * above / below

    at = half * steps
    in_specs = [
        pl.BlockSpec((share, block), lambda k, s: (0, at + k)),
        pl.BlockSpec((2 * rank, block), lambda k, s: (0, at + k)),
    ]
    in_specs += [pl.BlockSpec((share, block), lambda k, s: (0, k))] * len(parts)
    in_specs += [pl.BlockSpec((share, rank), lambda k, s: (0, part // rank))] * len(grams)
    operands = [scalars, own, foot, *parts, *grams]
    aliases = {}
    if carried is not None:
        operands.append(carried)
        in_specs.append(pl.BlockSpec(memory_space=pl.ANY))
        aliases = {len(operands) - 1: 0}
    return pl.pallas_call(
        kernel,
        grid_spec=pltpu.PrefetchScalarGridSpec(
            num_scalar_prefetch=1,
            grid=(steps,),
            in_specs=in_specs,
            out_specs=pl.BlockSpec((share, block), lambda k, s: (0, at + k)),
        ),
        out_shape=shaped(share, pixel_count),
        input_output_aliases=aliases,
        cost_estimate=cost(6 * share * rank * part, 4 * part * (rank + 5 * share)),
        name="final",
    )(*operands)


def line_gather(block, axis, count, here):
    up, down = {}, {}
    last_up = last_down = block
    for r in range(1, count):
        up_pairs = [(k, k + 1) for k in range(r - 1, count - 1)]
        down_pairs = [(k + 1, k) for k in range(0, count - r)]
        if r == count - 1 and count != 3:
            merged = jnp.where(here == 1, last_down, last_up) if count > 2 else block
            last_up = last_down = lax.ppermute(merged, axis, up_pairs + down_pairs)
        else:
            last_up = lax.ppermute(last_up, axis, up_pairs)
            last_down = lax.ppermute(last_down, axis, down_pairs)
        up[r], down[r] = last_up, last_down
    return [(down[s], up[count - s]) for s in range(1, count)]


def line_scatter(blocks, axis, count):
    up_last = down_last = None
    for r in range(1, count):
        up_pairs = [(k, k + 1) for k in range(r)]
        down_pairs = [(count - 1 - k, count - 2 - k) for k in range(r)]
        if r == 1 and count > 3:
            up_last = down_last = lax.ppermute(blocks[count], axis, up_pairs + down_pairs)
            continue
        up_block, down_block = blocks[count - r], blocks[r]
        if r > 1:
            up_block = up_block + up_last
            down_block = down_block + down_last
        up_last = lax.ppermute(up_block, axis, up_pairs)
        down_last = lax.ppermute(down_block, axis, down_pairs)
    return [blocks[0], up_last, down_last]


def compute(raw_movie, footprints, traces):
    rows, cols, frame_count = raw_movie.shape
    pixel_count = rows * cols
    pix_count = lax.axis_size("pix")
    count = lax.axis_size("tm")
    pix = lax.axis_index("pix")
    here = lax.axis_index("tm")
    core = lax.rem(pix, 2)
    trace_rows = traces.shape[0]
    frames = frame_count // CHUNKS
    halo = SUBSTEPS

    def swap(mask):
        return [(k, k ^ mask) for k in range(pix_count)]

    inner = (pix > 0).astype(jnp.int32)
    outer = (pix < pix_count - 1).astype(jnp.int32)
    corner = (lax.rem(pix, GROUP) == GROUP - 1).astype(jnp.int32)
    flags = jnp.stack([inner, outer, (lax.rem(pix, GROUP) == 0) * inner, corner * outer, corner]).astype(jnp.int32)
    first_out = lax.rem(here + jnp.where(here == 0, count - 1, 1), count)
    scalars = jnp.stack([here, core, lax.div(pix, 2), first_out]).astype(jnp.int32)

    pairs = line_gather(footprints, "tm", count, here)

    bent = [k for k in range(pix_count - 1) if k % GROUP == GROUP - 1] if pix_count % GROUP == 0 else []
    halos = []
    for c in range(CHUNKS):
        last = c == CHUNKS - 1 and bool(bent)
        send = [(k, k + 1) for k in range(pix_count - 1) if not (last and k in bent)]
        edges = edges_call(flags, raw_movie, halo, c, frames, last)
        detour = None
        if last:
            first = [(k, k + GROUP) for k in bent] + [(k + 1, k + 1 - GROUP) for k in bent]
            second = [(k + GROUP, k + 1) for k in bent] + [(k + 1 - GROUP, k) for k in bent]
            detour = lax.ppermute(edges[2], "pix", first)
            detour = lax.ppermute(detour, "pix", second)
        from_above = lax.ppermute(edges[1], "pix", send)
        from_below = lax.ppermute(edges[0], "pix", [(b, a) for a, b in send])
        halos.append((from_above, from_below, detour))

    near = traces[None]
    mask = 2
    while mask < pix_count:
        near = jnp.concatenate([near, lax.ppermute(near, "pix", swap(mask))], axis=0)
        mask *= 2
    far = lax.ppermute(near, "pix", swap(1))

    current = None
    movies = []
    for c in range(CHUNKS):
        current, pair = diffuse_call(flags, raw_movie, *halos[c], current, c)
        movies.append(pair.reshape(pixel_count, 2 * frames))

    foot, gram = footprints_call(scalars, footprints, pairs)
    keep, send = numerator_call(scalars, foot, movies, gram, trace_rows)
    arrived = lax.ppermute(send, "pix", swap(1))
    parts = []
    for k in range(1, keep.shape[0]):
        parts.append(lax.ppermute(keep[k] + arrived[k], "pix", swap(2 * k)))
    new_traces = traces_call(scalars, keep, arrived, parts, near, far)
    near = [new_traces]
    for k in range(1, keep.shape[0]):
        near.append(lax.ppermute(new_traces, "pix", swap(2 * k)))
    far = []
    for piece in near:
        far.append(lax.ppermute(piece, "pix", swap(1)))

    products = []
    for h in range(HALVES):
        products.append(products_call(scalars, near, far, movies, h, count, h == 0))
    sums = [line_scatter(blocks, "tm", count) for blocks in products]
    new_footprints = None
    for h in range(HALVES):
        new_footprints = final_call(scalars, footprints, foot, sums[h], sums[0], new_footprints, h)
    return current, new_footprints, new_traces


def solution(mesh):
    placed = (P("pix", None, "tm"), P("tm", "pix"), P("pix", "tm"))
    return jax.shard_map(
        compute,
        mesh=mesh,
        in_specs=placed,
        out_specs=(P("pix", None, "tm"), P("tm", "pix"), P("pix", "tm")),
        check_vma=False,
    )
```

time: 234 us -> 179 us (0.76)
  waiting for transfers between devices: 98.3 us -> 27.5 us
  Pallas kernels: 0 us -> 66.2 us
  starting transfers between devices: 41.9 us -> 73.4 us
  other arithmetic: 31.5 us -> 4.03 us
  matrix products: 23.3 us -> 0 us
  blocking collectives: 19.8 us -> 0 us
  between operations: 14 us -> 1.26 us
    reduce_scatter x2 -> x0, waiting for transfers between devices: 71.9 us -> none  [the longest x1 47.9 us: body(): lax.psum_scatter(jnp.concatenate([contract_last(part, pixels), contract_l...]
    pallas_call x0 -> x11, Pallas kernels: none -> 66.2 us  [the longest x2 22.7 us: diffuse_call(): pl.pallas_call(kernel, grid_spec=pltpu.PrefetchScalarGridSpec(num_scalar_...]
    ppermute x8 -> x35, starting transfers between devices: 41.7 us -> 73.4 us  [the longest x4 19.6 us: line_scatter(): up_last = lax.ppermute(up_block, axis, up_pairs)]
    add x4 -> x7, other arithmetic: 29.8 us -> 3.29 us  [the longest x1 1.17 us: compute(): parts.append(lax.ppermute(keep[k] + arrived[k], 'pix', swap(2 * k)))]
    dot_general x6 -> x0, matrix products: 23.3 us -> none  [the longest x3 13 us: matmul_hi(): jnp.dot(left, right, precision=lax.Precision.HIGHEST, preferred_element_t...]
    all_gather x2 -> x0, blocking collectives: 19.8 us -> none  [the longest x1 10 us: body(): new_full = lax.all_gather(new_traces, 'pix', axis=0, tiled=True)]
    ppermute x8 -> x35, waiting for transfers between devices: 11.8 us -> 27.5 us  [the longest x2 11.9 us: line_gather(): last_down = lax.ppermute(last_down, axis, down_pairs)]
    all_gather x1 -> x0, waiting for transfers between devices: 14.5 us -> none  [body(): foot_full = lax.all_gather(footprints, 'tm', axis=0, tiled=True)]
  transfers between devices with their start and end apart: 11 -> 35, of which waited for: 10 -> 13; matrix products, arithmetic and copies ran while one was open for 7% -> 2% of each run, Pallas kernels for 0% -> 28%
where the time goes in v1:
time: 179 us; the launch traced here: 177 us
  starting transfers between devices  73.4 us (41%)
  Pallas kernels  66.2 us (37%)
  waiting for transfers between devices  27.5 us (15%)
  local copies, waits for them, and re-layouts  4.92 us (3%)
  other arithmetic  4.03 us (2%)
    pallas_call x2, Pallas kernels, diffuse_call(): pl.pallas_call(kernel, grid_spec=pltpu.PrefetchScalarGridSpec(num_scalar_...  22.7 us
    ppermute x4, starting transfers between devices, line_scatter(): up_last = lax.ppermute(up_block, axis, up_pairs)  19.6 us
    pallas_call x2, Pallas kernels, products_call(): pl.pallas_call(kernel, grid_spec=pltpu.PrefetchScalarGridSpec(num_scalar_...  12.3 us
    ppermute x2, waiting for transfers between devices, line_gather(): last_down = lax.ppermute(last_down, axis, down_pairs)  11.9 us
    pallas_call x2, Pallas kernels, edges_call(): pl.pallas_call(kernel, grid_spec=pltpu.PrefetchScalarGridSpec(num_scalar_...  9.19 us
    ppermute x2, starting transfers between devices, line_scatter(): lax.ppermute(blocks[count], axis, up_pairs + down_pairs)  7.95 us
    ppermute x1, starting transfers between devices, compute(): arrived = lax.ppermute(send, 'pix', swap(1))  7.78 us
    pallas_call x1, Pallas kernels, numerator_call(): pl.pallas_call(kernel, grid_spec=pltpu.PrefetchScalarGridSpec(num_scalar_...  6.89 us
  transfers between devices with their start and end apart: 35, of which 13 were waited for; matrix products, arithmetic and copies ran while one was open for 2% of the time, Pallas kernels for 28%

profile of v1, /device:TPU:0, one launch (start us, length us, event | category | flops | bytes accessed | tf_op | source)
XLA Modules:
  0.0 177.3 jit_solution(2317055804819570683)
XLA Ops:
  1.3 4.8 %edges.2 = (f32[4,256,256]{2,1,0:T(8,128)}, f32[4,256,256]{2,1,0:T(8,128)}, f32[4,256,256]{2,1,0:T(8,128)}) custom-call(s32[5]{0:T(128)} %stack.46.flags, f32[8,256,512]{2,1,0:T(8,128)} %refs_0_.4, f32[8,256,512]{2,1,0:T(8,128)} %refs_0_.4), custom_call_target="tpu_custom_call" | custom-call | flops 1 | bytes 4194304 | tf_op jit(solution)/shard_map/edges/pallas_call | solution.py:64
  6.1 1.4 collective-permute-start.2
  7.5 1.3 collective-permute-start.6
  8.8 5.6 %collective-permute-start.8 = (f32[64,2048]{1,0:T(8,128)S(1)}, f32[64,2048]{1,0:T(8,128)S(1)}, u32[]{:S(2)}, u32[]{:S(2)}) collective-permute-start(f32[64,2048]{1,0:T(8,128)S(1)} %copy-done), channel_id=1, source_target_pairs={{0,1},{1,2},{2,3},{4,5},{5,6},{6,7},{8,9},{9,10},{10,11},{12,13},{... | collective-permute-start | bytes 1572872 | tf_op jit(solution)/shard_map/ppermute | solution.py:478
  14.4 4.4 %edges.3 = (f32[4,256,256]{2,1,0:T(8,128)}, f32[4,256,256]{2,1,0:T(8,128)}) custom-call(s32[5]{0:T(128)} %stack.46.flags, f32[8,256,512]{2,1,0:T(8,128)} %refs_0_.4, f32[8,256,512]{2,1,0:T(8,128)} %refs_0_.4), custom_call_target="tpu_custom_call" | custom-call | flops 1 | bytes 4194304 | tf_op jit(solution)/shard_map/edges/pallas_call | solution.py:64
  18.9 1.9 %collective-permute-start.4 = (f32[4,256,256]{2,1,0:T(8,128)}, f32[4,256,256]{2,1,0:T(8,128)S(1)}, u32[]{:S(2)}, u32[]{:S(2)}) collective-permute-start(f32[4,256,256]{2,1,0:T(8,128)} %get-tuple-element.29), channel_id=1, source_target_pairs={{0,4},{4,8},{8,12},{12,16},{16,20},{20,24},{24,28},{1,5},{5,9},{9,... | collective-permute-start | bytes 3145736 | tf_op jit(solution)/shard_map/ppermute | solution.py:537
  20.8 4.0 %collective-permute-done.6.refs_1_ = f32[64,2048]{1,0:T(8,128)S(1)} collective-permute-done((f32[64,2048]{1,0:T(8,128)S(1)}, f32[64,2048]{1,0:T(8,128)S(1)}, u32[]{:S(2)}, u32[]{:S(2)}) %collective-permute-start.6) | collective-permute-done | bytes 524320 | tf_op jit(solution)/shard_map/ppermute | solution.py:479
  24.8 1.3 collective-permute-start.7
  26.8 1.3 collective-permute-start.5
  28.1 4.1 %collective-permute-start = (f32[4,256,256]{2,1,0:T(8,128)}, f32[4,256,256]{2,1,0:T(8,128)}, u32[]{:S(2)}, u32[]{:S(2)}) collective-permute-start(f32[4,256,256]{2,1,0:T(8,128)} %get-tuple-element.26), channel_id=1, source_target_pairs={{0,4},{4,8},{8,12},{16,20},{20,24},{24,28},{1,5},{5,9},{9,13},{17,... | collective-permute-start | bytes 3145736 | tf_op jit(solution)/shard_map/ppermute | solution.py:537
  32.2 7.9 %collective-permute-done.7.refs_3_ = f32[64,2048]{1,0:T(8,128)S(1)} collective-permute-done((f32[64,2048]{1,0:T(8,128)S(1)}, f32[64,2048]{1,0:T(8,128)S(1)}, u32[]{:S(2)}, u32[]{:S(2)}) %collective-permute-start.7) | collective-permute-done | bytes 524320 | tf_op jit(solution)/shard_map/ppermute | solution.py:479
  40.1 1.3 collective-permute-start.1
  41.4 6.8 %collective-permute-start.3 = (f32[4,256,256]{2,1,0:T(8,128)}, f32[4,256,256]{2,1,0:T(8,128)}, u32[]{:S(2)}, u32[]{:S(2)}) collective-permute-start(f32[4,256,256]{2,1,0:T(8,128)} %collective-permute-done.2), channel_id=1, source_target_pairs={{28,16},{0,12},{29,17},{1,13},{30,18},{2,14},{31,19},{3,15}} | collective-permute-start | bytes 3145736 | tf_op jit(solution)/shard_map/ppermute | solution.py:536
  48.3 1.3 collective-permute-start.10
  50.3 11.2 %diffuse.2 = (f32[8,256,512]{2,1,0:T(8,128)}, bf16[8,256,512]{2,1,0:T(8,128)(2,1)}) custom-call(s32[5]{0:T(128)} %stack.46.flags, f32[8,256,512]{2,1,0:T(8,128)} %refs_0_.4, f32[4,256,256]{2,1,0:T(8,128)} %copy-done.7, f32[4,256,256]{2,1,0:T(8,128)} %collective-permute-done.5.refs_2_), custom_call_target="tpu_custom_call" | custom-call | flops 104857600 | bytes 8388608 | tf_op jit(solution)/shard_map/diffuse/pallas_call | solution.py:171
  61.5 0.8 copy-done.5
  62.3 5.9 %footprints.1 = (bf16[512,2048]{1,0:T(8,128)(2,1)}, f32[256,256]{1,0:T(8,128)}) custom-call(s32[4]{0:T(128)} %pad_add_fusion.scalars, f32[64,2048]{1,0:T(8,128)} %own_ref.3, f32[64,2048]{1,0:T(8,128)} %copy-done.9, f32[64,2048]{1,0:T(8,128)} %copy-done.5, f32[64,2048]{1,0:T(8,128)} %copy-done.3, f32[64,2048]{1,0:T(8,128)} %copy-done.4, ...), custom_call_target="tpu_custom_call" | custom-call | flops 536870912 | bytes 4194304 | tf_op jit(solution)/shard_map/footprints/pallas_call | solution.py:227
  68.3 11.4 %diffuse.3 = (f32[8,256,512]{2,1,0:T(8,128)}, bf16[8,256,512]{2,1,0:T(8,128)(2,1)}) custom-call(s32[5]{0:T(128)} %stack.46.flags, f32[8,256,512]{2,1,0:T(8,128)} %refs_0_.4, f32[4,256,256]{2,1,0:T(8,128)} %collective-permute-done.refs_1_, f32[4,256,256]{2,1,0:T(8,128)} %collective-permute-done.1.refs_2_, ...), custom_call_target="tpu_custom_call", output_to_operand_aliasing={{0}: (5, {})} | custom-call | flops 104857600 | bytes 8388608 | tf_op jit(solution)/shard_map/diffuse/pallas_call | solution.py:171
  79.7 6.9 %numerator.1 = (f32[4,32,768]{2,1,0:T(8,128)}, f32[4,32,768]{2,1,0:T(8,128)}) custom-call(s32[4]{0:T(128)} %pad_add_fusion.scalars, bf16[512,2048]{1,0:T(8,128)(2,1)} %get-tuple-element.33.foot_ref, f32[256,256]{1,0:T(8,128)} %get-tuple-element.34.gram_ref, bf16[2048,512]{1,0:T(8,128)(2,1)} %bitcast.18, bf16[2048,512]{1,0:T(8,128)(2,1)} %bitcast.21), custom_call_target="tpu_custom_call" | custom-call | flops 3221225472 | bytes 8388608 | tf_op jit(solution)/shard_map/numerator/pallas_call | solution.py:282
  86.6 7.8 %collective-permute-start.14 = (f32[4,32,768]{2,1,0:T(8,128)}, f32[4,32,768]{2,1,0:T(8,128)S(1)}, u32[]{:S(2)}, u32[]{:S(2)}) collective-permute-start(f32[4,32,768]{2,1,0:T(8,128)} %get-tuple-element.38), channel_id=1, source_target_pairs={{0,4},{4,0},{8,12},{12,8},{16,20},{20,16},{24,28},{28,24},{1,5},{5... | collective-permute-start | bytes 1179656 | tf_op jit(solution)/shard_map/ppermute | solution.py:556
  94.5 5.4 %collective-permute-done.12 = f32[2,32,512]{2,1,0:T(8,128)S(1)} collective-permute-done((f32[2,32,512]{2,1,0:T(8,128)S(1)}, f32[2,32,512]{2,1,0:T(8,128)S(1)}, u32[]{:S(2)}, u32[]{:S(2)}) %collective-permute-start.12) | collective-permute-done | bytes 131104 | tf_op jit(solution)/shard_map/ppermute | solution.py:544
  100.0 1.2 fusion
  101.6 0.7 collective-permute-start.16
  102.3 2.4 %collective-permute-start.17 = (f32[32,768]{1,0:T(8,128)S(1)}, f32[32,768]{1,0:T(8,128)S(1)}, u32[]{:S(2)}, u32[]{:S(2)}) collective-permute-start(f32[32,768]{1,0:T(8,128)S(1)} %get-tuple-element.49), channel_id=1, source_target_pairs={{0,24},{4,28},{8,16},{12,20},{16,8},{20,12},{24,0},{28,4},{1,25},{... | collective-permute-start | bytes 294920 | tf_op jit(solution)/shard_map/ppermute | solution.py:559
  104.8 2.2 %collective-permute-done.15.refs_2_ = f32[32,768]{1,0:T(8,128)S(1)} collective-permute-done((f32[32,768]{1,0:T(8,128)S(1)}, f32[32,768]{1,0:T(8,128)S(1)}, u32[]{:S(2)}, u32[]{:S(2)}) %collective-permute-start.15) | collective-permute-done | bytes 98336 | tf_op jit(solution)/shard_map/ppermute | solution.py:559
  106.9 1.7 collective-permute-done.16.refs_3_
  109.9 2.7 %traces.1.refs_0_ = f32[32,512]{1,0:T(8,128)} custom-call(s32[4]{0:T(128)} %pad_add_fusion.scalars, f32[4,32,512]{2,1,0:T(8,128)} %copy-done.8, f32[4,32,512]{2,1,0:T(8,128)} %copy-done.24, f32[4,32,768]{2,1,0:T(8,128)} %get-tuple-element.37.refs_0_, f32[4,32,768]{2,1,0:T(8,128)} %copy-done.6, f32[32,768]{1,0:T(8,128)} %copy-done.26, f32[32,768]{1,0:T(8,128)} %copy-done.27, ...), custom_call_target="tpu_custom_call" | custom-call | flops 25165824 | bytes 1048576 | tf_op jit(solution)/shard_map/traces/pallas_call | solution.py:323
  112.6 1.7 collective-permute-start.18
  114.3 1.8 %collective-permute-start.20 = (f32[32,512]{1,0:T(8,128)}, f32[32,512]{1,0:T(8,128)S(1)}, u32[]{:S(2)}, u32[]{:S(2)}) collective-permute-start(f32[32,512]{1,0:T(8,128)} %traces.1.refs_0_), channel_id=1, source_target_pairs={{0,24},{4,28},{8,16},{12,20},{16,8},{20,12},{24,0},{28,4},{1,25},{... | collective-permute-start | bytes 196616 | tf_op jit(solution)/shard_map/ppermute | solution.py:563
  116.1 1.0 collective-permute-done.18.refs_1_
  117.1 1.7 collective-permute-done.19.refs_2_
  118.8 0.9 collective-permute-done.20.refs_3_
  120.0 0.9 collective-permute-done.24.refs_7_
  121.6 6.4 %products.3 = (f32[64,1280]{1,0:T(8,128)}, f32[64,1280]{1,0:T(8,128)}, f32[64,1280]{1,0:T(8,128)}, f32[64,1280]{1,0:T(8,128)}, f32[64,1280]{1,0:T(8,128)}) custom-call(s32[4]{0:T(128)} %pad_add_fusion.scalars, f32[32,512]{1,0:T(8,128)} %traces.1.refs_0_, f32[32,512]{1,0:T(8,128)} %copy-done.14, f32[32,512]{1,0:T(8,128)} %copy-done.15, f32[32,512]{1,0:T(8,128)} %copy-done.16, ...), custom_call_target="tpu_custom_call" | custom-call | flops 1073741824 | bytes 3145728 | tf_op jit(solution)/shard_map/products/pallas_call | solution.py:399
  128.1 6.5 %collective-permute-start.30 = (f32[64,1280]{1,0:T(8,128)}, f32[64,1280]{1,0:T(8,128)S(1)}, u32[]{:S(2)}, u32[]{:S(2)}) collective-permute-start(f32[64,1280]{1,0:T(8,128)} %get-tuple-element.47), channel_id=1, source_target_pairs={{0,1},{3,2},{4,5},{7,6},{8,9},{11,10},{12,13},{15,14},{16,17},{19,... | collective-permute-start | bytes 983048 | tf_op jit(solution)/shard_map/ppermute | solution.py:490
  134.6 5.9 %products.2 = (f32[64,1024]{1,0:T(8,128)}, f32[64,1024]{1,0:T(8,128)}, f32[64,1024]{1,0:T(8,128)}, f32[64,1024]{1,0:T(8,128)}, f32[64,1024]{1,0:T(8,128)}) custom-call(s32[4]{0:T(128)} %pad_add_fusion.scalars, f32[32,512]{1,0:T(8,128)} %traces.1.refs_0_, f32[32,512]{1,0:T(8,128)} %copy-done.14, f32[32,512]{1,0:T(8,128)} %copy-done.15, f32[32,512]{1,0:T(8,128)} %copy-done.16, ...), custom_call_target="tpu_custom_call" | custom-call | flops 1073741824 | bytes 3145728 | tf_op jit(solution)/shard_map/products/pallas_call | solution.py:399
  140.5 1.4 collective-permute-start.25
  142.9 4.9 %collective-permute-start.31 = (f32[64,1280]{1,0:T(8,128)S(1)}, f32[64,1280]{1,0:T(8,128)S(1)}, u32[]{:S(2)}, u32[]{:S(2)}) collective-permute-start(f32[64,1280]{1,0:T(8,128)S(1)} %add.51), channel_id=1, source_target_pairs={{0,1},{1,2},{4,5},{5,6},{8,9},{9,10},{12,13},{13,14},{16,17},{17,1... | collective-permute-start | bytes 983048 | tf_op jit(solution)/shard_map/ppermute | solution.py:496
  147.8 1.1 collective-permute-done.25
  148.9 1.0 add.48
  150.6 4.9 %collective-permute-start.26 = (f32[64,1024]{1,0:T(8,128)S(1)}, f32[64,1024]{1,0:T(8,128)S(1)}, u32[]{:S(2)}, u32[]{:S(2)}) collective-permute-start(f32[64,1024]{1,0:T(8,128)S(1)} %add.48), channel_id=1, source_target_pairs={{0,1},{1,2},{4,5},{5,6},{8,9},{9,10},{12,13},{13,14},{16,17},{17,1... | collective-permute-start | bytes 786440 | tf_op jit(solution)/shard_map/ppermute | solution.py:496
  155.6 1.3 collective-permute-start.34
  157.0 5.2 %collective-permute-start.32 = (f32[64,1280]{1,0:T(8,128)S(1)}, f32[64,1280]{1,0:T(8,128)S(1)}, u32[]{:S(2)}, u32[]{:S(2)}) collective-permute-start(f32[64,1280]{1,0:T(8,128)S(1)} %add.52), channel_id=1, source_target_pairs={{0,1},{1,2},{2,3},{4,5},{5,6},{6,7},{8,9},{9,10},{10,11},{12,13},{... | collective-permute-start | bytes 983048 | tf_op jit(solution)/shard_map/ppermute | solution.py:496
  162.2 1.0 add.50
  163.1 1.3 collective-permute-start.29
  164.5 4.6 %collective-permute-start.27 = (f32[64,1024]{1,0:T(8,128)S(1)}, f32[64,1024]{1,0:T(8,128)S(1)}, u32[]{:S(2)}, u32[]{:S(2)}) collective-permute-start(f32[64,1024]{1,0:T(8,128)S(1)} %add.49), channel_id=1, source_target_pairs={{0,1},{1,2},{2,3},{4,5},{5,6},{6,7},{8,9},{9,10},{10,11},{12,13},{... | collective-permute-start | bytes 786440 | tf_op jit(solution)/shard_map/ppermute | solution.py:496
  170.0 3.2 %final.2.refs_6_ = f32[64,2048]{1,0:T(8,128)} custom-call(s32[4]{0:T(128)} %pad_add_fusion.scalars, f32[64,2048]{1,0:T(8,128)} %own_ref.3, bf16[512,2048]{1,0:T(8,128)(2,1)} %get-tuple-element.33.foot_ref, f32[64,1280]{1,0:T(8,128)} %get-tuple-element.44.refs_0_.refs_3_, f32[64,1280]{1,0:T(8,128)} %copy-done.2, f32[64,1280]{1,0:T(8,128)} %copy-done.1, ...), custom_call_target="tpu_custom_call" | custom-call | flops 100663296 | bytes 2359296 | tf_op jit(solution)/shard_map/final/pallas_call | solution.py:453
  174.0 3.2 %final.3 = f32[64,2048]{1,0:T(8,128)} custom-call(s32[4]{0:T(128)} %pad_add_fusion.scalars, f32[64,2048]{1,0:T(8,128)} %own_ref.3, bf16[512,2048]{1,0:T(8,128)(2,1)} %get-tuple-element.33.foot_ref, f32[64,1024]{1,0:T(8,128)} %get-tuple-element.39.refs_0_, f32[64,1024]{1,0:T(8,128)} %copy-done.23, ...), custom_call_target="tpu_custom_call", output_to_operand_aliasing={{}: (9, {})} | custom-call | flops 100663296 | bytes 2359296 | tf_op jit(solution)/shard_map/final/pallas_call | solution.py:453
  (103 shorter events, 8.4 us)
Async XLA Ops:
  1.3 6.2 %copy-start = (f32[64,2048]{1,0:T(8,128)S(1)}, f32[64,2048]{1,0:T(8,128)}, u32[]{:S(2)}) copy-start(f32[64,2048]{1,0:T(8,128)} %own_ref.3) | copy-start | bytes 1572868
  6.1 44.2 %copy-start.25 = (f32[32,512]{1,0:T(8,128)S(1)}, f32[32,512]{1,0:T(8,128)}, u32[]{:S(2)}) copy-start(f32[32,512]{1,0:T(8,128)} %param.5) | copy-start | bytes 196612
  6.1 22.0 %collective-permute-start.2 = (f32[4,256,256]{2,1,0:T(8,128)}, f32[4,256,256]{2,1,0:T(8,128)}, u32[]{:S(2)}, u32[]{:S(2)}) collective-permute-start(f32[4,256,256]{2,1,0:T(8,128)} %get-tuple-element.28), channel_id=1, source_target_pairs={{12,28},{16,0},{13,29},{17,1},{14,30},{18,2},{15,31},{19,3}} | collective-permute-start | bytes 3145736 | tf_op jit(solution)/shard_map/ppermute | solution.py:535
  7.5 17.2 %collective-permute-start.6 = (f32[64,2048]{1,0:T(8,128)S(1)}, f32[64,2048]{1,0:T(8,128)S(1)}, u32[]{:S(2)}, u32[]{:S(2)}) collective-permute-start(f32[64,2048]{1,0:T(8,128)S(1)} %copy-done), channel_id=1, source_target_pairs={{1,0},{2,1},{3,2},{5,4},{6,5},{7,6},{9,8},{10,9},{11,10},{13,12},{... | collective-permute-start | bytes 1572872 | tf_op jit(solution)/shard_map/ppermute | solution.py:479
  8.8 17.2 %collective-permute-start.8 = (f32[64,2048]{1,0:T(8,128)S(1)}, f32[64,2048]{1,0:T(8,128)S(1)}, u32[]{:S(2)}, u32[]{:S(2)}) collective-permute-start(f32[64,2048]{1,0:T(8,128)S(1)} %copy-done), channel_id=1, source_target_pairs={{0,1},{1,2},{2,3},{4,5},{5,6},{6,7},{8,9},{9,10},{10,11},{12,13},{... | collective-permute-start | bytes 1572872 | tf_op jit(solution)/shard_map/ppermute | solution.py:478
  18.9 29.4 %collective-permute-start.4 = (f32[4,256,256]{2,1,0:T(8,128)}, f32[4,256,256]{2,1,0:T(8,128)S(1)}, u32[]{:S(2)}, u32[]{:S(2)}) collective-permute-start(f32[4,256,256]{2,1,0:T(8,128)} %get-tuple-element.29), channel_id=1, source_target_pairs={{0,4},{4,8},{8,12},{12,16},{16,20},{20,24},{24,28},{1,5},{5,9},{9,... | collective-permute-start | bytes 3145736 | tf_op jit(solution)/shard_map/ppermute | solution.py:537
  24.8 23.5 %copy-start.9 = (f32[64,2048]{1,0:T(8,128)}, f32[64,2048]{1,0:T(8,128)S(1)}, u32[]{:S(2)}) copy-start(f32[64,2048]{1,0:T(8,128)S(1)} %collective-permute-done.6.refs_1_) | copy-start | bytes 1572868
  24.8 15.3 %collective-permute-start.7 = (f32[64,2048]{1,0:T(8,128)S(1)}, f32[64,2048]{1,0:T(8,128)S(1)}, u32[]{:S(2)}, u32[]{:S(2)}) collective-permute-start(f32[64,2048]{1,0:T(8,128)S(1)} %collective-permute-done.6.refs_1_), channel_id=1, source_target_pairs={{1,0},{2,1},{5,4},{6,5},{9,8},{10,9},{13,12},{14,13},{17,16},{18,1... | collective-permute-start | bytes 1572872 | tf_op jit(solution)/shard_map/ppermute | solution.py:479
  26.1 15.3 %copy-start.10 = (f32[64,2048]{1,0:T(8,128)}, f32[64,2048]{1,0:T(8,128)S(1)}, u32[]{:S(2)}) copy-start(f32[64,2048]{1,0:T(8,128)S(1)} %collective-permute-done.8.refs_6_) | copy-start | bytes 1572868
  26.1 15.3 %collective-permute-start.9 = (f32[64,2048]{1,0:T(8,128)S(1)}, f32[64,2048]{1,0:T(8,128)S(1)}, u32[]{:S(2)}, u32[]{:S(2)}) collective-permute-start(f32[64,2048]{1,0:T(8,128)S(1)} %collective-permute-done.8.refs_6_), channel_id=1, source_target_pairs={{1,2},{2,3},{5,6},{6,7},{9,10},{10,11},{13,14},{14,15},{17,18},{18... | collective-permute-start | bytes 1572872 | tf_op jit(solution)/shard_map/ppermute | solution.py:478
  26.8 23.5 %collective-permute-start.5 = (f32[4,256,256]{2,1,0:T(8,128)}, f32[4,256,256]{2,1,0:T(8,128)}, u32[]{:S(2)}, u32[]{:S(2)}) collective-permute-start(f32[4,256,256]{2,1,0:T(8,128)} %get-tuple-element.30), channel_id=1, source_target_pairs={{4,0},{8,4},{12,8},{16,12},{20,16},{24,20},{28,24},{5,1},{9,5},{13... | collective-permute-start | bytes 3145736 | tf_op jit(solution)/shard_map/ppermute | solution.py:538
  28.1 40.2 %collective-permute-start = (f32[4,256,256]{2,1,0:T(8,128)}, f32[4,256,256]{2,1,0:T(8,128)}, u32[]{:S(2)}, u32[]{:S(2)}) collective-permute-start(f32[4,256,256]{2,1,0:T(8,128)} %get-tuple-element.26), channel_id=1, source_target_pairs={{0,4},{4,8},{8,12},{16,20},{20,24},{24,28},{1,5},{5,9},{9,13},{17,... | collective-permute-start | bytes 3145736 | tf_op jit(solution)/shard_map/ppermute | solution.py:537
  40.1 21.4 %copy-start.3 = (f32[64,2048]{1,0:T(8,128)}, f32[64,2048]{1,0:T(8,128)S(1)}, u32[]{:S(2)}) copy-start(f32[64,2048]{1,0:T(8,128)S(1)} %collective-permute-done.7.refs_3_) | copy-start | bytes 1572868
  40.1 28.2 %collective-permute-start.1 = (f32[4,256,256]{2,1,0:T(8,128)}, f32[4,256,256]{2,1,0:T(8,128)}, u32[]{:S(2)}, u32[]{:S(2)}) collective-permute-start(f32[4,256,256]{2,1,0:T(8,128)} %get-tuple-element.27), channel_id=1, source_target_pairs={{4,0},{8,4},{12,8},{20,16},{24,20},{28,24},{5,1},{9,5},{13,9},{21,... | collective-permute-start | bytes 3145736 | tf_op jit(solution)/shard_map/ppermute | solution.py:538
  41.4 20.1 %copy-start.4 = (f32[64,2048]{1,0:T(8,128)}, f32[64,2048]{1,0:T(8,128)S(1)}, u32[]{:S(2)}) copy-start(f32[64,2048]{1,0:T(8,128)S(1)} %collective-permute-done.9.refs_4_) | copy-start | bytes 1572868
  41.4 26.9 %collective-permute-start.3 = (f32[4,256,256]{2,1,0:T(8,128)}, f32[4,256,256]{2,1,0:T(8,128)}, u32[]{:S(2)}, u32[]{:S(2)}) collective-permute-start(f32[4,256,256]{2,1,0:T(8,128)} %collective-permute-done.2), channel_id=1, source_target_pairs={{28,16},{0,12},{29,17},{1,13},{30,18},{2,14},{31,19},{3,15}} | collective-permute-start | bytes 3145736 | tf_op jit(solution)/shard_map/ppermute | solution.py:536
  48.3 13.2 %collective-permute-start.10 = (f32[64,2048]{1,0:T(8,128)S(1)}, f32[64,2048]{1,0:T(8,128)S(1)}, u32[]{:S(2)}, u32[]{:S(2)}) collective-permute-start(f32[64,2048]{1,0:T(8,128)S(1)} %broadcast_select_fusion), channel_id=1, source_target_pairs={{2,3},{1,0},{6,7},{5,4},{10,11},{9,8},{14,15},{13,12},{18,19},{17,... | collective-permute-start | bytes 1572872 | tf_op jit(solution)/shard_map/ppermute | solution.py:476
  50.3 44.1 %collective-permute-start.11 = (f32[1,32,512]{2,1,0:T(8,128)S(1)}, f32[1,32,512]{2,1,0:T(8,128)S(1)}, u32[]{:S(2)}, u32[]{:S(2)}) collective-permute-start(f32[1,32,512]{2,1,0:T(8,128)S(1)} %bitcast.24), channel_id=1, source_target_pairs={{0,8},{4,12},{8,0},{12,4},{16,24},{20,28},{24,16},{28,20},{1,9},{5... | collective-permute-start | bytes 196616 | tf_op jit(solution)/shard_map/ppermute | solution.py:544
  86.6 13.4 %collective-permute-start.14 = (f32[4,32,768]{2,1,0:T(8,128)}, f32[4,32,768]{2,1,0:T(8,128)S(1)}, u32[]{:S(2)}, u32[]{:S(2)}) collective-permute-start(f32[4,32,768]{2,1,0:T(8,128)} %get-tuple-element.38), channel_id=1, source_target_pairs={{0,4},{4,0},{8,12},{12,8},{16,20},{20,16},{24,28},{28,24},{1,5},{5... | collective-permute-start | bytes 1179656 | tf_op jit(solution)/shard_map/ppermute | solution.py:556
  94.4 5.5 %collective-permute-start.12 = (f32[2,32,512]{2,1,0:T(8,128)S(1)}, f32[2,32,512]{2,1,0:T(8,128)S(1)}, u32[]{:S(2)}, u32[]{:S(2)}) collective-permute-start(f32[2,32,512]{2,1,0:T(8,128)S(1)} %pad_maximum_fusion.1), channel_id=1, source_target_pairs={{0,16},{4,20},{8,24},{12,28},{16,0},{20,4},{24,8},{28,12},{1,17},{... | collective-permute-start | bytes 393224 | tf_op jit(solution)/shard_map/ppermute | solution.py:544
  99.9 8.7 %copy-start.8 = (f32[4,32,512]{2,1,0:T(8,128)}, f32[4,32,512]{2,1,0:T(8,128)S(1)}, u32[]{:S(2)}) copy-start(f32[4,32,512]{2,1,0:T(8,128)S(1)} %pad_maximum_fusion.near_ref) | copy-start | bytes 786436
  99.9 4.8 %collective-permute-start.13 = (f32[4,32,512]{2,1,0:T(8,128)S(1)}, f32[4,32,512]{2,1,0:T(8,128)S(1)}, u32[]{:S(2)}, u32[]{:S(2)}) collective-permute-start(f32[4,32,512]{2,1,0:T(8,128)S(1)} %pad_maximum_fusion.near_ref), channel_id=1, source_target_pairs={{0,4},{4,0},{8,12},{12,8},{16,20},{20,16},{24,28},{28,24},{1,5},{5... | collective-permute-start | bytes 786440 | tf_op jit(solution)/shard_map/ppermute | solution.py:546
  100.0 8.6 %copy-start.6 = (f32[4,32,768]{2,1,0:T(8,128)}, f32[4,32,768]{2,1,0:T(8,128)S(1)}, u32[]{:S(2)}) copy-start(f32[4,32,768]{2,1,0:T(8,128)S(1)} %collective-permute-done.14.refs_1_) | copy-start | bytes 1179652
  101.2 5.7 %collective-permute-start.15 = (f32[32,768]{1,0:T(8,128)S(1)}, f32[32,768]{1,0:T(8,128)S(1)}, u32[]{:S(2)}, u32[]{:S(2)}) collective-permute-start(f32[32,768]{1,0:T(8,128)S(1)} %get-tuple-element.51), channel_id=1, source_target_pairs={{0,8},{4,12},{8,0},{12,4},{16,24},{20,28},{24,16},{28,20},{1,9},{5... | collective-permute-start | bytes 294920 | tf_op jit(solution)/shard_map/ppermute | solution.py:559
  101.6 7.0 %collective-permute-start.16 = (f32[32,768]{1,0:T(8,128)S(1)}, f32[32,768]{1,0:T(8,128)S(1)}, u32[]{:S(2)}, u32[]{:S(2)}) collective-permute-start(f32[32,768]{1,0:T(8,128)S(1)} %get-tuple-element.50), channel_id=1, source_target_pairs={{0,16},{4,20},{8,24},{12,28},{16,0},{20,4},{24,8},{28,12},{1,17},{... | collective-permute-start | bytes 294920 | tf_op jit(solution)/shard_map/ppermute | solution.py:559
  102.3 6.3 %collective-permute-start.17 = (f32[32,768]{1,0:T(8,128)S(1)}, f32[32,768]{1,0:T(8,128)S(1)}, u32[]{:S(2)}, u32[]{:S(2)}) collective-permute-start(f32[32,768]{1,0:T(8,128)S(1)} %get-tuple-element.49), channel_id=1, source_target_pairs={{0,24},{4,28},{8,16},{12,20},{16,8},{20,12},{24,0},{28,4},{1,25},{... | collective-permute-start | bytes 294920 | tf_op jit(solution)/shard_map/ppermute | solution.py:559
  104.8 3.9 %copy-start.24 = (f32[4,32,512]{2,1,0:T(8,128)}, f32[4,32,512]{2,1,0:T(8,128)S(1)}, u32[]{:S(2)}) copy-start(f32[4,32,512]{2,1,0:T(8,128)S(1)} %collective-permute-done.13.far_ref) | copy-start | bytes 786436
  112.6 4.5 %collective-permute-start.18 = (f32[32,512]{1,0:T(8,128)}, f32[32,512]{1,0:T(8,128)S(1)}, u32[]{:S(2)}, u32[]{:S(2)}) collective-permute-start(f32[32,512]{1,0:T(8,128)} %traces.1.refs_0_), channel_id=1, source_target_pairs={{0,8},{4,12},{8,0},{12,4},{16,24},{20,28},{24,16},{28,20},{1,9},{5... | collective-permute-start | bytes 196616 | tf_op jit(solution)/shard_map/ppermute | solution.py:563
  114.3 4.5 %collective-permute-start.19 = (f32[32,512]{1,0:T(8,128)}, f32[32,512]{1,0:T(8,128)S(1)}, u32[]{:S(2)}, u32[]{:S(2)}) collective-permute-start(f32[32,512]{1,0:T(8,128)} %traces.1.refs_0_), channel_id=1, source_target_pairs={{0,16},{4,20},{8,24},{12,28},{16,0},{20,4},{24,8},{28,12},{1,17},{... | collective-permute-start | bytes 196616 | tf_op jit(solution)/shard_map/ppermute | solution.py:563
  114.3 5.4 %collective-permute-start.20 = (f32[32,512]{1,0:T(8,128)}, f32[32,512]{1,0:T(8,128)S(1)}, u32[]{:S(2)}, u32[]{:S(2)}) collective-permute-start(f32[32,512]{1,0:T(8,128)} %traces.1.refs_0_), channel_id=1, source_target_pairs={{0,24},{4,28},{8,16},{12,20},{16,8},{20,12},{24,0},{28,4},{1,25},{... | collective-permute-start | bytes 196616 | tf_op jit(solution)/shard_map/ppermute | solution.py:563
  116.1 3.6 %collective-permute-start.21 = (f32[32,512]{1,0:T(8,128)}, f32[32,512]{1,0:T(8,128)S(1)}, u32[]{:S(2)}, u32[]{:S(2)}) collective-permute-start(f32[32,512]{1,0:T(8,128)} %traces.1.refs_0_), channel_id=1, source_target_pairs={{0,4},{4,0},{8,12},{12,8},{16,20},{20,16},{24,28},{28,24},{1,5},{5... | collective-permute-start | bytes 196616 | tf_op jit(solution)/shard_map/ppermute | solution.py:566
  117.1 2.6 %collective-permute-start.22 = (f32[32,512]{1,0:T(8,128)S(1)}, f32[32,512]{1,0:T(8,128)S(1)}, u32[]{:S(2)}, u32[]{:S(2)}) collective-permute-start(f32[32,512]{1,0:T(8,128)S(1)} %collective-permute-done.18.refs_1_), channel_id=1, source_target_pairs={{0,4},{4,0},{8,12},{12,8},{16,20},{20,16},{24,28},{28,24},{1,5},{5... | collective-permute-start | bytes 196616 | tf_op jit(solution)/shard_map/ppermute | solution.py:566
  118.8 1.3 collective-permute-start.23
  119.7 1.3 collective-permute-start.24
  128.1 14.1 %copy-start.13 = (f32[64,1280]{1,0:T(8,128)S(1)}, f32[64,1280]{1,0:T(8,128)}, u32[]{:S(2)}) copy-start(f32[64,1280]{1,0:T(8,128)} %get-tuple-element.46) | copy-start | bytes 983044
  128.1 27.5 %copy-start.12 = (f32[64,1280]{1,0:T(8,128)S(1)}, f32[64,1280]{1,0:T(8,128)}, u32[]{:S(2)}) copy-start(f32[64,1280]{1,0:T(8,128)} %get-tuple-element.48) | copy-start | bytes 983044
  128.1 28.8 %copy-start.11 = (f32[64,1280]{1,0:T(8,128)S(1)}, f32[64,1280]{1,0:T(8,128)}, u32[]{:S(2)}) copy-start(f32[64,1280]{1,0:T(8,128)} %get-tuple-element.45) | copy-start | bytes 983044
  128.1 14.1 %collective-permute-start.30 = (f32[64,1280]{1,0:T(8,128)}, f32[64,1280]{1,0:T(8,128)S(1)}, u32[]{:S(2)}, u32[]{:S(2)}) collective-permute-start(f32[64,1280]{1,0:T(8,128)} %get-tuple-element.47), channel_id=1, source_target_pairs={{0,1},{3,2},{4,5},{7,6},{8,9},{11,10},{12,13},{15,14},{16,17},{19,... | collective-permute-start | bytes 983048 | tf_op jit(solution)/shard_map/ppermute | solution.py:490
  140.5 23.9 %copy-start.21 = (f32[64,1024]{1,0:T(8,128)S(1)}, f32[64,1024]{1,0:T(8,128)}, u32[]{:S(2)}) copy-start(f32[64,1024]{1,0:T(8,128)} %get-tuple-element.40) | copy-start | bytes 786436
  140.5 8.4 %collective-permute-start.25 = (f32[64,1024]{1,0:T(8,128)}, f32[64,1024]{1,0:T(8,128)S(1)}, u32[]{:S(2)}, u32[]{:S(2)}) collective-permute-start(f32[64,1024]{1,0:T(8,128)} %get-tuple-element.42), channel_id=1, source_target_pairs={{0,1},{3,2},{4,5},{7,6},{8,9},{11,10},{12,13},{15,14},{16,17},{19,... | collective-permute-start | bytes 786440 | tf_op jit(solution)/shard_map/ppermute | solution.py:490
  142.2 13.3 %collective-permute-start.33 = (f32[64,1280]{1,0:T(8,128)S(1)}, f32[64,1280]{1,0:T(8,128)S(1)}, u32[]{:S(2)}, u32[]{:S(2)}) collective-permute-start(f32[64,1280]{1,0:T(8,128)S(1)} %add.51), channel_id=1, source_target_pairs={{3,2},{2,1},{7,6},{6,5},{11,10},{10,9},{15,14},{14,13},{19,18},{18... | collective-permute-start | bytes 983048 | tf_op jit(solution)/shard_map/ppermute | solution.py:497
  142.9 14.0 %collective-permute-start.31 = (f32[64,1280]{1,0:T(8,128)S(1)}, f32[64,1280]{1,0:T(8,128)S(1)}, u32[]{:S(2)}, u32[]{:S(2)}) collective-permute-start(f32[64,1280]{1,0:T(8,128)S(1)} %add.51), channel_id=1, source_target_pairs={{0,1},{1,2},{4,5},{5,6},{8,9},{9,10},{12,13},{13,14},{16,17},{17,1... | collective-permute-start | bytes 983048 | tf_op jit(solution)/shard_map/ppermute | solution.py:496
  149.9 12.2 %collective-permute-start.28 = (f32[64,1024]{1,0:T(8,128)S(1)}, f32[64,1024]{1,0:T(8,128)S(1)}, u32[]{:S(2)}, u32[]{:S(2)}) collective-permute-start(f32[64,1024]{1,0:T(8,128)S(1)} %add.48), channel_id=1, source_target_pairs={{3,2},{2,1},{7,6},{6,5},{11,10},{10,9},{15,14},{14,13},{19,18},{18... | collective-permute-start | bytes 786440 | tf_op jit(solution)/shard_map/ppermute | solution.py:497
  150.6 13.8 %collective-permute-start.26 = (f32[64,1024]{1,0:T(8,128)S(1)}, f32[64,1024]{1,0:T(8,128)S(1)}, u32[]{:S(2)}, u32[]{:S(2)}) collective-permute-start(f32[64,1024]{1,0:T(8,128)S(1)} %add.48), channel_id=1, source_target_pairs={{0,1},{1,2},{4,5},{5,6},{8,9},{9,10},{12,13},{13,14},{16,17},{17,1... | collective-permute-start | bytes 786440 | tf_op jit(solution)/shard_map/ppermute | solution.py:496
  155.6 13.5 %collective-permute-start.34 = (f32[64,1280]{1,0:T(8,128)S(1)}, f32[64,1280]{1,0:T(8,128)S(1)}, u32[]{:S(2)}, u32[]{:S(2)}) collective-permute-start(f32[64,1280]{1,0:T(8,128)S(1)} %add.53), channel_id=1, source_target_pairs={{3,2},{2,1},{1,0},{7,6},{6,5},{5,4},{11,10},{10,9},{9,8},{15,14},{... | collective-permute-start | bytes 983048 | tf_op jit(solution)/shard_map/ppermute | solution.py:497
  157.0 12.2 %collective-permute-start.32 = (f32[64,1280]{1,0:T(8,128)S(1)}, f32[64,1280]{1,0:T(8,128)S(1)}, u32[]{:S(2)}, u32[]{:S(2)}) collective-permute-start(f32[64,1280]{1,0:T(8,128)S(1)} %add.52), channel_id=1, source_target_pairs={{0,1},{1,2},{2,3},{4,5},{5,6},{6,7},{8,9},{9,10},{10,11},{12,13},{... | collective-permute-start | bytes 983048 | tf_op jit(solution)/shard_map/ppermute | solution.py:496
  163.1 10.0 %collective-permute-start.29 = (f32[64,1024]{1,0:T(8,128)S(1)}, f32[64,1024]{1,0:T(8,128)S(1)}, u32[]{:S(2)}, u32[]{:S(2)}) collective-permute-start(f32[64,1024]{1,0:T(8,128)S(1)} %add.50), channel_id=1, source_target_pairs={{3,2},{2,1},{1,0},{7,6},{6,5},{5,4},{11,10},{10,9},{9,8},{15,14},{... | collective-permute-start | bytes 786440 | tf_op jit(solution)/shard_map/ppermute | solution.py:497
  164.5 8.8 %collective-permute-start.27 = (f32[64,1024]{1,0:T(8,128)S(1)}, f32[64,1024]{1,0:T(8,128)S(1)}, u32[]{:S(2)}, u32[]{:S(2)}) collective-permute-start(f32[64,1024]{1,0:T(8,128)S(1)} %add.49), channel_id=1, source_target_pairs={{0,1},{1,2},{2,3},{4,5},{5,6},{6,7},{8,9},{9,10},{10,11},{12,13},{... | collective-permute-start | bytes 786440 | tf_op jit(solution)/shard_map/ppermute | solution.py:496
  (16 other events, 20.1 us)

commit v2 on v1

--- a/solution.py
+++ b/solution.py
@@ -14,6 +14,8 @@
 HALVES = 2
 CHUNKS = 2
 
+HERE, CORE, CHIP, FIRST, TURNED, INSIDE, BENT, CORNER = 0, 1, 2, 3, 4, 5, 7, 9
+
 NN = ((1,), (0,))
 NT = ((1,), (1,))
 
@@ -41,6 +43,10 @@
     return value[:half] + value[half:]
 
 
+def grant(mebibytes):
+    return pltpu.CompilerParams(vmem_limit_bytes=mebibytes * 1024 * 1024)
+
+
 def cost(flops, moved):
     return pl.CostEstimate(flops=flops, bytes_accessed=moved, transcendentals=0)
 
@@ -52,30 +58,37 @@
 def edges_call(flags, raw, halo, chunk, frames, with_corner):
     rows, cols, _ = raw.shape
     shift = rows - halo
-
-    def kernel(flags, head_ref, tail_ref, head_out, tail_out, *corner_out):
-        head_out[...] = head_ref[...]
-        tail_out[...] = tail_ref[...]
-        if with_corner:
-            corner_out[0][...] = jnp.where(flags[4] == 1, tail_ref[...], head_ref[...])
-
-    block = (1, cols, frames)
     outs = 3 if with_corner else 2
+
+    def kernel(flags, raw_ref, *refs):
+        out_refs, sems = refs[:outs], refs[outs]
+        starts = [0, shift, flags[CORNER] * shift]
+        copies = [
+            pltpu.make_async_copy(
+                raw_ref.at[pl.ds(starts[k], halo), :, pl.ds(chunk * frames, frames)], out_refs[k], sems.at[k]
+            )
+            for k in range(outs)
+        ]
+        for copy in copies:
+            copy.start()
+        for copy in copies:
+            copy.wait()
+
+    block = (halo, cols, frames)
     return pl.pallas_call(
         kernel,
         grid_spec=pltpu.PrefetchScalarGridSpec(
             num_scalar_prefetch=1,
-            grid=(halo,),
-            in_specs=[
-                pl.BlockSpec(block, lambda i, flags: (i, 0, chunk)),
-                pl.BlockSpec(block, lambda i, flags: (shift + i, 0, chunk)),
-            ],
-            out_specs=[pl.BlockSpec(block, lambda i, flags: (i, 0, 0))] * outs,
-        ),
-        out_shape=[shaped(halo, cols, frames)] * outs,
-        cost_estimate=cost(1, 4 * halo * cols * frames * 4),
+            grid=(1,),
+            in_specs=[pl.BlockSpec(memory_space=pltpu.HBM)],
+            out_specs=[pl.BlockSpec(block, lambda i, flags: (0, 0, 0))] * outs,
+            scratch_shapes=[pltpu.SemaphoreType.DMA((outs,))],
+        ),
+        out_shape=[shaped(*block)] * outs,
+        cost_estimate=cost(1, 2 * outs * halo * cols * frames * 4),
+        compiler_params=grant(8),
         name="edges",
-    )(flags, raw, raw)
+    )(flags, raw)
 
 
 def diffuse_call(flags, raw, halo_up, halo_down, detour, carried, chunk):
@@ -85,37 +98,70 @@
     width = 64
     pad = 8
     extended = rows + 2 * halo
+    inputs = 3 if detour is None else 4
 
     def kernel(flags, *refs):
-        if detour is None:
-            raw_ref, up_ref, down_ref = refs[:3]
-            refs = refs[3:]
-        else:
-            raw_ref, up_ref, down_ref, detour_ref = refs[:4]
-            refs = refs[4:]
+        sources, refs = refs[:inputs], refs[inputs:]
         if carried is not None:
             refs = refs[1:]
-        out_ref, pair_ref, first_buf, second_buf = refs
+        out_ref, pair_ref, first_bufs, second_buf, out_bufs, in_sems, out_sems = refs
+        group = pl.program_id(0)
+        slot = lax.rem(group, 2)
+        inside = pl.ds(pad, cols)
+
+        def fetches(at):
+            here = lax.rem(at, 2)
+            lanes = pl.ds(pl.multiple_of(at * LANES, LANES), LANES)
+            wide = pl.ds(pl.multiple_of(chunk * frames + at * LANES, LANES), LANES)
+
+            def one(ref, cut, start, count, part):
+                return pltpu.make_async_copy(
+                    ref.at[:, :, cut], first_bufs.at[here, pl.ds(start, count), inside, :], in_sems.at[here, part]
+                )
+
+            made = [(None, one(sources[0], wide, halo, rows, 0))]
+            for part, start, source in ((1, 0, 1), (2, halo + rows, 2)):
+                plain = one(sources[source], lanes, start, halo, part)
+                if detour is None:
+                    made.append((None, plain))
+                else:
+                    made.append((flags[BENT + part - 1] == 0, plain))
+                    made.append((flags[BENT + part - 1] == 1, one(sources[3], lanes, start, halo, part)))
+            return made
+
+        def run(at, act):
+            for condition, copy in fetches(at):
+                if condition is None:
+                    act(copy)
+                else:
+                    pl.when(condition)(lambda copy=copy: act(copy))
+
+        def give(at):
+            wide = pl.ds(pl.multiple_of(chunk * frames + at * LANES, LANES), LANES)
+            here = lax.rem(at, 2)
+            return pltpu.make_async_copy(out_bufs.at[here], out_ref.at[:, :, wide], out_sems.at[here])
+
+        @pl.when(group == 0)
+        def _():
+            run(group, lambda copy: copy.start())
+
+        @pl.when(group + 1 < groups)
+        def _():
+            run(group + 1, lambda copy: copy.start())
+
         zero = jnp.zeros((extended, pad, LANES), jnp.float32)
+        first_buf = first_bufs.at[slot]
         for buf in (first_buf, second_buf):
             buf[:, 0:pad, :] = zero
             buf[:, pad + cols :, :] = zero
-        inside = slice(pad, pad + cols)
-        first_buf[0:halo, inside, :] = up_ref[...]
-        first_buf[halo : halo + rows, inside, :] = raw_ref[...]
-        first_buf[halo + rows :, inside, :] = down_ref[...]
-        if detour is not None:
-
-            @pl.when(flags[2] == 1)
-            def _():
-                first_buf[0:halo, inside, :] = detour_ref[...]
-
-            @pl.when(flags[3] == 1)
-            def _():
-                first_buf[halo + rows :, inside, :] = detour_ref[...]
-
-        scale_up = step_scale * flags[0].astype(jnp.float32)
-        scale_down = step_scale * flags[1].astype(jnp.float32)
+        run(group, lambda copy: copy.wait())
+
+        @pl.when(group >= 2)
+        def _():
+            give(group - 2).wait()
+
+        scale_up = step_scale * flags[INSIDE].astype(jnp.float32)
+        scale_down = step_scale * flags[INSIDE + 1].astype(jnp.float32)
         head = lax.broadcasted_iota(jnp.int32, (width, LANES), 0) == 0
         bufs = (first_buf, second_buf)
         for step in range(SUBSTEPS):
@@ -145,7 +191,7 @@
                     if step + 1 < SUBSTEPS:
                         dst[row, pl.ds(base, width), :] = value
                     else:
-                        out_ref[row - halo, pl.ds(col, width), :] = value
+                        out_bufs[slot, row - halo, pl.ds(col, width), :] = value
                         high, low = split(value)
                         pair_ref[row - halo, pl.ds(col, width), 0:LANES] = high
                         pair_ref[row - halo, pl.ds(col, width), LANES:] = low
@@ -154,35 +200,42 @@
 
             edge = tuple(flux_quarter(src[row, pl.ds(pad, width), :]) for row in middle)
             lax.fori_loop(0, cols // width, tile, edge)
-
-    def spec(count, at):
-        return pl.BlockSpec((count, cols, LANES), lambda i, flags: (0, 0, at + i))
-
+        give(group).start()
+
+        @pl.when(group == groups - 1)
+        def _():
+            if groups > 1:
+                give(group - 1).wait()
+            give(group).wait()
+
+    outside = pl.BlockSpec(memory_space=pltpu.HBM)
     operands = [flags, raw, halo_up, halo_down]
-    in_specs = [spec(rows, chunk * groups), spec(halo, 0), spec(halo, 0)]
     if detour is not None:
         operands.append(detour)
-        in_specs.append(spec(halo, 0))
     aliases = {}
     if carried is not None:
         operands.append(carried)
-        in_specs.append(pl.BlockSpec(memory_space=pl.ANY))
         aliases = {len(operands) - 1: 0}
+    padded = (extended, cols + 2 * pad, LANES)
     return pl.pallas_call(
         kernel,
         grid_spec=pltpu.PrefetchScalarGridSpec(
             num_scalar_prefetch=1,
             grid=(groups,),
-            in_specs=in_specs,
-            out_specs=[
-                spec(rows, chunk * groups),
-                pl.BlockSpec((rows, cols, 2 * LANES), lambda i, flags: (0, 0, i)),
+            in_specs=[outside] * (len(operands) - 1),
+            out_specs=[outside, pl.BlockSpec((rows, cols, 2 * LANES), lambda i, flags: (0, 0, i))],
+            scratch_shapes=[
+                pltpu.VMEM((2, *padded), jnp.float32),
+                pltpu.VMEM(padded, jnp.float32),
+                pltpu.VMEM((2, rows, cols, LANES), jnp.float32),
+                pltpu.SemaphoreType.DMA((2, 3)),
+                pltpu.SemaphoreType.DMA((2,)),
             ],
-            scratch_shapes=[pltpu.VMEM((extended, cols + 2 * pad, LANES), jnp.float32)] * 2,
         ),
         out_shape=[shaped(rows, cols, total), shaped(rows, cols, 2 * frames, dtype=jnp.bfloat16)],
         input_output_aliases=aliases,
         cost_estimate=cost(rows * cols * frames * 200, rows * cols * frames * 16),
+        compiler_params=grant(16),
         name="diffuse",
     )(*operands)
 
@@ -198,7 +251,7 @@
         own_ref = refs[0]
         pair_refs = [(refs[1 + 2 * k], refs[2 + 2 * k]) for k in range(count - 1)]
         out_ref, gram_ref, total = refs[2 * count - 1 :]
-        here = scalars[0]
+        here = scalars[HERE]
         step = pl.program_id(0)
 
         def put(slot, value):
@@ -238,6 +291,7 @@
         ),
         out_shape=[shaped(2 * rank, pixel_count, dtype=jnp.bfloat16), shaped(rank, rank)],
         cost_estimate=cost(4 * rank * rank * pixel_count, 8 * rank * pixel_count),
+        compiler_params=grant(8),
         name="footprints",
     )(scalars, own, *flat)
 
@@ -270,9 +324,9 @@
         @pl.when(step == steps - 1)
         def _():
             total[:, frames * len(movies) :] = gram_ref[...]
-            core = scalars[1]
+            core = scalars[CORE]
             for k in range(chips):
-                chip = scalars[2] ^ k
+                chip = scalars[CHIP] ^ k
                 mine = pl.multiple_of((2 * chip + core) * trace_rows, trace_rows)
                 other = pl.multiple_of((2 * chip + 1 - core) * trace_rows, trace_rows)
                 keep_ref[k] = total[pl.ds(mine, trace_rows), :]
@@ -294,6 +348,7 @@
         ),
         out_shape=[shaped(chips, trace_rows, columns)] * 2,
         cost_estimate=cost(8 * rank * pixel_count * columns, 4 * pixel_count * (rank + columns)),
+        compiler_params=grant(10),
         name="numerator",
     )(scalars, foot, gram, *movies)
 
@@ -305,11 +360,11 @@
     chips = near.shape[0]
 
     def kernel(scalars, near_ref, far_ref, *refs):
-        part_refs, (out_ref, full) = refs[:-2], refs[-2:]
+        part_refs, (out_ref, copy_ref, full) = refs[:-3], refs[-3:]
         for k in range(chips):
-            device = 2 * (scalars[2] ^ k) + scalars[1]
+            device = 2 * (scalars[CHIP] ^ k) + scalars[CORE]
             full[pl.ds(pl.multiple_of(device * trace_rows, trace_rows), trace_rows), :] = near_ref[k]
-            device = 2 * (scalars[2] ^ k) + 1 - scalars[1]
+            device = 2 * (scalars[CHIP] ^ k) + 1 - scalars[CORE]
             full[pl.ds(pl.multiple_of(device * trace_rows, trace_rows), trace_rows), :] = far_ref[k]
         total = part_refs[0][0] + part_refs[1][0]
         for part_ref in part_refs[2:]:
@@ -317,7 +372,9 @@
         gram = stacked(total[:, frames:])
         high, low = split(full[...])
         below = fold(dot(gram, high, NN)) + dot(gram[0:trace_rows], low, NN)
-        out_ref[...] = near_ref[0] * total[:, 0:frames] / below
+        value = near_ref[0] * total[:, 0:frames] / below
+        out_ref[...] = value
+        copy_ref[...] = value
 
     whole = pl.BlockSpec(near.shape, lambda k, s: (0, 0, 0))
     return pl.pallas_call(
@@ -328,11 +385,12 @@
             in_specs=[whole, whole]
             + [pl.BlockSpec((1, trace_rows, columns), lambda k, s: (0, 0, 0))] * 2
             + [pl.BlockSpec((trace_rows, columns), lambda k, s: (0, 0))] * len(parts),
-            out_specs=pl.BlockSpec((trace_rows, frames), lambda k, s: (0, 0)),
+            out_specs=[pl.BlockSpec((trace_rows, frames), lambda k, s: (0, 0))] * 2,
             scratch_shapes=[pltpu.VMEM((rank, frames), jnp.float32)],
         ),
-        out_shape=shaped(trace_rows, frames),
+        out_shape=[shaped(trace_rows, frames)] * 2,
         cost_estimate=cost(6 * trace_rows * rank * frames, 8 * rank * frames),
+        compiler_params=grant(6),
         name="traces",
     )(scalars, near, far, keep, arrived, *parts)
 
@@ -357,14 +415,14 @@
         out_refs = refs[:outs]
         full, left, result = refs[outs:]
         step = pl.program_id(0)
-        here = scalars[0]
+        here = scalars[HERE]
 
         @pl.when(step == 0)
         def _():
             for k in range(chips):
-                device = 2 * (scalars[2] ^ k) + scalars[1]
+                device = 2 * (scalars[CHIP] ^ k) + scalars[CORE]
                 full[pl.ds(pl.multiple_of(device * trace_rows, trace_rows), trace_rows), :] = near_refs[k][...]
-                device = 2 * (scalars[2] ^ k) + 1 - scalars[1]
+                device = 2 * (scalars[CHIP] ^ k) + 1 - scalars[CORE]
                 full[pl.ds(pl.multiple_of(device * trace_rows, trace_rows), trace_rows), :] = far_refs[k][...]
             high, low = split(full[...])
             for g in range(groups):
@@ -378,7 +436,7 @@
         def emit(total, at):
             result[...] = total
             for k, out_ref in enumerate(out_refs):
-                slot = lax.rem(here + k, count) if k < count else scalars[3]
+                slot = lax.rem(here + k, count) if k < count else scalars[FIRST]
                 row = pl.multiple_of(slot * share, share)
                 out_ref[:, pl.ds(at, block)] = result[pl.ds(row, share), :]
 
@@ -412,6 +470,7 @@
         ),
         out_shape=[shaped(share, columns)] * outs,
         cost_estimate=cost(8 * rank * part * frames, 4 * part * (frames + rank)),
+        compiler_params=grant(10),
         name="products",
     )(scalars, *near, *far, *movies)
 
@@ -461,18 +520,39 @@
         out_shape=shaped(share, pixel_count),
         input_output_aliases=aliases,
         cost_estimate=cost(6 * share * rank * part, 4 * part * (rank + 5 * share)),
+        compiler_params=grant(8),
         name="final",
     )(*operands)
 
 
-def line_gather(block, axis, count, here):
+def choose_call(scalars, down, up):
+    rows, columns = up.shape
+    block = columns // 2
+
+    def kernel(scalars, down_ref, up_ref, out_ref):
+        out_ref[...] = jnp.where(scalars[TURNED] == 1, down_ref[...], up_ref[...])
+
+    spec = pl.BlockSpec((rows, block), lambda k, s: (0, k))
+    return pl.pallas_call(
+        kernel,
+        grid_spec=pltpu.PrefetchScalarGridSpec(
+            num_scalar_prefetch=1, grid=(2,), in_specs=[spec, spec], out_specs=spec
+        ),
+        out_shape=shaped(rows, columns),
+        cost_estimate=cost(rows * columns, 12 * rows * columns),
+        compiler_params=grant(4),
+        name="choose",
+    )(scalars, down, up)
+
+
+def line_gather(scalars, block, axis, count):
     up, down = {}, {}
     last_up = last_down = block
     for r in range(1, count):
         up_pairs = [(k, k + 1) for k in range(r - 1, count - 1)]
         down_pairs = [(k + 1, k) for k in range(0, count - r)]
         if r == count - 1 and count != 3:
-            merged = jnp.where(here == 1, last_down, last_up) if count > 2 else block
+            merged = choose_call(scalars, last_down, last_up) if count > 2 else block
             last_up = last_down = lax.ppermute(merged, axis, up_pairs + down_pairs)
         else:
             last_up = lax.ppermute(last_up, axis, up_pairs)
@@ -516,11 +596,14 @@
     inner = (pix > 0).astype(jnp.int32)
     outer = (pix < pix_count - 1).astype(jnp.int32)
     corner = (lax.rem(pix, GROUP) == GROUP - 1).astype(jnp.int32)
-    flags = jnp.stack([inner, outer, (lax.rem(pix, GROUP) == 0) * inner, corner * outer, corner]).astype(jnp.int32)
     first_out = lax.rem(here + jnp.where(here == 0, count - 1, 1), count)
-    scalars = jnp.stack([here, core, lax.div(pix, 2), first_out]).astype(jnp.int32)
-
-    pairs = line_gather(footprints, "tm", count, here)
+    turned = (here == 1).astype(jnp.int32)
+    bend_up = (lax.rem(pix, GROUP) == 0) * inner
+    flags = scalars = jnp.stack(
+        [here, core, lax.div(pix, 2), first_out, turned, inner, outer, bend_up, corner * outer, corner]
+    ).astype(jnp.int32)
+
+    pairs = line_gather(scalars, footprints, "tm", count)
 
     bent = [k for k in range(pix_count - 1) if k % GROUP == GROUP - 1] if pix_count % GROUP == 0 else []
     halos = []
@@ -557,10 +640,10 @@
     parts = []
     for k in range(1, keep.shape[0]):
         parts.append(lax.ppermute(keep[k] + arrived[k], "pix", swap(2 * k)))
-    new_traces = traces_call(scalars, keep, arrived, parts, near, far)
-    near = [new_traces]
+    new_traces, again = traces_call(scalars, keep, arrived, parts, near, far)
+    near = [again]
     for k in range(1, keep.shape[0]):
-        near.append(lax.ppermute(new_traces, "pix", swap(2 * k)))
+        near.append(lax.ppermute(again, "pix", swap(2 * k)))
     far = []
     for piece in near:
         far.append(lax.ppermute(piece, "pix", swap(1)))

time: 179 us -> 154 us (0.86)
  Pallas kernels: 66.2 us -> 40.3 us
  waiting for transfers between devices: 27.5 us -> 37.7 us
  other arithmetic: 4.03 us -> 0.26 us
  local copies, waits for them, and re-layouts: 4.92 us -> 2.29 us
  starting transfers between devices: 73.4 us -> 71.4 us
    pallas_call x2, Pallas kernels: 9.19 us -> 1.83 us  [edges_call(): pl.pallas_call(kernel, grid_spec=pltpu.PrefetchScalarGridSpec(num_scalar_...]
    pallas_call x2, Pallas kernels: 12.3 us -> 6.38 us  [products_call(): pl.pallas_call(kernel, grid_spec=pltpu.PrefetchScalarGridSpec(num_scalar_...]
    ppermute x4, waiting for transfers between devices: 0.17 us -> 3.76 us  [line_scatter(): up_last = lax.ppermute(up_block, axis, up_pairs)]
    pallas_call x2, Pallas kernels: 22.7 us -> 19.2 us  [diffuse_call(): pl.pallas_call(kernel, grid_spec=pltpu.PrefetchScalarGridSpec(num_scalar_...]
    ppermute x2, waiting for transfers between devices: 11.9 us -> 15.2 us  [line_gather(): last_down = lax.ppermute(last_down, axis, down_pairs)]
    pallas_call x1, Pallas kernels: 6.89 us -> 3.72 us  [numerator_call(): pl.pallas_call(kernel, grid_spec=pltpu.PrefetchScalarGridSpec(num_scalar_...]
    pallas_call x1, Pallas kernels: 5.92 us -> 2.87 us  [footprints_call(): pl.pallas_call(kernel, grid_spec=pltpu.PrefetchScalarGridSpec(num_scalar_...]
    ppermute x2, waiting for transfers between devices: 1.33 us -> 3.79 us  [line_scatter(): lax.ppermute(blocks[count], axis, up_pairs + down_pairs)]
  transfers between devices with their start and end apart: 35 -> 35, of which waited for: 13 -> 14; matrix products, arithmetic and copies ran while one was open for 2% -> 0% of each run, Pallas kernels for 28% -> 21%
where the time goes in v2:
time: 154 us; the launch traced here: 153 us
  starting transfers between devices  71.4 us (46%)
  Pallas kernels  40.3 us (26%)
  waiting for transfers between devices  37.7 us (24%)
  local copies, waits for them, and re-layouts  2.29 us (1%)
    ppermute x4, starting transfers between devices, line_scatter(): up_last = lax.ppermute(up_block, axis, up_pairs)  19.9 us
    pallas_call x2, Pallas kernels, diffuse_call(): pl.pallas_call(kernel, grid_spec=pltpu.PrefetchScalarGridSpec(num_scalar_...  19.2 us
    ppermute x2, waiting for transfers between devices, line_gather(): last_down = lax.ppermute(last_down, axis, down_pairs)  15.2 us
    ppermute x1, starting transfers between devices, compute(): arrived = lax.ppermute(send, 'pix', swap(1))  7.88 us
    ppermute x2, starting transfers between devices, line_scatter(): lax.ppermute(blocks[count], axis, up_pairs + down_pairs)  6.84 us
    pallas_call x2, Pallas kernels, products_call(): pl.pallas_call(kernel, grid_spec=pltpu.PrefetchScalarGridSpec(num_scalar_...  6.38 us
    ppermute x2, starting transfers between devices, line_gather(): last_up = lax.ppermute(last_up, axis, up_pairs)  6.32 us
    ppermute x1, starting transfers between devices, compute(): detour = lax.ppermute(detour, 'pix', second)  5.97 us
  transfers between devices with their start and end apart: 35, of which 14 were waited for; matrix products, arithmetic and copies ran while one was open for 0% of the time, Pallas kernels for 21%

profile of v2, /device:TPU:0, one launch (start us, length us, event | category | flops | bytes accessed | tf_op | source)
XLA Modules:
  0.0 153.1 jit_solution(5680930333198280637)
XLA Ops:
  0.7 2.2 %copy-done = f32[8,256,512]{2,1,0:T(8,128)S(1)} copy-done((f32[8,256,512]{2,1,0:T(8,128)S(1)}, f32[8,256,512]{2,1,0:T(8,128)}, u32[]{:S(2)}) %copy-start) | copy-done | bytes 4194328
  2.9 1.0 edges.2
  3.9 1.4 collective-permute-start.2
  5.4 1.3 collective-permute-start.6
  6.7 5.6 %collective-permute-start.8 = (f32[64,2048]{1,0:T(8,128)}, f32[64,2048]{1,0:T(8,128)S(1)}, u32[]{:S(2)}, u32[]{:S(2)}) collective-permute-start(f32[64,2048]{1,0:T(8,128)} %own_ref.3), channel_id=1, source_target_pairs={{0,1},{1,2},{2,3},{4,5},{5,6},{6,7},{8,9},{9,10},{10,11},{12,13},{... | collective-permute-start | bytes 1572872 | tf_op jit(solution)/shard_map/ppermute | solution.py:558
  12.3 0.8 edges.3
  13.2 1.5 collective-permute-start.4
  14.7 7.2 %collective-permute-done.6.refs_1_ = f32[64,2048]{1,0:T(8,128)S(1)} collective-permute-done((f32[64,2048]{1,0:T(8,128)}, f32[64,2048]{1,0:T(8,128)S(1)}, u32[]{:S(2)}, u32[]{:S(2)}) %collective-permute-start.6) | collective-permute-done | bytes 524320 | tf_op jit(solution)/shard_map/ppermute | solution.py:559
  21.9 1.3 collective-permute-start.7
  23.9 1.3 collective-permute-start.5
  25.2 3.1 %collective-permute-start = (f32[4,256,256]{2,1,0:T(8,128)S(1)}, f32[4,256,256]{2,1,0:T(8,128)S(1)}, u32[]{:S(2)}, u32[]{:S(2)}) collective-permute-start(f32[4,256,256]{2,1,0:T(8,128)S(1)} %get-tuple-element.28), channel_id=1, source_target_pairs={{0,4},{4,8},{8,12},{16,20},{20,24},{24,28},{1,5},{5,9},{9,13},{17,... | collective-permute-start | bytes 3145736 | tf_op jit(solution)/shard_map/ppermute | solution.py:620
  28.3 8.0 %collective-permute-done.7.down_ref.refs_3_ = f32[64,2048]{1,0:T(8,128)S(1)} collective-permute-done((f32[64,2048]{1,0:T(8,128)S(1)}, f32[64,2048]{1,0:T(8,128)S(1)}, u32[]{:S(2)}, u32[]{:S(2)}) %collective-permute-start.7) | collective-permute-done | bytes 524320 | tf_op jit(solution)/shard_map/ppermute | solution.py:559
  36.3 1.3 collective-permute-start.1
  37.6 6.0 %collective-permute-start.3 = (f32[4,256,256]{2,1,0:T(8,128)S(1)}, f32[4,256,256]{2,1,0:T(8,128)S(1)}, u32[]{:S(2)}, u32[]{:S(2)}) collective-permute-start(f32[4,256,256]{2,1,0:T(8,128)S(1)} %collective-permute-done.2), channel_id=1, source_target_pairs={{28,16},{0,12},{29,17},{1,13},{30,18},{2,14},{31,19},{3,15}} | collective-permute-start | bytes 3145736 | tf_op jit(solution)/shard_map/ppermute | solution.py:619
  44.4 1.3 collective-permute-start.10
  45.8 9.6 %diffuse.2 = (f32[8,256,512]{2,1,0:T(8,128)}, bf16[8,256,512]{2,1,0:T(8,128)(2,1)S(1)}) custom-call(s32[10]{0:T(128)S(1)} %stack.55.flags.scalars, f32[8,256,512]{2,1,0:T(8,128)S(1)} %copy-done.1, f32[4,256,256]{2,1,0:T(8,128)S(1)} %collective-permute-done.4.refs_1_, f32[4,256,256]{2,1,0:T(8,128)S(1)} %collective-permute-done.5.refs_2_), custom_call_target="tpu_custom_call" | custom-call | flops 104857600 | bytes 8388608 | tf_op jit(solution)/shard_map/diffuse/pallas_call | solution.py:220
  56.0 2.9 %footprints.1 = (bf16[512,2048]{1,0:T(8,128)(2,1)S(1)}, f32[256,256]{1,0:T(8,128)S(1)}) custom-call(s32[10]{0:T(128)S(1)} %stack.55.flags.scalars, f32[64,2048]{1,0:T(8,128)S(1)} %copy-done.2, f32[64,2048]{1,0:T(8,128)S(1)} %collective-permute-done.6.refs_1_, f32[64,2048]{1,0:T(8,128)S(1)} %collective-permute-done.10.refs_2_.refs_5_, ...), custom_call_target="tpu_custom_call" | custom-call | flops 536870912 | bytes 4194304 | tf_op jit(solution)/shard_map/footprints/pallas_call | solution.py:280
  58.9 9.6 %diffuse.3 = (f32[8,256,512]{2,1,0:T(8,128)}, bf16[8,256,512]{2,1,0:T(8,128)(2,1)S(1)}) custom-call(s32[10]{0:T(128)S(1)} %stack.55.flags.scalars, f32[8,256,512]{2,1,0:T(8,128)S(1)} %copy-done.1, f32[4,256,256]{2,1,0:T(8,128)S(1)} %collective-permute-done.refs_1_, ...), custom_call_target="tpu_custom_call", output_to_operand_aliasing={{0}: (5, {})} | custom-call | flops 104857600 | bytes 8388608 | tf_op jit(solution)/shard_map/diffuse/pallas_call | solution.py:220
  68.5 3.7 %numerator.1 = (f32[4,32,768]{2,1,0:T(8,128)S(1)}, f32[4,32,768]{2,1,0:T(8,128)S(1)}) custom-call(s32[10]{0:T(128)S(1)} %stack.55.flags.scalars, bf16[512,2048]{1,0:T(8,128)(2,1)S(1)} %get-tuple-element.35.foot_ref, f32[256,256]{1,0:T(8,128)S(1)} %get-tuple-element.36.gram_ref, bf16[2048,512]{1,0:T(8,128)(2,1)S(1)} %bitcast.19, bf16[2048,512]{1,0:T(8,128)(2,1)S(1)} %bitcast.22), custom_call_target="tpu_custom_call" | custom-call | flops 3221225472 | bytes 8388608 | tf_op jit(solution)/shard_map/numerator/pallas_call | solution.py:336
  72.3 7.9 %collective-permute-start.14 = (f32[4,32,768]{2,1,0:T(8,128)S(1)}, f32[4,32,768]{2,1,0:T(8,128)S(1)}, u32[]{:S(2)}, u32[]{:S(2)}) collective-permute-start(f32[4,32,768]{2,1,0:T(8,128)S(1)} %get-tuple-element.40), channel_id=1, source_target_pairs={{0,4},{4,0},{8,12},{12,8},{16,20},{20,16},{24,28},{28,24},{1,5},{5... | collective-permute-start | bytes 1179656 | tf_op jit(solution)/shard_map/ppermute | solution.py:639
  80.2 0.9 collective-permute-start.12
  81.0 4.6 %collective-permute-done.12 = f32[2,32,512]{2,1,0:T(8,128)S(1)} collective-permute-done((f32[2,32,512]{2,1,0:T(8,128)S(1)}, f32[2,32,512]{2,1,0:T(8,128)S(1)}, u32[]{:S(2)}, u32[]{:S(2)}) %collective-permute-start.12) | collective-permute-done | bytes 131104 | tf_op jit(solution)/shard_map/ppermute | solution.py:627
  86.2 1.1 collective-permute-start.16
  87.2 2.1 %collective-permute-start.17 = (f32[32,768]{1,0:T(8,128)S(1)}, f32[32,768]{1,0:T(8,128)S(1)}, u32[]{:S(2)}, u32[]{:S(2)}) collective-permute-start(f32[32,768]{1,0:T(8,128)S(1)} %get-tuple-element.53), channel_id=1, source_target_pairs={{0,24},{4,28},{8,16},{12,20},{16,8},{20,12},{24,0},{28,4},{1,25},{... | collective-permute-start | bytes 294920 | tf_op jit(solution)/shard_map/ppermute | solution.py:642
  89.4 2.2 %collective-permute-done.15.refs_2_ = f32[32,768]{1,0:T(8,128)S(1)} collective-permute-done((f32[32,768]{1,0:T(8,128)S(1)}, f32[32,768]{1,0:T(8,128)S(1)}, u32[]{:S(2)}, u32[]{:S(2)}) %collective-permute-start.15) | collective-permute-done | bytes 98336 | tf_op jit(solution)/shard_map/ppermute | solution.py:642
  91.5 2.3 %collective-permute-done.17.refs_4_ = f32[32,768]{1,0:T(8,128)S(1)} collective-permute-done((f32[32,768]{1,0:T(8,128)S(1)}, f32[32,768]{1,0:T(8,128)S(1)}, u32[]{:S(2)}, u32[]{:S(2)}) %collective-permute-start.17) | collective-permute-done | bytes 98336 | tf_op jit(solution)/shard_map/ppermute | solution.py:642
  93.9 1.4 traces.1
  95.3 1.1 collective-permute-start.18
  96.3 1.3 collective-permute-start.19
  97.6 1.2 collective-permute-start.20
  98.8 1.4 collective-permute-done.18.refs_1_
  100.8 2.0 %collective-permute-done.20.refs_3_ = f32[32,512]{1,0:T(8,128)S(1)} collective-permute-done((f32[32,512]{1,0:T(8,128)S(1)}, f32[32,512]{1,0:T(8,128)S(1)}, u32[]{:S(2)}, u32[]{:S(2)}) %collective-permute-start.20) | collective-permute-done | bytes 65568 | tf_op jit(solution)/shard_map/ppermute | solution.py:646
  102.8 1.2 collective-permute-done.24.refs_7_
  104.0 3.4 %products.3 = (f32[64,1280]{1,0:T(8,128)S(1)}, f32[64,1280]{1,0:T(8,128)S(1)}, f32[64,1280]{1,0:T(8,128)S(1)}, f32[64,1280]{1,0:T(8,128)S(1)}, f32[64,1280]{1,0:T(8,128)S(1)}) custom-call(s32[10]{0:T(128)S(1)} %stack.55.flags.scalars, f32[32,512]{1,0:T(8,128)S(1)} %get-tuple-element.41.refs_0_, f32[32,512]{1,0:T(8,128)S(1)} %collective-permute-done.18.refs_1_, ...), custom_call_target="tpu_custom_call" | custom-call | flops 1073741824 | bytes 3145728 | tf_op jit(solution)/shard_map/products/pallas_call | solution.py:457
  107.5 5.5 %collective-permute-start.30 = (f32[64,1280]{1,0:T(8,128)S(1)}, f32[64,1280]{1,0:T(8,128)S(1)}, u32[]{:S(2)}, u32[]{:S(2)}) collective-permute-start(f32[64,1280]{1,0:T(8,128)S(1)} %get-tuple-element.50), channel_id=1, source_target_pairs={{0,1},{3,2},{4,5},{7,6},{8,9},{11,10},{12,13},{15,14},{16,17},{19,... | collective-permute-start | bytes 983048 | tf_op jit(solution)/shard_map/ppermute | solution.py:570
  113.0 3.0 %products.2 = (f32[64,1024]{1,0:T(8,128)S(1)}, f32[64,1024]{1,0:T(8,128)S(1)}, f32[64,1024]{1,0:T(8,128)S(1)}, f32[64,1024]{1,0:T(8,128)S(1)}, f32[64,1024]{1,0:T(8,128)S(1)}) custom-call(s32[10]{0:T(128)S(1)} %stack.55.flags.scalars, f32[32,512]{1,0:T(8,128)S(1)} %get-tuple-element.41.refs_0_, f32[32,512]{1,0:T(8,128)S(1)} %collective-permute-done.18.refs_1_, ...), custom_call_target="tpu_custom_call" | custom-call | flops 1073741824 | bytes 3145728 | tf_op jit(solution)/shard_map/products/pallas_call | solution.py:457
  116.0 1.3 collective-permute-start.25
  117.3 3.8 %collective-permute-done.30 = f32[64,1280]{1,0:T(8,128)S(1)} collective-permute-done((f32[64,1280]{1,0:T(8,128)S(1)}, f32[64,1280]{1,0:T(8,128)S(1)}, u32[]{:S(2)}, u32[]{:S(2)}) %collective-permute-start.30) | collective-permute-done | bytes 327712 | tf_op jit(solution)/shard_map/ppermute | solution.py:570
  121.8 5.0 %collective-permute-start.31 = (f32[64,1280]{1,0:T(8,128)S(1)}, f32[64,1280]{1,0:T(8,128)S(1)}, u32[]{:S(2)}, u32[]{:S(2)}) collective-permute-start(f32[64,1280]{1,0:T(8,128)S(1)} %add.51), channel_id=1, source_target_pairs={{0,1},{1,2},{4,5},{5,6},{8,9},{9,10},{12,13},{13,14},{16,17},{17,1... | collective-permute-start | bytes 983048 | tf_op jit(solution)/shard_map/ppermute | solution.py:576
  127.6 5.2 %collective-permute-start.26 = (f32[64,1024]{1,0:T(8,128)S(1)}, f32[64,1024]{1,0:T(8,128)S(1)}, u32[]{:S(2)}, u32[]{:S(2)}) collective-permute-start(f32[64,1024]{1,0:T(8,128)S(1)} %add.48), channel_id=1, source_target_pairs={{0,1},{1,2},{4,5},{5,6},{8,9},{9,10},{12,13},{13,14},{16,17},{17,1... | collective-permute-start | bytes 786440 | tf_op jit(solution)/shard_map/ppermute | solution.py:576
  132.8 1.3 collective-permute-start.34
  134.8 4.5 %collective-permute-start.32 = (f32[64,1280]{1,0:T(8,128)S(1)}, f32[64,1280]{1,0:T(8,128)S(1)}, u32[]{:S(2)}, u32[]{:S(2)}) collective-permute-start(f32[64,1280]{1,0:T(8,128)S(1)} %add.52), channel_id=1, source_target_pairs={{0,1},{1,2},{2,3},{4,5},{5,6},{6,7},{8,9},{9,10},{10,11},{12,13},{... | collective-permute-start | bytes 983048 | tf_op jit(solution)/shard_map/ppermute | solution.py:576
  139.4 1.3 collective-permute-start.29
  140.7 5.2 %collective-permute-start.27 = (f32[64,1024]{1,0:T(8,128)S(1)}, f32[64,1024]{1,0:T(8,128)S(1)}, u32[]{:S(2)}, u32[]{:S(2)}) collective-permute-start(f32[64,1024]{1,0:T(8,128)S(1)} %add.49), channel_id=1, source_target_pairs={{0,1},{1,2},{2,3},{4,5},{5,6},{6,7},{8,9},{9,10},{10,11},{12,13},{... | collective-permute-start | bytes 786440 | tf_op jit(solution)/shard_map/ppermute | solution.py:576
  146.0 0.8 collective-permute-done.32.refs_1_.refs_4_
  146.8 2.1 %final.2.refs_6_ = f32[64,2048]{1,0:T(8,128)} custom-call(s32[10]{0:T(128)S(1)} %stack.55.flags.scalars, f32[64,2048]{1,0:T(8,128)S(1)} %copy-done.2, bf16[512,2048]{1,0:T(8,128)(2,1)S(1)} %get-tuple-element.35.foot_ref, f32[64,1280]{1,0:T(8,128)S(1)} %get-tuple-element.47.refs_0_.refs_3_, f32[64,1280]{1,0:T(8,128)S(1)} %collective-permute-done.32.refs_1_.refs_4_, ...), custom_call_target="tpu_custom_call" | custom-call | flops 100663296 | bytes 2359296 | tf_op jit(solution)/shard_map/final/pallas_call | solution.py:512
  148.9 2.2 %collective-permute-done.27.refs_1_ = f32[64,1024]{1,0:T(8,128)S(1)} collective-permute-done((f32[64,1024]{1,0:T(8,128)S(1)}, f32[64,1024]{1,0:T(8,128)S(1)}, u32[]{:S(2)}, u32[]{:S(2)}) %collective-permute-start.27) | collective-permute-done | bytes 262176 | tf_op jit(solution)/shard_map/ppermute | solution.py:576
  151.2 1.9 %final.3 = f32[64,2048]{1,0:T(8,128)} custom-call(s32[10]{0:T(128)S(1)} %stack.55.flags.scalars, f32[64,2048]{1,0:T(8,128)S(1)} %copy-done.2, bf16[512,2048]{1,0:T(8,128)(2,1)S(1)} %get-tuple-element.35.foot_ref, f32[64,1024]{1,0:T(8,128)S(1)} %get-tuple-element.42.refs_0_, ...), custom_call_target="tpu_custom_call", output_to_operand_aliasing={{}: (9, {})} | custom-call | flops 100663296 | bytes 2359296 | tf_op jit(solution)/shard_map/final/pallas_call | solution.py:512
  (52 shorter events, 5.7 us)
Async XLA Ops:
  0.7 2.2 %copy-start = (f32[8,256,512]{2,1,0:T(8,128)S(1)}, f32[8,256,512]{2,1,0:T(8,128)}, u32[]{:S(2)}) copy-start(f32[8,256,512]{2,1,0:T(8,128)} %refs_0_.4) | copy-start | bytes 12582916
  2.9 42.8 %copy-start.3 = (f32[32,512]{1,0:T(8,128)S(1)}, f32[32,512]{1,0:T(8,128)}, u32[]{:S(2)}) copy-start(f32[32,512]{1,0:T(8,128)} %param.5) | copy-start | bytes 196612
  2.9 42.8 %copy-start.1 = (f32[8,256,512]{2,1,0:T(8,128)S(1)}, f32[8,256,512]{2,1,0:T(8,128)}, u32[]{:S(2)}) copy-start(f32[8,256,512]{2,1,0:T(8,128)} %refs_0_.4) | copy-start | bytes 12582916
  3.9 21.3 %collective-permute-start.2 = (f32[4,256,256]{2,1,0:T(8,128)S(1)}, f32[4,256,256]{2,1,0:T(8,128)S(1)}, u32[]{:S(2)}, u32[]{:S(2)}) collective-permute-start(f32[4,256,256]{2,1,0:T(8,128)S(1)} %get-tuple-element.30), channel_id=1, source_target_pairs={{12,28},{16,0},{13,29},{17,1},{14,30},{18,2},{15,31},{19,3}} | collective-permute-start | bytes 3145736 | tf_op jit(solution)/shard_map/ppermute | solution.py:618
  5.4 16.5 %collective-permute-start.6 = (f32[64,2048]{1,0:T(8,128)}, f32[64,2048]{1,0:T(8,128)S(1)}, u32[]{:S(2)}, u32[]{:S(2)}) collective-permute-start(f32[64,2048]{1,0:T(8,128)} %own_ref.3), channel_id=1, source_target_pairs={{1,0},{2,1},{3,2},{5,4},{6,5},{7,6},{9,8},{10,9},{11,10},{13,12},{... | collective-permute-start | bytes 1572872 | tf_op jit(solution)/shard_map/ppermute | solution.py:559
  6.7 16.5 %collective-permute-start.8 = (f32[64,2048]{1,0:T(8,128)}, f32[64,2048]{1,0:T(8,128)S(1)}, u32[]{:S(2)}, u32[]{:S(2)}) collective-permute-start(f32[64,2048]{1,0:T(8,128)} %own_ref.3), channel_id=1, source_target_pairs={{0,1},{1,2},{2,3},{4,5},{5,6},{6,7},{8,9},{9,10},{10,11},{12,13},{... | collective-permute-start | bytes 1572872 | tf_op jit(solution)/shard_map/ppermute | solution.py:558
  13.2 42.8 %copy-start.2 = (f32[64,2048]{1,0:T(8,128)S(1)}, f32[64,2048]{1,0:T(8,128)}, u32[]{:S(2)}) copy-start(f32[64,2048]{1,0:T(8,128)} %own_ref.3) | copy-start | bytes 1572868
  13.2 31.2 %collective-permute-start.4 = (f32[4,256,256]{2,1,0:T(8,128)S(1)}, f32[4,256,256]{2,1,0:T(8,128)S(1)}, u32[]{:S(2)}, u32[]{:S(2)}) collective-permute-start(f32[4,256,256]{2,1,0:T(8,128)S(1)} %get-tuple-element.31), channel_id=1, source_target_pairs={{0,4},{4,8},{8,12},{12,16},{16,20},{20,24},{24,28},{1,5},{5,9},{9,... | collective-permute-start | bytes 3145736 | tf_op jit(solution)/shard_map/ppermute | solution.py:620
  21.9 14.4 %collective-permute-start.7 = (f32[64,2048]{1,0:T(8,128)S(1)}, f32[64,2048]{1,0:T(8,128)S(1)}, u32[]{:S(2)}, u32[]{:S(2)}) collective-permute-start(f32[64,2048]{1,0:T(8,128)S(1)} %collective-permute-done.6.refs_1_), channel_id=1, source_target_pairs={{1,0},{2,1},{5,4},{6,5},{9,8},{10,9},{13,12},{14,13},{17,16},{18,1... | collective-permute-start | bytes 1572872 | tf_op jit(solution)/shard_map/ppermute | solution.py:559
  23.2 14.4 %collective-permute-start.9 = (f32[64,2048]{1,0:T(8,128)S(1)}, f32[64,2048]{1,0:T(8,128)S(1)}, u32[]{:S(2)}, u32[]{:S(2)}) collective-permute-start(f32[64,2048]{1,0:T(8,128)S(1)} %collective-permute-done.8.refs_6_), channel_id=1, source_target_pairs={{1,2},{2,3},{5,6},{6,7},{9,10},{10,11},{13,14},{14,15},{17,18},{18... | collective-permute-start | bytes 1572872 | tf_op jit(solution)/shard_map/ppermute | solution.py:558
  23.9 21.8 %collective-permute-start.5 = (f32[4,256,256]{2,1,0:T(8,128)S(1)}, f32[4,256,256]{2,1,0:T(8,128)S(1)}, u32[]{:S(2)}, u32[]{:S(2)}) collective-permute-start(f32[4,256,256]{2,1,0:T(8,128)S(1)} %get-tuple-element.32), channel_id=1, source_target_pairs={{4,0},{8,4},{12,8},{16,12},{20,16},{24,20},{28,24},{5,1},{9,5},{13... | collective-permute-start | bytes 3145736 | tf_op jit(solution)/shard_map/ppermute | solution.py:621
  25.2 33.7 %collective-permute-start = (f32[4,256,256]{2,1,0:T(8,128)S(1)}, f32[4,256,256]{2,1,0:T(8,128)S(1)}, u32[]{:S(2)}, u32[]{:S(2)}) collective-permute-start(f32[4,256,256]{2,1,0:T(8,128)S(1)} %get-tuple-element.28), channel_id=1, source_target_pairs={{0,4},{4,8},{8,12},{16,20},{20,24},{24,28},{1,5},{5,9},{9,13},{17,... | collective-permute-start | bytes 3145736 | tf_op jit(solution)/shard_map/ppermute | solution.py:620
  36.3 22.6 %collective-permute-start.1 = (f32[4,256,256]{2,1,0:T(8,128)S(1)}, f32[4,256,256]{2,1,0:T(8,128)S(1)}, u32[]{:S(2)}, u32[]{:S(2)}) collective-permute-start(f32[4,256,256]{2,1,0:T(8,128)S(1)} %get-tuple-element.29), channel_id=1, source_target_pairs={{4,0},{8,4},{12,8},{20,16},{24,20},{28,24},{5,1},{9,5},{13,9},{21,... | collective-permute-start | bytes 3145736 | tf_op jit(solution)/shard_map/ppermute | solution.py:621
  37.6 21.3 %collective-permute-start.3 = (f32[4,256,256]{2,1,0:T(8,128)S(1)}, f32[4,256,256]{2,1,0:T(8,128)S(1)}, u32[]{:S(2)}, u32[]{:S(2)}) collective-permute-start(f32[4,256,256]{2,1,0:T(8,128)S(1)} %collective-permute-done.2), channel_id=1, source_target_pairs={{28,16},{0,12},{29,17},{1,13},{30,18},{2,14},{31,19},{3,15}} | collective-permute-start | bytes 3145736 | tf_op jit(solution)/shard_map/ppermute | solution.py:619
  44.4 11.6 %collective-permute-start.10 = (f32[64,2048]{1,0:T(8,128)S(1)}, f32[64,2048]{1,0:T(8,128)S(1)}, u32[]{:S(2)}, u32[]{:S(2)}) collective-permute-start(f32[64,2048]{1,0:T(8,128)S(1)} %choose.1), channel_id=1, source_target_pairs={{2,3},{1,0},{6,7},{5,4},{10,11},{9,8},{14,15},{13,12},{18,19},{17,... | collective-permute-start | bytes 1572872 | tf_op jit(solution)/shard_map/ppermute | solution.py:556
  45.7 34.5 %collective-permute-start.11 = (f32[1,32,512]{2,1,0:T(8,128)S(1)}, f32[1,32,512]{2,1,0:T(8,128)S(1)}, u32[]{:S(2)}, u32[]{:S(2)}) collective-permute-start(f32[1,32,512]{2,1,0:T(8,128)S(1)} %bitcast.25), channel_id=1, source_target_pairs={{0,8},{4,12},{8,0},{12,4},{16,24},{20,28},{24,16},{28,20},{1,9},{5... | collective-permute-start | bytes 196616 | tf_op jit(solution)/shard_map/ppermute | solution.py:627
  72.3 13.5 %collective-permute-start.14 = (f32[4,32,768]{2,1,0:T(8,128)S(1)}, f32[4,32,768]{2,1,0:T(8,128)S(1)}, u32[]{:S(2)}, u32[]{:S(2)}) collective-permute-start(f32[4,32,768]{2,1,0:T(8,128)S(1)} %get-tuple-element.40), channel_id=1, source_target_pairs={{0,4},{4,0},{8,12},{12,8},{16,20},{20,16},{24,28},{28,24},{1,5},{5... | collective-permute-start | bytes 1179656 | tf_op jit(solution)/shard_map/ppermute | solution.py:639
  80.2 5.5 %collective-permute-start.12 = (f32[2,32,512]{2,1,0:T(8,128)S(1)}, f32[2,32,512]{2,1,0:T(8,128)S(1)}, u32[]{:S(2)}, u32[]{:S(2)}) collective-permute-start(f32[2,32,512]{2,1,0:T(8,128)S(1)} %pad_maximum_fusion.1), channel_id=1, source_target_pairs={{0,16},{4,20},{8,24},{12,28},{16,0},{20,4},{24,8},{28,12},{1,17},{... | collective-permute-start | bytes 393224 | tf_op jit(solution)/shard_map/ppermute | solution.py:627
  85.7 3.7 %collective-permute-start.13 = (f32[4,32,512]{2,1,0:T(8,128)S(1)}, f32[4,32,512]{2,1,0:T(8,128)S(1)}, u32[]{:S(2)}, u32[]{:S(2)}) collective-permute-start(f32[4,32,512]{2,1,0:T(8,128)S(1)} %pad_maximum_fusion.near_ref), channel_id=1, source_target_pairs={{0,4},{4,0},{8,12},{12,8},{16,20},{20,16},{24,28},{28,24},{1,5},{5... | collective-permute-start | bytes 786440 | tf_op jit(solution)/shard_map/ppermute | solution.py:629
  85.8 5.7 %collective-permute-start.15 = (f32[32,768]{1,0:T(8,128)S(1)}, f32[32,768]{1,0:T(8,128)S(1)}, u32[]{:S(2)}, u32[]{:S(2)}) collective-permute-start(f32[32,768]{1,0:T(8,128)S(1)} %get-tuple-element.55), channel_id=1, source_target_pairs={{0,8},{4,12},{8,0},{12,4},{16,24},{20,28},{24,16},{28,20},{1,9},{5... | collective-permute-start | bytes 294920 | tf_op jit(solution)/shard_map/ppermute | solution.py:642
  86.2 5.4 %collective-permute-start.16 = (f32[32,768]{1,0:T(8,128)S(1)}, f32[32,768]{1,0:T(8,128)S(1)}, u32[]{:S(2)}, u32[]{:S(2)}) collective-permute-start(f32[32,768]{1,0:T(8,128)S(1)} %get-tuple-element.54), channel_id=1, source_target_pairs={{0,16},{4,20},{8,24},{12,28},{16,0},{20,4},{24,8},{28,12},{1,17},{... | collective-permute-start | bytes 294920 | tf_op jit(solution)/shard_map/ppermute | solution.py:642
  87.2 6.6 %collective-permute-start.17 = (f32[32,768]{1,0:T(8,128)S(1)}, f32[32,768]{1,0:T(8,128)S(1)}, u32[]{:S(2)}, u32[]{:S(2)}) collective-permute-start(f32[32,768]{1,0:T(8,128)S(1)} %get-tuple-element.53), channel_id=1, source_target_pairs={{0,24},{4,28},{8,16},{12,20},{16,8},{20,12},{24,0},{28,4},{1,25},{... | collective-permute-start | bytes 294920 | tf_op jit(solution)/shard_map/ppermute | solution.py:642
  95.3 4.9 %collective-permute-start.18 = (f32[32,512]{1,0:T(8,128)S(1)}, f32[32,512]{1,0:T(8,128)S(1)}, u32[]{:S(2)}, u32[]{:S(2)}) collective-permute-start(f32[32,512]{1,0:T(8,128)S(1)} %get-tuple-element.41.refs_0_), channel_id=1, source_target_pairs={{0,8},{4,12},{8,0},{12,4},{16,24},{20,28},{24,16},{28,20},{1,9},{5... | collective-permute-start | bytes 196616 | tf_op jit(solution)/shard_map/ppermute | solution.py:646
  96.3 4.5 %collective-permute-start.19 = (f32[32,512]{1,0:T(8,128)S(1)}, f32[32,512]{1,0:T(8,128)S(1)}, u32[]{:S(2)}, u32[]{:S(2)}) collective-permute-start(f32[32,512]{1,0:T(8,128)S(1)} %get-tuple-element.41.refs_0_), channel_id=1, source_target_pairs={{0,16},{4,20},{8,24},{12,28},{16,0},{20,4},{24,8},{28,12},{1,17},{... | collective-permute-start | bytes 196616 | tf_op jit(solution)/shard_map/ppermute | solution.py:646
  97.6 5.2 %collective-permute-start.20 = (f32[32,512]{1,0:T(8,128)S(1)}, f32[32,512]{1,0:T(8,128)S(1)}, u32[]{:S(2)}, u32[]{:S(2)}) collective-permute-start(f32[32,512]{1,0:T(8,128)S(1)} %get-tuple-element.41.refs_0_), channel_id=1, source_target_pairs={{0,24},{4,28},{8,16},{12,20},{16,8},{20,12},{24,0},{28,4},{1,25},{... | collective-permute-start | bytes 196616 | tf_op jit(solution)/shard_map/ppermute | solution.py:646
  98.8 4.0 %collective-permute-start.21 = (f32[32,512]{1,0:T(8,128)S(1)}, f32[32,512]{1,0:T(8,128)S(1)}, u32[]{:S(2)}, u32[]{:S(2)}) collective-permute-start(f32[32,512]{1,0:T(8,128)S(1)} %get-tuple-element.41.refs_0_), channel_id=1, source_target_pairs={{0,4},{4,0},{8,12},{12,8},{16,20},{20,16},{24,28},{28,24},{1,5},{5... | collective-permute-start | bytes 196616 | tf_op jit(solution)/shard_map/ppermute | solution.py:649
  100.2 2.6 %collective-permute-start.22 = (f32[32,512]{1,0:T(8,128)S(1)}, f32[32,512]{1,0:T(8,128)S(1)}, u32[]{:S(2)}, u32[]{:S(2)}) collective-permute-start(f32[32,512]{1,0:T(8,128)S(1)} %collective-permute-done.18.refs_1_), channel_id=1, source_target_pairs={{0,4},{4,0},{8,12},{12,8},{16,20},{20,16},{24,28},{28,24},{1,5},{5... | collective-permute-start | bytes 196616 | tf_op jit(solution)/shard_map/ppermute | solution.py:649
  100.8 2.0 %collective-permute-start.23 = (f32[32,512]{1,0:T(8,128)S(1)}, f32[32,512]{1,0:T(8,128)S(1)}, u32[]{:S(2)}, u32[]{:S(2)}) collective-permute-start(f32[32,512]{1,0:T(8,128)S(1)} %collective-permute-done.19.refs_2_), channel_id=1, source_target_pairs={{0,4},{4,0},{8,12},{12,8},{16,20},{20,16},{24,28},{28,24},{1,5},{5... | collective-permute-start | bytes 196616 | tf_op jit(solution)/shard_map/ppermute | solution.py:649
  102.8 1.3 collective-permute-start.24
  107.5 13.6 %collective-permute-start.30 = (f32[64,1280]{1,0:T(8,128)S(1)}, f32[64,1280]{1,0:T(8,128)S(1)}, u32[]{:S(2)}, u32[]{:S(2)}) collective-permute-start(f32[64,1280]{1,0:T(8,128)S(1)} %get-tuple-element.50), channel_id=1, source_target_pairs={{0,1},{3,2},{4,5},{7,6},{8,9},{11,10},{12,13},{15,14},{16,17},{19,... | collective-permute-start | bytes 983048 | tf_op jit(solution)/shard_map/ppermute | solution.py:570
  116.0 10.9 %collective-permute-start.25 = (f32[64,1024]{1,0:T(8,128)S(1)}, f32[64,1024]{1,0:T(8,128)S(1)}, u32[]{:S(2)}, u32[]{:S(2)}) collective-permute-start(f32[64,1024]{1,0:T(8,128)S(1)} %get-tuple-element.45), channel_id=1, source_target_pairs={{0,1},{3,2},{4,5},{7,6},{8,9},{11,10},{12,13},{15,14},{16,17},{19,... | collective-permute-start | bytes 786440 | tf_op jit(solution)/shard_map/ppermute | solution.py:570
  121.1 11.6 %collective-permute-start.33 = (f32[64,1280]{1,0:T(8,128)S(1)}, f32[64,1280]{1,0:T(8,128)S(1)}, u32[]{:S(2)}, u32[]{:S(2)}) collective-permute-start(f32[64,1280]{1,0:T(8,128)S(1)} %add.51), channel_id=1, source_target_pairs={{3,2},{2,1},{7,6},{6,5},{11,10},{10,9},{15,14},{14,13},{19,18},{18... | collective-permute-start | bytes 983048 | tf_op jit(solution)/shard_map/ppermute | solution.py:577
  121.8 13.0 %collective-permute-start.31 = (f32[64,1280]{1,0:T(8,128)S(1)}, f32[64,1280]{1,0:T(8,128)S(1)}, u32[]{:S(2)}, u32[]{:S(2)}) collective-permute-start(f32[64,1280]{1,0:T(8,128)S(1)} %add.51), channel_id=1, source_target_pairs={{0,1},{1,2},{4,5},{5,6},{8,9},{9,10},{12,13},{13,14},{16,17},{17,1... | collective-permute-start | bytes 983048 | tf_op jit(solution)/shard_map/ppermute | solution.py:576
  126.9 12.5 %collective-permute-start.28 = (f32[64,1024]{1,0:T(8,128)S(1)}, f32[64,1024]{1,0:T(8,128)S(1)}, u32[]{:S(2)}, u32[]{:S(2)}) collective-permute-start(f32[64,1024]{1,0:T(8,128)S(1)} %add.48), channel_id=1, source_target_pairs={{3,2},{2,1},{7,6},{6,5},{11,10},{10,9},{15,14},{14,13},{19,18},{18... | collective-permute-start | bytes 786440 | tf_op jit(solution)/shard_map/ppermute | solution.py:577
  127.6 13.1 %collective-permute-start.26 = (f32[64,1024]{1,0:T(8,128)S(1)}, f32[64,1024]{1,0:T(8,128)S(1)}, u32[]{:S(2)}, u32[]{:S(2)}) collective-permute-start(f32[64,1024]{1,0:T(8,128)S(1)} %add.48), channel_id=1, source_target_pairs={{0,1},{1,2},{4,5},{5,6},{8,9},{9,10},{12,13},{13,14},{16,17},{17,1... | collective-permute-start | bytes 786440 | tf_op jit(solution)/shard_map/ppermute | solution.py:576
  132.8 13.2 %collective-permute-start.34 = (f32[64,1280]{1,0:T(8,128)S(1)}, f32[64,1280]{1,0:T(8,128)S(1)}, u32[]{:S(2)}, u32[]{:S(2)}) collective-permute-start(f32[64,1280]{1,0:T(8,128)S(1)} %add.53), channel_id=1, source_target_pairs={{3,2},{2,1},{1,0},{7,6},{6,5},{5,4},{11,10},{10,9},{9,8},{15,14},{... | collective-permute-start | bytes 983048 | tf_op jit(solution)/shard_map/ppermute | solution.py:577
  134.8 12.0 %collective-permute-start.32 = (f32[64,1280]{1,0:T(8,128)S(1)}, f32[64,1280]{1,0:T(8,128)S(1)}, u32[]{:S(2)}, u32[]{:S(2)}) collective-permute-start(f32[64,1280]{1,0:T(8,128)S(1)} %add.52), channel_id=1, source_target_pairs={{0,1},{1,2},{2,3},{4,5},{5,6},{6,7},{8,9},{9,10},{10,11},{12,13},{... | collective-permute-start | bytes 983048 | tf_op jit(solution)/shard_map/ppermute | solution.py:576
  139.4 9.6 %collective-permute-start.29 = (f32[64,1024]{1,0:T(8,128)S(1)}, f32[64,1024]{1,0:T(8,128)S(1)}, u32[]{:S(2)}, u32[]{:S(2)}) collective-permute-start(f32[64,1024]{1,0:T(8,128)S(1)} %add.50), channel_id=1, source_target_pairs={{3,2},{2,1},{1,0},{7,6},{6,5},{5,4},{11,10},{10,9},{9,8},{15,14},{... | collective-permute-start | bytes 786440 | tf_op jit(solution)/shard_map/ppermute | solution.py:577
  140.7 10.4 %collective-permute-start.27 = (f32[64,1024]{1,0:T(8,128)S(1)}, f32[64,1024]{1,0:T(8,128)S(1)}, u32[]{:S(2)}, u32[]{:S(2)}) collective-permute-start(f32[64,1024]{1,0:T(8,128)S(1)} %add.49), channel_id=1, source_target_pairs={{0,1},{1,2},{2,3},{4,5},{5,6},{6,7},{8,9},{9,10},{10,11},{12,13},{... | collective-permute-start | bytes 786440 | tf_op jit(solution)/shard_map/ppermute | solution.py:576

commit v3 on v2

--- a/solution.py
+++ b/solution.py
@@ -12,7 +12,6 @@
 LANES = 128
 GROUP = 4
 HALVES = 2
-CHUNKS = 2
 
 HERE, CORE, CHIP, FIRST, TURNED, INSIDE, BENT, CORNER = 0, 1, 2, 3, 4, 5, 7, 9
 
@@ -55,7 +54,7 @@
     return jax.ShapeDtypeStruct(shape, dtype)
 
 
-def edges_call(flags, raw, halo, chunk, frames, with_corner):
+def edges_call(flags, raw, halo, begin, frames, with_corner):
     rows, cols, _ = raw.shape
     shift = rows - halo
     outs = 3 if with_corner else 2
@@ -65,7 +64,7 @@
         starts = [0, shift, flags[CORNER] * shift]
         copies = [
             pltpu.make_async_copy(
-                raw_ref.at[pl.ds(starts[k], halo), :, pl.ds(chunk * frames, frames)], out_refs[k], sems.at[k]
+                raw_ref.at[pl.ds(starts[k], halo), :, pl.ds(begin, frames)], out_refs[k], sems.at[k]
             )
             for k in range(outs)
         ]
@@ -91,10 +90,11 @@
     )(flags, raw)
 
 
-def diffuse_call(flags, raw, halo_up, halo_down, detour, carried, chunk):
+def diffuse_call(flags, raw, halo_up, halo_down, detour, movie, pair, begin, pair_begin, pair_frames):
     rows, cols, total = raw.shape
     halo, _, frames = halo_up.shape
     groups = frames // LANES
+    carried = [array for array in (movie, *pair) if array is not None]
     width = 64
     pad = 8
     extended = rows + 2 * halo
@@ -102,9 +102,8 @@
 
     def kernel(flags, *refs):
         sources, refs = refs[:inputs], refs[inputs:]
-        if carried is not None:
-            refs = refs[1:]
-        out_ref, pair_ref, first_bufs, second_buf, out_bufs, in_sems, out_sems = refs
+        refs = refs[len(carried) :]
+        out_ref, high_ref, low_ref, first_bufs, second_buf, out_bufs, in_sems, out_sems = refs
         group = pl.program_id(0)
         slot = lax.rem(group, 2)
         inside = pl.ds(pad, cols)
@@ -112,7 +111,7 @@
         def fetches(at):
             here = lax.rem(at, 2)
             lanes = pl.ds(pl.multiple_of(at * LANES, LANES), LANES)
-            wide = pl.ds(pl.multiple_of(chunk * frames + at * LANES, LANES), LANES)
+            wide = pl.ds(pl.multiple_of((begin + at) * LANES, LANES), LANES)
 
             def one(ref, cut, start, count, part):
                 return pltpu.make_async_copy(
@@ -137,7 +136,7 @@
                     pl.when(condition)(lambda copy=copy: act(copy))
 
         def give(at):
-            wide = pl.ds(pl.multiple_of(chunk * frames + at * LANES, LANES), LANES)
+            wide = pl.ds(pl.multiple_of((begin + at) * LANES, LANES), LANES)
             here = lax.rem(at, 2)
             return pltpu.make_async_copy(out_bufs.at[here], out_ref.at[:, :, wide], out_sems.at[here])
 
@@ -193,8 +192,8 @@
                     else:
                         out_bufs[slot, row - halo, pl.ds(col, width), :] = value
                         high, low = split(value)
-                        pair_ref[row - halo, pl.ds(col, width), 0:LANES] = high
-                        pair_ref[row - halo, pl.ds(col, width), LANES:] = low
+                        high_ref[row - halo, pl.ds(col, width), :] = high
+                        low_ref[row - halo, pl.ds(col, width), :] = low
                     current, flux_up = below, flux_down
                 return tuple(kept)
 
@@ -212,18 +211,18 @@
     operands = [flags, raw, halo_up, halo_down]
     if detour is not None:
         operands.append(detour)
-    aliases = {}
-    if carried is not None:
-        operands.append(carried)
-        aliases = {len(operands) - 1: 0}
+    outputs = [k for k, array in enumerate((movie, *pair)) if array is not None]
+    aliases = {len(operands) + k: output for k, output in enumerate(outputs)}
+    operands += carried
     padded = (extended, cols + 2 * pad, LANES)
     return pl.pallas_call(
         kernel,
         grid_spec=pltpu.PrefetchScalarGridSpec(
             num_scalar_prefetch=1,
             grid=(groups,),
-            in_specs=[outside] * (len(operands) - 1),
-            out_specs=[outside, pl.BlockSpec((rows, cols, 2 * LANES), lambda i, flags: (0, 0, i))],
+            in_specs=[outside] * (len(operands) - 1 - len(carried))
+            + [pl.BlockSpec(memory_space=pl.ANY)] * len(carried),
+            out_specs=[outside] + [pl.BlockSpec((rows, cols, LANES), lambda i, flags: (0, 0, pair_begin + i))] * 2,
             scratch_shapes=[
                 pltpu.VMEM((2, *padded), jnp.float32),
                 pltpu.VMEM(padded, jnp.float32),
@@ -232,9 +231,9 @@
                 pltpu.SemaphoreType.DMA((2,)),
             ],
         ),
-        out_shape=[shaped(rows, cols, total), shaped(rows, cols, 2 * frames, dtype=jnp.bfloat16)],
+        out_shape=[shaped(rows, cols, total)] + [shaped(rows, cols, pair_frames, dtype=jnp.bfloat16)] * 2,
         input_output_aliases=aliases,
-        cost_estimate=cost(rows * cols * frames * 200, rows * cols * frames * 16),
+        cost_estimate=cost(rows * cols * groups * LANES * 200, rows * cols * groups * LANES * 16),
         compiler_params=grant(16),
         name="diffuse",
     )(*operands)
@@ -298,32 +297,31 @@
 
 def numerator_call(scalars, foot, movies, gram, trace_rows):
     rank = foot.shape[0] // 2
-    pixel_count, pair = movies[0].shape
-    frames = pair // 2
-    columns = frames * len(movies) + rank
+    pixel_count = movies[0][0].shape[0]
+    spans = [high.shape[1] for high, _ in movies]
+    frames = sum(spans)
+    columns = frames + rank
     block = 512
     steps = pixel_count // block
     chips = rank // (2 * trace_rows)
 
     def kernel(scalars, foot_ref, gram_ref, *refs):
-        movie_refs = refs[: len(movies)]
-        keep_ref, send_ref, total = refs[len(movies) :]
+        movie_refs = refs[: 2 * len(movies)]
+        keep_ref, send_ref, total = refs[2 * len(movies) :]
         step = pl.program_id(0)
 
         @pl.when(step == 0)
         def _():
             total[...] = jnp.zeros_like(total)
 
-        for k, movie_ref in enumerate(movie_refs):
-            part = fold(dot(foot_ref[...], movie_ref[...], NN))
-            for g in range(frames // LANES):
-                at = k * frames + g * LANES
-                both = part[:, 2 * g * LANES : 2 * (g + 1) * LANES]
-                total[:, at : at + LANES] += both[:, 0:LANES] + both[:, LANES:]
+        for k in range(len(movies)):
+            high_ref, low_ref = movie_refs[2 * k : 2 * k + 2]
+            part = fold(dot(foot_ref[...], high_ref[...], NN)) + dot(foot_ref[0:rank, :], low_ref[...], NN)
+            total[:, sum(spans[:k]) : sum(spans[: k + 1])] += part
 
         @pl.when(step == steps - 1)
         def _():
-            total[:, frames * len(movies) :] = gram_ref[...]
+            total[:, frames:] = gram_ref[...]
             core = scalars[CORE]
             for k in range(chips):
                 chip = scalars[CHIP] ^ k
@@ -342,7 +340,7 @@
                 pl.BlockSpec((2 * rank, block), lambda k, s: (0, k)),
                 pl.BlockSpec((rank, rank), lambda k, s: (0, 0)),
             ]
-            + [pl.BlockSpec((block, pair), lambda k, s: (k, 0))] * len(movies),
+            + [pl.BlockSpec((block, array.shape[1]), lambda k, s: (k, 0)) for movie in movies for array in movie],
             out_specs=[out_spec, out_spec],
             scratch_shapes=[pltpu.VMEM((rank, columns), jnp.float32)],
         ),
@@ -350,39 +348,39 @@
         cost_estimate=cost(8 * rank * pixel_count * columns, 4 * pixel_count * (rank + columns)),
         compiler_params=grant(10),
         name="numerator",
-    )(scalars, foot, gram, *movies)
-
-
-def traces_call(scalars, keep, arrived, parts, near, far):
+    )(scalars, foot, gram, *[array for movie in movies for array in movie])
+
+
+def traces_call(scalars, keep, arrived, parts, gathered):
     _, trace_rows, columns = keep.shape
-    frames = near.shape[2]
+    frames = gathered[0][0].shape[2]
     rank = columns - frames
-    chips = near.shape[0]
-
-    def kernel(scalars, near_ref, far_ref, *refs):
+    stacks = [stack for stack, _ in gathered]
+
+    def kernel(scalars, *refs):
+        stack_refs, refs = refs[: len(stacks)], refs[len(stacks) :]
         part_refs, (out_ref, copy_ref, full) = refs[:-3], refs[-3:]
-        for k in range(chips):
-            device = 2 * (scalars[CHIP] ^ k) + scalars[CORE]
-            full[pl.ds(pl.multiple_of(device * trace_rows, trace_rows), trace_rows), :] = near_ref[k]
-            device = 2 * (scalars[CHIP] ^ k) + 1 - scalars[CORE]
-            full[pl.ds(pl.multiple_of(device * trace_rows, trace_rows), trace_rows), :] = far_ref[k]
+        for stack_ref, (_, masks) in zip(stack_refs, gathered):
+            for k, mask in enumerate(masks):
+                device = 2 * (scalars[CHIP] ^ (mask // 2))
+                device = device + (1 - scalars[CORE] if mask % 2 else scalars[CORE])
+                full[pl.ds(pl.multiple_of(device * trace_rows, trace_rows), trace_rows), :] = stack_ref[k]
         total = part_refs[0][0] + part_refs[1][0]
         for part_ref in part_refs[2:]:
             total = total + part_ref[...]
         gram = stacked(total[:, frames:])
         high, low = split(full[...])
         below = fold(dot(gram, high, NN)) + dot(gram[0:trace_rows], low, NN)
-        value = near_ref[0] * total[:, 0:frames] / below
+        value = stack_refs[0][0] * total[:, 0:frames] / below
         out_ref[...] = value
         copy_ref[...] = value
 
-    whole = pl.BlockSpec(near.shape, lambda k, s: (0, 0, 0))
     return pl.pallas_call(
         kernel,
         grid_spec=pltpu.PrefetchScalarGridSpec(
             num_scalar_prefetch=1,
             grid=(1,),
-            in_specs=[whole, whole]
+            in_specs=[pl.BlockSpec(stack.shape, lambda k, s: (0, 0, 0)) for stack in stacks]
             + [pl.BlockSpec((1, trace_rows, columns), lambda k, s: (0, 0, 0))] * 2
             + [pl.BlockSpec((trace_rows, columns), lambda k, s: (0, 0))] * len(parts),
             out_specs=[pl.BlockSpec((trace_rows, frames), lambda k, s: (0, 0))] * 2,
@@ -392,26 +390,27 @@
         cost_estimate=cost(6 * trace_rows * rank * frames, 8 * rank * frames),
         compiler_params=grant(6),
         name="traces",
-    )(scalars, near, far, keep, arrived, *parts)
+    )(scalars, *stacks, keep, arrived, *parts)
 
 
 def products_call(scalars, near, far, movies, half, count, with_gram):
     chips = len(near)
     trace_rows, frames = near[0].shape
     rank = 2 * chips * trace_rows
+    half_rank = rank // 2
     share = rank // count
-    pixel_count, pair = movies[0].shape
+    pixel_count = movies[0][0].shape[0]
+    spans = [high.shape[1] for high, _ in movies]
     part = pixel_count // HALVES
     block = rank
     steps = part // block
-    columns = part + (rank if with_gram else 0)
-    groups = frames // LANES
+    columns = part + (half_rank if with_gram else 0)
     outs = count + 1
 
     def kernel(scalars, *refs):
         near_refs, far_refs, refs = refs[:chips], refs[chips : 2 * chips], refs[2 * chips :]
-        movie_refs = refs[: len(movies)]
-        refs = refs[len(movies) :]
+        movie_refs = refs[: 2 * len(movies)]
+        refs = refs[2 * len(movies) :]
         out_refs = refs[:outs]
         full, left, result = refs[outs:]
         step = pl.program_id(0)
@@ -424,34 +423,32 @@
                 full[pl.ds(pl.multiple_of(device * trace_rows, trace_rows), trace_rows), :] = near_refs[k][...]
                 device = 2 * (scalars[CHIP] ^ k) + 1 - scalars[CORE]
                 full[pl.ds(pl.multiple_of(device * trace_rows, trace_rows), trace_rows), :] = far_refs[k][...]
-            high, low = split(full[...])
-            for g in range(groups):
-                cut = slice(g * LANES, (g + 1) * LANES)
-                at = 2 * g * LANES
-                left[0:rank, at : at + LANES] = high[:, cut]
-                left[0:rank, at + LANES : at + 2 * LANES] = high[:, cut]
-                left[rank:, at : at + LANES] = low[:, cut]
-                left[rank:, at + LANES : at + 2 * LANES] = jnp.zeros_like(low[:, cut])
+            left[...] = stacked(full[...])
 
         def emit(total, at):
-            result[...] = total
+            width = total.shape[1]
+            result[:, 0:width] = total
             for k, out_ref in enumerate(out_refs):
                 slot = lax.rem(here + k, count) if k < count else scalars[FIRST]
                 row = pl.multiple_of(slot * share, share)
-                out_ref[:, pl.ds(at, block)] = result[pl.ds(row, share), :]
-
-        total = dot(left[:, 0:pair], movie_refs[0][...], NT)
-        for k in range(1, len(movies)):
-            total += dot(left[:, k * pair : (k + 1) * pair], movie_refs[k][...], NT)
-        emit(fold(total), pl.multiple_of(step * block, block))
+                out_ref[:, pl.ds(at, width)] = result[pl.ds(row, share), 0:width]
+
+        both = jnp.zeros((2 * rank, block), jnp.float32)
+        upper = jnp.zeros((rank, block), jnp.float32)
+        for k in range(len(movies)):
+            high_ref, low_ref = movie_refs[2 * k : 2 * k + 2]
+            cut = slice(sum(spans[:k]), sum(spans[: k + 1]))
+            both += dot(left[:, cut], high_ref[...], NT)
+            upper += dot(left[0:rank, cut], low_ref[...], NT)
+        emit(fold(both) + upper, pl.multiple_of(step * block, block))
         if with_gram:
 
             @pl.when(step == steps - 1)
             def _():
-                high, low = split(full[...])
-                both = dot(jnp.concatenate([high, low], axis=0), high, NT)
-                cross = both[rank:]
-                emit(both[0:rank] + (cross + cross.T), part)
+                at = pl.multiple_of(scalars[CORE] * half_rank, half_rank)
+                both = dot(left[...], left[pl.ds(at, half_rank), :], NT)
+                upper = dot(left[0:rank, :], left[pl.ds(rank + at, half_rank), :], NT)
+                emit(fold(both) + upper, part)
 
     piece = pl.BlockSpec((trace_rows, frames), lambda j, s: (0, 0))
     return pl.pallas_call(
@@ -460,11 +457,15 @@
             num_scalar_prefetch=1,
             grid=(steps,),
             in_specs=[piece] * (2 * chips)
-            + [pl.BlockSpec((block, pair), lambda j, s: (half * steps + j, 0))] * len(movies),
+            + [
+                pl.BlockSpec((block, array.shape[1]), lambda j, s: (half * steps + j, 0))
+                for movie in movies
+                for array in movie
+            ],
             out_specs=[pl.BlockSpec((share, columns), lambda j, s: (0, 0))] * outs,
             scratch_shapes=[
                 pltpu.VMEM((rank, frames), jnp.float32),
-                pltpu.VMEM((2 * rank, 2 * frames), jnp.bfloat16),
+                pltpu.VMEM((2 * rank, frames), jnp.bfloat16),
                 pltpu.VMEM((rank, block), jnp.float32),
             ],
         ),
@@ -472,10 +473,10 @@
         cost_estimate=cost(8 * rank * part * frames, 4 * part * (frames + rank)),
         compiler_params=grant(10),
         name="products",
-    )(scalars, *near, *far, *movies)
-
-
-def final_call(scalars, own, foot, parts, grams, carried, half):
+    )(scalars, *near, *far, *[array for movie in movies for array in movie])
+
+
+def final_call(scalars, own, foot, parts, gram_mine, gram_other, carried, half):
     share, pixel_count = own.shape
     rank = foot.shape[0] // 2
     part = pixel_count // HALVES
@@ -484,14 +485,13 @@
 
     def kernel(scalars, own_ref, foot_ref, *refs):
         part_refs = refs[: len(parts)]
-        gram_refs = refs[len(parts) : len(parts) + len(grams)]
+        mine, other = refs[len(parts)][...], refs[len(parts) + 1][...]
         out_ref = refs[-1]
         above = part_refs[0][...]
         for part_ref in part_refs[1:]:
             above = above + part_ref[...]
-        gram = gram_refs[0][...]
-        for gram_ref in gram_refs[1:]:
-            gram = gram + gram_ref[...]
+        first = scalars[CORE] == 0
+        gram = jnp.concatenate([jnp.where(first, mine, other), jnp.where(first, other, mine)], axis=1)
         both = stacked(gram)
         below = fold(dot(both, foot_ref[0:rank, :], NN)) + dot(both[0:share], foot_ref[rank:, :], NN)
         out_ref[...] = own_ref[...] * above / below
@@ -502,8 +502,8 @@
         pl.BlockSpec((2 * rank, block), lambda k, s: (0, at + k)),
     ]
     in_specs += [pl.BlockSpec((share, block), lambda k, s: (0, k))] * len(parts)
-    in_specs += [pl.BlockSpec((share, rank), lambda k, s: (0, part // rank))] * len(grams)
-    operands = [scalars, own, foot, *parts, *grams]
+    in_specs += [pl.BlockSpec((share, rank // 2), lambda k, s: (0, 0))] * 2
+    operands = [scalars, own, foot, *parts, gram_mine, gram_other]
     aliases = {}
     if carried is not None:
         operands.append(carried)
@@ -587,7 +587,9 @@
     here = lax.axis_index("tm")
     core = lax.rem(pix, 2)
     trace_rows = traces.shape[0]
-    frames = frame_count // CHUNKS
+    blocks = frame_count // LANES
+    quarter = max(blocks // 4, 1)
+    widths = [2 * quarter, blocks - 2 * quarter]
     halo = SUBSTEPS
 
     def swap(mask):
@@ -607,10 +609,14 @@
 
     bent = [k for k in range(pix_count - 1) if k % GROUP == GROUP - 1] if pix_count % GROUP == 0 else []
     halos = []
-    for c in range(CHUNKS):
-        last = c == CHUNKS - 1 and bool(bent)
+    for c, width in enumerate(widths):
+        begin = sum(widths[:c]) * LANES
+        last = c == len(widths) - 1 and bool(bent)
         send = [(k, k + 1) for k in range(pix_count - 1) if not (last and k in bent)]
-        edges = edges_call(flags, raw_movie, halo, c, frames, last)
+        if c == 0:
+            edges = raw_movie[:halo, :, : width * LANES], raw_movie[rows - halo :, :, : width * LANES]
+        else:
+            edges = edges_call(flags, raw_movie, halo, begin, width * LANES, last)
         detour = None
         if last:
             first = [(k, k + GROUP) for k in bent] + [(k + 1, k + 1 - GROUP) for k in bent]
@@ -621,18 +627,27 @@
         from_below = lax.ppermute(edges[0], "pix", [(b, a) for a, b in send])
         halos.append((from_above, from_below, detour))
 
-    near = traces[None]
-    mask = 2
-    while mask < pix_count:
-        near = jnp.concatenate([near, lax.ppermute(near, "pix", swap(mask))], axis=0)
-        mask *= 2
-    far = lax.ppermute(near, "pix", swap(1))
+    held, masks = traces[None], [0]
+    hops = [mask for mask in (4, 8, 16, 32, 64, 1) if mask < pix_count]
+    for mask in hops:
+        held = jnp.concatenate([held, lax.ppermute(held, "pix", swap(mask))], axis=0)
+        masks = masks + [mask ^ m for m in masks]
+    gathered = [(held, masks)]
+    if pix_count > 2:
+        gathered.append((lax.ppermute(held, "pix", swap(2)), [2 ^ m for m in masks]))
 
     current = None
     movies = []
-    for c in range(CHUNKS):
-        current, pair = diffuse_call(flags, raw_movie, *halos[c], current, c)
-        movies.append(pair.reshape(pixel_count, 2 * frames))
+    for members in ((0,), (1,)):
+        pair = (None, None)
+        pair_frames = sum(widths[c] for c in members) * LANES
+        pair_begin = 0
+        for c in members:
+            current, *pair = diffuse_call(
+                flags, raw_movie, *halos[c], current, pair, sum(widths[:c]), pair_begin, pair_frames
+            )
+            pair_begin += widths[c]
+        movies.append(tuple(array.reshape(pixel_count, pair_frames) for array in pair))
 
     foot, gram = footprints_call(scalars, footprints, pairs)
     keep, send = numerator_call(scalars, foot, movies, gram, trace_rows)
@@ -640,7 +655,7 @@
     parts = []
     for k in range(1, keep.shape[0]):
         parts.append(lax.ppermute(keep[k] + arrived[k], "pix", swap(2 * k)))
-    new_traces, again = traces_call(scalars, keep, arrived, parts, near, far)
+    new_traces, again = traces_call(scalars, keep, arrived, parts, gathered)
     near = [again]
     for k in range(1, keep.shape[0]):
         near.append(lax.ppermute(again, "pix", swap(2 * k)))
@@ -652,9 +667,14 @@
     for h in range(HALVES):
         products.append(products_call(scalars, near, far, movies, h, count, h == 0))
     sums = [line_scatter(blocks, "tm", count) for blocks in products]
+    part = pixel_count // HALVES
+    gram_mine = sum(array[:, part:] for array in sums[0])
+    gram_other = lax.ppermute(gram_mine, "pix", swap(1))
     new_footprints = None
     for h in range(HALVES):
-        new_footprints = final_call(scalars, footprints, foot, sums[h], sums[0], new_footprints, h)
+        new_footprints = final_call(
+            scalars, footprints, foot, sums[h], gram_mine, gram_other, new_footprints, h
+        )
     return current, new_footprints, new_traces
 
 

time: 154 us -> 162 us (1.052)
  waiting for transfers between devices: 37.7 us -> 44.7 us
  starting transfers between devices: 71.4 us -> 74.2 us
  Pallas kernels: 40.3 us -> 38 us
    ppermute x3 -> x4, starting transfers between devices: 1.01 us -> 9.04 us  [the longest x2 7.55 us: compute(): lax.ppermute(held, 'pix', swap(mask))]
    ppermute x1, starting transfers between devices: 7.88 us -> 0.07 us  [compute(): arrived = lax.ppermute(send, 'pix', swap(1))]
    ppermute x2, waiting for transfers between devices: 3.79 us -> 9.34 us  [line_scatter(): lax.ppermute(blocks[count], axis, up_pairs + down_pairs)]
    ppermute x2, starting transfers between devices: 6.84 us -> 10.7 us  [line_scatter(): lax.ppermute(blocks[count], axis, up_pairs + down_pairs)]
    ppermute x3 -> x4, waiting for transfers between devices: 4.63 us -> 6.74 us  [the longest x1 4.23 us: compute(): lax.ppermute(held, 'pix', swap(2))]
  transfers between devices with their start and end apart: 35 -> 36, of which waited for: 14 -> 16; matrix products, arithmetic and copies ran while one was open for 0% -> 0% of each run, Pallas kernels for 21% -> 19%
where the time goes in v3:
time: 162 us; the launch traced here: 161 us
  starting transfers between devices  74.2 us (46%)
  waiting for transfers between devices  44.7 us (28%)
  Pallas kernels  38 us (23%)
  local copies, waits for them, and re-layouts  2.53 us (2%)
    pallas_call x2, Pallas kernels, diffuse_call(): pl.pallas_call(kernel, grid_spec=pltpu.PrefetchScalarGridSpec(num_scalar_...  19.4 us
    ppermute x4, starting transfers between devices, line_scatter(): up_last = lax.ppermute(up_block, axis, up_pairs)  18.7 us
    ppermute x2, waiting for transfers between devices, line_gather(): last_down = lax.ppermute(last_down, axis, down_pairs)  15.8 us
    ppermute x2, starting transfers between devices, line_scatter(): lax.ppermute(blocks[count], axis, up_pairs + down_pairs)  10.7 us
    ppermute x2, waiting for transfers between devices, line_scatter(): lax.ppermute(blocks[count], axis, up_pairs + down_pairs)  9.34 us
    ppermute x2, starting transfers between devices, compute(): lax.ppermute(held, 'pix', swap(mask))  7.55 us
    ppermute x2, starting transfers between devices, line_gather(): last_up = lax.ppermute(last_up, axis, up_pairs)  6.32 us
    ppermute x1, starting transfers between devices, compute(): detour = lax.ppermute(detour, 'pix', second)  5.97 us
  transfers between devices with their start and end apart: 36, of which 16 were waited for; matrix products, arithmetic and copies ran while one was open for 0% of the time, Pallas kernels for 19%

profile of v3, /device:TPU:0, one launch (start us, length us, event | category | flops | bytes accessed | tf_op | source)
XLA Modules:
  0.0 160.8 jit_solution(15342093280106231638)
XLA Ops:
  0.7 2.2 %copy-done = f32[8,256,512]{2,1,0:T(8,128)S(1)} copy-done((f32[8,256,512]{2,1,0:T(8,128)S(1)}, f32[8,256,512]{2,1,0:T(8,128)}, u32[]{:S(2)}) %copy-start) | copy-done | bytes 4194328
  2.9 1.0 edges.1
  3.9 1.4 collective-permute-start.2
  5.4 1.3 collective-permute-start.6
  6.7 5.6 %collective-permute-start.8 = (f32[64,2048]{1,0:T(8,128)}, f32[64,2048]{1,0:T(8,128)S(1)}, u32[]{:S(2)}, u32[]{:S(2)}) collective-permute-start(f32[64,2048]{1,0:T(8,128)} %own_ref.3), channel_id=1, source_target_pairs={{0,1},{1,2},{2,3},{4,5},{5,6},{6,7},{8,9},{9,10},{10,11},{12,13},{... | collective-permute-start | bytes 1572872 | tf_op jit(solution)/shard_map/ppermute | solution.py:558
  12.6 1.5 collective-permute-start.4
  14.1 7.8 %collective-permute-done.6.refs_1_ = f32[64,2048]{1,0:T(8,128)S(1)} collective-permute-done((f32[64,2048]{1,0:T(8,128)}, f32[64,2048]{1,0:T(8,128)S(1)}, u32[]{:S(2)}, u32[]{:S(2)}) %collective-permute-start.6) | collective-permute-done | bytes 524320 | tf_op jit(solution)/shard_map/ppermute | solution.py:559
  21.9 1.3 collective-permute-start.7
  23.9 1.3 collective-permute-start.5
  25.2 3.1 %collective-permute-start = (f32[4,256,256]{2,1,0:T(8,128)S(1)}, f32[4,256,256]{2,1,0:T(8,128)S(1)}, u32[]{:S(2)}, u32[]{:S(2)}) collective-permute-start(f32[4,256,256]{2,1,0:T(8,128)S(1)} %get-tuple-element.28), channel_id=1, source_target_pairs={{0,4},{4,8},{8,12},{16,20},{20,24},{24,28},{1,5},{5,9},{9,13},{17,... | collective-permute-start | bytes 3145736 | tf_op jit(solution)/shard_map/ppermute | solution.py:626
  28.3 8.0 %collective-permute-done.7.down_ref.refs_3_ = f32[64,2048]{1,0:T(8,128)S(1)} collective-permute-done((f32[64,2048]{1,0:T(8,128)S(1)}, f32[64,2048]{1,0:T(8,128)S(1)}, u32[]{:S(2)}, u32[]{:S(2)}) %collective-permute-start.7) | collective-permute-done | bytes 524320 | tf_op jit(solution)/shard_map/ppermute | solution.py:559
  36.3 1.3 collective-permute-start.1
  37.6 6.0 %collective-permute-start.3 = (f32[4,256,256]{2,1,0:T(8,128)S(1)}, f32[4,256,256]{2,1,0:T(8,128)S(1)}, u32[]{:S(2)}, u32[]{:S(2)}) collective-permute-start(f32[4,256,256]{2,1,0:T(8,128)S(1)} %collective-permute-done.2), channel_id=1, source_target_pairs={{28,16},{0,12},{29,17},{1,13},{30,18},{2,14},{31,19},{3,15}} | collective-permute-start | bytes 3145736 | tf_op jit(solution)/shard_map/ppermute | solution.py:625
  44.4 1.3 collective-permute-start.10
  45.7 7.0 %collective-permute-start.11 = (f32[1,32,512]{2,1,0:T(8,128)S(1)}, f32[1,32,512]{2,1,0:T(8,128)S(1)}, u32[]{:S(2)}, u32[]{:S(2)}) collective-permute-start(f32[1,32,512]{2,1,0:T(8,128)S(1)} %bitcast.33), channel_id=1, source_target_pairs={{0,16},{4,20},{8,24},{12,28},{16,0},{20,4},{24,8},{28,12},{1,17},{... | collective-permute-start | bytes 196616 | tf_op jit(solution)/shard_map/ppermute | solution.py:633
  52.7 9.7 %diffuse.2 = (f32[8,256,512]{2,1,0:T(8,128)}, bf16[8,256,256]{2,1,0:T(8,128)(2,1)S(1)}, bf16[8,256,256]{2,1,0:T(8,128)(2,1)S(1)}) custom-call(s32[10]{0:T(128)S(1)} %stack.55.flags.scalars, f32[8,256,512]{2,1,0:T(8,128)S(1)} %copy-done.1, f32[4,256,256]{2,1,0:T(8,128)S(1)} %collective-permute-done.4.refs_1_, f32[4,256,256]{2,1,0:T(8,128)S(1)} %collective-permute-done.5.refs_2_), custom_call_target="tpu_custom_call" | custom-call | flops 104857600 | bytes 8388608 | tf_op jit(solution)/shard_map/diffuse/pallas_call | solution.py:218
  62.4 2.9 %footprints.1 = (bf16[512,2048]{1,0:T(8,128)(2,1)S(1)}, f32[256,256]{1,0:T(8,128)S(1)}) custom-call(s32[10]{0:T(128)S(1)} %stack.55.flags.scalars, f32[64,2048]{1,0:T(8,128)S(1)} %copy-done.2, f32[64,2048]{1,0:T(8,128)S(1)} %collective-permute-done.6.refs_1_, f32[64,2048]{1,0:T(8,128)S(1)} %collective-permute-done.10.refs_2_.refs_5_, ...), custom_call_target="tpu_custom_call" | custom-call | flops 536870912 | bytes 4194304 | tf_op jit(solution)/shard_map/footprints/pallas_call | solution.py:279
  65.4 9.7 %diffuse.3 = (f32[8,256,512]{2,1,0:T(8,128)}, bf16[8,256,256]{2,1,0:T(8,128)(2,1)S(1)}, bf16[8,256,256]{2,1,0:T(8,128)(2,1)S(1)}) custom-call(s32[10]{0:T(128)S(1)} %stack.55.flags.scalars, f32[8,256,512]{2,1,0:T(8,128)S(1)} %copy-done.1, f32[4,256,256]{2,1,0:T(8,128)S(1)} %collective-permute-done.refs_1_, ...), custom_call_target="tpu_custom_call", output_to_operand_aliasing={{0}: (5, {})} | custom-call | flops 104857600 | bytes 8388608 | tf_op jit(solution)/shard_map/diffuse/pallas_call | solution.py:218
  75.1 3.2 %numerator.1 = (f32[4,32,768]{2,1,0:T(8,128)S(1)}, f32[4,32,768]{2,1,0:T(8,128)S(1)}) custom-call(s32[10]{0:T(128)S(1)} %stack.55.flags.scalars, bf16[512,2048]{1,0:T(8,128)(2,1)S(1)} %get-tuple-element.33.foot_ref, f32[256,256]{1,0:T(8,128)S(1)} %get-tuple-element.34.gram_ref, bf16[2048,256]{1,0:T(8,128)(2,1)S(1)} %bitcast.21, ...), custom_call_target="tpu_custom_call" | custom-call | flops 3221225472 | bytes 8388608 | tf_op jit(solution)/shard_map/numerator/pallas_call | solution.py:334
  78.9 1.3 collective-permute-done.12
  80.3 1.4 collective-permute-start.13
  82.5 1.4 collective-permute-start.16
  83.9 1.4 collective-permute-start.17
  85.3 4.2 %collective-permute-done.13.refs_1_ = f32[4,32,512]{2,1,0:T(8,128)S(1)} collective-permute-done((f32[4,32,512]{2,1,0:T(8,128)S(1)}, f32[4,32,512]{2,1,0:T(8,128)S(1)}, u32[]{:S(2)}, u32[]{:S(2)}) %collective-permute-start.13) | collective-permute-done | bytes 262176 | tf_op jit(solution)/shard_map/ppermute | solution.py:637
  89.5 2.1 %collective-permute-done.15.refs_4_ = f32[32,768]{1,0:T(8,128)S(1)} collective-permute-done((f32[32,768]{1,0:T(8,128)S(1)}, f32[32,768]{1,0:T(8,128)S(1)}, u32[]{:S(2)}, u32[]{:S(2)}) %collective-permute-start.15) | collective-permute-done | bytes 98336 | tf_op jit(solution)/shard_map/ppermute | solution.py:657
  91.6 2.3 %collective-permute-done.17.refs_6_ = f32[32,768]{1,0:T(8,128)S(1)} collective-permute-done((f32[32,768]{1,0:T(8,128)S(1)}, f32[32,768]{1,0:T(8,128)S(1)}, u32[]{:S(2)}, u32[]{:S(2)}) %collective-permute-start.17) | collective-permute-done | bytes 98336 | tf_op jit(solution)/shard_map/ppermute | solution.py:657
  94.0 1.4 traces.1
  95.4 1.7 %collective-permute-start.18 = (f32[32,512]{1,0:T(8,128)S(1)}, f32[32,512]{1,0:T(8,128)S(1)}, u32[]{:S(2)}, u32[]{:S(2)}) collective-permute-start(f32[32,512]{1,0:T(8,128)S(1)} %get-tuple-element.41.refs_0_), channel_id=1, source_target_pairs={{0,8},{4,12},{8,0},{12,4},{16,24},{20,28},{24,16},{28,20},{1,9},{5... | collective-permute-start | bytes 196616 | tf_op jit(solution)/shard_map/ppermute | solution.py:661
  97.4 1.5 collective-permute-start.20
  99.7 1.7 %collective-permute-done.19.refs_2_ = f32[32,512]{1,0:T(8,128)S(1)} collective-permute-done((f32[32,512]{1,0:T(8,128)S(1)}, f32[32,512]{1,0:T(8,128)S(1)}, u32[]{:S(2)}, u32[]{:S(2)}) %collective-permute-start.19) | collective-permute-done | bytes 65568 | tf_op jit(solution)/shard_map/ppermute | solution.py:661
  101.4 1.2 collective-permute-done.20.refs_3_
  102.7 1.2 collective-permute-done.24.refs_7_
  103.8 2.9 %products.3 = (f32[64,1152]{1,0:T(8,128)S(1)}, f32[64,1152]{1,0:T(8,128)S(1)}, f32[64,1152]{1,0:T(8,128)S(1)}, f32[64,1152]{1,0:T(8,128)S(1)}, f32[64,1152]{1,0:T(8,128)S(1)}) custom-call(s32[10]{0:T(128)S(1)} %stack.55.flags.scalars, f32[32,512]{1,0:T(8,128)S(1)} %get-tuple-element.41.refs_0_, f32[32,512]{1,0:T(8,128)S(1)} %collective-permute-done.18.refs_1_, ...), custom_call_target="tpu_custom_call" | custom-call | flops 1073741824 | bytes 3145728 | tf_op jit(solution)/shard_map/products/pallas_call | solution.py:454
  106.7 6.3 %collective-permute-start.30 = (f32[64,1152]{1,0:T(8,128)S(1)}, f32[64,1152]{1,0:T(8,128)S(1)}, u32[]{:S(2)}, u32[]{:S(2)}) collective-permute-start(f32[64,1152]{1,0:T(8,128)S(1)} %get-tuple-element.50), channel_id=1, source_target_pairs={{0,1},{3,2},{4,5},{7,6},{8,9},{11,10},{12,13},{15,14},{16,17},{19,... | collective-permute-start | bytes 884744 | tf_op jit(solution)/shard_map/ppermute | solution.py:570
  113.0 6.6 %collective-permute-done.30 = f32[64,1152]{1,0:T(8,128)S(1)} collective-permute-done((f32[64,1152]{1,0:T(8,128)S(1)}, f32[64,1152]{1,0:T(8,128)S(1)}, u32[]{:S(2)}, u32[]{:S(2)}) %collective-permute-start.30) | collective-permute-done | bytes 294944 | tf_op jit(solution)/shard_map/ppermute | solution.py:570
  119.6 4.4 %collective-permute-start.31 = (f32[64,1152]{1,0:T(8,128)S(1)}, f32[64,1152]{1,0:T(8,128)S(1)}, u32[]{:S(2)}, u32[]{:S(2)}) collective-permute-start(f32[64,1152]{1,0:T(8,128)S(1)} %add.57), channel_id=1, source_target_pairs={{0,1},{1,2},{4,5},{5,6},{8,9},{9,10},{12,13},{13,14},{16,17},{17,1... | collective-permute-start | bytes 884744 | tf_op jit(solution)/shard_map/ppermute | solution.py:576
  124.7 2.5 %products.2 = (f32[64,1024]{1,0:T(8,128)S(1)}, f32[64,1024]{1,0:T(8,128)S(1)}, f32[64,1024]{1,0:T(8,128)S(1)}, f32[64,1024]{1,0:T(8,128)S(1)}, f32[64,1024]{1,0:T(8,128)S(1)}) custom-call(s32[10]{0:T(128)S(1)} %stack.55.flags.scalars, f32[32,512]{1,0:T(8,128)S(1)} %get-tuple-element.41.refs_0_, f32[32,512]{1,0:T(8,128)S(1)} %collective-permute-done.18.refs_1_, ...), custom_call_target="tpu_custom_call" | custom-call | flops 1073741824 | bytes 3145728 | tf_op jit(solution)/shard_map/products/pallas_call | solution.py:454
  127.2 4.4 %collective-permute-start.25 = (f32[64,1024]{1,0:T(8,128)S(1)}, f32[64,1024]{1,0:T(8,128)S(1)}, u32[]{:S(2)}, u32[]{:S(2)}) collective-permute-start(f32[64,1024]{1,0:T(8,128)S(1)} %get-tuple-element.45), channel_id=1, source_target_pairs={{0,1},{3,2},{4,5},{7,6},{8,9},{11,10},{12,13},{15,14},{16,17},{19,... | collective-permute-start | bytes 786440 | tf_op jit(solution)/shard_map/ppermute | solution.py:570
  131.7 2.5 %collective-permute-start.32 = (f32[64,1152]{1,0:T(8,128)S(1)}, f32[64,1152]{1,0:T(8,128)S(1)}, u32[]{:S(2)}, u32[]{:S(2)}) collective-permute-start(f32[64,1152]{1,0:T(8,128)S(1)} %add.58), channel_id=1, source_target_pairs={{0,1},{1,2},{2,3},{4,5},{5,6},{6,7},{8,9},{9,10},{10,11},{12,13},{... | collective-permute-start | bytes 884744 | tf_op jit(solution)/shard_map/ppermute | solution.py:576
  134.2 1.3 collective-permute-start.34
  135.5 2.8 %collective-permute-done.25 = f32[64,1024]{1,0:T(8,128)S(1)} collective-permute-done((f32[64,1024]{1,0:T(8,128)S(1)}, f32[64,1024]{1,0:T(8,128)S(1)}, u32[]{:S(2)}, u32[]{:S(2)}) %collective-permute-start.25) | collective-permute-done | bytes 262176 | tf_op jit(solution)/shard_map/ppermute | solution.py:570
  139.0 5.0 %collective-permute-start.26 = (f32[64,1024]{1,0:T(8,128)S(1)}, f32[64,1024]{1,0:T(8,128)S(1)}, u32[]{:S(2)}, u32[]{:S(2)}) collective-permute-start(f32[64,1024]{1,0:T(8,128)S(1)} %add.54), channel_id=1, source_target_pairs={{0,1},{1,2},{4,5},{5,6},{8,9},{9,10},{12,13},{13,14},{16,17},{17,1... | collective-permute-start | bytes 786440 | tf_op jit(solution)/shard_map/ppermute | solution.py:576
  144.1 1.3 collective-permute-start.29
  145.4 2.9 %collective-permute-done.26 = f32[64,1024]{1,0:T(8,128)S(1)} collective-permute-done((f32[64,1024]{1,0:T(8,128)S(1)}, f32[64,1024]{1,0:T(8,128)S(1)}, u32[]{:S(2)}, u32[]{:S(2)}) %collective-permute-start.26) | collective-permute-done | bytes 262176 | tf_op jit(solution)/shard_map/ppermute | solution.py:576
  148.3 6.8 %collective-permute-start.27 = (f32[64,1024]{1,0:T(8,128)S(1)}, f32[64,1024]{1,0:T(8,128)S(1)}, u32[]{:S(2)}, u32[]{:S(2)}) collective-permute-start(f32[64,1024]{1,0:T(8,128)S(1)} %add.55), channel_id=1, source_target_pairs={{0,1},{1,2},{2,3},{4,5},{5,6},{6,7},{8,9},{9,10},{10,11},{12,13},{... | collective-permute-start | bytes 786440 | tf_op jit(solution)/shard_map/ppermute | solution.py:576
  155.2 1.2 collective-permute-done.35.refs_4_
  156.4 2.1 %final.2.refs_5_ = f32[64,2048]{1,0:T(8,128)} custom-call(s32[10]{0:T(128)S(1)} %stack.55.flags.scalars, f32[64,2048]{1,0:T(8,128)S(1)} %copy-done.2, bf16[512,2048]{1,0:T(8,128)(2,1)S(1)} %get-tuple-element.33.foot_ref, f32[64,1152]{1,0:T(8,128)S(1)} %get-tuple-element.47.refs_0_, f32[64,1152]{1,0:T(8,128)S(1)} %collective-permute-done.32.refs_1_, ...), custom_call_target="tpu_custom_call" | custom-call | flops 100663296 | bytes 2359296 | tf_op jit(solution)/shard_map/final/pallas_call | solution.py:512
  159.0 1.9 %final.3 = f32[64,2048]{1,0:T(8,128)} custom-call(s32[10]{0:T(128)S(1)} %stack.55.flags.scalars, f32[64,2048]{1,0:T(8,128)S(1)} %copy-done.2, bf16[512,2048]{1,0:T(8,128)(2,1)S(1)} %get-tuple-element.33.foot_ref, f32[64,1024]{1,0:T(8,128)S(1)} %get-tuple-element.42.refs_0_, ...), custom_call_target="tpu_custom_call", output_to_operand_aliasing={{}: (8, {})} | custom-call | flops 100663296 | bytes 2359296 | tf_op jit(solution)/shard_map/final/pallas_call | solution.py:512
  (55 shorter events, 6.5 us)
Async XLA Ops:
  0.7 2.2 %copy-start = (f32[8,256,512]{2,1,0:T(8,128)S(1)}, f32[8,256,512]{2,1,0:T(8,128)}, u32[]{:S(2)}) copy-start(f32[8,256,512]{2,1,0:T(8,128)} %refs_0_.4) | copy-start | bytes 12582916
  2.9 9.4 %copy-start.1 = (f32[8,256,512]{2,1,0:T(8,128)S(1)}, f32[8,256,512]{2,1,0:T(8,128)}, u32[]{:S(2)}) copy-start(f32[8,256,512]{2,1,0:T(8,128)} %refs_0_.4) | copy-start | bytes 12582916
  2.9 42.8 %copy-start.3 = (f32[32,512]{1,0:T(8,128)S(1)}, f32[32,512]{1,0:T(8,128)}, u32[]{:S(2)}) copy-start(f32[32,512]{1,0:T(8,128)} %param.5) | copy-start | bytes 196612
  3.9 21.3 %collective-permute-start.2 = (f32[4,256,256]{2,1,0:T(8,128)S(1)}, f32[4,256,256]{2,1,0:T(8,128)S(1)}, u32[]{:S(2)}, u32[]{:S(2)}) collective-permute-start(f32[4,256,256]{2,1,0:T(8,128)S(1)} %get-tuple-element.30), channel_id=1, source_target_pairs={{12,28},{16,0},{13,29},{17,1},{14,30},{18,2},{15,31},{19,3}} | collective-permute-start | bytes 3145736 | tf_op jit(solution)/shard_map/ppermute | solution.py:624
  5.4 16.5 %collective-permute-start.6 = (f32[64,2048]{1,0:T(8,128)}, f32[64,2048]{1,0:T(8,128)S(1)}, u32[]{:S(2)}, u32[]{:S(2)}) collective-permute-start(f32[64,2048]{1,0:T(8,128)} %own_ref.3), channel_id=1, source_target_pairs={{1,0},{2,1},{3,2},{5,4},{6,5},{7,6},{9,8},{10,9},{11,10},{13,12},{... | collective-permute-start | bytes 1572872 | tf_op jit(solution)/shard_map/ppermute | solution.py:559
  6.7 16.5 %collective-permute-start.8 = (f32[64,2048]{1,0:T(8,128)}, f32[64,2048]{1,0:T(8,128)S(1)}, u32[]{:S(2)}, u32[]{:S(2)}) collective-permute-start(f32[64,2048]{1,0:T(8,128)} %own_ref.3), channel_id=1, source_target_pairs={{0,1},{1,2},{2,3},{4,5},{5,6},{6,7},{8,9},{9,10},{10,11},{12,13},{... | collective-permute-start | bytes 1572872 | tf_op jit(solution)/shard_map/ppermute | solution.py:558
  12.6 49.9 %copy-start.2 = (f32[64,2048]{1,0:T(8,128)S(1)}, f32[64,2048]{1,0:T(8,128)}, u32[]{:S(2)}) copy-start(f32[64,2048]{1,0:T(8,128)} %own_ref.3) | copy-start | bytes 1572868
  12.6 31.8 %collective-permute-start.4 = (f32[4,256,256]{2,1,0:T(8,128)S(1)}, f32[4,256,256]{2,1,0:T(8,128)S(1)}, u32[]{:S(2)}, u32[]{:S(2)}) collective-permute-start(f32[4,256,256]{2,1,0:T(8,128)S(1)} %get-tuple-element.54), channel_id=1, source_target_pairs={{0,4},{4,8},{8,12},{12,16},{16,20},{20,24},{24,28},{1,5},{5,9},{9,... | collective-permute-start | bytes 3145736 | tf_op jit(solution)/shard_map/ppermute | solution.py:626
  21.9 14.4 %collective-permute-start.7 = (f32[64,2048]{1,0:T(8,128)S(1)}, f32[64,2048]{1,0:T(8,128)S(1)}, u32[]{:S(2)}, u32[]{:S(2)}) collective-permute-start(f32[64,2048]{1,0:T(8,128)S(1)} %collective-permute-done.6.refs_1_), channel_id=1, source_target_pairs={{1,0},{2,1},{5,4},{6,5},{9,8},{10,9},{13,12},{14,13},{17,16},{18,1... | collective-permute-start | bytes 1572872 | tf_op jit(solution)/shard_map/ppermute | solution.py:559
  23.2 14.4 %collective-permute-start.9 = (f32[64,2048]{1,0:T(8,128)S(1)}, f32[64,2048]{1,0:T(8,128)S(1)}, u32[]{:S(2)}, u32[]{:S(2)}) collective-permute-start(f32[64,2048]{1,0:T(8,128)S(1)} %collective-permute-done.8.refs_6_), channel_id=1, source_target_pairs={{1,2},{2,3},{5,6},{6,7},{9,10},{10,11},{13,14},{14,15},{17,18},{18... | collective-permute-start | bytes 1572872 | tf_op jit(solution)/shard_map/ppermute | solution.py:558
  23.9 21.8 %collective-permute-start.5 = (f32[4,256,256]{2,1,0:T(8,128)S(1)}, f32[4,256,256]{2,1,0:T(8,128)S(1)}, u32[]{:S(2)}, u32[]{:S(2)}) collective-permute-start(f32[4,256,256]{2,1,0:T(8,128)S(1)} %get-tuple-element.53), channel_id=1, source_target_pairs={{4,0},{8,4},{12,8},{16,12},{20,16},{24,20},{28,24},{5,1},{9,5},{13... | collective-permute-start | bytes 3145736 | tf_op jit(solution)/shard_map/ppermute | solution.py:627
  25.2 40.1 %collective-permute-start = (f32[4,256,256]{2,1,0:T(8,128)S(1)}, f32[4,256,256]{2,1,0:T(8,128)S(1)}, u32[]{:S(2)}, u32[]{:S(2)}) collective-permute-start(f32[4,256,256]{2,1,0:T(8,128)S(1)} %get-tuple-element.28), channel_id=1, source_target_pairs={{0,4},{4,8},{8,12},{16,20},{20,24},{24,28},{1,5},{5,9},{9,13},{17,... | collective-permute-start | bytes 3145736 | tf_op jit(solution)/shard_map/ppermute | solution.py:626
  36.3 29.0 %collective-permute-start.1 = (f32[4,256,256]{2,1,0:T(8,128)S(1)}, f32[4,256,256]{2,1,0:T(8,128)S(1)}, u32[]{:S(2)}, u32[]{:S(2)}) collective-permute-start(f32[4,256,256]{2,1,0:T(8,128)S(1)} %get-tuple-element.29), channel_id=1, source_target_pairs={{4,0},{8,4},{12,8},{20,16},{24,20},{28,24},{5,1},{9,5},{13,9},{21,... | collective-permute-start | bytes 3145736 | tf_op jit(solution)/shard_map/ppermute | solution.py:627
  37.6 27.7 %collective-permute-start.3 = (f32[4,256,256]{2,1,0:T(8,128)S(1)}, f32[4,256,256]{2,1,0:T(8,128)S(1)}, u32[]{:S(2)}, u32[]{:S(2)}) collective-permute-start(f32[4,256,256]{2,1,0:T(8,128)S(1)} %collective-permute-done.2), channel_id=1, source_target_pairs={{28,16},{0,12},{29,17},{1,13},{30,18},{2,14},{31,19},{3,15}} | collective-permute-start | bytes 3145736 | tf_op jit(solution)/shard_map/ppermute | solution.py:625
  44.4 18.0 %collective-permute-start.10 = (f32[64,2048]{1,0:T(8,128)S(1)}, f32[64,2048]{1,0:T(8,128)S(1)}, u32[]{:S(2)}, u32[]{:S(2)}) collective-permute-start(f32[64,2048]{1,0:T(8,128)S(1)} %choose.1), channel_id=1, source_target_pairs={{2,3},{1,0},{6,7},{5,4},{10,11},{9,8},{14,15},{13,12},{18,19},{17,... | collective-permute-start | bytes 1572872 | tf_op jit(solution)/shard_map/ppermute | solution.py:556
  45.7 32.7 %collective-permute-start.11 = (f32[1,32,512]{2,1,0:T(8,128)S(1)}, f32[1,32,512]{2,1,0:T(8,128)S(1)}, u32[]{:S(2)}, u32[]{:S(2)}) collective-permute-start(f32[1,32,512]{2,1,0:T(8,128)S(1)} %bitcast.33), channel_id=1, source_target_pairs={{0,16},{4,20},{8,24},{12,28},{16,0},{20,4},{24,8},{28,12},{1,17},{... | collective-permute-start | bytes 196616 | tf_op jit(solution)/shard_map/ppermute | solution.py:633
  78.3 3.4 %collective-permute-start.14 = (f32[4,32,768]{2,1,0:T(8,128)S(1)}, f32[4,32,768]{2,1,0:T(8,128)S(1)}, u32[]{:S(2)}, u32[]{:S(2)}) collective-permute-start(f32[4,32,768]{2,1,0:T(8,128)S(1)} %get-tuple-element.40), channel_id=1, source_target_pairs={{0,4},{4,0},{8,12},{12,8},{16,20},{20,16},{24,28},{28,24},{1,5},{5... | collective-permute-start | bytes 1179656 | tf_op jit(solution)/shard_map/ppermute | solution.py:654
  78.4 1.9 %collective-permute-start.12 = (f32[2,32,512]{2,1,0:T(8,128)S(1)}, f32[2,32,512]{2,1,0:T(8,128)S(1)}, u32[]{:S(2)}, u32[]{:S(2)}) collective-permute-start(f32[2,32,512]{2,1,0:T(8,128)S(1)} %pad_maximum_fusion.1), channel_id=1, source_target_pairs={{0,4},{4,0},{8,12},{12,8},{16,20},{20,16},{24,28},{28,24},{1,5},{5... | collective-permute-start | bytes 393224 | tf_op jit(solution)/shard_map/ppermute | solution.py:633
  80.3 9.2 %collective-permute-start.13 = (f32[4,32,512]{2,1,0:T(8,128)S(1)}, f32[4,32,512]{2,1,0:T(8,128)S(1)}, u32[]{:S(2)}, u32[]{:S(2)}) collective-permute-start(f32[4,32,512]{2,1,0:T(8,128)S(1)} %pad_maximum_fusion.refs_0_), channel_id=1, source_target_pairs={{0,8},{4,12},{8,0},{12,4},{16,24},{20,28},{24,16},{28,20},{1,9},{5... | collective-permute-start | bytes 786440 | tf_op jit(solution)/shard_map/ppermute | solution.py:637
  81.7 9.9 %collective-permute-start.15 = (f32[32,768]{1,0:T(8,128)S(1)}, f32[32,768]{1,0:T(8,128)S(1)}, u32[]{:S(2)}, u32[]{:S(2)}) collective-permute-start(f32[32,768]{1,0:T(8,128)S(1)} %get-tuple-element.57), channel_id=1, source_target_pairs={{0,8},{4,12},{8,0},{12,4},{16,24},{20,28},{24,16},{28,20},{1,9},{5... | collective-permute-start | bytes 294920 | tf_op jit(solution)/shard_map/ppermute | solution.py:657
  82.5 9.2 %collective-permute-start.16 = (f32[32,768]{1,0:T(8,128)S(1)}, f32[32,768]{1,0:T(8,128)S(1)}, u32[]{:S(2)}, u32[]{:S(2)}) collective-permute-start(f32[32,768]{1,0:T(8,128)S(1)} %get-tuple-element.56), channel_id=1, source_target_pairs={{0,16},{4,20},{8,24},{12,28},{16,0},{20,4},{24,8},{28,12},{1,17},{... | collective-permute-start | bytes 294920 | tf_op jit(solution)/shard_map/ppermute | solution.py:657
  83.9 10.0 %collective-permute-start.17 = (f32[32,768]{1,0:T(8,128)S(1)}, f32[32,768]{1,0:T(8,128)S(1)}, u32[]{:S(2)}, u32[]{:S(2)}) collective-permute-start(f32[32,768]{1,0:T(8,128)S(1)} %get-tuple-element.55), channel_id=1, source_target_pairs={{0,24},{4,28},{8,16},{12,20},{16,8},{20,12},{24,0},{28,4},{1,25},{... | collective-permute-start | bytes 294920 | tf_op jit(solution)/shard_map/ppermute | solution.py:657
  95.4 4.3 %collective-permute-start.18 = (f32[32,512]{1,0:T(8,128)S(1)}, f32[32,512]{1,0:T(8,128)S(1)}, u32[]{:S(2)}, u32[]{:S(2)}) collective-permute-start(f32[32,512]{1,0:T(8,128)S(1)} %get-tuple-element.41.refs_0_), channel_id=1, source_target_pairs={{0,8},{4,12},{8,0},{12,4},{16,24},{20,28},{24,16},{28,20},{1,9},{5... | collective-permute-start | bytes 196616 | tf_op jit(solution)/shard_map/ppermute | solution.py:661
  97.1 4.3 %collective-permute-start.19 = (f32[32,512]{1,0:T(8,128)S(1)}, f32[32,512]{1,0:T(8,128)S(1)}, u32[]{:S(2)}, u32[]{:S(2)}) collective-permute-start(f32[32,512]{1,0:T(8,128)S(1)} %get-tuple-element.41.refs_0_), channel_id=1, source_target_pairs={{0,16},{4,20},{8,24},{12,28},{16,0},{20,4},{24,8},{28,12},{1,17},{... | collective-permute-start | bytes 196616 | tf_op jit(solution)/shard_map/ppermute | solution.py:661
  97.4 5.2 %collective-permute-start.20 = (f32[32,512]{1,0:T(8,128)S(1)}, f32[32,512]{1,0:T(8,128)S(1)}, u32[]{:S(2)}, u32[]{:S(2)}) collective-permute-start(f32[32,512]{1,0:T(8,128)S(1)} %get-tuple-element.41.refs_0_), channel_id=1, source_target_pairs={{0,24},{4,28},{8,16},{12,20},{16,8},{20,12},{24,0},{28,4},{1,25},{... | collective-permute-start | bytes 196616 | tf_op jit(solution)/shard_map/ppermute | solution.py:661
  98.9 3.7 %collective-permute-start.21 = (f32[32,512]{1,0:T(8,128)S(1)}, f32[32,512]{1,0:T(8,128)S(1)}, u32[]{:S(2)}, u32[]{:S(2)}) collective-permute-start(f32[32,512]{1,0:T(8,128)S(1)} %get-tuple-element.41.refs_0_), channel_id=1, source_target_pairs={{0,4},{4,0},{8,12},{12,8},{16,20},{20,16},{24,28},{28,24},{1,5},{5... | collective-permute-start | bytes 196616 | tf_op jit(solution)/shard_map/ppermute | solution.py:664
  99.7 2.9 %collective-permute-start.22 = (f32[32,512]{1,0:T(8,128)S(1)}, f32[32,512]{1,0:T(8,128)S(1)}, u32[]{:S(2)}, u32[]{:S(2)}) collective-permute-start(f32[32,512]{1,0:T(8,128)S(1)} %collective-permute-done.18.refs_1_), channel_id=1, source_target_pairs={{0,4},{4,0},{8,12},{12,8},{16,20},{20,16},{24,28},{28,24},{1,5},{5... | collective-permute-start | bytes 196616 | tf_op jit(solution)/shard_map/ppermute | solution.py:664
  101.4 1.3 collective-permute-start.23
  102.6 1.3 collective-permute-start.24
  106.7 12.8 %collective-permute-start.30 = (f32[64,1152]{1,0:T(8,128)S(1)}, f32[64,1152]{1,0:T(8,128)S(1)}, u32[]{:S(2)}, u32[]{:S(2)}) collective-permute-start(f32[64,1152]{1,0:T(8,128)S(1)} %get-tuple-element.50), channel_id=1, source_target_pairs={{0,1},{3,2},{4,5},{7,6},{8,9},{11,10},{12,13},{15,14},{16,17},{19,... | collective-permute-start | bytes 884744 | tf_op jit(solution)/shard_map/ppermute | solution.py:570
  119.6 12.0 %collective-permute-start.31 = (f32[64,1152]{1,0:T(8,128)S(1)}, f32[64,1152]{1,0:T(8,128)S(1)}, u32[]{:S(2)}, u32[]{:S(2)}) collective-permute-start(f32[64,1152]{1,0:T(8,128)S(1)} %add.57), channel_id=1, source_target_pairs={{0,1},{1,2},{4,5},{5,6},{8,9},{9,10},{12,13},{13,14},{16,17},{17,1... | collective-permute-start | bytes 884744 | tf_op jit(solution)/shard_map/ppermute | solution.py:576
  124.0 10.2 %collective-permute-start.33 = (f32[64,1152]{1,0:T(8,128)S(1)}, f32[64,1152]{1,0:T(8,128)S(1)}, u32[]{:S(2)}, u32[]{:S(2)}) collective-permute-start(f32[64,1152]{1,0:T(8,128)S(1)} %add.57), channel_id=1, source_target_pairs={{3,2},{2,1},{7,6},{6,5},{11,10},{10,9},{15,14},{14,13},{19,18},{18... | collective-permute-start | bytes 884744 | tf_op jit(solution)/shard_map/ppermute | solution.py:577
  127.2 11.1 %collective-permute-start.25 = (f32[64,1024]{1,0:T(8,128)S(1)}, f32[64,1024]{1,0:T(8,128)S(1)}, u32[]{:S(2)}, u32[]{:S(2)}) collective-permute-start(f32[64,1024]{1,0:T(8,128)S(1)} %get-tuple-element.45), channel_id=1, source_target_pairs={{0,1},{3,2},{4,5},{7,6},{8,9},{11,10},{12,13},{15,14},{16,17},{19,... | collective-permute-start | bytes 786440 | tf_op jit(solution)/shard_map/ppermute | solution.py:570
  131.7 23.5 %collective-permute-start.32 = (f32[64,1152]{1,0:T(8,128)S(1)}, f32[64,1152]{1,0:T(8,128)S(1)}, u32[]{:S(2)}, u32[]{:S(2)}) collective-permute-start(f32[64,1152]{1,0:T(8,128)S(1)} %add.58), channel_id=1, source_target_pairs={{0,1},{1,2},{2,3},{4,5},{5,6},{6,7},{8,9},{9,10},{10,11},{12,13},{... | collective-permute-start | bytes 884744 | tf_op jit(solution)/shard_map/ppermute | solution.py:576
  134.2 20.9 %collective-permute-start.34 = (f32[64,1152]{1,0:T(8,128)S(1)}, f32[64,1152]{1,0:T(8,128)S(1)}, u32[]{:S(2)}, u32[]{:S(2)}) collective-permute-start(f32[64,1152]{1,0:T(8,128)S(1)} %add.60), channel_id=1, source_target_pairs={{3,2},{2,1},{1,0},{7,6},{6,5},{5,4},{11,10},{10,9},{9,8},{15,14},{... | collective-permute-start | bytes 884744 | tf_op jit(solution)/shard_map/ppermute | solution.py:577
  138.3 5.7 %collective-permute-start.28 = (f32[64,1024]{1,0:T(8,128)S(1)}, f32[64,1024]{1,0:T(8,128)S(1)}, u32[]{:S(2)}, u32[]{:S(2)}) collective-permute-start(f32[64,1024]{1,0:T(8,128)S(1)} %add.54), channel_id=1, source_target_pairs={{3,2},{2,1},{7,6},{6,5},{11,10},{10,9},{15,14},{14,13},{19,18},{18... | collective-permute-start | bytes 786440 | tf_op jit(solution)/shard_map/ppermute | solution.py:577
  139.0 9.3 %collective-permute-start.26 = (f32[64,1024]{1,0:T(8,128)S(1)}, f32[64,1024]{1,0:T(8,128)S(1)}, u32[]{:S(2)}, u32[]{:S(2)}) collective-permute-start(f32[64,1024]{1,0:T(8,128)S(1)} %add.54), channel_id=1, source_target_pairs={{0,1},{1,2},{4,5},{5,6},{8,9},{9,10},{12,13},{13,14},{16,17},{17,1... | collective-permute-start | bytes 786440 | tf_op jit(solution)/shard_map/ppermute | solution.py:576
  144.1 14.4 %collective-permute-start.29 = (f32[64,1024]{1,0:T(8,128)S(1)}, f32[64,1024]{1,0:T(8,128)S(1)}, u32[]{:S(2)}, u32[]{:S(2)}) collective-permute-start(f32[64,1024]{1,0:T(8,128)S(1)} %add.56), channel_id=1, source_target_pairs={{3,2},{2,1},{1,0},{7,6},{6,5},{5,4},{11,10},{10,9},{9,8},{15,14},{... | collective-permute-start | bytes 786440 | tf_op jit(solution)/shard_map/ppermute | solution.py:577
  148.3 10.7 %collective-permute-start.27 = (f32[64,1024]{1,0:T(8,128)S(1)}, f32[64,1024]{1,0:T(8,128)S(1)}, u32[]{:S(2)}, u32[]{:S(2)}) collective-permute-start(f32[64,1024]{1,0:T(8,128)S(1)} %add.55), channel_id=1, source_target_pairs={{0,1},{1,2},{2,3},{4,5},{5,6},{6,7},{8,9},{9,10},{10,11},{12,13},{... | collective-permute-start | bytes 786440 | tf_op jit(solution)/shard_map/ppermute | solution.py:576
  155.1 1.3 collective-permute-start.35

commit v4 on v3

--- a/solution.py
+++ b/solution.py
@@ -13,7 +13,7 @@
 GROUP = 4
 HALVES = 2
 
-HERE, CORE, CHIP, FIRST, TURNED, INSIDE, BENT, CORNER = 0, 1, 2, 3, 4, 5, 7, 9
+HERE, CORE, CHIP, TURNED, INSIDE, BENT = 0, 1, 2, 3, 4, 6
 
 NN = ((1,), (0,))
 NT = ((1,), (1,))
@@ -54,19 +54,16 @@
     return jax.ShapeDtypeStruct(shape, dtype)
 
 
-def edges_call(flags, raw, halo, begin, frames, with_corner):
+def edges_call(flags, raw, halo, begin, frames):
     rows, cols, _ = raw.shape
     shift = rows - halo
-    outs = 3 if with_corner else 2
-
-    def kernel(flags, raw_ref, *refs):
-        out_refs, sems = refs[:outs], refs[outs]
-        starts = [0, shift, flags[CORNER] * shift]
+
+    def kernel(flags, raw_ref, inner_ref, outer_ref, sems):
+        core = flags[CORE]
+        lanes = pl.ds(begin, frames)
         copies = [
-            pltpu.make_async_copy(
-                raw_ref.at[pl.ds(starts[k], halo), :, pl.ds(begin, frames)], out_refs[k], sems.at[k]
-            )
-            for k in range(outs)
+            pltpu.make_async_copy(raw_ref.at[pl.ds(start, halo), :, lanes], out_ref, sems.at[k])
+            for k, (start, out_ref) in enumerate((((1 - core) * shift, inner_ref), (core * shift, outer_ref)))
         ]
         for copy in copies:
             copy.start()
@@ -80,19 +77,19 @@
             num_scalar_prefetch=1,
             grid=(1,),
             in_specs=[pl.BlockSpec(memory_space=pltpu.HBM)],
-            out_specs=[pl.BlockSpec(block, lambda i, flags: (0, 0, 0))] * outs,
-            scratch_shapes=[pltpu.SemaphoreType.DMA((outs,))],
+            out_specs=[pl.BlockSpec(block, lambda i, flags: (0, 0, 0))] * 2,
+            scratch_shapes=[pltpu.SemaphoreType.DMA((2,))],
         ),
-        out_shape=[shaped(*block)] * outs,
-        cost_estimate=cost(1, 2 * outs * halo * cols * frames * 4),
+        out_shape=[shaped(*block)] * 2,
+        cost_estimate=cost(1, 4 * halo * cols * frames * 4),
         compiler_params=grant(8),
         name="edges",
     )(flags, raw)
 
 
-def diffuse_call(flags, raw, halo_up, halo_down, detour, movie, pair, begin, pair_begin, pair_frames):
+def diffuse_call(flags, raw, halo_inner, halo_outer, detour, movie, pair, begin, pair_begin, pair_frames):
     rows, cols, total = raw.shape
-    halo, _, frames = halo_up.shape
+    halo, _, frames = halo_inner.shape
     groups = frames // LANES
     carried = [array for array in (movie, *pair) if array is not None]
     width = 64
@@ -118,14 +115,19 @@
                     ref.at[:, :, cut], first_bufs.at[here, pl.ds(start, count), inside, :], in_sems.at[here, part]
                 )
 
-            made = [(None, one(sources[0], wide, halo, rows, 0))]
-            for part, start, source in ((1, 0, 1), (2, halo + rows, 2)):
-                plain = one(sources[source], lanes, start, halo, part)
-                if detour is None:
-                    made.append((None, plain))
-                else:
-                    made.append((flags[BENT + part - 1] == 0, plain))
-                    made.append((flags[BENT + part - 1] == 1, one(sources[3], lanes, start, halo, part)))
+            far_side = halo + rows
+            inner_at = (1 - flags[CORE]) * far_side
+            outer_at = flags[CORE] * far_side
+            made = [
+                (None, one(sources[0], wide, halo, rows, 0)),
+                (None, one(sources[1], lanes, inner_at, halo, 1)),
+            ]
+            plain = one(sources[2], lanes, outer_at, halo, 2)
+            if detour is None:
+                made.append((None, plain))
+            else:
+                made.append((flags[BENT] == 0, plain))
+                made.append((flags[BENT] == 1, one(sources[3], lanes, outer_at, halo, 2)))
             return made
 
         def run(at, act):
@@ -208,7 +210,7 @@
             give(group).wait()
 
     outside = pl.BlockSpec(memory_space=pltpu.HBM)
-    operands = [flags, raw, halo_up, halo_down]
+    operands = [flags, raw, halo_inner, halo_outer]
     if detour is not None:
         operands.append(detour)
     outputs = [k for k, array in enumerate((movie, *pair)) if array is not None]
@@ -239,8 +241,8 @@
     )(*operands)
 
 
-def footprints_call(scalars, own, pairs):
-    count = len(pairs) + 1
+def footprints_call(scalars, own, entries):
+    count = len(entries) + 1
     share, pixel_count = own.shape
     rank = share * count
     block = 512
@@ -248,20 +250,20 @@
 
     def kernel(scalars, *refs):
         own_ref = refs[0]
-        pair_refs = [(refs[1 + 2 * k], refs[2 + 2 * k]) for k in range(count - 1)]
+        entry_refs = [(refs[1 + 2 * k], refs[2 + 2 * k]) for k in range(count - 1)]
         out_ref, gram_ref, total = refs[2 * count - 1 :]
         here = scalars[HERE]
         step = pl.program_id(0)
 
-        def put(slot, value):
-            at = pl.multiple_of(lax.rem(here + slot, count) * share, share)
+        def put(place, value):
+            at = pl.multiple_of(place * share, share)
             high, low = split(value)
             out_ref[pl.ds(at, share), :] = high
             out_ref[pl.ds(rank + at, share), :] = low
 
-        put(0, own_ref[...])
-        for s, (from_above, from_below) in enumerate(pair_refs, 1):
-            put(s, jnp.where(here + s < count, from_above[...], from_below[...]))
+        put(here, own_ref[...])
+        for (first_ref, second_ref), (_, _, test, place) in zip(entry_refs, entries):
+            put(place(here), jnp.where(test(here), first_ref[...], second_ref[...]))
 
         @pl.when(step == 0)
         def _():
@@ -275,7 +277,7 @@
             gram_ref[...] = total[0:rank, :] + (cross + cross.T)
 
     foot_spec = pl.BlockSpec((share, block), lambda k, s: (0, k))
-    flat = [array for pair in pairs for array in pair]
+    flat = [array for entry in entries for array in entry[:2]]
     return pl.pallas_call(
         kernel,
         grid_spec=pltpu.PrefetchScalarGridSpec(
@@ -393,7 +395,7 @@
     )(scalars, *stacks, keep, arrived, *parts)
 
 
-def products_call(scalars, near, far, movies, half, count, with_gram):
+def products_call(scalars, near, far, movies, half, count, places, with_gram):
     chips = len(near)
     trace_rows, frames = near[0].shape
     rank = 2 * chips * trace_rows
@@ -405,7 +407,7 @@
     block = rank
     steps = part // block
     columns = part + (half_rank if with_gram else 0)
-    outs = count + 1
+    outs = len(places)
 
     def kernel(scalars, *refs):
         near_refs, far_refs, refs = refs[:chips], refs[chips : 2 * chips], refs[2 * chips :]
@@ -429,8 +431,7 @@
             width = total.shape[1]
             result[:, 0:width] = total
             for k, out_ref in enumerate(out_refs):
-                slot = lax.rem(here + k, count) if k < count else scalars[FIRST]
-                row = pl.multiple_of(slot * share, share)
+                row = pl.multiple_of(places[k](here) * share, share)
                 out_ref[:, pl.ds(at, width)] = result[pl.ds(row, share), 0:width]
 
         both = jnp.zeros((2 * rank, block), jnp.float32)
@@ -546,6 +547,23 @@
 
 
 def line_gather(scalars, block, axis, count):
+    if count == 4:
+        middle = [(1, 2), (2, 1)]
+        outward = [(1, 0), (2, 3)]
+        near = lax.ppermute(block, axis, [(k, k ^ 1) for k in range(count)])
+        across = lax.ppermute(block, axis, middle)
+        far = lax.ppermute(near, axis, middle)
+        out_across = lax.ppermute(across, axis, outward)
+        out_far = lax.ppermute(far, axis, outward)
+
+        def between(here):
+            return (here == 1) | (here == 2)
+
+        return [
+            (near, near, between, lambda here: here ^ 1),
+            (across, out_across, between, lambda here: jnp.where(here < 2, 2, 1)),
+            (far, out_far, between, lambda here: jnp.where(here < 2, 3, 0)),
+        ]
     up, down = {}, {}
     last_up = last_down = block
     for r in range(1, count):
@@ -558,10 +576,35 @@
             last_up = lax.ppermute(last_up, axis, up_pairs)
             last_down = lax.ppermute(last_down, axis, down_pairs)
         up[r], down[r] = last_up, last_down
-    return [(down[s], up[count - s]) for s in range(1, count)]
+    return [
+        (down[s], up[count - s], lambda here, s=s: here + s < count, lambda here, s=s: lax.rem(here + s, count))
+        for s in range(1, count)
+    ]
+
+
+def scatter_places(count):
+    if count == 4:
+        return [
+            lambda here: here,
+            lambda here: here ^ 1,
+            lambda here: 3 - here,
+            lambda here: lax.rem(here + 2, count),
+        ]
+    slots = [lambda here, s=s: lax.rem(here + s, count) for s in range(count)]
+    return slots + [lambda here: lax.rem(here + jnp.where(here == 0, count - 1, 1), count)]
 
 
 def line_scatter(blocks, axis, count):
+    if count == 4:
+        own, beside, opposite, remaining = blocks
+        inward = [(0, 1), (3, 2)]
+        middle = [(1, 2), (2, 1)]
+        first = lax.ppermute(opposite, axis, inward)
+        second = lax.ppermute(remaining, axis, inward)
+        third = lax.ppermute(remaining + first, axis, middle)
+        fourth = lax.ppermute(beside + third, axis, [(k, k ^ 1) for k in range(count)])
+        fifth = lax.ppermute(opposite + second, axis, middle)
+        return [own, fourth, fifth]
     up_last = down_last = None
     for r in range(1, count):
         up_pairs = [(k, k + 1) for k in range(r)]
@@ -597,35 +640,35 @@
 
     inner = (pix > 0).astype(jnp.int32)
     outer = (pix < pix_count - 1).astype(jnp.int32)
-    corner = (lax.rem(pix, GROUP) == GROUP - 1).astype(jnp.int32)
-    first_out = lax.rem(here + jnp.where(here == 0, count - 1, 1), count)
     turned = (here == 1).astype(jnp.int32)
-    bend_up = (lax.rem(pix, GROUP) == 0) * inner
-    flags = scalars = jnp.stack(
-        [here, core, lax.div(pix, 2), first_out, turned, inner, outer, bend_up, corner * outer, corner]
-    ).astype(jnp.int32)
-
-    pairs = line_gather(scalars, footprints, "tm", count)
+    bend = (lax.rem(pix, GROUP) == 0) * inner + (lax.rem(pix, GROUP) == GROUP - 1) * outer
+    flags = scalars = jnp.stack([here, core, lax.div(pix, 2), turned, inner, outer, bend]).astype(jnp.int32)
+
+    entries = line_gather(scalars, footprints, "tm", count)
 
     bent = [k for k in range(pix_count - 1) if k % GROUP == GROUP - 1] if pix_count % GROUP == 0 else []
     halos = []
     for c, width in enumerate(widths):
         begin = sum(widths[:c]) * LANES
         last = c == len(widths) - 1 and bool(bent)
-        send = [(k, k + 1) for k in range(pix_count - 1) if not (last and k in bent)]
+        joins = [(k, k + 1) for k in range(1, pix_count - 1, 2) if not (last and k in bent)]
+        joins += [(b, a) for a, b in joins]
         if c == 0:
-            edges = raw_movie[:halo, :, : width * LANES], raw_movie[rows - halo :, :, : width * LANES]
+            shift = rows - halo
+            size = (halo, cols, width * LANES)
+            inward = lax.dynamic_slice(raw_movie, ((1 - core) * shift, 0, begin), size)
+            outward = lax.dynamic_slice(raw_movie, (core * shift, 0, begin), size)
         else:
-            edges = edges_call(flags, raw_movie, halo, begin, width * LANES, last)
+            inward, outward = edges_call(flags, raw_movie, halo, begin, width * LANES)
         detour = None
         if last:
             first = [(k, k + GROUP) for k in bent] + [(k + 1, k + 1 - GROUP) for k in bent]
             second = [(k + GROUP, k + 1) for k in bent] + [(k + 1 - GROUP, k) for k in bent]
-            detour = lax.ppermute(edges[2], "pix", first)
+            detour = lax.ppermute(outward, "pix", first)
             detour = lax.ppermute(detour, "pix", second)
-        from_above = lax.ppermute(edges[1], "pix", send)
-        from_below = lax.ppermute(edges[0], "pix", [(b, a) for a, b in send])
-        halos.append((from_above, from_below, detour))
+        from_outer = lax.ppermute(outward, "pix", joins)
+        from_inner = lax.ppermute(inward, "pix", swap(1))
+        halos.append((from_inner, from_outer, detour))
 
     held, masks = traces[None], [0]
     hops = [mask for mask in (4, 8, 16, 32, 64, 1) if mask < pix_count]
@@ -649,7 +692,7 @@
             pair_begin += widths[c]
         movies.append(tuple(array.reshape(pixel_count, pair_frames) for array in pair))
 
-    foot, gram = footprints_call(scalars, footprints, pairs)
+    foot, gram = footprints_call(scalars, footprints, entries)
     keep, send = numerator_call(scalars, foot, movies, gram, trace_rows)
     arrived = lax.ppermute(send, "pix", swap(1))
     parts = []
@@ -665,7 +708,7 @@
 
     products = []
     for h in range(HALVES):
-        products.append(products_call(scalars, near, far, movies, h, count, h == 0))
+        products.append(products_call(scalars, near, far, movies, h, count, scatter_places(count), h == 0))
     sums = [line_scatter(blocks, "tm", count) for blocks in products]
     part = pixel_count // HALVES
     gram_mine = sum(array[:, part:] for array in sums[0])

time: 162 us -> 153 us (0.944)
  starting transfers between devices: 74.2 us -> 53.3 us
  waiting for transfers between devices: 44.7 us -> 55.7 us
  local copies, waits for them, and re-layouts: 2.53 us -> 4.99 us
    ppermute x20, starting transfers between devices: 52.1 us -> 35.3 us  [the longest x2 9.55 us: line_scatter(): first = lax.ppermute(opposite, axis, inward)]
    ppermute x20, waiting for transfers between devices: 28.6 us -> 39.6 us  [the longest x1 10.4 us: line_gather(): near = lax.ppermute(block, axis, [(k, k ^ 1) for k in range(count)])]
    ppermute x1, starting transfers between devices: 5.97 us -> 2.68 us  [compute(): detour = lax.ppermute(detour, 'pix', second)]
    dynamic_slice x0 -> x1, local copies, waits for them, and re-layouts: none -> 2.71 us  [compute(): outward = lax.dynamic_slice(raw_movie, (core * shift, 0, begin), size)]
  transfers between devices with their start and end apart: 36 -> 36, of which waited for: 16 -> 16; matrix products, arithmetic and copies ran while one was open for 0% -> 0% of each run, Pallas kernels for 19% -> 20%
where the time goes in v4:
time: 153 us; the launch traced here: 152 us
  waiting for transfers between devices  55.7 us (36%)
  starting transfers between devices  53.3 us (35%)
  Pallas kernels  37.1 us (24%)
  local copies, waits for them, and re-layouts  4.99 us (3%)
    pallas_call x2, Pallas kernels, diffuse_call(): pl.pallas_call(kernel, grid_spec=pltpu.PrefetchScalarGridSpec(num_scalar_...  19.4 us
    ppermute x1, waiting for transfers between devices, line_gather(): near = lax.ppermute(block, axis, [(k, k ^ 1) for k in range(count)])  10.4 us
    ppermute x2, starting transfers between devices, line_scatter(): first = lax.ppermute(opposite, axis, inward)  9.55 us
    ppermute x2, waiting for transfers between devices, line_scatter(): second = lax.ppermute(remaining, axis, inward)  8.46 us
    ppermute x2, waiting for transfers between devices, line_scatter(): first = lax.ppermute(opposite, axis, inward)  7.91 us
    ppermute x1, waiting for transfers between devices, line_gather(): out_across = lax.ppermute(across, axis, outward)  6.33 us
    ppermute x2, starting transfers between devices, compute(): lax.ppermute(held, 'pix', swap(mask))  6.21 us
    ppermute x1, waiting for transfers between devices, line_gather(): out_far = lax.ppermute(far, axis, outward)  5.47 us
  transfers between devices with their start and end apart: 36, of which 16 were waited for; matrix products, arithmetic and copies ran while one was open for 0% of the time, Pallas kernels for 20%

profile of v4, /device:TPU:0, one launch (start us, length us, event | category | flops | bytes accessed | tf_op | source)
XLA Modules:
  0.0 152.3 jit_solution(15598937015048192781)
XLA Ops:
  0.7 2.7 %constant_dynamic-slice_fusion = (f32[4,256,256]{2,1,0:T(8,128)S(1)}, f32[4,256,256]{2,1,0:T(8,128)}) fusion(f32[8,256,512]{2,1,0:T(8,128)} %refs_0_.4, s32[]{:T(128)S(6)} %select_n.7, s32[]{:T(128)S(6)} %select_n.6), kind=kLoop, calls=%fused_computation.10 | loop fusion | bytes 4194312 | tf_op jit(solution)/shard_map/dynamic_slice | solution.py:660
  3.9 2.2 %copy-done = f32[8,256,512]{2,1,0:T(8,128)S(1)} copy-done((f32[8,256,512]{2,1,0:T(8,128)S(1)}, f32[8,256,512]{2,1,0:T(8,128)}, u32[]{:S(2)}) %copy-start) | copy-done | bytes 4194328
  6.1 0.8 edges.1
  7.0 1.4 collective-permute-start.2
  8.4 0.7 collective-permute-start.5
  9.2 2.6 %collective-permute-start.6 = (f32[64,2048]{1,0:T(8,128)S(1)}, f32[64,2048]{1,0:T(8,128)S(1)}, u32[]{:S(2)}, u32[]{:S(2)}) collective-permute-start(f32[64,2048]{1,0:T(8,128)S(1)} %copy-done.2), channel_id=1, source_target_pairs={{0,1},{1,0},{2,3},{3,2},{4,5},{5,4},{6,7},{7,6},{8,9},{9,8},{10,11... | collective-permute-start | bytes 1572872 | tf_op jit(solution)/shard_map/ppermute | solution.py:553
  12.5 10.4 %collective-permute-done.6.refs_1_.refs_2_ = f32[64,2048]{1,0:T(8,128)S(1)} collective-permute-done((f32[64,2048]{1,0:T(8,128)S(1)}, f32[64,2048]{1,0:T(8,128)S(1)}, u32[]{:S(2)}, u32[]{:S(2)}) %collective-permute-start.6) | collective-permute-done | bytes 524320 | tf_op jit(solution)/shard_map/ppermute | solution.py:553
  23.6 0.7 collective-permute-start.1
  24.3 3.8 %collective-permute-start = (f32[4,256,256]{2,1,0:T(8,128)S(1)}, f32[4,256,256]{2,1,0:T(8,128)S(1)}, u32[]{:S(2)}, u32[]{:S(2)}) collective-permute-start(f32[4,256,256]{2,1,0:T(8,128)S(1)} %get-tuple-element.25), channel_id=1, source_target_pairs={{0,4},{4,0},{8,12},{12,8},{16,20},{20,16},{24,28},{28,24},{1,5},{5... | collective-permute-start | bytes 3145736 | tf_op jit(solution)/shard_map/ppermute | solution.py:670
  28.1 2.7 %collective-permute-start.3 = (f32[4,256,256]{2,1,0:T(8,128)S(1)}, f32[4,256,256]{2,1,0:T(8,128)S(1)}, u32[]{:S(2)}, u32[]{:S(2)}) collective-permute-start(f32[4,256,256]{2,1,0:T(8,128)S(1)} %collective-permute-done.2), channel_id=1, source_target_pairs={{28,16},{0,12},{29,17},{1,13},{30,18},{2,14},{31,19},{3,15}} | collective-permute-start | bytes 3145736 | tf_op jit(solution)/shard_map/ppermute | solution.py:668
  30.8 1.3 collective-permute-start.8
  32.1 1.3 collective-permute-start.10
  33.4 9.7 %diffuse.2 = (f32[8,256,512]{2,1,0:T(8,128)}, bf16[8,256,256]{2,1,0:T(8,128)(2,1)S(1)}, bf16[8,256,256]{2,1,0:T(8,128)(2,1)S(1)}) custom-call(s32[7]{0:T(128)S(1)} %stack.43.flags.scalars, f32[8,256,512]{2,1,0:T(8,128)S(1)} %copy-done.1, f32[4,256,256]{2,1,0:T(8,128)S(1)} %collective-permute-done.4.refs_1_, f32[4,256,256]{2,1,0:T(8,128)S(1)} %collective-permute-done.5.refs_2_), custom_call_target="tpu_custom_call" | custom-call | flops 104857600 | bytes 8388608 | tf_op jit(solution)/shard_map/diffuse/pallas_call | solution.py:220
  43.2 6.3 %collective-permute-done.8.refs_4_ = f32[64,2048]{1,0:T(8,128)S(1)} collective-permute-done((f32[64,2048]{1,0:T(8,128)S(1)}, f32[64,2048]{1,0:T(8,128)S(1)}, u32[]{:S(2)}, u32[]{:S(2)}) %collective-permute-start.8) | collective-permute-done | bytes 524320 | tf_op jit(solution)/shard_map/ppermute | solution.py:556
  49.5 5.8 %collective-permute-start.11 = (f32[1,32,512]{2,1,0:T(8,128)S(1)}, f32[1,32,512]{2,1,0:T(8,128)S(1)}, u32[]{:S(2)}, u32[]{:S(2)}) collective-permute-start(f32[1,32,512]{2,1,0:T(8,128)S(1)} %bitcast.30), channel_id=1, source_target_pairs={{0,16},{4,20},{8,24},{12,28},{16,0},{20,4},{24,8},{28,12},{1,17},{... | collective-permute-start | bytes 196616 | tf_op jit(solution)/shard_map/ppermute | solution.py:676
  55.2 5.5 %collective-permute-done.10.refs_6_ = f32[64,2048]{1,0:T(8,128)S(1)} collective-permute-done((f32[64,2048]{1,0:T(8,128)S(1)}, f32[64,2048]{1,0:T(8,128)S(1)}, u32[]{:S(2)}, u32[]{:S(2)}) %collective-permute-start.10) | collective-permute-done | bytes 524320 | tf_op jit(solution)/shard_map/ppermute | solution.py:557
  60.7 2.9 %footprints.1 = (bf16[512,2048]{1,0:T(8,128)(2,1)S(1)}, f32[256,256]{1,0:T(8,128)S(1)}) custom-call(s32[7]{0:T(128)S(1)} %stack.43.flags.scalars, f32[64,2048]{1,0:T(8,128)S(1)} %copy-done.2, f32[64,2048]{1,0:T(8,128)S(1)} %collective-permute-done.6.refs_1_.refs_2_, f32[64,2048]{1,0:T(8,128)S(1)} %collective-permute-done.6.refs_1_.refs_2_, ...), custom_call_target="tpu_custom_call" | custom-call | flops 536870912 | bytes 4194304 | tf_op jit(solution)/shard_map/footprints/pallas_call | solution.py:281
  63.6 9.7 %diffuse.3 = (f32[8,256,512]{2,1,0:T(8,128)}, bf16[8,256,256]{2,1,0:T(8,128)(2,1)S(1)}, bf16[8,256,256]{2,1,0:T(8,128)(2,1)S(1)}) custom-call(s32[7]{0:T(128)S(1)} %stack.43.flags.scalars, f32[8,256,512]{2,1,0:T(8,128)S(1)} %copy-done.1, f32[4,256,256]{2,1,0:T(8,128)S(1)} %collective-permute-done.refs_1_, ...), custom_call_target="tpu_custom_call", output_to_operand_aliasing={{0}: (5, {})} | custom-call | flops 104857600 | bytes 8388608 | tf_op jit(solution)/shard_map/diffuse/pallas_call | solution.py:220
  73.3 3.2 %numerator.1 = (f32[4,32,768]{2,1,0:T(8,128)S(1)}, f32[4,32,768]{2,1,0:T(8,128)S(1)}) custom-call(s32[7]{0:T(128)S(1)} %stack.43.flags.scalars, bf16[512,2048]{1,0:T(8,128)(2,1)S(1)} %get-tuple-element.29.foot_ref, f32[256,256]{1,0:T(8,128)S(1)} %get-tuple-element.30.gram_ref, bf16[2048,256]{1,0:T(8,128)(2,1)S(1)} %bitcast.18, ...), custom_call_target="tpu_custom_call" | custom-call | flops 3221225472 | bytes 8388608 | tf_op jit(solution)/shard_map/numerator/pallas_call | solution.py:336
  77.2 1.3 collective-permute-done.12
  78.5 1.7 %collective-permute-start.13 = (f32[4,32,512]{2,1,0:T(8,128)S(1)}, f32[4,32,512]{2,1,0:T(8,128)S(1)}, u32[]{:S(2)}, u32[]{:S(2)}) collective-permute-start(f32[4,32,512]{2,1,0:T(8,128)S(1)} %pad_maximum_fusion.refs_0_), channel_id=1, source_target_pairs={{0,8},{4,12},{8,0},{12,4},{16,24},{20,28},{24,16},{28,20},{1,9},{5... | collective-permute-start | bytes 786440 | tf_op jit(solution)/shard_map/ppermute | solution.py:680
  80.7 1.1 collective-permute-start.16
  81.9 2.0 %collective-permute-start.17 = (f32[32,768]{1,0:T(8,128)S(1)}, f32[32,768]{1,0:T(8,128)S(1)}, u32[]{:S(2)}, u32[]{:S(2)}) collective-permute-start(f32[32,768]{1,0:T(8,128)S(1)} %get-tuple-element.49), channel_id=1, source_target_pairs={{0,24},{4,28},{8,16},{12,20},{16,8},{20,12},{24,0},{28,4},{1,25},{... | collective-permute-start | bytes 294920 | tf_op jit(solution)/shard_map/ppermute | solution.py:700
  83.8 3.9 %collective-permute-done.13.refs_1_ = f32[4,32,512]{2,1,0:T(8,128)S(1)} collective-permute-done((f32[4,32,512]{2,1,0:T(8,128)S(1)}, f32[4,32,512]{2,1,0:T(8,128)S(1)}, u32[]{:S(2)}, u32[]{:S(2)}) %collective-permute-start.13) | collective-permute-done | bytes 262176 | tf_op jit(solution)/shard_map/ppermute | solution.py:680
  87.8 2.1 %collective-permute-done.15.refs_4_ = f32[32,768]{1,0:T(8,128)S(1)} collective-permute-done((f32[32,768]{1,0:T(8,128)S(1)}, f32[32,768]{1,0:T(8,128)S(1)}, u32[]{:S(2)}, u32[]{:S(2)}) %collective-permute-start.15) | collective-permute-done | bytes 98336 | tf_op jit(solution)/shard_map/ppermute | solution.py:700
  89.9 2.0 %collective-permute-done.17.refs_6_ = f32[32,768]{1,0:T(8,128)S(1)} collective-permute-done((f32[32,768]{1,0:T(8,128)S(1)}, f32[32,768]{1,0:T(8,128)S(1)}, u32[]{:S(2)}, u32[]{:S(2)}) %collective-permute-start.17) | collective-permute-done | bytes 98336 | tf_op jit(solution)/shard_map/ppermute | solution.py:700
  91.9 1.4 traces.1
  93.4 1.7 %collective-permute-start.18 = (f32[32,512]{1,0:T(8,128)S(1)}, f32[32,512]{1,0:T(8,128)S(1)}, u32[]{:S(2)}, u32[]{:S(2)}) collective-permute-start(f32[32,512]{1,0:T(8,128)S(1)} %get-tuple-element.37.refs_0_), channel_id=1, source_target_pairs={{0,8},{4,12},{8,0},{12,4},{16,24},{20,28},{24,16},{28,20},{1,9},{5... | collective-permute-start | bytes 196616 | tf_op jit(solution)/shard_map/ppermute | solution.py:704
  95.1 0.8 collective-permute-start.19
  95.9 0.9 collective-permute-start.20
  96.9 0.8 collective-permute-done.18.refs_1_
  97.6 2.2 %collective-permute-done.19.refs_2_ = f32[32,512]{1,0:T(8,128)S(1)} collective-permute-done((f32[32,512]{1,0:T(8,128)S(1)}, f32[32,512]{1,0:T(8,128)S(1)}, u32[]{:S(2)}, u32[]{:S(2)}) %collective-permute-start.19) | collective-permute-done | bytes 65568 | tf_op jit(solution)/shard_map/ppermute | solution.py:704
  99.8 1.3 collective-permute-done.20.refs_3_
  101.1 1.2 collective-permute-done.24.refs_7_
  102.4 2.9 %products.3 = (f32[64,1152]{1,0:T(8,128)S(1)}, f32[64,1152]{1,0:T(8,128)S(1)}, f32[64,1152]{1,0:T(8,128)S(1)}, f32[64,1152]{1,0:T(8,128)S(1)}) custom-call(s32[7]{0:T(128)S(1)} %stack.43.flags.scalars, f32[32,512]{1,0:T(8,128)S(1)} %get-tuple-element.37.refs_0_, f32[32,512]{1,0:T(8,128)S(1)} %collective-permute-done.18.refs_1_, ...), custom_call_target="tpu_custom_call" | custom-call | flops 1073741824 | bytes 3145728 | tf_op jit(solution)/shard_map/products/pallas_call | solution.py:455
  105.2 1.8 %collective-permute-start.30 = (f32[64,1152]{1,0:T(8,128)S(1)}, f32[64,1152]{1,0:T(8,128)S(1)}, u32[]{:S(2)}, u32[]{:S(2)}) collective-permute-start(f32[64,1152]{1,0:T(8,128)S(1)} %get-tuple-element.45), channel_id=1, source_target_pairs={{0,1},{3,2},{4,5},{7,6},{8,9},{11,10},{12,13},{15,14},{16,17},{19,... | collective-permute-start | bytes 884744 | tf_op jit(solution)/shard_map/ppermute | solution.py:602
  107.0 1.3 collective-permute-start.33
  108.4 6.0 %collective-permute-done.30 = f32[64,1152]{1,0:T(8,128)S(1)} collective-permute-done((f32[64,1152]{1,0:T(8,128)S(1)}, f32[64,1152]{1,0:T(8,128)S(1)}, u32[]{:S(2)}, u32[]{:S(2)}) %collective-permute-start.30) | collective-permute-done | bytes 294944 | tf_op jit(solution)/shard_map/ppermute | solution.py:602
  115.1 2.5 %products.2 = (f32[64,1024]{1,0:T(8,128)S(1)}, f32[64,1024]{1,0:T(8,128)S(1)}, f32[64,1024]{1,0:T(8,128)S(1)}, f32[64,1024]{1,0:T(8,128)S(1)}) custom-call(s32[7]{0:T(128)S(1)} %stack.43.flags.scalars, f32[32,512]{1,0:T(8,128)S(1)} %get-tuple-element.37.refs_0_, f32[32,512]{1,0:T(8,128)S(1)} %collective-permute-done.18.refs_1_, ...), custom_call_target="tpu_custom_call" | custom-call | flops 1073741824 | bytes 3145728 | tf_op jit(solution)/shard_map/products/pallas_call | solution.py:455
  117.6 7.8 %collective-permute-start.25 = (f32[64,1024]{1,0:T(8,128)S(1)}, f32[64,1024]{1,0:T(8,128)S(1)}, u32[]{:S(2)}, u32[]{:S(2)}) collective-permute-start(f32[64,1024]{1,0:T(8,128)S(1)} %get-tuple-element.41), channel_id=1, source_target_pairs={{0,1},{3,2},{4,5},{7,6},{8,9},{11,10},{12,13},{15,14},{16,17},{19,... | collective-permute-start | bytes 786440 | tf_op jit(solution)/shard_map/ppermute | solution.py:602
  126.9 3.3 %collective-permute-start.28 = (f32[64,1024]{1,0:T(8,128)S(1)}, f32[64,1024]{1,0:T(8,128)S(1)}, u32[]{:S(2)}, u32[]{:S(2)}) collective-permute-start(f32[64,1024]{1,0:T(8,128)S(1)} %get-tuple-element.40), channel_id=1, source_target_pairs={{0,1},{3,2},{4,5},{7,6},{8,9},{11,10},{12,13},{15,14},{16,17},{19,... | collective-permute-start | bytes 786440 | tf_op jit(solution)/shard_map/ppermute | solution.py:603
  130.2 1.9 %collective-permute-done.25 = f32[64,1024]{1,0:T(8,128)S(1)} collective-permute-done((f32[64,1024]{1,0:T(8,128)S(1)}, f32[64,1024]{1,0:T(8,128)S(1)}, u32[]{:S(2)}, u32[]{:S(2)}) %collective-permute-start.25) | collective-permute-done | bytes 262176 | tf_op jit(solution)/shard_map/ppermute | solution.py:602
  132.8 8.5 %collective-permute-done.28 = f32[64,1024]{1,0:T(8,128)S(1)} collective-permute-done((f32[64,1024]{1,0:T(8,128)S(1)}, f32[64,1024]{1,0:T(8,128)S(1)}, u32[]{:S(2)}, u32[]{:S(2)}) %collective-permute-start.28) | collective-permute-done | bytes 262176 | tf_op jit(solution)/shard_map/ppermute | solution.py:603
  142.0 4.0 %collective-permute-start.27 = (f32[64,1024]{1,0:T(8,128)S(1)}, f32[64,1024]{1,0:T(8,128)S(1)}, u32[]{:S(2)}, u32[]{:S(2)}) collective-permute-start(f32[64,1024]{1,0:T(8,128)S(1)} %add.61), channel_id=1, source_target_pairs={{0,1},{1,0},{2,3},{3,2},{4,5},{5,4},{6,7},{7,6},{8,9},{9,8},{10,11... | collective-permute-start | bytes 786440 | tf_op jit(solution)/shard_map/ppermute | solution.py:605
  146.2 1.2 collective-permute-done.35.refs_4_
  147.4 2.1 %final.2.refs_5_ = f32[64,2048]{1,0:T(8,128)} custom-call(s32[7]{0:T(128)S(1)} %stack.43.flags.scalars, f32[64,2048]{1,0:T(8,128)S(1)} %copy-done.2, bf16[512,2048]{1,0:T(8,128)(2,1)S(1)} %get-tuple-element.29.foot_ref, f32[64,1152]{1,0:T(8,128)S(1)} %get-tuple-element.42.refs_0_, f32[64,1152]{1,0:T(8,128)S(1)} %collective-permute-done.32.refs_1_, ...), custom_call_target="tpu_custom_call" | custom-call | flops 100663296 | bytes 2359296 | tf_op jit(solution)/shard_map/final/pallas_call | solution.py:513
  149.4 1.0 collective-permute-done.27.refs_1_
  150.4 1.9 %final.3 = f32[64,2048]{1,0:T(8,128)} custom-call(s32[7]{0:T(128)S(1)} %stack.43.flags.scalars, f32[64,2048]{1,0:T(8,128)S(1)} %copy-done.2, bf16[512,2048]{1,0:T(8,128)(2,1)S(1)} %get-tuple-element.29.foot_ref, f32[64,1024]{1,0:T(8,128)S(1)} %get-tuple-element.38.refs_0_, ...), custom_call_target="tpu_custom_call", output_to_operand_aliasing={{}: (8, {})} | custom-call | flops 100663296 | bytes 2359296 | tf_op jit(solution)/shard_map/final/pallas_call | solution.py:513
  (54 shorter events, 6.8 us)
Async XLA Ops:
  0.6 8.5 %copy-start.2 = (f32[64,2048]{1,0:T(8,128)S(1)}, f32[64,2048]{1,0:T(8,128)}, u32[]{:S(2)}) copy-start(f32[64,2048]{1,0:T(8,128)} %own_ref.3) | copy-start | bytes 1572868
  3.4 21.0 %collective-permute-start.4 = (f32[4,256,256]{2,1,0:T(8,128)}, f32[4,256,256]{2,1,0:T(8,128)S(1)}, u32[]{:S(2)}, u32[]{:S(2)}) collective-permute-start(f32[4,256,256]{2,1,0:T(8,128)} %get-tuple-element.48), channel_id=1, source_target_pairs={{0,4},{4,0},{8,12},{12,8},{16,20},{20,16},{24,28},{28,24},{1,5},{5... | collective-permute-start | bytes 3145736 | tf_op jit(solution)/shard_map/ppermute | solution.py:670
  3.9 2.2 %copy-start = (f32[8,256,512]{2,1,0:T(8,128)S(1)}, f32[8,256,512]{2,1,0:T(8,128)}, u32[]{:S(2)}) copy-start(f32[8,256,512]{2,1,0:T(8,128)} %refs_0_.4) | copy-start | bytes 12582916
  6.1 27.3 %copy-start.1 = (f32[8,256,512]{2,1,0:T(8,128)S(1)}, f32[8,256,512]{2,1,0:T(8,128)}, u32[]{:S(2)}) copy-start(f32[8,256,512]{2,1,0:T(8,128)} %refs_0_.4) | copy-start | bytes 12582916
  7.0 42.5 %copy-start.3 = (f32[32,512]{1,0:T(8,128)S(1)}, f32[32,512]{1,0:T(8,128)}, u32[]{:S(2)}) copy-start(f32[32,512]{1,0:T(8,128)} %param.5) | copy-start | bytes 196612
  7.0 21.1 %collective-permute-start.2 = (f32[4,256,256]{2,1,0:T(8,128)S(1)}, f32[4,256,256]{2,1,0:T(8,128)S(1)}, u32[]{:S(2)}, u32[]{:S(2)}) collective-permute-start(f32[4,256,256]{2,1,0:T(8,128)S(1)} %get-tuple-element.26), channel_id=1, source_target_pairs={{12,28},{16,0},{13,29},{17,1},{14,30},{18,2},{15,31},{19,3}} | collective-permute-start | bytes 3145736 | tf_op jit(solution)/shard_map/ppermute | solution.py:667
  8.4 22.4 %collective-permute-start.5 = (f32[4,256,256]{2,1,0:T(8,128)S(1)}, f32[4,256,256]{2,1,0:T(8,128)S(1)}, u32[]{:S(2)}, u32[]{:S(2)}) collective-permute-start(f32[4,256,256]{2,1,0:T(8,128)S(1)} %get-tuple-element.47), channel_id=1, source_target_pairs={{4,8},{12,16},{20,24},{8,4},{16,12},{24,20},{5,9},{13,17},{21,25},... | collective-permute-start | bytes 3145736 | tf_op jit(solution)/shard_map/ppermute | solution.py:669
  9.2 13.7 %collective-permute-start.6 = (f32[64,2048]{1,0:T(8,128)S(1)}, f32[64,2048]{1,0:T(8,128)S(1)}, u32[]{:S(2)}, u32[]{:S(2)}) collective-permute-start(f32[64,2048]{1,0:T(8,128)S(1)} %copy-done.2), channel_id=1, source_target_pairs={{0,1},{1,0},{2,3},{3,2},{4,5},{5,4},{6,7},{7,6},{8,9},{9,8},{10,11... | collective-permute-start | bytes 1572872 | tf_op jit(solution)/shard_map/ppermute | solution.py:553
  11.8 11.8 %collective-permute-start.7 = (f32[64,2048]{1,0:T(8,128)S(1)}, f32[64,2048]{1,0:T(8,128)S(1)}, u32[]{:S(2)}, u32[]{:S(2)}) collective-permute-start(f32[64,2048]{1,0:T(8,128)S(1)} %copy-done.2), channel_id=1, source_target_pairs={{1,2},{2,1},{5,6},{6,5},{9,10},{10,9},{13,14},{14,13},{17,18},{18,... | collective-permute-start | bytes 1572872 | tf_op jit(solution)/shard_map/ppermute | solution.py:554
  22.9 9.2 %collective-permute-start.9 = (f32[64,2048]{1,0:T(8,128)S(1)}, f32[64,2048]{1,0:T(8,128)S(1)}, u32[]{:S(2)}, u32[]{:S(2)}) collective-permute-start(f32[64,2048]{1,0:T(8,128)S(1)} %collective-permute-done.6.refs_1_.refs_2_), channel_id=1, source_target_pairs={{1,2},{2,1},{5,6},{6,5},{9,10},{10,9},{13,14},{14,13},{17,18},{18,... | collective-permute-start | bytes 1572872 | tf_op jit(solution)/shard_map/ppermute | solution.py:555
  23.6 40.0 %collective-permute-start.1 = (f32[4,256,256]{2,1,0:T(8,128)S(1)}, f32[4,256,256]{2,1,0:T(8,128)S(1)}, u32[]{:S(2)}, u32[]{:S(2)}) collective-permute-start(f32[4,256,256]{2,1,0:T(8,128)S(1)} %get-tuple-element.26), channel_id=1, source_target_pairs={{4,8},{20,24},{8,4},{24,20},{5,9},{21,25},{9,5},{25,21},{6,10},{22... | collective-permute-start | bytes 3145736 | tf_op jit(solution)/shard_map/ppermute | solution.py:669
  24.3 39.3 %collective-permute-start = (f32[4,256,256]{2,1,0:T(8,128)S(1)}, f32[4,256,256]{2,1,0:T(8,128)S(1)}, u32[]{:S(2)}, u32[]{:S(2)}) collective-permute-start(f32[4,256,256]{2,1,0:T(8,128)S(1)} %get-tuple-element.25), channel_id=1, source_target_pairs={{0,4},{4,0},{8,12},{12,8},{16,20},{20,16},{24,28},{28,24},{1,5},{5... | collective-permute-start | bytes 3145736 | tf_op jit(solution)/shard_map/ppermute | solution.py:670
  28.1 35.5 %collective-permute-start.3 = (f32[4,256,256]{2,1,0:T(8,128)S(1)}, f32[4,256,256]{2,1,0:T(8,128)S(1)}, u32[]{:S(2)}, u32[]{:S(2)}) collective-permute-start(f32[4,256,256]{2,1,0:T(8,128)S(1)} %collective-permute-done.2), channel_id=1, source_target_pairs={{28,16},{0,12},{29,17},{1,13},{30,18},{2,14},{31,19},{3,15}} | collective-permute-start | bytes 3145736 | tf_op jit(solution)/shard_map/ppermute | solution.py:668
  30.8 18.7 %collective-permute-start.8 = (f32[64,2048]{1,0:T(8,128)S(1)}, f32[64,2048]{1,0:T(8,128)S(1)}, u32[]{:S(2)}, u32[]{:S(2)}) collective-permute-start(f32[64,2048]{1,0:T(8,128)S(1)} %collective-permute-done.7.refs_3_), channel_id=1, source_target_pairs={{1,0},{2,3},{5,4},{6,7},{9,8},{10,11},{13,12},{14,15},{17,16},{18,... | collective-permute-start | bytes 1572872 | tf_op jit(solution)/shard_map/ppermute | solution.py:556
  32.1 28.6 %collective-permute-start.10 = (f32[64,2048]{1,0:T(8,128)S(1)}, f32[64,2048]{1,0:T(8,128)S(1)}, u32[]{:S(2)}, u32[]{:S(2)}) collective-permute-start(f32[64,2048]{1,0:T(8,128)S(1)} %collective-permute-done.9.refs_5_), channel_id=1, source_target_pairs={{1,0},{2,3},{5,4},{6,7},{9,8},{10,11},{13,12},{14,15},{17,16},{18,... | collective-permute-start | bytes 1572872 | tf_op jit(solution)/shard_map/ppermute | solution.py:557
  49.5 27.2 %collective-permute-start.11 = (f32[1,32,512]{2,1,0:T(8,128)S(1)}, f32[1,32,512]{2,1,0:T(8,128)S(1)}, u32[]{:S(2)}, u32[]{:S(2)}) collective-permute-start(f32[1,32,512]{2,1,0:T(8,128)S(1)} %bitcast.30), channel_id=1, source_target_pairs={{0,16},{4,20},{8,24},{12,28},{16,0},{20,4},{24,8},{28,12},{1,17},{... | collective-permute-start | bytes 196616 | tf_op jit(solution)/shard_map/ppermute | solution.py:676
  76.5 3.7 %collective-permute-start.14 = (f32[4,32,768]{2,1,0:T(8,128)S(1)}, f32[4,32,768]{2,1,0:T(8,128)S(1)}, u32[]{:S(2)}, u32[]{:S(2)}) collective-permute-start(f32[4,32,768]{2,1,0:T(8,128)S(1)} %get-tuple-element.36), channel_id=1, source_target_pairs={{0,4},{4,0},{8,12},{12,8},{16,20},{20,16},{24,28},{28,24},{1,5},{5... | collective-permute-start | bytes 1179656 | tf_op jit(solution)/shard_map/ppermute | solution.py:697
  76.7 1.8 %collective-permute-start.12 = (f32[2,32,512]{2,1,0:T(8,128)S(1)}, f32[2,32,512]{2,1,0:T(8,128)S(1)}, u32[]{:S(2)}, u32[]{:S(2)}) collective-permute-start(f32[2,32,512]{2,1,0:T(8,128)S(1)} %pad_maximum_fusion.1), channel_id=1, source_target_pairs={{0,4},{4,0},{8,12},{12,8},{16,20},{20,16},{24,28},{28,24},{1,5},{5... | collective-permute-start | bytes 393224 | tf_op jit(solution)/shard_map/ppermute | solution.py:676
  78.5 9.2 %collective-permute-start.13 = (f32[4,32,512]{2,1,0:T(8,128)S(1)}, f32[4,32,512]{2,1,0:T(8,128)S(1)}, u32[]{:S(2)}, u32[]{:S(2)}) collective-permute-start(f32[4,32,512]{2,1,0:T(8,128)S(1)} %pad_maximum_fusion.refs_0_), channel_id=1, source_target_pairs={{0,8},{4,12},{8,0},{12,4},{16,24},{20,28},{24,16},{28,20},{1,9},{5... | collective-permute-start | bytes 786440 | tf_op jit(solution)/shard_map/ppermute | solution.py:680
  80.3 9.6 %collective-permute-start.15 = (f32[32,768]{1,0:T(8,128)S(1)}, f32[32,768]{1,0:T(8,128)S(1)}, u32[]{:S(2)}, u32[]{:S(2)}) collective-permute-start(f32[32,768]{1,0:T(8,128)S(1)} %get-tuple-element.51), channel_id=1, source_target_pairs={{0,8},{4,12},{8,0},{12,4},{16,24},{20,28},{24,16},{28,20},{1,9},{5... | collective-permute-start | bytes 294920 | tf_op jit(solution)/shard_map/ppermute | solution.py:700
  80.7 9.2 %collective-permute-start.16 = (f32[32,768]{1,0:T(8,128)S(1)}, f32[32,768]{1,0:T(8,128)S(1)}, u32[]{:S(2)}, u32[]{:S(2)}) collective-permute-start(f32[32,768]{1,0:T(8,128)S(1)} %get-tuple-element.50), channel_id=1, source_target_pairs={{0,16},{4,20},{8,24},{12,28},{16,0},{20,4},{24,8},{28,12},{1,17},{... | collective-permute-start | bytes 294920 | tf_op jit(solution)/shard_map/ppermute | solution.py:700
  81.9 10.1 %collective-permute-start.17 = (f32[32,768]{1,0:T(8,128)S(1)}, f32[32,768]{1,0:T(8,128)S(1)}, u32[]{:S(2)}, u32[]{:S(2)}) collective-permute-start(f32[32,768]{1,0:T(8,128)S(1)} %get-tuple-element.49), channel_id=1, source_target_pairs={{0,24},{4,28},{8,16},{12,20},{16,8},{20,12},{24,0},{28,4},{1,25},{... | collective-permute-start | bytes 294920 | tf_op jit(solution)/shard_map/ppermute | solution.py:700
  93.4 4.3 %collective-permute-start.18 = (f32[32,512]{1,0:T(8,128)S(1)}, f32[32,512]{1,0:T(8,128)S(1)}, u32[]{:S(2)}, u32[]{:S(2)}) collective-permute-start(f32[32,512]{1,0:T(8,128)S(1)} %get-tuple-element.37.refs_0_), channel_id=1, source_target_pairs={{0,8},{4,12},{8,0},{12,4},{16,24},{20,28},{24,16},{28,20},{1,9},{5... | collective-permute-start | bytes 196616 | tf_op jit(solution)/shard_map/ppermute | solution.py:704
  95.1 4.7 %collective-permute-start.19 = (f32[32,512]{1,0:T(8,128)S(1)}, f32[32,512]{1,0:T(8,128)S(1)}, u32[]{:S(2)}, u32[]{:S(2)}) collective-permute-start(f32[32,512]{1,0:T(8,128)S(1)} %get-tuple-element.37.refs_0_), channel_id=1, source_target_pairs={{0,16},{4,20},{8,24},{12,28},{16,0},{20,4},{24,8},{28,12},{1,17},{... | collective-permute-start | bytes 196616 | tf_op jit(solution)/shard_map/ppermute | solution.py:704
  95.9 5.2 %collective-permute-start.20 = (f32[32,512]{1,0:T(8,128)S(1)}, f32[32,512]{1,0:T(8,128)S(1)}, u32[]{:S(2)}, u32[]{:S(2)}) collective-permute-start(f32[32,512]{1,0:T(8,128)S(1)} %get-tuple-element.37.refs_0_), channel_id=1, source_target_pairs={{0,24},{4,28},{8,16},{12,20},{16,8},{20,12},{24,0},{28,4},{1,25},{... | collective-permute-start | bytes 196616 | tf_op jit(solution)/shard_map/ppermute | solution.py:704
  96.9 4.3 %collective-permute-start.21 = (f32[32,512]{1,0:T(8,128)S(1)}, f32[32,512]{1,0:T(8,128)S(1)}, u32[]{:S(2)}, u32[]{:S(2)}) collective-permute-start(f32[32,512]{1,0:T(8,128)S(1)} %get-tuple-element.37.refs_0_), channel_id=1, source_target_pairs={{0,4},{4,0},{8,12},{12,8},{16,20},{20,16},{24,28},{28,24},{1,5},{5... | collective-permute-start | bytes 196616 | tf_op jit(solution)/shard_map/ppermute | solution.py:707
  97.6 3.5 %collective-permute-start.22 = (f32[32,512]{1,0:T(8,128)S(1)}, f32[32,512]{1,0:T(8,128)S(1)}, u32[]{:S(2)}, u32[]{:S(2)}) collective-permute-start(f32[32,512]{1,0:T(8,128)S(1)} %collective-permute-done.18.refs_1_), channel_id=1, source_target_pairs={{0,4},{4,0},{8,12},{12,8},{16,20},{20,16},{24,28},{28,24},{1,5},{5... | collective-permute-start | bytes 196616 | tf_op jit(solution)/shard_map/ppermute | solution.py:707
  99.8 1.3 collective-permute-start.23
  101.1 1.3 collective-permute-start.24
  105.2 9.2 %collective-permute-start.30 = (f32[64,1152]{1,0:T(8,128)S(1)}, f32[64,1152]{1,0:T(8,128)S(1)}, u32[]{:S(2)}, u32[]{:S(2)}) collective-permute-start(f32[64,1152]{1,0:T(8,128)S(1)} %get-tuple-element.45), channel_id=1, source_target_pairs={{0,1},{3,2},{4,5},{7,6},{8,9},{11,10},{12,13},{15,14},{16,17},{19,... | collective-permute-start | bytes 884744 | tf_op jit(solution)/shard_map/ppermute | solution.py:602
  107.0 18.4 %collective-permute-start.33 = (f32[64,1152]{1,0:T(8,128)S(1)}, f32[64,1152]{1,0:T(8,128)S(1)}, u32[]{:S(2)}, u32[]{:S(2)}) collective-permute-start(f32[64,1152]{1,0:T(8,128)S(1)} %get-tuple-element.44), channel_id=1, source_target_pairs={{0,1},{3,2},{4,5},{7,6},{8,9},{11,10},{12,13},{15,14},{16,17},{19,... | collective-permute-start | bytes 884744 | tf_op jit(solution)/shard_map/ppermute | solution.py:603
  114.4 11.7 %collective-permute-start.31 = (f32[64,1152]{1,0:T(8,128)S(1)}, f32[64,1152]{1,0:T(8,128)S(1)}, u32[]{:S(2)}, u32[]{:S(2)}) collective-permute-start(f32[64,1152]{1,0:T(8,128)S(1)} %add.63), channel_id=1, source_target_pairs={{1,2},{2,1},{5,6},{6,5},{9,10},{10,9},{13,14},{14,13},{17,18},{18,... | collective-permute-start | bytes 884744 | tf_op jit(solution)/shard_map/ppermute | solution.py:604
  117.6 14.4 %collective-permute-start.25 = (f32[64,1024]{1,0:T(8,128)S(1)}, f32[64,1024]{1,0:T(8,128)S(1)}, u32[]{:S(2)}, u32[]{:S(2)}) collective-permute-start(f32[64,1024]{1,0:T(8,128)S(1)} %get-tuple-element.41), channel_id=1, source_target_pairs={{0,1},{3,2},{4,5},{7,6},{8,9},{11,10},{12,13},{15,14},{16,17},{19,... | collective-permute-start | bytes 786440 | tf_op jit(solution)/shard_map/ppermute | solution.py:602
  125.5 20.6 %collective-permute-start.34 = (f32[64,1152]{1,0:T(8,128)S(1)}, f32[64,1152]{1,0:T(8,128)S(1)}, u32[]{:S(2)}, u32[]{:S(2)}) collective-permute-start(f32[64,1152]{1,0:T(8,128)S(1)} %add.66), channel_id=1, source_target_pairs={{1,2},{2,1},{5,6},{6,5},{9,10},{10,9},{13,14},{14,13},{17,18},{18,... | collective-permute-start | bytes 884744 | tf_op jit(solution)/shard_map/ppermute | solution.py:606
  126.2 19.9 %collective-permute-start.32 = (f32[64,1152]{1,0:T(8,128)S(1)}, f32[64,1152]{1,0:T(8,128)S(1)}, u32[]{:S(2)}, u32[]{:S(2)}) collective-permute-start(f32[64,1152]{1,0:T(8,128)S(1)} %add.64), channel_id=1, source_target_pairs={{0,1},{1,0},{2,3},{3,2},{4,5},{5,4},{6,7},{7,6},{8,9},{9,8},{10,11... | collective-permute-start | bytes 884744 | tf_op jit(solution)/shard_map/ppermute | solution.py:605
  126.9 14.4 %collective-permute-start.28 = (f32[64,1024]{1,0:T(8,128)S(1)}, f32[64,1024]{1,0:T(8,128)S(1)}, u32[]{:S(2)}, u32[]{:S(2)}) collective-permute-start(f32[64,1024]{1,0:T(8,128)S(1)} %get-tuple-element.40), channel_id=1, source_target_pairs={{0,1},{3,2},{4,5},{7,6},{8,9},{11,10},{12,13},{15,14},{16,17},{19,... | collective-permute-start | bytes 786440 | tf_op jit(solution)/shard_map/ppermute | solution.py:603
  132.1 9.9 %collective-permute-start.26 = (f32[64,1024]{1,0:T(8,128)S(1)}, f32[64,1024]{1,0:T(8,128)S(1)}, u32[]{:S(2)}, u32[]{:S(2)}) collective-permute-start(f32[64,1024]{1,0:T(8,128)S(1)} %add.60), channel_id=1, source_target_pairs={{1,2},{2,1},{5,6},{6,5},{9,10},{10,9},{13,14},{14,13},{17,18},{18,... | collective-permute-start | bytes 786440 | tf_op jit(solution)/shard_map/ppermute | solution.py:604
  141.3 8.1 %collective-permute-start.29 = (f32[64,1024]{1,0:T(8,128)S(1)}, f32[64,1024]{1,0:T(8,128)S(1)}, u32[]{:S(2)}, u32[]{:S(2)}) collective-permute-start(f32[64,1024]{1,0:T(8,128)S(1)} %add.62), channel_id=1, source_target_pairs={{1,2},{2,1},{5,6},{6,5},{9,10},{10,9},{13,14},{14,13},{17,18},{18,... | collective-permute-start | bytes 786440 | tf_op jit(solution)/shard_map/ppermute | solution.py:606
  142.0 8.4 %collective-permute-start.27 = (f32[64,1024]{1,0:T(8,128)S(1)}, f32[64,1024]{1,0:T(8,128)S(1)}, u32[]{:S(2)}, u32[]{:S(2)}) collective-permute-start(f32[64,1024]{1,0:T(8,128)S(1)} %add.61), channel_id=1, source_target_pairs={{0,1},{1,0},{2,3},{3,2},{4,5},{5,4},{6,7},{7,6},{8,9},{9,8},{10,11... | collective-permute-start | bytes 786440 | tf_op jit(solution)/shard_map/ppermute | solution.py:605
  146.1 1.3 collective-permute-start.35

commit v5 on v4

--- a/solution.py
+++ b/solution.py
@@ -54,43 +54,46 @@
     return jax.ShapeDtypeStruct(shape, dtype)
 
 
-def edges_call(flags, raw, halo, begin, frames):
+def edges_call(flags, raw, halo, wanted):
     rows, cols, _ = raw.shape
     shift = rows - halo
 
-    def kernel(flags, raw_ref, inner_ref, outer_ref, sems):
+    def kernel(flags, raw_ref, *refs):
+        out_refs, sems = refs[:-1], refs[-1]
         core = flags[CORE]
-        lanes = pl.ds(begin, frames)
-        copies = [
-            pltpu.make_async_copy(raw_ref.at[pl.ds(start, halo), :, lanes], out_ref, sems.at[k])
-            for k, (start, out_ref) in enumerate((((1 - core) * shift, inner_ref), (core * shift, outer_ref)))
-        ]
+        copies = []
+        for k, (outward, begin, frames) in enumerate(wanted):
+            start = (core if outward else 1 - core) * shift
+            copies.append(
+                pltpu.make_async_copy(
+                    raw_ref.at[pl.ds(start, halo), :, pl.ds(begin, frames)], out_refs[k], sems.at[k]
+                )
+            )
         for copy in copies:
             copy.start()
         for copy in copies:
             copy.wait()
 
-    block = (halo, cols, frames)
+    blocks = [(halo, cols, frames) for _, _, frames in wanted]
     return pl.pallas_call(
         kernel,
         grid_spec=pltpu.PrefetchScalarGridSpec(
             num_scalar_prefetch=1,
             grid=(1,),
             in_specs=[pl.BlockSpec(memory_space=pltpu.HBM)],
-            out_specs=[pl.BlockSpec(block, lambda i, flags: (0, 0, 0))] * 2,
-            scratch_shapes=[pltpu.SemaphoreType.DMA((2,))],
+            out_specs=[pl.BlockSpec(block, lambda i, flags: (0, 0, 0)) for block in blocks],
+            scratch_shapes=[pltpu.SemaphoreType.DMA((len(wanted),))],
         ),
-        out_shape=[shaped(*block)] * 2,
-        cost_estimate=cost(1, 4 * halo * cols * frames * 4),
-        compiler_params=grant(8),
+        out_shape=[shaped(*block) for block in blocks],
+        cost_estimate=cost(1, sum(8 * halo * cols * frames for _, _, frames in wanted)),
+        compiler_params=grant(10),
         name="edges",
     )(flags, raw)
 
 
-def diffuse_call(flags, raw, halo_inner, halo_outer, detour, movie, pair, begin, pair_begin, pair_frames):
+def diffuse_call(flags, raw, halo_inner, halo_outer, detour, movie, pair, begin, pair_begin, pair_frames, skip, groups):
     rows, cols, total = raw.shape
-    halo, _, frames = halo_inner.shape
-    groups = frames // LANES
+    halo = halo_inner.shape[0]
     carried = [array for array in (movie, *pair) if array is not None]
     width = 64
     pad = 8
@@ -107,7 +110,7 @@
 
         def fetches(at):
             here = lax.rem(at, 2)
-            lanes = pl.ds(pl.multiple_of(at * LANES, LANES), LANES)
+            lanes = pl.ds(pl.multiple_of((skip + at) * LANES, LANES), LANES)
             wide = pl.ds(pl.multiple_of((begin + at) * LANES, LANES), LANES)
 
             def one(ref, cut, start, count, part):
@@ -477,51 +480,76 @@
     )(scalars, *near, *far, *[array for movie in movies for array in movie])
 
 
-def final_call(scalars, own, foot, parts, gram_mine, gram_other, carried, half):
+def first_final_call(scalars, own, foot, parts, gram_mine, gram_other):
     share, pixel_count = own.shape
     rank = foot.shape[0] // 2
     part = pixel_count // HALVES
     block = 512
     steps = part // block
 
-    def kernel(scalars, own_ref, foot_ref, *refs):
+    def kernel(scalars, own_ref, foot_ref, later_ref, *refs):
         part_refs = refs[: len(parts)]
         mine, other = refs[len(parts)][...], refs[len(parts) + 1][...]
-        out_ref = refs[-1]
+        out_ref, below_ref = refs[-2:]
         above = part_refs[0][...]
         for part_ref in part_refs[1:]:
             above = above + part_ref[...]
         first = scalars[CORE] == 0
         gram = jnp.concatenate([jnp.where(first, mine, other), jnp.where(first, other, mine)], axis=1)
         both = stacked(gram)
-        below = fold(dot(both, foot_ref[0:rank, :], NN)) + dot(both[0:share], foot_ref[rank:, :], NN)
-        out_ref[...] = own_ref[...] * above / below
-
-    at = half * steps
+
+        def divisor(ref):
+            return fold(dot(both, ref[0:rank, :], NN)) + dot(both[0:share], ref[rank:, :], NN)
+
+        out_ref[...] = own_ref[...] * above / divisor(foot_ref)
+        below_ref[...] = divisor(later_ref)
+
     in_specs = [
-        pl.BlockSpec((share, block), lambda k, s: (0, at + k)),
-        pl.BlockSpec((2 * rank, block), lambda k, s: (0, at + k)),
+        pl.BlockSpec((share, block), lambda k, s: (0, k)),
+        pl.BlockSpec((2 * rank, block), lambda k, s: (0, k)),
+        pl.BlockSpec((2 * rank, block), lambda k, s: (0, steps + k)),
     ]
     in_specs += [pl.BlockSpec((share, block), lambda k, s: (0, k))] * len(parts)
     in_specs += [pl.BlockSpec((share, rank // 2), lambda k, s: (0, 0))] * 2
-    operands = [scalars, own, foot, *parts, gram_mine, gram_other]
-    aliases = {}
-    if carried is not None:
-        operands.append(carried)
-        in_specs.append(pl.BlockSpec(memory_space=pl.ANY))
-        aliases = {len(operands) - 1: 0}
     return pl.pallas_call(
         kernel,
         grid_spec=pltpu.PrefetchScalarGridSpec(
             num_scalar_prefetch=1,
             grid=(steps,),
             in_specs=in_specs,
-            out_specs=pl.BlockSpec((share, block), lambda k, s: (0, at + k)),
+            out_specs=[pl.BlockSpec((share, block), lambda k, s: (0, k))] * 2,
         ),
+        out_shape=[shaped(share, pixel_count), shaped(share, part)],
+        cost_estimate=cost(12 * share * rank * part, 4 * part * (2 * rank + 5 * share)),
+        compiler_params=grant(8),
+        name="final",
+    )(scalars, own, foot, foot, *parts, gram_mine, gram_other)
+
+
+def second_final_call(own, parts, below, carried):
+    share, pixel_count = own.shape
+    part = pixel_count // HALVES
+    block = 512
+    steps = part // block
+
+    def kernel(own_ref, below_ref, *refs):
+        above = refs[0][...]
+        for part_ref in refs[1 : len(parts)]:
+            above = above + part_ref[...]
+        refs[-1][...] = own_ref[...] * above / below_ref[...]
+
+    near = pl.BlockSpec((share, block), lambda k: (0, k))
+    far = pl.BlockSpec((share, block), lambda k: (0, steps + k))
+    operands = [own, below, *parts, carried]
+    return pl.pallas_call(
+        kernel,
+        grid=(steps,),
+        in_specs=[far, near] + [near] * len(parts) + [pl.BlockSpec(memory_space=pl.ANY)],
+        out_specs=far,
         out_shape=shaped(share, pixel_count),
-        input_output_aliases=aliases,
-        cost_estimate=cost(6 * share * rank * part, 4 * part * (rank + 5 * share)),
-        compiler_params=grant(8),
+        input_output_aliases={len(operands) - 1: 0},
+        cost_estimate=cost(4 * share * part, 24 * share * part),
+        compiler_params=grant(6),
         name="final",
     )(*operands)
 
@@ -647,19 +675,21 @@
     entries = line_gather(scalars, footprints, "tm", count)
 
     bent = [k for k in range(pix_count - 1) if k % GROUP == GROUP - 1] if pix_count % GROUP == 0 else []
+    begins = [sum(widths[:c]) * LANES for c in range(len(widths))]
+    spans = [(begin, width * LANES) for begin, width in zip(begins, widths)]
+    outward_rows = [
+        lax.dynamic_slice(raw_movie, (core * (rows - halo), 0, 0), (halo, cols, widths[0] * LANES))
+    ]
+    later = edges_call(
+        flags, raw_movie, halo, [(True, *span) for span in spans[1:]] + [(False, *span) for span in spans]
+    )
+    outward_rows += later[: len(spans) - 1]
+    inward_rows = later[len(spans) - 1 :]
     halos = []
-    for c, width in enumerate(widths):
-        begin = sum(widths[:c]) * LANES
+    for c, (inward, outward) in enumerate(zip(inward_rows, outward_rows)):
         last = c == len(widths) - 1 and bool(bent)
         joins = [(k, k + 1) for k in range(1, pix_count - 1, 2) if not (last and k in bent)]
         joins += [(b, a) for a, b in joins]
-        if c == 0:
-            shift = rows - halo
-            size = (halo, cols, width * LANES)
-            inward = lax.dynamic_slice(raw_movie, ((1 - core) * shift, 0, begin), size)
-            outward = lax.dynamic_slice(raw_movie, (core * shift, 0, begin), size)
-        else:
-            inward, outward = edges_call(flags, raw_movie, halo, begin, width * LANES)
         detour = None
         if last:
             first = [(k, k + GROUP) for k in bent] + [(k + 1, k + 1 - GROUP) for k in bent]
@@ -681,16 +711,17 @@
 
     current = None
     movies = []
-    for members in ((0,), (1,)):
+    for c, width in enumerate(widths):
         pair = (None, None)
-        pair_frames = sum(widths[c] for c in members) * LANES
-        pair_begin = 0
-        for c in members:
+        calls = 1
+        for part in range(calls):
+            groups = width // calls
+            skip = part * groups
             current, *pair = diffuse_call(
-                flags, raw_movie, *halos[c], current, pair, sum(widths[:c]), pair_begin, pair_frames
+                flags, raw_movie, *halos[c], current, pair,
+                sum(widths[:c]) + skip, skip, width * LANES, skip, groups,
             )
-            pair_begin += widths[c]
-        movies.append(tuple(array.reshape(pixel_count, pair_frames) for array in pair))
+        movies.append(tuple(array.reshape(pixel_count, width * LANES) for array in pair))
 
     foot, gram = footprints_call(scalars, footprints, entries)
     keep, send = numerator_call(scalars, foot, movies, gram, trace_rows)
@@ -713,11 +744,8 @@
     part = pixel_count // HALVES
     gram_mine = sum(array[:, part:] for array in sums[0])
     gram_other = lax.ppermute(gram_mine, "pix", swap(1))
-    new_footprints = None
-    for h in range(HALVES):
-        new_footprints = final_call(
-            scalars, footprints, foot, sums[h], gram_mine, gram_other, new_footprints, h
-        )
+    new_footprints, below = first_final_call(scalars, footprints, foot, sums[0], gram_mine, gram_other)
+    new_footprints = second_final_call(footprints, sums[1], below, new_footprints)
     return current, new_footprints, new_traces
 
 

time: 153 us -> 153 us (level)
  waiting for transfers between devices: 55.7 us -> 51.3 us
  starting transfers between devices: 53.3 us -> 56 us
  local copies, waits for them, and re-layouts: 4.99 us -> 6.79 us
    unnamed x8 -> x10, local copies, waits for them, and re-layouts: 2.2 us -> 5.37 us
    ppermute x1, waiting for transfers between devices: 6.33 us -> 3.8 us  [line_gather(): out_across = lax.ppermute(across, axis, outward)]
    ppermute x2, starting transfers between devices: 4.28 us -> 6.09 us  [compute(): from_inner = lax.ppermute(inward, 'pix', swap(1))]
  transfers between devices with their start and end apart: 36 -> 36, of which waited for: 16 -> 16; matrix products, arithmetic and copies ran while one was open for 0% -> 1% of each run, Pallas kernels for 20% -> 20%
where the time goes in v5:
time: 153 us
  starting transfers between devices  56 us (37%)
  waiting for transfers between devices  51.3 us (34%)
  Pallas kernels  37.3 us (24%)
  local copies, waits for them, and re-layouts  6.79 us (4%)
    pallas_call x2, Pallas kernels, diffuse_call(): pl.pallas_call(kernel, grid_spec=pltpu.PrefetchScalarGridSpec(num_scalar_...  19.4 us
    ppermute x2, starting transfers between devices, line_scatter(): first = lax.ppermute(opposite, axis, inward)  9.55 us
    ppermute x1, waiting for transfers between devices, line_gather(): near = lax.ppermute(block, axis, [(k, k ^ 1) for k in range(count)])  9.48 us
    ppermute x2, waiting for transfers between devices, line_scatter(): second = lax.ppermute(remaining, axis, inward)  8.47 us
    ppermute x2, waiting for transfers between devices, line_scatter(): first = lax.ppermute(opposite, axis, inward)  7.91 us
    ppermute x2, starting transfers between devices, compute(): lax.ppermute(held, 'pix', swap(mask))  6.74 us
    ppermute x2, starting transfers between devices, compute(): from_inner = lax.ppermute(inward, 'pix', swap(1))  6.09 us
    unnamed x10, local copies, waits for them, and re-layouts  5.37 us
  transfers between devices with their start and end apart: 36, of which 16 were waited for; matrix products, arithmetic and copies ran while one was open for 1% of the time, Pallas kernels for 20%

profile of v5, /device:TPU:0, one launch (start us, length us, event | category | flops | bytes accessed | tf_op | source)
XLA Modules:
  0.0 152.8 jit_solution(17069452515874180550)
XLA Ops:
  0.7 2.2 %copy-done = f32[8,256,512]{2,1,0:T(8,128)S(1)} copy-done((f32[8,256,512]{2,1,0:T(8,128)S(1)}, f32[8,256,512]{2,1,0:T(8,128)}, u32[]{:S(2)}) %copy-start) | copy-done | bytes 4194328
  2.9 2.0 %edges.1 = (f32[4,256,256]{2,1,0:T(8,128)S(1)}, f32[4,256,256]{2,1,0:T(8,128)}, f32[4,256,256]{2,1,0:T(8,128)S(1)}) custom-call(s32[7]{0:T(128)S(1)} %stack.43.flags.scalars, f32[8,256,512]{2,1,0:T(8,128)S(1)} %copy-done), custom_call_target="tpu_custom_call" | custom-call | flops 1 | bytes 6291456 | tf_op jit(solution)/shard_map/edges/pallas_call | solution.py:78
  4.9 1.0 copy-done.3
  6.4 1.3 collective-permute-start.2
  7.7 1.3 constant_dynamic-slice_fusion
  9.8 2.6 %collective-permute-start.6 = (f32[64,2048]{1,0:T(8,128)S(1)}, f32[64,2048]{1,0:T(8,128)S(1)}, u32[]{:S(2)}, u32[]{:S(2)}) collective-permute-start(f32[64,2048]{1,0:T(8,128)S(1)} %copy-done.2), channel_id=1, source_target_pairs={{0,1},{1,0},{2,3},{3,2},{4,5},{5,4},{6,7},{7,6},{8,9},{9,8},{10,11... | collective-permute-start | bytes 1572872 | tf_op jit(solution)/shard_map/ppermute | solution.py:581
  13.1 9.5 %collective-permute-done.6.refs_1_.refs_2_ = f32[64,2048]{1,0:T(8,128)S(1)} collective-permute-done((f32[64,2048]{1,0:T(8,128)S(1)}, f32[64,2048]{1,0:T(8,128)S(1)}, u32[]{:S(2)}, u32[]{:S(2)}) %collective-permute-start.6) | collective-permute-done | bytes 524320 | tf_op jit(solution)/shard_map/ppermute | solution.py:581
  24.0 5.6 %collective-permute-start = (f32[4,256,256]{2,1,0:T(8,128)}, f32[4,256,256]{2,1,0:T(8,128)S(1)}, u32[]{:S(2)}, u32[]{:S(2)}) collective-permute-start(f32[4,256,256]{2,1,0:T(8,128)} %copy-done.3), channel_id=1, source_target_pairs={{0,4},{4,0},{8,12},{12,8},{16,20},{20,16},{24,28},{28,24},{1,5},{5... | collective-permute-start | bytes 3145736 | tf_op jit(solution)/shard_map/ppermute | solution.py:700
  29.6 2.1 %collective-permute-start.3 = (f32[4,256,256]{2,1,0:T(8,128)}, f32[4,256,256]{2,1,0:T(8,128)S(1)}, u32[]{:S(2)}, u32[]{:S(2)}) collective-permute-start(f32[4,256,256]{2,1,0:T(8,128)} %collective-permute-done.2), channel_id=1, source_target_pairs={{28,16},{0,12},{29,17},{1,13},{30,18},{2,14},{31,19},{3,15}} | collective-permute-start | bytes 3145736 | tf_op jit(solution)/shard_map/ppermute | solution.py:698
  31.8 1.3 collective-permute-start.8
  33.1 1.3 collective-permute-start.10
  34.4 2.2 %copy-done.1 = f32[8,256,512]{2,1,0:T(8,128)S(1)} copy-done((f32[8,256,512]{2,1,0:T(8,128)S(1)}, f32[8,256,512]{2,1,0:T(8,128)}, u32[]{:S(2)}) %copy-start.1) | copy-done | bytes 4194328
  36.6 9.7 %diffuse.2 = (f32[8,256,512]{2,1,0:T(8,128)}, bf16[8,256,256]{2,1,0:T(8,128)(2,1)S(1)}, bf16[8,256,256]{2,1,0:T(8,128)(2,1)S(1)}) custom-call(s32[7]{0:T(128)S(1)} %stack.43.flags.scalars, f32[8,256,512]{2,1,0:T(8,128)S(1)} %copy-done.1, f32[4,256,256]{2,1,0:T(8,128)S(1)} %collective-permute-done.4.refs_1_, f32[4,256,256]{2,1,0:T(8,128)S(1)} %collective-permute-done.5.refs_2_), custom_call_target="tpu_custom_call" | custom-call | flops 104857600 | bytes 8388608 | tf_op jit(solution)/shard_map/diffuse/pallas_call | solution.py:223
  46.3 3.8 %collective-permute-done.8.refs_4_ = f32[64,2048]{1,0:T(8,128)S(1)} collective-permute-done((f32[64,2048]{1,0:T(8,128)S(1)}, f32[64,2048]{1,0:T(8,128)S(1)}, u32[]{:S(2)}, u32[]{:S(2)}) %collective-permute-start.8) | collective-permute-done | bytes 524320 | tf_op jit(solution)/shard_map/ppermute | solution.py:584
  50.1 6.6 %collective-permute-start.11 = (f32[1,32,512]{2,1,0:T(8,128)S(1)}, f32[1,32,512]{2,1,0:T(8,128)S(1)}, u32[]{:S(2)}, u32[]{:S(2)}) collective-permute-start(f32[1,32,512]{2,1,0:T(8,128)S(1)} %bitcast.30), channel_id=1, source_target_pairs={{0,16},{4,20},{8,24},{12,28},{16,0},{20,4},{24,8},{28,12},{1,17},{... | collective-permute-start | bytes 196616 | tf_op jit(solution)/shard_map/ppermute | solution.py:706
  56.8 4.6 %collective-permute-done.10.refs_6_ = f32[64,2048]{1,0:T(8,128)S(1)} collective-permute-done((f32[64,2048]{1,0:T(8,128)S(1)}, f32[64,2048]{1,0:T(8,128)S(1)}, u32[]{:S(2)}, u32[]{:S(2)}) %collective-permute-start.10) | collective-permute-done | bytes 524320 | tf_op jit(solution)/shard_map/ppermute | solution.py:585
  61.3 2.9 %footprints.1 = (bf16[512,2048]{1,0:T(8,128)(2,1)S(1)}, f32[256,256]{1,0:T(8,128)S(1)}) custom-call(s32[7]{0:T(128)S(1)} %stack.43.flags.scalars, f32[64,2048]{1,0:T(8,128)S(1)} %copy-done.2, f32[64,2048]{1,0:T(8,128)S(1)} %collective-permute-done.6.refs_1_.refs_2_, f32[64,2048]{1,0:T(8,128)S(1)} %collective-permute-done.6.refs_1_.refs_2_, ...), custom_call_target="tpu_custom_call" | custom-call | flops 536870912 | bytes 4194304 | tf_op jit(solution)/shard_map/footprints/pallas_call | solution.py:284
  64.2 9.7 %diffuse.3 = (f32[8,256,512]{2,1,0:T(8,128)}, bf16[8,256,256]{2,1,0:T(8,128)(2,1)S(1)}, bf16[8,256,256]{2,1,0:T(8,128)(2,1)S(1)}) custom-call(s32[7]{0:T(128)S(1)} %stack.43.flags.scalars, f32[8,256,512]{2,1,0:T(8,128)S(1)} %copy-done.1, f32[4,256,256]{2,1,0:T(8,128)S(1)} %collective-permute-done.refs_1_, ...), custom_call_target="tpu_custom_call", output_to_operand_aliasing={{0}: (5, {})} | custom-call | flops 104857600 | bytes 8388608 | tf_op jit(solution)/shard_map/diffuse/pallas_call | solution.py:223
  74.0 3.2 %numerator.1 = (f32[4,32,768]{2,1,0:T(8,128)S(1)}, f32[4,32,768]{2,1,0:T(8,128)S(1)}) custom-call(s32[7]{0:T(128)S(1)} %stack.43.flags.scalars, bf16[512,2048]{1,0:T(8,128)(2,1)S(1)} %get-tuple-element.33.foot_ref.later_ref, f32[256,256]{1,0:T(8,128)S(1)} %get-tuple-element.34.gram_ref, bf16[2048,256]{1,0:T(8,128)(2,1)S(1)} %bitcast.18, ...), custom_call_target="tpu_custom_call" | custom-call | flops 3221225472 | bytes 8388608 | tf_op jit(solution)/shard_map/numerator/pallas_call | solution.py:339
  77.8 1.4 collective-permute-done.12
  79.3 2.5 %collective-permute-start.13 = (f32[4,32,512]{2,1,0:T(8,128)S(1)}, f32[4,32,512]{2,1,0:T(8,128)S(1)}, u32[]{:S(2)}, u32[]{:S(2)}) collective-permute-start(f32[4,32,512]{2,1,0:T(8,128)S(1)} %pad_maximum_fusion.refs_0_), channel_id=1, source_target_pairs={{0,8},{4,12},{8,0},{12,4},{16,24},{20,28},{24,16},{28,20},{1,9},{5... | collective-permute-start | bytes 786440 | tf_op jit(solution)/shard_map/ppermute | solution.py:710
  81.9 1.4 collective-permute-start.16
  83.3 2.0 %collective-permute-start.17 = (f32[32,768]{1,0:T(8,128)S(1)}, f32[32,768]{1,0:T(8,128)S(1)}, u32[]{:S(2)}, u32[]{:S(2)}) collective-permute-start(f32[32,768]{1,0:T(8,128)S(1)} %get-tuple-element.53), channel_id=1, source_target_pairs={{0,24},{4,28},{8,16},{12,20},{16,8},{20,12},{24,0},{28,4},{1,25},{... | collective-permute-start | bytes 294920 | tf_op jit(solution)/shard_map/ppermute | solution.py:731
  85.4 3.6 %collective-permute-done.13.refs_1_ = f32[4,32,512]{2,1,0:T(8,128)S(1)} collective-permute-done((f32[4,32,512]{2,1,0:T(8,128)S(1)}, f32[4,32,512]{2,1,0:T(8,128)S(1)}, u32[]{:S(2)}, u32[]{:S(2)}) %collective-permute-start.13) | collective-permute-done | bytes 262176 | tf_op jit(solution)/shard_map/ppermute | solution.py:710
  88.9 2.1 %collective-permute-done.15.refs_4_ = f32[32,768]{1,0:T(8,128)S(1)} collective-permute-done((f32[32,768]{1,0:T(8,128)S(1)}, f32[32,768]{1,0:T(8,128)S(1)}, u32[]{:S(2)}, u32[]{:S(2)}) %collective-permute-start.15) | collective-permute-done | bytes 98336 | tf_op jit(solution)/shard_map/ppermute | solution.py:731
  91.0 2.4 %collective-permute-done.17.refs_6_ = f32[32,768]{1,0:T(8,128)S(1)} collective-permute-done((f32[32,768]{1,0:T(8,128)S(1)}, f32[32,768]{1,0:T(8,128)S(1)}, u32[]{:S(2)}, u32[]{:S(2)}) %collective-permute-start.17) | collective-permute-done | bytes 98336 | tf_op jit(solution)/shard_map/ppermute | solution.py:731
  93.4 1.4 traces.1
  94.8 1.7 %collective-permute-start.18 = (f32[32,512]{1,0:T(8,128)S(1)}, f32[32,512]{1,0:T(8,128)S(1)}, u32[]{:S(2)}, u32[]{:S(2)}) collective-permute-start(f32[32,512]{1,0:T(8,128)S(1)} %get-tuple-element.41.refs_0_), channel_id=1, source_target_pairs={{0,8},{4,12},{8,0},{12,4},{16,24},{20,28},{24,16},{28,20},{1,9},{5... | collective-permute-start | bytes 196616 | tf_op jit(solution)/shard_map/ppermute | solution.py:735
  96.6 0.9 collective-permute-start.19
  97.5 0.9 collective-permute-start.20
  98.3 0.8 collective-permute-done.18.refs_1_
  99.1 2.2 %collective-permute-done.19.refs_2_ = f32[32,512]{1,0:T(8,128)S(1)} collective-permute-done((f32[32,512]{1,0:T(8,128)S(1)}, f32[32,512]{1,0:T(8,128)S(1)}, u32[]{:S(2)}, u32[]{:S(2)}) %collective-permute-start.19) | collective-permute-done | bytes 65568 | tf_op jit(solution)/shard_map/ppermute | solution.py:735
  101.3 1.3 collective-permute-done.20.refs_3_
  102.6 1.2 collective-permute-done.24.refs_7_
  103.9 2.9 %products.2 = (f32[64,1152]{1,0:T(8,128)S(1)}, f32[64,1152]{1,0:T(8,128)S(1)}, f32[64,1152]{1,0:T(8,128)S(1)}, f32[64,1152]{1,0:T(8,128)S(1)}) custom-call(s32[7]{0:T(128)S(1)} %stack.43.flags.scalars, f32[32,512]{1,0:T(8,128)S(1)} %get-tuple-element.41.refs_0_, f32[32,512]{1,0:T(8,128)S(1)} %collective-permute-done.18.refs_1_, ...), custom_call_target="tpu_custom_call" | custom-call | flops 1073741824 | bytes 3145728 | tf_op jit(solution)/shard_map/products/pallas_call | solution.py:458
  106.7 1.8 %collective-permute-start.25 = (f32[64,1152]{1,0:T(8,128)S(1)}, f32[64,1152]{1,0:T(8,128)S(1)}, u32[]{:S(2)}, u32[]{:S(2)}) collective-permute-start(f32[64,1152]{1,0:T(8,128)S(1)} %get-tuple-element.45), channel_id=1, source_target_pairs={{0,1},{3,2},{4,5},{7,6},{8,9},{11,10},{12,13},{15,14},{16,17},{19,... | collective-permute-start | bytes 884744 | tf_op jit(solution)/shard_map/ppermute | solution.py:630
  108.5 1.3 collective-permute-start.28
  109.9 6.0 %collective-permute-done.25 = f32[64,1152]{1,0:T(8,128)S(1)} collective-permute-done((f32[64,1152]{1,0:T(8,128)S(1)}, f32[64,1152]{1,0:T(8,128)S(1)}, u32[]{:S(2)}, u32[]{:S(2)}) %collective-permute-start.25) | collective-permute-done | bytes 294944 | tf_op jit(solution)/shard_map/ppermute | solution.py:630
  116.6 2.5 %products.3 = (f32[64,1024]{1,0:T(8,128)S(1)}, f32[64,1024]{1,0:T(8,128)S(1)}, f32[64,1024]{1,0:T(8,128)S(1)}, f32[64,1024]{1,0:T(8,128)S(1)}) custom-call(s32[7]{0:T(128)S(1)} %stack.43.flags.scalars, f32[32,512]{1,0:T(8,128)S(1)} %get-tuple-element.41.refs_0_, f32[32,512]{1,0:T(8,128)S(1)} %collective-permute-done.18.refs_1_, ...), custom_call_target="tpu_custom_call" | custom-call | flops 1073741824 | bytes 3145728 | tf_op jit(solution)/shard_map/products/pallas_call | solution.py:458
  119.1 7.7 %collective-permute-start.31 = (f32[64,1024]{1,0:T(8,128)S(1)}, f32[64,1024]{1,0:T(8,128)S(1)}, u32[]{:S(2)}, u32[]{:S(2)}) collective-permute-start(f32[64,1024]{1,0:T(8,128)S(1)} %get-tuple-element.50), channel_id=1, source_target_pairs={{0,1},{3,2},{4,5},{7,6},{8,9},{11,10},{12,13},{15,14},{16,17},{19,... | collective-permute-start | bytes 786440 | tf_op jit(solution)/shard_map/ppermute | solution.py:630
  128.4 3.3 %collective-permute-start.34 = (f32[64,1024]{1,0:T(8,128)S(1)}, f32[64,1024]{1,0:T(8,128)S(1)}, u32[]{:S(2)}, u32[]{:S(2)}) collective-permute-start(f32[64,1024]{1,0:T(8,128)S(1)} %get-tuple-element.49), channel_id=1, source_target_pairs={{0,1},{3,2},{4,5},{7,6},{8,9},{11,10},{12,13},{15,14},{16,17},{19,... | collective-permute-start | bytes 786440 | tf_op jit(solution)/shard_map/ppermute | solution.py:631
  131.7 1.9 %collective-permute-done.31 = f32[64,1024]{1,0:T(8,128)S(1)} collective-permute-done((f32[64,1024]{1,0:T(8,128)S(1)}, f32[64,1024]{1,0:T(8,128)S(1)}, u32[]{:S(2)}, u32[]{:S(2)}) %collective-permute-start.31) | collective-permute-done | bytes 262176 | tf_op jit(solution)/shard_map/ppermute | solution.py:630
  134.3 8.5 %collective-permute-done.34 = f32[64,1024]{1,0:T(8,128)S(1)} collective-permute-done((f32[64,1024]{1,0:T(8,128)S(1)}, f32[64,1024]{1,0:T(8,128)S(1)}, u32[]{:S(2)}, u32[]{:S(2)}) %collective-permute-start.34) | collective-permute-done | bytes 262176 | tf_op jit(solution)/shard_map/ppermute | solution.py:631
  143.5 4.0 %collective-permute-start.33 = (f32[64,1024]{1,0:T(8,128)S(1)}, f32[64,1024]{1,0:T(8,128)S(1)}, u32[]{:S(2)}, u32[]{:S(2)}) collective-permute-start(f32[64,1024]{1,0:T(8,128)S(1)} %add.62), channel_id=1, source_target_pairs={{0,1},{1,0},{2,3},{3,2},{4,5},{5,4},{6,7},{7,6},{8,9},{9,8},{10,11... | collective-permute-start | bytes 786440 | tf_op jit(solution)/shard_map/ppermute | solution.py:633
  147.6 1.2 collective-permute-done.30.refs_4_
  148.8 2.3 %final.2 = (f32[64,2048]{1,0:T(8,128)}, f32[64,1024]{1,0:T(8,128)S(1)}) custom-call(s32[7]{0:T(128)S(1)} %stack.43.flags.scalars, f32[64,2048]{1,0:T(8,128)S(1)} %copy-done.2, bf16[512,2048]{1,0:T(8,128)(2,1)S(1)} %get-tuple-element.33.foot_ref.later_ref, bf16[512,2048]{1,0:T(8,128)(2,1)S(1)} %get-tuple-element.33.foot_ref.later_ref, ...), custom_call_target="tpu_custom_call" | custom-call | flops 201326592 | bytes 3407872 | tf_op jit(solution)/shard_map/final/pallas_call | solution.py:514
  151.1 0.8 collective-permute-done.33.refs_1_
  151.9 0.9 final.3
  (56 shorter events, 7.9 us)
Async XLA Ops:
  0.7 2.2 %copy-start = (f32[8,256,512]{2,1,0:T(8,128)S(1)}, f32[8,256,512]{2,1,0:T(8,128)}, u32[]{:S(2)}) copy-start(f32[8,256,512]{2,1,0:T(8,128)} %refs_0_.4) | copy-start | bytes 12582916
  2.9 6.8 %copy-start.2 = (f32[64,2048]{1,0:T(8,128)S(1)}, f32[64,2048]{1,0:T(8,128)}, u32[]{:S(2)}) copy-start(f32[64,2048]{1,0:T(8,128)} %own_ref.3) | copy-start | bytes 1572868
  4.9 1.0 copy-start.3
  5.9 18.1 %collective-permute-start.4 = (f32[4,256,256]{2,1,0:T(8,128)}, f32[4,256,256]{2,1,0:T(8,128)S(1)}, u32[]{:S(2)}, u32[]{:S(2)}) collective-permute-start(f32[4,256,256]{2,1,0:T(8,128)} %get-tuple-element.30), channel_id=1, source_target_pairs={{0,4},{4,0},{8,12},{12,8},{16,20},{20,16},{24,28},{28,24},{1,5},{5... | collective-permute-start | bytes 3145736 | tf_op jit(solution)/shard_map/ppermute | solution.py:700
  6.4 23.3 %collective-permute-start.2 = (f32[4,256,256]{2,1,0:T(8,128)S(1)}, f32[4,256,256]{2,1,0:T(8,128)}, u32[]{:S(2)}, u32[]{:S(2)}) collective-permute-start(f32[4,256,256]{2,1,0:T(8,128)S(1)} %get-tuple-element.29), channel_id=1, source_target_pairs={{12,28},{16,0},{13,29},{17,1},{14,30},{18,2},{15,31},{19,3}} | collective-permute-start | bytes 3145736 | tf_op jit(solution)/shard_map/ppermute | solution.py:697
  7.7 42.4 %copy-start.4 = (f32[32,512]{1,0:T(8,128)S(1)}, f32[32,512]{1,0:T(8,128)}, u32[]{:S(2)}) copy-start(f32[32,512]{1,0:T(8,128)} %param.5) | copy-start | bytes 196612
  9.0 22.8 %collective-permute-start.5 = (f32[4,256,256]{2,1,0:T(8,128)S(1)}, f32[4,256,256]{2,1,0:T(8,128)S(1)}, u32[]{:S(2)}, u32[]{:S(2)}) collective-permute-start(f32[4,256,256]{2,1,0:T(8,128)S(1)} %constant_dynamic-slice_fusion), channel_id=1, source_target_pairs={{4,8},{12,16},{20,24},{8,4},{16,12},{24,20},{5,9},{13,17},{21,25},... | collective-permute-start | bytes 3145736 | tf_op jit(solution)/shard_map/ppermute | solution.py:699
  9.8 12.8 %collective-permute-start.6 = (f32[64,2048]{1,0:T(8,128)S(1)}, f32[64,2048]{1,0:T(8,128)S(1)}, u32[]{:S(2)}, u32[]{:S(2)}) collective-permute-start(f32[64,2048]{1,0:T(8,128)S(1)} %copy-done.2), channel_id=1, source_target_pairs={{0,1},{1,0},{2,3},{3,2},{4,5},{5,4},{6,7},{7,6},{8,9},{9,8},{10,11... | collective-permute-start | bytes 1572872 | tf_op jit(solution)/shard_map/ppermute | solution.py:581
  12.4 10.9 %collective-permute-start.7 = (f32[64,2048]{1,0:T(8,128)S(1)}, f32[64,2048]{1,0:T(8,128)S(1)}, u32[]{:S(2)}, u32[]{:S(2)}) collective-permute-start(f32[64,2048]{1,0:T(8,128)S(1)} %copy-done.2), channel_id=1, source_target_pairs={{1,2},{2,1},{5,6},{6,5},{9,10},{10,9},{13,14},{14,13},{17,18},{18,... | collective-permute-start | bytes 1572872 | tf_op jit(solution)/shard_map/ppermute | solution.py:582
  22.6 10.5 %collective-permute-start.9 = (f32[64,2048]{1,0:T(8,128)S(1)}, f32[64,2048]{1,0:T(8,128)S(1)}, u32[]{:S(2)}, u32[]{:S(2)}) collective-permute-start(f32[64,2048]{1,0:T(8,128)S(1)} %collective-permute-done.6.refs_1_.refs_2_), channel_id=1, source_target_pairs={{1,2},{2,1},{5,6},{6,5},{9,10},{10,9},{13,14},{14,13},{17,18},{18,... | collective-permute-start | bytes 1572872 | tf_op jit(solution)/shard_map/ppermute | solution.py:583
  23.3 40.9 %collective-permute-start.1 = (f32[4,256,256]{2,1,0:T(8,128)S(1)}, f32[4,256,256]{2,1,0:T(8,128)S(1)}, u32[]{:S(2)}, u32[]{:S(2)}) collective-permute-start(f32[4,256,256]{2,1,0:T(8,128)S(1)} %get-tuple-element.29), channel_id=1, source_target_pairs={{4,8},{20,24},{8,4},{24,20},{5,9},{21,25},{9,5},{25,21},{6,10},{22... | collective-permute-start | bytes 3145736 | tf_op jit(solution)/shard_map/ppermute | solution.py:699
  24.0 40.2 %collective-permute-start = (f32[4,256,256]{2,1,0:T(8,128)}, f32[4,256,256]{2,1,0:T(8,128)S(1)}, u32[]{:S(2)}, u32[]{:S(2)}) collective-permute-start(f32[4,256,256]{2,1,0:T(8,128)} %copy-done.3), channel_id=1, source_target_pairs={{0,4},{4,0},{8,12},{12,8},{16,20},{20,16},{24,28},{28,24},{1,5},{5... | collective-permute-start | bytes 3145736 | tf_op jit(solution)/shard_map/ppermute | solution.py:700
  29.6 34.6 %collective-permute-start.3 = (f32[4,256,256]{2,1,0:T(8,128)}, f32[4,256,256]{2,1,0:T(8,128)S(1)}, u32[]{:S(2)}, u32[]{:S(2)}) collective-permute-start(f32[4,256,256]{2,1,0:T(8,128)} %collective-permute-done.2), channel_id=1, source_target_pairs={{28,16},{0,12},{29,17},{1,13},{30,18},{2,14},{31,19},{3,15}} | collective-permute-start | bytes 3145736 | tf_op jit(solution)/shard_map/ppermute | solution.py:698
  31.8 18.3 %collective-permute-start.8 = (f32[64,2048]{1,0:T(8,128)S(1)}, f32[64,2048]{1,0:T(8,128)S(1)}, u32[]{:S(2)}, u32[]{:S(2)}) collective-permute-start(f32[64,2048]{1,0:T(8,128)S(1)} %collective-permute-done.7.refs_3_), channel_id=1, source_target_pairs={{1,0},{2,3},{5,4},{6,7},{9,8},{10,11},{13,12},{14,15},{17,16},{18,... | collective-permute-start | bytes 1572872 | tf_op jit(solution)/shard_map/ppermute | solution.py:584
  33.1 28.2 %collective-permute-start.10 = (f32[64,2048]{1,0:T(8,128)S(1)}, f32[64,2048]{1,0:T(8,128)S(1)}, u32[]{:S(2)}, u32[]{:S(2)}) collective-permute-start(f32[64,2048]{1,0:T(8,128)S(1)} %collective-permute-done.9.refs_5_), channel_id=1, source_target_pairs={{1,0},{2,3},{5,4},{6,7},{9,8},{10,11},{13,12},{14,15},{17,16},{18,... | collective-permute-start | bytes 1572872 | tf_op jit(solution)/shard_map/ppermute | solution.py:585
  34.4 2.2 %copy-start.1 = (f32[8,256,512]{2,1,0:T(8,128)S(1)}, f32[8,256,512]{2,1,0:T(8,128)}, u32[]{:S(2)}) copy-start(f32[8,256,512]{2,1,0:T(8,128)} %refs_0_.4) | copy-start | bytes 12582916
  50.1 27.6 %collective-permute-start.11 = (f32[1,32,512]{2,1,0:T(8,128)S(1)}, f32[1,32,512]{2,1,0:T(8,128)S(1)}, u32[]{:S(2)}, u32[]{:S(2)}) collective-permute-start(f32[1,32,512]{2,1,0:T(8,128)S(1)} %bitcast.30), channel_id=1, source_target_pairs={{0,16},{4,20},{8,24},{12,28},{16,0},{20,4},{24,8},{28,12},{1,17},{... | collective-permute-start | bytes 196616 | tf_op jit(solution)/shard_map/ppermute | solution.py:706
  77.2 4.6 %collective-permute-start.14 = (f32[4,32,768]{2,1,0:T(8,128)S(1)}, f32[4,32,768]{2,1,0:T(8,128)S(1)}, u32[]{:S(2)}, u32[]{:S(2)}) collective-permute-start(f32[4,32,768]{2,1,0:T(8,128)S(1)} %get-tuple-element.40), channel_id=1, source_target_pairs={{0,4},{4,0},{8,12},{12,8},{16,20},{20,16},{24,28},{28,24},{1,5},{5... | collective-permute-start | bytes 1179656 | tf_op jit(solution)/shard_map/ppermute | solution.py:728
  77.7 1.5 collective-permute-start.12
  79.3 9.6 %collective-permute-start.13 = (f32[4,32,512]{2,1,0:T(8,128)S(1)}, f32[4,32,512]{2,1,0:T(8,128)S(1)}, u32[]{:S(2)}, u32[]{:S(2)}) collective-permute-start(f32[4,32,512]{2,1,0:T(8,128)S(1)} %pad_maximum_fusion.refs_0_), channel_id=1, source_target_pairs={{0,8},{4,12},{8,0},{12,4},{16,24},{20,28},{24,16},{28,20},{1,9},{5... | collective-permute-start | bytes 786440 | tf_op jit(solution)/shard_map/ppermute | solution.py:710
  81.8 9.2 %collective-permute-start.15 = (f32[32,768]{1,0:T(8,128)S(1)}, f32[32,768]{1,0:T(8,128)S(1)}, u32[]{:S(2)}, u32[]{:S(2)}) collective-permute-start(f32[32,768]{1,0:T(8,128)S(1)} %get-tuple-element.55), channel_id=1, source_target_pairs={{0,8},{4,12},{8,0},{12,4},{16,24},{20,28},{24,16},{28,20},{1,9},{5... | collective-permute-start | bytes 294920 | tf_op jit(solution)/shard_map/ppermute | solution.py:731
  81.9 9.1 %collective-permute-start.16 = (f32[32,768]{1,0:T(8,128)S(1)}, f32[32,768]{1,0:T(8,128)S(1)}, u32[]{:S(2)}, u32[]{:S(2)}) collective-permute-start(f32[32,768]{1,0:T(8,128)S(1)} %get-tuple-element.54), channel_id=1, source_target_pairs={{0,16},{4,20},{8,24},{12,28},{16,0},{20,4},{24,8},{28,12},{1,17},{... | collective-permute-start | bytes 294920 | tf_op jit(solution)/shard_map/ppermute | solution.py:731
  83.3 10.1 %collective-permute-start.17 = (f32[32,768]{1,0:T(8,128)S(1)}, f32[32,768]{1,0:T(8,128)S(1)}, u32[]{:S(2)}, u32[]{:S(2)}) collective-permute-start(f32[32,768]{1,0:T(8,128)S(1)} %get-tuple-element.53), channel_id=1, source_target_pairs={{0,24},{4,28},{8,16},{12,20},{16,8},{20,12},{24,0},{28,4},{1,25},{... | collective-permute-start | bytes 294920 | tf_op jit(solution)/shard_map/ppermute | solution.py:731
  94.8 4.3 %collective-permute-start.18 = (f32[32,512]{1,0:T(8,128)S(1)}, f32[32,512]{1,0:T(8,128)S(1)}, u32[]{:S(2)}, u32[]{:S(2)}) collective-permute-start(f32[32,512]{1,0:T(8,128)S(1)} %get-tuple-element.41.refs_0_), channel_id=1, source_target_pairs={{0,8},{4,12},{8,0},{12,4},{16,24},{20,28},{24,16},{28,20},{1,9},{5... | collective-permute-start | bytes 196616 | tf_op jit(solution)/shard_map/ppermute | solution.py:735
  96.6 4.7 %collective-permute-start.19 = (f32[32,512]{1,0:T(8,128)S(1)}, f32[32,512]{1,0:T(8,128)S(1)}, u32[]{:S(2)}, u32[]{:S(2)}) collective-permute-start(f32[32,512]{1,0:T(8,128)S(1)} %get-tuple-element.41.refs_0_), channel_id=1, source_target_pairs={{0,16},{4,20},{8,24},{12,28},{16,0},{20,4},{24,8},{28,12},{1,17},{... | collective-permute-start | bytes 196616 | tf_op jit(solution)/shard_map/ppermute | solution.py:735
  97.5 5.2 %collective-permute-start.20 = (f32[32,512]{1,0:T(8,128)S(1)}, f32[32,512]{1,0:T(8,128)S(1)}, u32[]{:S(2)}, u32[]{:S(2)}) collective-permute-start(f32[32,512]{1,0:T(8,128)S(1)} %get-tuple-element.41.refs_0_), channel_id=1, source_target_pairs={{0,24},{4,28},{8,16},{12,20},{16,8},{20,12},{24,0},{28,4},{1,25},{... | collective-permute-start | bytes 196616 | tf_op jit(solution)/shard_map/ppermute | solution.py:735
  98.3 4.3 %collective-permute-start.21 = (f32[32,512]{1,0:T(8,128)S(1)}, f32[32,512]{1,0:T(8,128)S(1)}, u32[]{:S(2)}, u32[]{:S(2)}) collective-permute-start(f32[32,512]{1,0:T(8,128)S(1)} %get-tuple-element.41.refs_0_), channel_id=1, source_target_pairs={{0,4},{4,0},{8,12},{12,8},{16,20},{20,16},{24,28},{28,24},{1,5},{5... | collective-permute-start | bytes 196616 | tf_op jit(solution)/shard_map/ppermute | solution.py:738
  99.1 3.5 %collective-permute-start.22 = (f32[32,512]{1,0:T(8,128)S(1)}, f32[32,512]{1,0:T(8,128)S(1)}, u32[]{:S(2)}, u32[]{:S(2)}) collective-permute-start(f32[32,512]{1,0:T(8,128)S(1)} %collective-permute-done.18.refs_1_), channel_id=1, source_target_pairs={{0,4},{4,0},{8,12},{12,8},{16,20},{20,16},{24,28},{28,24},{1,5},{5... | collective-permute-start | bytes 196616 | tf_op jit(solution)/shard_map/ppermute | solution.py:738
  101.3 1.3 collective-permute-start.23
  102.6 1.3 collective-permute-start.24
  106.7 9.2 %collective-permute-start.25 = (f32[64,1152]{1,0:T(8,128)S(1)}, f32[64,1152]{1,0:T(8,128)S(1)}, u32[]{:S(2)}, u32[]{:S(2)}) collective-permute-start(f32[64,1152]{1,0:T(8,128)S(1)} %get-tuple-element.45), channel_id=1, source_target_pairs={{0,1},{3,2},{4,5},{7,6},{8,9},{11,10},{12,13},{15,14},{16,17},{19,... | collective-permute-start | bytes 884744 | tf_op jit(solution)/shard_map/ppermute | solution.py:630
  108.5 18.3 %collective-permute-start.28 = (f32[64,1152]{1,0:T(8,128)S(1)}, f32[64,1152]{1,0:T(8,128)S(1)}, u32[]{:S(2)}, u32[]{:S(2)}) collective-permute-start(f32[64,1152]{1,0:T(8,128)S(1)} %get-tuple-element.44), channel_id=1, source_target_pairs={{0,1},{3,2},{4,5},{7,6},{8,9},{11,10},{12,13},{15,14},{16,17},{19,... | collective-permute-start | bytes 884744 | tf_op jit(solution)/shard_map/ppermute | solution.py:631
  115.9 11.7 %collective-permute-start.26 = (f32[64,1152]{1,0:T(8,128)S(1)}, f32[64,1152]{1,0:T(8,128)S(1)}, u32[]{:S(2)}, u32[]{:S(2)}) collective-permute-start(f32[64,1152]{1,0:T(8,128)S(1)} %add.56), channel_id=1, source_target_pairs={{1,2},{2,1},{5,6},{6,5},{9,10},{10,9},{13,14},{14,13},{17,18},{18,... | collective-permute-start | bytes 884744 | tf_op jit(solution)/shard_map/ppermute | solution.py:632
  119.1 14.4 %collective-permute-start.31 = (f32[64,1024]{1,0:T(8,128)S(1)}, f32[64,1024]{1,0:T(8,128)S(1)}, u32[]{:S(2)}, u32[]{:S(2)}) collective-permute-start(f32[64,1024]{1,0:T(8,128)S(1)} %get-tuple-element.50), channel_id=1, source_target_pairs={{0,1},{3,2},{4,5},{7,6},{8,9},{11,10},{12,13},{15,14},{16,17},{19,... | collective-permute-start | bytes 786440 | tf_op jit(solution)/shard_map/ppermute | solution.py:630
  126.9 20.6 %collective-permute-start.29 = (f32[64,1152]{1,0:T(8,128)S(1)}, f32[64,1152]{1,0:T(8,128)S(1)}, u32[]{:S(2)}, u32[]{:S(2)}) collective-permute-start(f32[64,1152]{1,0:T(8,128)S(1)} %add.58), channel_id=1, source_target_pairs={{1,2},{2,1},{5,6},{6,5},{9,10},{10,9},{13,14},{14,13},{17,18},{18,... | collective-permute-start | bytes 884744 | tf_op jit(solution)/shard_map/ppermute | solution.py:634
  127.7 19.9 %collective-permute-start.27 = (f32[64,1152]{1,0:T(8,128)S(1)}, f32[64,1152]{1,0:T(8,128)S(1)}, u32[]{:S(2)}, u32[]{:S(2)}) collective-permute-start(f32[64,1152]{1,0:T(8,128)S(1)} %add.57), channel_id=1, source_target_pairs={{0,1},{1,0},{2,3},{3,2},{4,5},{5,4},{6,7},{7,6},{8,9},{9,8},{10,11... | collective-permute-start | bytes 884744 | tf_op jit(solution)/shard_map/ppermute | solution.py:633
  128.4 14.4 %collective-permute-start.34 = (f32[64,1024]{1,0:T(8,128)S(1)}, f32[64,1024]{1,0:T(8,128)S(1)}, u32[]{:S(2)}, u32[]{:S(2)}) collective-permute-start(f32[64,1024]{1,0:T(8,128)S(1)} %get-tuple-element.49), channel_id=1, source_target_pairs={{0,1},{3,2},{4,5},{7,6},{8,9},{11,10},{12,13},{15,14},{16,17},{19,... | collective-permute-start | bytes 786440 | tf_op jit(solution)/shard_map/ppermute | solution.py:631
  133.6 9.9 %collective-permute-start.32 = (f32[64,1024]{1,0:T(8,128)S(1)}, f32[64,1024]{1,0:T(8,128)S(1)}, u32[]{:S(2)}, u32[]{:S(2)}) collective-permute-start(f32[64,1024]{1,0:T(8,128)S(1)} %add.61), channel_id=1, source_target_pairs={{1,2},{2,1},{5,6},{6,5},{9,10},{10,9},{13,14},{14,13},{17,18},{18,... | collective-permute-start | bytes 786440 | tf_op jit(solution)/shard_map/ppermute | solution.py:632
  142.8 8.3 %collective-permute-start.35 = (f32[64,1024]{1,0:T(8,128)S(1)}, f32[64,1024]{1,0:T(8,128)S(1)}, u32[]{:S(2)}, u32[]{:S(2)}) collective-permute-start(f32[64,1024]{1,0:T(8,128)S(1)} %add.63), channel_id=1, source_target_pairs={{1,2},{2,1},{5,6},{6,5},{9,10},{10,9},{13,14},{14,13},{17,18},{18,... | collective-permute-start | bytes 786440 | tf_op jit(solution)/shard_map/ppermute | solution.py:634
  143.5 8.4 %collective-permute-start.33 = (f32[64,1024]{1,0:T(8,128)S(1)}, f32[64,1024]{1,0:T(8,128)S(1)}, u32[]{:S(2)}, u32[]{:S(2)}) collective-permute-start(f32[64,1024]{1,0:T(8,128)S(1)} %add.62), channel_id=1, source_target_pairs={{0,1},{1,0},{2,3},{3,2},{4,5},{5,4},{6,7},{7,6},{8,9},{9,8},{10,11... | collective-permute-start | bytes 786440 | tf_op jit(solution)/shard_map/ppermute | solution.py:633
  147.5 1.3 collective-permute-start.30

commit v6 on v5

--- a/solution.py
+++ b/solution.py
@@ -95,7 +95,7 @@
     rows, cols, total = raw.shape
     halo = halo_inner.shape[0]
     carried = [array for array in (movie, *pair) if array is not None]
-    width = 64
+    width = 128
     pad = 8
     extended = rows + 2 * halo
     inputs = 3 if detour is None else 4
@@ -248,7 +248,7 @@
     count = len(entries) + 1
     share, pixel_count = own.shape
     rank = share * count
-    block = 512
+    block = pixel_count
     steps = pixel_count // block
 
     def kernel(scalars, *refs):
@@ -295,7 +295,7 @@
         ),
         out_shape=[shaped(2 * rank, pixel_count, dtype=jnp.bfloat16), shaped(rank, rank)],
         cost_estimate=cost(4 * rank * rank * pixel_count, 8 * rank * pixel_count),
-        compiler_params=grant(8),
+        compiler_params=grant(20),
         name="footprints",
     )(scalars, own, *flat)
 
@@ -306,7 +306,7 @@
     spans = [high.shape[1] for high, _ in movies]
     frames = sum(spans)
     columns = frames + rank
-    block = 512
+    block = pixel_count
     steps = pixel_count // block
     chips = rank // (2 * trace_rows)
 
@@ -351,7 +351,7 @@
         ),
         out_shape=[shaped(chips, trace_rows, columns)] * 2,
         cost_estimate=cost(8 * rank * pixel_count * columns, 4 * pixel_count * (rank + columns)),
-        compiler_params=grant(10),
+        compiler_params=grant(24),
         name="numerator",
     )(scalars, foot, gram, *[array for movie in movies for array in movie])
 
@@ -407,7 +407,7 @@
     pixel_count = movies[0][0].shape[0]
     spans = [high.shape[1] for high, _ in movies]
     part = pixel_count // HALVES
-    block = rank
+    block = part
     steps = part // block
     columns = part + (half_rank if with_gram else 0)
     outs = len(places)
@@ -475,7 +475,7 @@
         ),
         out_shape=[shaped(share, columns)] * outs,
         cost_estimate=cost(8 * rank * part * frames, 4 * part * (frames + rank)),
-        compiler_params=grant(10),
+        compiler_params=grant(18),
         name="products",
     )(scalars, *near, *far, *[array for movie in movies for array in movie])
 
@@ -484,7 +484,7 @@
     share, pixel_count = own.shape
     rank = foot.shape[0] // 2
     part = pixel_count // HALVES
-    block = 512
+    block = part
     steps = part // block
 
     def kernel(scalars, own_ref, foot_ref, later_ref, *refs):
@@ -529,7 +529,7 @@
 def second_final_call(own, parts, below, carried):
     share, pixel_count = own.shape
     part = pixel_count // HALVES
-    block = 512
+    block = part
     steps = part // block
 
     def kernel(own_ref, below_ref, *refs):

time: 153 us -> 149 us (0.974)
  Pallas kernels: 37.3 us -> 32.4 us
    pallas_call x2, Pallas kernels: 5.34 us -> 3.52 us  [products_call(): pl.pallas_call(kernel, grid_spec=pltpu.PrefetchScalarGridSpec(num_scalar_...]
    unnamed x10 -> x12, local copies, waits for them, and re-layouts: 5.37 us -> 5.37 us
  transfers between devices with their start and end apart: 36 -> 36, of which waited for: 16 -> 16; matrix products, arithmetic and copies ran while one was open for 1% -> 1% of each run, Pallas kernels for 20% -> 18%
where the time goes in v6:
time: 149 us
  starting transfers between devices  56 us (38%)
  waiting for transfers between devices  52.1 us (35%)
  Pallas kernels  32.4 us (22%)
  local copies, waits for them, and re-layouts  6.79 us (5%)
    pallas_call x2, Pallas kernels, diffuse_call(): pl.pallas_call(kernel, grid_spec=pltpu.PrefetchScalarGridSpec(num_scalar_...  19 us
    ppermute x2, starting transfers between devices, line_scatter(): first = lax.ppermute(opposite, axis, inward)  9.53 us
    ppermute x1, waiting for transfers between devices, line_gather(): near = lax.ppermute(block, axis, [(k, k ^ 1) for k in range(count)])  9.49 us
    ppermute x2, waiting for transfers between devices, line_scatter(): second = lax.ppermute(remaining, axis, inward)  8.51 us
    ppermute x2, waiting for transfers between devices, line_scatter(): first = lax.ppermute(opposite, axis, inward)  7.87 us
    ppermute x2, starting transfers between devices, compute(): lax.ppermute(held, 'pix', swap(mask))  6.75 us
    ppermute x2, starting transfers between devices, compute(): from_inner = lax.ppermute(inward, 'pix', swap(1))  6.08 us
    ppermute x2, starting transfers between devices, line_scatter(): lax.ppermute(beside + third, axis, [(k, k ^ 1) for k in range(count)])  5.44 us
  transfers between devices with their start and end apart: 36, of which 16 were waited for; matrix products, arithmetic and copies ran while one was open for 1% of the time, Pallas kernels for 18%

profile of v6, /device:TPU:0, one launch (start us, length us, event | category | flops | bytes accessed | tf_op | source)
XLA Modules:
  0.0 148.7 jit_solution(6813418612614060502)
XLA Ops:
  0.7 2.2 %copy-done = f32[8,256,512]{2,1,0:T(8,128)S(1)} copy-done((f32[8,256,512]{2,1,0:T(8,128)S(1)}, f32[8,256,512]{2,1,0:T(8,128)}, u32[]{:S(2)}) %copy-start) | copy-done | bytes 4194328
  2.9 2.0 %edges.1 = (f32[4,256,256]{2,1,0:T(8,128)S(1)}, f32[4,256,256]{2,1,0:T(8,128)}, f32[4,256,256]{2,1,0:T(8,128)S(1)}) custom-call(s32[7]{0:T(128)S(1)} %stack.43.flags.scalars, f32[8,256,512]{2,1,0:T(8,128)S(1)} %copy-done), custom_call_target="tpu_custom_call" | custom-call | flops 1 | bytes 6291456 | tf_op jit(solution)/shard_map/edges/pallas_call | solution.py:78
  4.9 1.0 copy-done.4
  6.4 1.3 collective-permute-start.2
  7.7 1.3 constant_dynamic-slice_fusion
  9.8 2.6 %collective-permute-start.6 = (f32[64,2048]{1,0:T(8,128)S(1)}, f32[64,2048]{1,0:T(8,128)S(1)}, u32[]{:S(2)}, u32[]{:S(2)}) collective-permute-start(f32[64,2048]{1,0:T(8,128)S(1)} %copy-done.3), channel_id=1, source_target_pairs={{0,1},{1,0},{2,3},{3,2},{4,5},{5,4},{6,7},{7,6},{8,9},{9,8},{10,11... | collective-permute-start | bytes 1572872 | tf_op jit(solution)/shard_map/ppermute | solution.py:581
  13.1 9.5 %collective-permute-done.6.refs_1_.refs_2_ = f32[64,2048]{1,0:T(8,128)S(1)} collective-permute-done((f32[64,2048]{1,0:T(8,128)S(1)}, f32[64,2048]{1,0:T(8,128)S(1)}, u32[]{:S(2)}, u32[]{:S(2)}) %collective-permute-start.6) | collective-permute-done | bytes 524320 | tf_op jit(solution)/shard_map/ppermute | solution.py:581
  24.0 5.6 %collective-permute-start = (f32[4,256,256]{2,1,0:T(8,128)}, f32[4,256,256]{2,1,0:T(8,128)S(1)}, u32[]{:S(2)}, u32[]{:S(2)}) collective-permute-start(f32[4,256,256]{2,1,0:T(8,128)} %copy-done.4), channel_id=1, source_target_pairs={{0,4},{4,0},{8,12},{12,8},{16,20},{20,16},{24,28},{28,24},{1,5},{5... | collective-permute-start | bytes 3145736 | tf_op jit(solution)/shard_map/ppermute | solution.py:700
  29.6 2.1 %collective-permute-start.3 = (f32[4,256,256]{2,1,0:T(8,128)}, f32[4,256,256]{2,1,0:T(8,128)S(1)}, u32[]{:S(2)}, u32[]{:S(2)}) collective-permute-start(f32[4,256,256]{2,1,0:T(8,128)} %collective-permute-done.2), channel_id=1, source_target_pairs={{28,16},{0,12},{29,17},{1,13},{30,18},{2,14},{31,19},{3,15}} | collective-permute-start | bytes 3145736 | tf_op jit(solution)/shard_map/ppermute | solution.py:698
  31.8 1.3 collective-permute-start.8
  33.1 1.3 collective-permute-start.10
  34.4 2.2 %copy-done.1 = f32[8,256,512]{2,1,0:T(8,128)S(1)} copy-done((f32[8,256,512]{2,1,0:T(8,128)S(1)}, f32[8,256,512]{2,1,0:T(8,128)}, u32[]{:S(2)}) %copy-start.1) | copy-done | bytes 4194328
  36.6 9.5 %diffuse.2 = (f32[8,256,512]{2,1,0:T(8,128)}, bf16[8,256,256]{2,1,0:T(8,128)(2,1)S(1)}, bf16[8,256,256]{2,1,0:T(8,128)(2,1)S(1)}) custom-call(s32[7]{0:T(128)S(1)} %stack.43.flags.scalars, f32[8,256,512]{2,1,0:T(8,128)S(1)} %copy-done.1, f32[4,256,256]{2,1,0:T(8,128)S(1)} %collective-permute-done.4.refs_1_, f32[4,256,256]{2,1,0:T(8,128)S(1)} %collective-permute-done.5.refs_2_), custom_call_target="tpu_custom_call" | custom-call | flops 104857600 | bytes 8388608 | tf_op jit(solution)/shard_map/diffuse/pallas_call | solution.py:223
  46.1 4.0 %collective-permute-done.8.refs_4_ = f32[64,2048]{1,0:T(8,128)S(1)} collective-permute-done((f32[64,2048]{1,0:T(8,128)S(1)}, f32[64,2048]{1,0:T(8,128)S(1)}, u32[]{:S(2)}, u32[]{:S(2)}) %collective-permute-start.8) | collective-permute-done | bytes 524320 | tf_op jit(solution)/shard_map/ppermute | solution.py:584
  50.1 6.6 %collective-permute-start.11 = (f32[1,32,512]{2,1,0:T(8,128)S(1)}, f32[1,32,512]{2,1,0:T(8,128)S(1)}, u32[]{:S(2)}, u32[]{:S(2)}) collective-permute-start(f32[1,32,512]{2,1,0:T(8,128)S(1)} %bitcast.30), channel_id=1, source_target_pairs={{0,16},{4,20},{8,24},{12,28},{16,0},{20,4},{24,8},{28,12},{1,17},{... | collective-permute-start | bytes 196616 | tf_op jit(solution)/shard_map/ppermute | solution.py:706
  56.8 4.6 %collective-permute-done.10.refs_6_ = f32[64,2048]{1,0:T(8,128)S(1)} collective-permute-done((f32[64,2048]{1,0:T(8,128)S(1)}, f32[64,2048]{1,0:T(8,128)S(1)}, u32[]{:S(2)}, u32[]{:S(2)}) %collective-permute-start.10) | collective-permute-done | bytes 524320 | tf_op jit(solution)/shard_map/ppermute | solution.py:585
  61.3 1.8 %footprints.1 = (bf16[512,2048]{1,0:T(8,128)(2,1)S(1)}, f32[256,256]{1,0:T(8,128)S(1)}) custom-call(s32[7]{0:T(128)S(1)} %stack.43.flags.scalars, f32[64,2048]{1,0:T(8,128)S(1)} %copy-done.3, f32[64,2048]{1,0:T(8,128)S(1)} %collective-permute-done.6.refs_1_.refs_2_, f32[64,2048]{1,0:T(8,128)S(1)} %collective-permute-done.6.refs_1_.refs_2_, ...), custom_call_target="tpu_custom_call" | custom-call | flops 536870912 | bytes 4194304 | tf_op jit(solution)/shard_map/footprints/pallas_call | solution.py:284
  63.2 9.5 %diffuse.3 = (f32[8,256,512]{2,1,0:T(8,128)}, bf16[8,256,256]{2,1,0:T(8,128)(2,1)S(1)}, bf16[8,256,256]{2,1,0:T(8,128)(2,1)S(1)}) custom-call(s32[7]{0:T(128)S(1)} %stack.43.flags.scalars, f32[8,256,512]{2,1,0:T(8,128)S(1)} %copy-done.2, f32[4,256,256]{2,1,0:T(8,128)S(1)} %collective-permute-done.refs_1_, ...), custom_call_target="tpu_custom_call", output_to_operand_aliasing={{0}: (5, {})} | custom-call | flops 104857600 | bytes 8388608 | tf_op jit(solution)/shard_map/diffuse/pallas_call | solution.py:223
  72.7 2.4 %numerator.1 = (f32[4,32,768]{2,1,0:T(8,128)S(1)}, f32[4,32,768]{2,1,0:T(8,128)S(1)}) custom-call(s32[7]{0:T(128)S(1)} %stack.43.flags.scalars, bf16[512,2048]{1,0:T(8,128)(2,1)S(1)} %get-tuple-element.33.foot_ref.later_ref, f32[256,256]{1,0:T(8,128)S(1)} %get-tuple-element.34.gram_ref, bf16[2048,256]{1,0:T(8,128)(2,1)S(1)} %bitcast.18, ...), custom_call_target="tpu_custom_call" | custom-call | flops 3221225472 | bytes 8388608 | tf_op jit(solution)/shard_map/numerator/pallas_call | solution.py:339
  75.8 1.4 collective-permute-done.12
  77.2 2.5 %collective-permute-start.13 = (f32[4,32,512]{2,1,0:T(8,128)S(1)}, f32[4,32,512]{2,1,0:T(8,128)S(1)}, u32[]{:S(2)}, u32[]{:S(2)}) collective-permute-start(f32[4,32,512]{2,1,0:T(8,128)S(1)} %pad_maximum_fusion.refs_0_), channel_id=1, source_target_pairs={{0,8},{4,12},{8,0},{12,4},{16,24},{20,28},{24,16},{28,20},{1,9},{5... | collective-permute-start | bytes 786440 | tf_op jit(solution)/shard_map/ppermute | solution.py:710
  79.8 1.5 collective-permute-start.16
  81.3 2.0 %collective-permute-start.17 = (f32[32,768]{1,0:T(8,128)S(1)}, f32[32,768]{1,0:T(8,128)S(1)}, u32[]{:S(2)}, u32[]{:S(2)}) collective-permute-start(f32[32,768]{1,0:T(8,128)S(1)} %get-tuple-element.53), channel_id=1, source_target_pairs={{0,24},{4,28},{8,16},{12,20},{16,8},{20,12},{24,0},{28,4},{1,25},{... | collective-permute-start | bytes 294920 | tf_op jit(solution)/shard_map/ppermute | solution.py:731
  83.3 3.6 %collective-permute-done.13.refs_1_ = f32[4,32,512]{2,1,0:T(8,128)S(1)} collective-permute-done((f32[4,32,512]{2,1,0:T(8,128)S(1)}, f32[4,32,512]{2,1,0:T(8,128)S(1)}, u32[]{:S(2)}, u32[]{:S(2)}) %collective-permute-start.13) | collective-permute-done | bytes 262176 | tf_op jit(solution)/shard_map/ppermute | solution.py:710
  86.8 2.1 %collective-permute-done.15.refs_4_ = f32[32,768]{1,0:T(8,128)S(1)} collective-permute-done((f32[32,768]{1,0:T(8,128)S(1)}, f32[32,768]{1,0:T(8,128)S(1)}, u32[]{:S(2)}, u32[]{:S(2)}) %collective-permute-start.15) | collective-permute-done | bytes 98336 | tf_op jit(solution)/shard_map/ppermute | solution.py:731
  89.0 2.4 %collective-permute-done.17.refs_6_ = f32[32,768]{1,0:T(8,128)S(1)} collective-permute-done((f32[32,768]{1,0:T(8,128)S(1)}, f32[32,768]{1,0:T(8,128)S(1)}, u32[]{:S(2)}, u32[]{:S(2)}) %collective-permute-start.17) | collective-permute-done | bytes 98336 | tf_op jit(solution)/shard_map/ppermute | solution.py:731
  91.4 1.4 traces.1
  92.8 1.7 %collective-permute-start.18 = (f32[32,512]{1,0:T(8,128)S(1)}, f32[32,512]{1,0:T(8,128)S(1)}, u32[]{:S(2)}, u32[]{:S(2)}) collective-permute-start(f32[32,512]{1,0:T(8,128)S(1)} %get-tuple-element.41.refs_0_), channel_id=1, source_target_pairs={{0,8},{4,12},{8,0},{12,4},{16,24},{20,28},{24,16},{28,20},{1,9},{5... | collective-permute-start | bytes 196616 | tf_op jit(solution)/shard_map/ppermute | solution.py:735
  94.5 0.9 collective-permute-start.19
  95.4 0.9 collective-permute-start.20
  96.3 0.8 collective-permute-done.18.refs_1_
  97.1 2.2 %collective-permute-done.19.refs_2_ = f32[32,512]{1,0:T(8,128)S(1)} collective-permute-done((f32[32,512]{1,0:T(8,128)S(1)}, f32[32,512]{1,0:T(8,128)S(1)}, u32[]{:S(2)}, u32[]{:S(2)}) %collective-permute-start.19) | collective-permute-done | bytes 65568 | tf_op jit(solution)/shard_map/ppermute | solution.py:735
  99.2 1.3 collective-permute-done.20.refs_3_
  100.6 1.2 collective-permute-done.24.refs_7_
  101.8 1.9 %products.2 = (f32[64,1152]{1,0:T(8,128)S(1)}, f32[64,1152]{1,0:T(8,128)S(1)}, f32[64,1152]{1,0:T(8,128)S(1)}, f32[64,1152]{1,0:T(8,128)S(1)}) custom-call(s32[7]{0:T(128)S(1)} %stack.43.flags.scalars, f32[32,512]{1,0:T(8,128)S(1)} %get-tuple-element.41.refs_0_, f32[32,512]{1,0:T(8,128)S(1)} %collective-permute-done.18.refs_1_, ...), custom_call_target="tpu_custom_call" | custom-call | flops 1073741824 | bytes 3145728 | tf_op jit(solution)/shard_map/products/pallas_call | solution.py:458
  103.7 1.8 %collective-permute-start.25 = (f32[64,1152]{1,0:T(8,128)S(1)}, f32[64,1152]{1,0:T(8,128)S(1)}, u32[]{:S(2)}, u32[]{:S(2)}) collective-permute-start(f32[64,1152]{1,0:T(8,128)S(1)} %get-tuple-element.45), channel_id=1, source_target_pairs={{0,1},{3,2},{4,5},{7,6},{8,9},{11,10},{12,13},{15,14},{16,17},{19,... | collective-permute-start | bytes 884744 | tf_op jit(solution)/shard_map/ppermute | solution.py:630
  105.5 1.3 collective-permute-start.28
  106.8 6.0 %collective-permute-done.25 = f32[64,1152]{1,0:T(8,128)S(1)} collective-permute-done((f32[64,1152]{1,0:T(8,128)S(1)}, f32[64,1152]{1,0:T(8,128)S(1)}, u32[]{:S(2)}, u32[]{:S(2)}) %collective-permute-start.25) | collective-permute-done | bytes 294944 | tf_op jit(solution)/shard_map/ppermute | solution.py:630
  113.6 1.6 %products.3 = (f32[64,1024]{1,0:T(8,128)S(1)}, f32[64,1024]{1,0:T(8,128)S(1)}, f32[64,1024]{1,0:T(8,128)S(1)}, f32[64,1024]{1,0:T(8,128)S(1)}) custom-call(s32[7]{0:T(128)S(1)} %stack.43.flags.scalars, f32[32,512]{1,0:T(8,128)S(1)} %get-tuple-element.41.refs_0_, f32[32,512]{1,0:T(8,128)S(1)} %collective-permute-done.18.refs_1_, ...), custom_call_target="tpu_custom_call" | custom-call | flops 1073741824 | bytes 3145728 | tf_op jit(solution)/shard_map/products/pallas_call | solution.py:458
  115.2 7.8 %collective-permute-start.31 = (f32[64,1024]{1,0:T(8,128)S(1)}, f32[64,1024]{1,0:T(8,128)S(1)}, u32[]{:S(2)}, u32[]{:S(2)}) collective-permute-start(f32[64,1024]{1,0:T(8,128)S(1)} %get-tuple-element.50), channel_id=1, source_target_pairs={{0,1},{3,2},{4,5},{7,6},{8,9},{11,10},{12,13},{15,14},{16,17},{19,... | collective-permute-start | bytes 786440 | tf_op jit(solution)/shard_map/ppermute | solution.py:630
  123.8 1.4 collective-permute-start.27
  125.1 2.6 %collective-permute-start.34 = (f32[64,1024]{1,0:T(8,128)S(1)}, f32[64,1024]{1,0:T(8,128)S(1)}, u32[]{:S(2)}, u32[]{:S(2)}) collective-permute-start(f32[64,1024]{1,0:T(8,128)S(1)} %get-tuple-element.49), channel_id=1, source_target_pairs={{0,1},{3,2},{4,5},{7,6},{8,9},{11,10},{12,13},{15,14},{16,17},{19,... | collective-permute-start | bytes 786440 | tf_op jit(solution)/shard_map/ppermute | solution.py:631
  127.8 1.8 %collective-permute-done.31 = f32[64,1024]{1,0:T(8,128)S(1)} collective-permute-done((f32[64,1024]{1,0:T(8,128)S(1)}, f32[64,1024]{1,0:T(8,128)S(1)}, u32[]{:S(2)}, u32[]{:S(2)}) %collective-permute-start.31) | collective-permute-done | bytes 262176 | tf_op jit(solution)/shard_map/ppermute | solution.py:630
  130.3 8.5 %collective-permute-done.34 = f32[64,1024]{1,0:T(8,128)S(1)} collective-permute-done((f32[64,1024]{1,0:T(8,128)S(1)}, f32[64,1024]{1,0:T(8,128)S(1)}, u32[]{:S(2)}, u32[]{:S(2)}) %collective-permute-start.34) | collective-permute-done | bytes 262176 | tf_op jit(solution)/shard_map/ppermute | solution.py:631
  139.6 4.1 %collective-permute-start.33 = (f32[64,1024]{1,0:T(8,128)S(1)}, f32[64,1024]{1,0:T(8,128)S(1)}, u32[]{:S(2)}, u32[]{:S(2)}) collective-permute-start(f32[64,1024]{1,0:T(8,128)S(1)} %add.62), channel_id=1, source_target_pairs={{0,1},{1,0},{2,3},{3,2},{4,5},{5,4},{6,7},{7,6},{8,9},{9,8},{10,11... | collective-permute-start | bytes 786440 | tf_op jit(solution)/shard_map/ppermute | solution.py:633
  143.7 1.2 collective-permute-done.30.refs_4_
  144.9 1.6 %final.2 = (f32[64,2048]{1,0:T(8,128)}, f32[64,1024]{1,0:T(8,128)S(1)}) custom-call(s32[7]{0:T(128)S(1)} %stack.43.flags.scalars, f32[64,2048]{1,0:T(8,128)S(1)} %copy-done.3, bf16[512,2048]{1,0:T(8,128)(2,1)S(1)} %get-tuple-element.33.foot_ref.later_ref, bf16[512,2048]{1,0:T(8,128)(2,1)S(1)} %get-tuple-element.33.foot_ref.later_ref, ...), custom_call_target="tpu_custom_call" | custom-call | flops 201326592 | bytes 3407872 | tf_op jit(solution)/shard_map/final/pallas_call | solution.py:514
  146.5 1.5 collective-permute-done.33.refs_1_
  (58 shorter events, 8.0 us)
Async XLA Ops:
  0.7 2.2 %copy-start = (f32[8,256,512]{2,1,0:T(8,128)S(1)}, f32[8,256,512]{2,1,0:T(8,128)}, u32[]{:S(2)}) copy-start(f32[8,256,512]{2,1,0:T(8,128)} %refs_0_.4) | copy-start | bytes 12582916
  2.9 6.8 %copy-start.3 = (f32[64,2048]{1,0:T(8,128)S(1)}, f32[64,2048]{1,0:T(8,128)}, u32[]{:S(2)}) copy-start(f32[64,2048]{1,0:T(8,128)} %own_ref.3) | copy-start | bytes 1572868
  4.9 1.0 copy-start.4
  5.9 18.1 %collective-permute-start.4 = (f32[4,256,256]{2,1,0:T(8,128)}, f32[4,256,256]{2,1,0:T(8,128)S(1)}, u32[]{:S(2)}, u32[]{:S(2)}) collective-permute-start(f32[4,256,256]{2,1,0:T(8,128)} %get-tuple-element.30), channel_id=1, source_target_pairs={{0,4},{4,0},{8,12},{12,8},{16,20},{20,16},{24,28},{28,24},{1,5},{5... | collective-permute-start | bytes 3145736 | tf_op jit(solution)/shard_map/ppermute | solution.py:700
  6.4 23.3 %collective-permute-start.2 = (f32[4,256,256]{2,1,0:T(8,128)S(1)}, f32[4,256,256]{2,1,0:T(8,128)}, u32[]{:S(2)}, u32[]{:S(2)}) collective-permute-start(f32[4,256,256]{2,1,0:T(8,128)S(1)} %get-tuple-element.29), channel_id=1, source_target_pairs={{12,28},{16,0},{13,29},{17,1},{14,30},{18,2},{15,31},{19,3}} | collective-permute-start | bytes 3145736 | tf_op jit(solution)/shard_map/ppermute | solution.py:697
  7.7 42.4 %copy-start.5 = (f32[32,512]{1,0:T(8,128)S(1)}, f32[32,512]{1,0:T(8,128)}, u32[]{:S(2)}) copy-start(f32[32,512]{1,0:T(8,128)} %param.5) | copy-start | bytes 196612
  9.0 22.7 %collective-permute-start.5 = (f32[4,256,256]{2,1,0:T(8,128)S(1)}, f32[4,256,256]{2,1,0:T(8,128)S(1)}, u32[]{:S(2)}, u32[]{:S(2)}) collective-permute-start(f32[4,256,256]{2,1,0:T(8,128)S(1)} %constant_dynamic-slice_fusion), channel_id=1, source_target_pairs={{4,8},{12,16},{20,24},{8,4},{16,12},{24,20},{5,9},{13,17},{21,25},... | collective-permute-start | bytes 3145736 | tf_op jit(solution)/shard_map/ppermute | solution.py:699
  9.8 12.8 %collective-permute-start.6 = (f32[64,2048]{1,0:T(8,128)S(1)}, f32[64,2048]{1,0:T(8,128)S(1)}, u32[]{:S(2)}, u32[]{:S(2)}) collective-permute-start(f32[64,2048]{1,0:T(8,128)S(1)} %copy-done.3), channel_id=1, source_target_pairs={{0,1},{1,0},{2,3},{3,2},{4,5},{5,4},{6,7},{7,6},{8,9},{9,8},{10,11... | collective-permute-start | bytes 1572872 | tf_op jit(solution)/shard_map/ppermute | solution.py:581
  12.4 10.9 %collective-permute-start.7 = (f32[64,2048]{1,0:T(8,128)S(1)}, f32[64,2048]{1,0:T(8,128)S(1)}, u32[]{:S(2)}, u32[]{:S(2)}) collective-permute-start(f32[64,2048]{1,0:T(8,128)S(1)} %copy-done.3), channel_id=1, source_target_pairs={{1,2},{2,1},{5,6},{6,5},{9,10},{10,9},{13,14},{14,13},{17,18},{18,... | collective-permute-start | bytes 1572872 | tf_op jit(solution)/shard_map/ppermute | solution.py:582
  22.6 10.5 %collective-permute-start.9 = (f32[64,2048]{1,0:T(8,128)S(1)}, f32[64,2048]{1,0:T(8,128)S(1)}, u32[]{:S(2)}, u32[]{:S(2)}) collective-permute-start(f32[64,2048]{1,0:T(8,128)S(1)} %collective-permute-done.6.refs_1_.refs_2_), channel_id=1, source_target_pairs={{1,2},{2,1},{5,6},{6,5},{9,10},{10,9},{13,14},{14,13},{17,18},{18,... | collective-permute-start | bytes 1572872 | tf_op jit(solution)/shard_map/ppermute | solution.py:583
  23.3 39.9 %collective-permute-start.1 = (f32[4,256,256]{2,1,0:T(8,128)S(1)}, f32[4,256,256]{2,1,0:T(8,128)S(1)}, u32[]{:S(2)}, u32[]{:S(2)}) collective-permute-start(f32[4,256,256]{2,1,0:T(8,128)S(1)} %get-tuple-element.29), channel_id=1, source_target_pairs={{4,8},{20,24},{8,4},{24,20},{5,9},{21,25},{9,5},{25,21},{6,10},{22... | collective-permute-start | bytes 3145736 | tf_op jit(solution)/shard_map/ppermute | solution.py:699
  24.0 39.1 %collective-permute-start = (f32[4,256,256]{2,1,0:T(8,128)}, f32[4,256,256]{2,1,0:T(8,128)S(1)}, u32[]{:S(2)}, u32[]{:S(2)}) collective-permute-start(f32[4,256,256]{2,1,0:T(8,128)} %copy-done.4), channel_id=1, source_target_pairs={{0,4},{4,0},{8,12},{12,8},{16,20},{20,16},{24,28},{28,24},{1,5},{5... | collective-permute-start | bytes 3145736 | tf_op jit(solution)/shard_map/ppermute | solution.py:700
  29.6 33.6 %collective-permute-start.3 = (f32[4,256,256]{2,1,0:T(8,128)}, f32[4,256,256]{2,1,0:T(8,128)S(1)}, u32[]{:S(2)}, u32[]{:S(2)}) collective-permute-start(f32[4,256,256]{2,1,0:T(8,128)} %collective-permute-done.2), channel_id=1, source_target_pairs={{28,16},{0,12},{29,17},{1,13},{30,18},{2,14},{31,19},{3,15}} | collective-permute-start | bytes 3145736 | tf_op jit(solution)/shard_map/ppermute | solution.py:698
  31.8 18.3 %collective-permute-start.8 = (f32[64,2048]{1,0:T(8,128)S(1)}, f32[64,2048]{1,0:T(8,128)S(1)}, u32[]{:S(2)}, u32[]{:S(2)}) collective-permute-start(f32[64,2048]{1,0:T(8,128)S(1)} %collective-permute-done.7.refs_3_), channel_id=1, source_target_pairs={{1,0},{2,3},{5,4},{6,7},{9,8},{10,11},{13,12},{14,15},{17,16},{18,... | collective-permute-start | bytes 1572872 | tf_op jit(solution)/shard_map/ppermute | solution.py:584
  33.1 28.2 %collective-permute-start.10 = (f32[64,2048]{1,0:T(8,128)S(1)}, f32[64,2048]{1,0:T(8,128)S(1)}, u32[]{:S(2)}, u32[]{:S(2)}) collective-permute-start(f32[64,2048]{1,0:T(8,128)S(1)} %collective-permute-done.9.refs_5_), channel_id=1, source_target_pairs={{1,0},{2,3},{5,4},{6,7},{9,8},{10,11},{13,12},{14,15},{17,16},{18,... | collective-permute-start | bytes 1572872 | tf_op jit(solution)/shard_map/ppermute | solution.py:585
  34.4 2.2 %copy-start.1 = (f32[8,256,512]{2,1,0:T(8,128)S(1)}, f32[8,256,512]{2,1,0:T(8,128)}, u32[]{:S(2)}) copy-start(f32[8,256,512]{2,1,0:T(8,128)} %refs_0_.4) | copy-start | bytes 12582916
  36.6 26.6 %copy-start.2 = (f32[8,256,512]{2,1,0:T(8,128)S(1)}, f32[8,256,512]{2,1,0:T(8,128)}, u32[]{:S(2)}) copy-start(f32[8,256,512]{2,1,0:T(8,128)} %refs_0_.4) | copy-start | bytes 12582916
  50.1 25.5 %collective-permute-start.11 = (f32[1,32,512]{2,1,0:T(8,128)S(1)}, f32[1,32,512]{2,1,0:T(8,128)S(1)}, u32[]{:S(2)}, u32[]{:S(2)}) collective-permute-start(f32[1,32,512]{2,1,0:T(8,128)S(1)} %bitcast.30), channel_id=1, source_target_pairs={{0,16},{4,20},{8,24},{12,28},{16,0},{20,4},{24,8},{28,12},{1,17},{... | collective-permute-start | bytes 196616 | tf_op jit(solution)/shard_map/ppermute | solution.py:706
  75.1 4.6 %collective-permute-start.14 = (f32[4,32,768]{2,1,0:T(8,128)S(1)}, f32[4,32,768]{2,1,0:T(8,128)S(1)}, u32[]{:S(2)}, u32[]{:S(2)}) collective-permute-start(f32[4,32,768]{2,1,0:T(8,128)S(1)} %get-tuple-element.40), channel_id=1, source_target_pairs={{0,4},{4,0},{8,12},{12,8},{16,20},{20,16},{24,28},{28,24},{1,5},{5... | collective-permute-start | bytes 1179656 | tf_op jit(solution)/shard_map/ppermute | solution.py:728
  75.7 1.5 %collective-permute-start.12 = (f32[2,32,512]{2,1,0:T(8,128)S(1)}, f32[2,32,512]{2,1,0:T(8,128)S(1)}, u32[]{:S(2)}, u32[]{:S(2)}) collective-permute-start(f32[2,32,512]{2,1,0:T(8,128)S(1)} %pad_maximum_fusion.1), channel_id=1, source_target_pairs={{0,4},{4,0},{8,12},{12,8},{16,20},{20,16},{24,28},{28,24},{1,5},{5... | collective-permute-start | bytes 393224 | tf_op jit(solution)/shard_map/ppermute | solution.py:706
  77.2 9.6 %collective-permute-start.13 = (f32[4,32,512]{2,1,0:T(8,128)S(1)}, f32[4,32,512]{2,1,0:T(8,128)S(1)}, u32[]{:S(2)}, u32[]{:S(2)}) collective-permute-start(f32[4,32,512]{2,1,0:T(8,128)S(1)} %pad_maximum_fusion.refs_0_), channel_id=1, source_target_pairs={{0,8},{4,12},{8,0},{12,4},{16,24},{20,28},{24,16},{28,20},{1,9},{5... | collective-permute-start | bytes 786440 | tf_op jit(solution)/shard_map/ppermute | solution.py:710
  79.7 9.2 %collective-permute-start.15 = (f32[32,768]{1,0:T(8,128)S(1)}, f32[32,768]{1,0:T(8,128)S(1)}, u32[]{:S(2)}, u32[]{:S(2)}) collective-permute-start(f32[32,768]{1,0:T(8,128)S(1)} %get-tuple-element.55), channel_id=1, source_target_pairs={{0,8},{4,12},{8,0},{12,4},{16,24},{20,28},{24,16},{28,20},{1,9},{5... | collective-permute-start | bytes 294920 | tf_op jit(solution)/shard_map/ppermute | solution.py:731
  79.8 9.1 %collective-permute-start.16 = (f32[32,768]{1,0:T(8,128)S(1)}, f32[32,768]{1,0:T(8,128)S(1)}, u32[]{:S(2)}, u32[]{:S(2)}) collective-permute-start(f32[32,768]{1,0:T(8,128)S(1)} %get-tuple-element.54), channel_id=1, source_target_pairs={{0,16},{4,20},{8,24},{12,28},{16,0},{20,4},{24,8},{28,12},{1,17},{... | collective-permute-start | bytes 294920 | tf_op jit(solution)/shard_map/ppermute | solution.py:731
  81.3 10.1 %collective-permute-start.17 = (f32[32,768]{1,0:T(8,128)S(1)}, f32[32,768]{1,0:T(8,128)S(1)}, u32[]{:S(2)}, u32[]{:S(2)}) collective-permute-start(f32[32,768]{1,0:T(8,128)S(1)} %get-tuple-element.53), channel_id=1, source_target_pairs={{0,24},{4,28},{8,16},{12,20},{16,8},{20,12},{24,0},{28,4},{1,25},{... | collective-permute-start | bytes 294920 | tf_op jit(solution)/shard_map/ppermute | solution.py:731
  92.8 4.3 %collective-permute-start.18 = (f32[32,512]{1,0:T(8,128)S(1)}, f32[32,512]{1,0:T(8,128)S(1)}, u32[]{:S(2)}, u32[]{:S(2)}) collective-permute-start(f32[32,512]{1,0:T(8,128)S(1)} %get-tuple-element.41.refs_0_), channel_id=1, source_target_pairs={{0,8},{4,12},{8,0},{12,4},{16,24},{20,28},{24,16},{28,20},{1,9},{5... | collective-permute-start | bytes 196616 | tf_op jit(solution)/shard_map/ppermute | solution.py:735
  94.5 4.7 %collective-permute-start.19 = (f32[32,512]{1,0:T(8,128)S(1)}, f32[32,512]{1,0:T(8,128)S(1)}, u32[]{:S(2)}, u32[]{:S(2)}) collective-permute-start(f32[32,512]{1,0:T(8,128)S(1)} %get-tuple-element.41.refs_0_), channel_id=1, source_target_pairs={{0,16},{4,20},{8,24},{12,28},{16,0},{20,4},{24,8},{28,12},{1,17},{... | collective-permute-start | bytes 196616 | tf_op jit(solution)/shard_map/ppermute | solution.py:735
  95.4 5.2 %collective-permute-start.20 = (f32[32,512]{1,0:T(8,128)S(1)}, f32[32,512]{1,0:T(8,128)S(1)}, u32[]{:S(2)}, u32[]{:S(2)}) collective-permute-start(f32[32,512]{1,0:T(8,128)S(1)} %get-tuple-element.41.refs_0_), channel_id=1, source_target_pairs={{0,24},{4,28},{8,16},{12,20},{16,8},{20,12},{24,0},{28,4},{1,25},{... | collective-permute-start | bytes 196616 | tf_op jit(solution)/shard_map/ppermute | solution.py:735
  96.3 4.3 %collective-permute-start.21 = (f32[32,512]{1,0:T(8,128)S(1)}, f32[32,512]{1,0:T(8,128)S(1)}, u32[]{:S(2)}, u32[]{:S(2)}) collective-permute-start(f32[32,512]{1,0:T(8,128)S(1)} %get-tuple-element.41.refs_0_), channel_id=1, source_target_pairs={{0,4},{4,0},{8,12},{12,8},{16,20},{20,16},{24,28},{28,24},{1,5},{5... | collective-permute-start | bytes 196616 | tf_op jit(solution)/shard_map/ppermute | solution.py:738
  97.0 3.5 %collective-permute-start.22 = (f32[32,512]{1,0:T(8,128)S(1)}, f32[32,512]{1,0:T(8,128)S(1)}, u32[]{:S(2)}, u32[]{:S(2)}) collective-permute-start(f32[32,512]{1,0:T(8,128)S(1)} %collective-permute-done.18.refs_1_), channel_id=1, source_target_pairs={{0,4},{4,0},{8,12},{12,8},{16,20},{20,16},{24,28},{28,24},{1,5},{5... | collective-permute-start | bytes 196616 | tf_op jit(solution)/shard_map/ppermute | solution.py:738
  99.2 1.3 collective-permute-start.23
  100.5 1.3 collective-permute-start.24
  103.7 9.1 %collective-permute-start.25 = (f32[64,1152]{1,0:T(8,128)S(1)}, f32[64,1152]{1,0:T(8,128)S(1)}, u32[]{:S(2)}, u32[]{:S(2)}) collective-permute-start(f32[64,1152]{1,0:T(8,128)S(1)} %get-tuple-element.45), channel_id=1, source_target_pairs={{0,1},{3,2},{4,5},{7,6},{8,9},{11,10},{12,13},{15,14},{16,17},{19,... | collective-permute-start | bytes 884744 | tf_op jit(solution)/shard_map/ppermute | solution.py:630
  105.5 17.5 %collective-permute-start.28 = (f32[64,1152]{1,0:T(8,128)S(1)}, f32[64,1152]{1,0:T(8,128)S(1)}, u32[]{:S(2)}, u32[]{:S(2)}) collective-permute-start(f32[64,1152]{1,0:T(8,128)S(1)} %get-tuple-element.44), channel_id=1, source_target_pairs={{0,1},{3,2},{4,5},{7,6},{8,9},{11,10},{12,13},{15,14},{16,17},{19,... | collective-permute-start | bytes 884744 | tf_op jit(solution)/shard_map/ppermute | solution.py:631
  112.9 10.8 %collective-permute-start.26 = (f32[64,1152]{1,0:T(8,128)S(1)}, f32[64,1152]{1,0:T(8,128)S(1)}, u32[]{:S(2)}, u32[]{:S(2)}) collective-permute-start(f32[64,1152]{1,0:T(8,128)S(1)} %add.56), channel_id=1, source_target_pairs={{1,2},{2,1},{5,6},{6,5},{9,10},{10,9},{13,14},{14,13},{17,18},{18,... | collective-permute-start | bytes 884744 | tf_op jit(solution)/shard_map/ppermute | solution.py:632
  115.2 14.4 %collective-permute-start.31 = (f32[64,1024]{1,0:T(8,128)S(1)}, f32[64,1024]{1,0:T(8,128)S(1)}, u32[]{:S(2)}, u32[]{:S(2)}) collective-permute-start(f32[64,1024]{1,0:T(8,128)S(1)} %get-tuple-element.50), channel_id=1, source_target_pairs={{0,1},{3,2},{4,5},{7,6},{8,9},{11,10},{12,13},{15,14},{16,17},{19,... | collective-permute-start | bytes 786440 | tf_op jit(solution)/shard_map/ppermute | solution.py:630
  123.0 20.6 %collective-permute-start.29 = (f32[64,1152]{1,0:T(8,128)S(1)}, f32[64,1152]{1,0:T(8,128)S(1)}, u32[]{:S(2)}, u32[]{:S(2)}) collective-permute-start(f32[64,1152]{1,0:T(8,128)S(1)} %add.58), channel_id=1, source_target_pairs={{1,2},{2,1},{5,6},{6,5},{9,10},{10,9},{13,14},{14,13},{17,18},{18,... | collective-permute-start | bytes 884744 | tf_op jit(solution)/shard_map/ppermute | solution.py:634
  123.8 19.9 %collective-permute-start.27 = (f32[64,1152]{1,0:T(8,128)S(1)}, f32[64,1152]{1,0:T(8,128)S(1)}, u32[]{:S(2)}, u32[]{:S(2)}) collective-permute-start(f32[64,1152]{1,0:T(8,128)S(1)} %add.57), channel_id=1, source_target_pairs={{0,1},{1,0},{2,3},{3,2},{4,5},{5,4},{6,7},{7,6},{8,9},{9,8},{10,11... | collective-permute-start | bytes 884744 | tf_op jit(solution)/shard_map/ppermute | solution.py:633
  125.1 13.7 %collective-permute-start.34 = (f32[64,1024]{1,0:T(8,128)S(1)}, f32[64,1024]{1,0:T(8,128)S(1)}, u32[]{:S(2)}, u32[]{:S(2)}) collective-permute-start(f32[64,1024]{1,0:T(8,128)S(1)} %get-tuple-element.49), channel_id=1, source_target_pairs={{0,1},{3,2},{4,5},{7,6},{8,9},{11,10},{12,13},{15,14},{16,17},{19,... | collective-permute-start | bytes 786440 | tf_op jit(solution)/shard_map/ppermute | solution.py:631
  129.6 9.9 %collective-permute-start.32 = (f32[64,1024]{1,0:T(8,128)S(1)}, f32[64,1024]{1,0:T(8,128)S(1)}, u32[]{:S(2)}, u32[]{:S(2)}) collective-permute-start(f32[64,1024]{1,0:T(8,128)S(1)} %add.61), channel_id=1, source_target_pairs={{1,2},{2,1},{5,6},{6,5},{9,10},{10,9},{13,14},{14,13},{17,18},{18,... | collective-permute-start | bytes 786440 | tf_op jit(solution)/shard_map/ppermute | solution.py:632
  138.8 7.7 %collective-permute-start.35 = (f32[64,1024]{1,0:T(8,128)S(1)}, f32[64,1024]{1,0:T(8,128)S(1)}, u32[]{:S(2)}, u32[]{:S(2)}) collective-permute-start(f32[64,1024]{1,0:T(8,128)S(1)} %add.63), channel_id=1, source_target_pairs={{1,2},{2,1},{5,6},{6,5},{9,10},{10,9},{13,14},{14,13},{17,18},{18,... | collective-permute-start | bytes 786440 | tf_op jit(solution)/shard_map/ppermute | solution.py:634
  139.6 8.4 %collective-permute-start.33 = (f32[64,1024]{1,0:T(8,128)S(1)}, f32[64,1024]{1,0:T(8,128)S(1)}, u32[]{:S(2)}, u32[]{:S(2)}) collective-permute-start(f32[64,1024]{1,0:T(8,128)S(1)} %add.62), channel_id=1, source_target_pairs={{0,1},{1,0},{2,3},{3,2},{4,5},{5,4},{6,7},{7,6},{8,9},{9,8},{10,11... | collective-permute-start | bytes 786440 | tf_op jit(solution)/shard_map/ppermute | solution.py:633
  143.6 1.3 collective-permute-start.30

commit v7 on v6

--- a/solution.py
+++ b/solution.py
@@ -246,6 +246,11 @@
 
 def footprints_call(scalars, own, entries):
     count = len(entries) + 1
+    flat, positions = [], []
+    for first, second, _, _ in entries:
+        at = len(flat)
+        flat += [first] if second is first else [first, second]
+        positions.append((at, len(flat) - 1))
     share, pixel_count = own.shape
     rank = share * count
     block = pixel_count
@@ -253,8 +258,8 @@
 
     def kernel(scalars, *refs):
         own_ref = refs[0]
-        entry_refs = [(refs[1 + 2 * k], refs[2 + 2 * k]) for k in range(count - 1)]
-        out_ref, gram_ref, total = refs[2 * count - 1 :]
+        entry_refs = [(refs[1 + a], refs[1 + b]) for a, b in positions]
+        out_ref, gram_ref, total = refs[1 + len(flat) :]
         here = scalars[HERE]
         step = pl.program_id(0)
 
@@ -280,7 +285,6 @@
             gram_ref[...] = total[0:rank, :] + (cross + cross.T)
 
     foot_spec = pl.BlockSpec((share, block), lambda k, s: (0, k))
-    flat = [array for entry in entries for array in entry[:2]]
     return pl.pallas_call(
         kernel,
         grid_spec=pltpu.PrefetchScalarGridSpec(

time: 149 us -> 149 us (level)
  no operation moved by 1% of the time
where the time goes in v7:
time: 149 us
  starting transfers between devices  56 us (38%)
  waiting for transfers between devices  52.2 us (35%)
  Pallas kernels  32.4 us (22%)
  local copies, waits for them, and re-layouts  6.79 us (5%)
    pallas_call x2, Pallas kernels, diffuse_call(): pl.pallas_call(kernel, grid_spec=pltpu.PrefetchScalarGridSpec(num_scalar_...  19 us
    ppermute x2, starting transfers between devices, line_scatter(): first = lax.ppermute(opposite, axis, inward)  9.53 us
    ppermute x1, waiting for transfers between devices, line_gather(): near = lax.ppermute(block, axis, [(k, k ^ 1) for k in range(count)])  9.49 us
    ppermute x2, waiting for transfers between devices, line_scatter(): second = lax.ppermute(remaining, axis, inward)  8.5 us
    ppermute x2, waiting for transfers between devices, line_scatter(): first = lax.ppermute(opposite, axis, inward)  7.88 us
    ppermute x2, starting transfers between devices, compute(): lax.ppermute(held, 'pix', swap(mask))  6.75 us
    ppermute x2, starting transfers between devices, compute(): from_inner = lax.ppermute(inward, 'pix', swap(1))  6.08 us
    ppermute x2, starting transfers between devices, line_scatter(): lax.ppermute(beside + third, axis, [(k, k ^ 1) for k in range(count)])  5.43 us
  transfers between devices with their start and end apart: 36, of which 16 were waited for; matrix products, arithmetic and copies ran while one was open for 1% of the time, Pallas kernels for 18%

profile of v7, /device:TPU:0, one launch (start us, length us, event | category | flops | bytes accessed | tf_op | source)
XLA Modules:
  0.0 148.7 jit_solution(17833181863079394587)
XLA Ops:
  0.7 2.2 %copy-done = f32[8,256,512]{2,1,0:T(8,128)S(1)} copy-done((f32[8,256,512]{2,1,0:T(8,128)S(1)}, f32[8,256,512]{2,1,0:T(8,128)}, u32[]{:S(2)}) %copy-start) | copy-done | bytes 4194328
  2.9 2.0 %edges.1 = (f32[4,256,256]{2,1,0:T(8,128)S(1)}, f32[4,256,256]{2,1,0:T(8,128)}, f32[4,256,256]{2,1,0:T(8,128)S(1)}) custom-call(s32[7]{0:T(128)S(1)} %stack.43.flags.scalars, f32[8,256,512]{2,1,0:T(8,128)S(1)} %copy-done), custom_call_target="tpu_custom_call" | custom-call | flops 1 | bytes 6291456 | tf_op jit(solution)/shard_map/edges/pallas_call | solution.py:78
  4.9 1.0 copy-done.4
  6.4 1.3 collective-permute-start.2
  7.7 1.3 constant_dynamic-slice_fusion
  9.8 2.6 %collective-permute-start.6 = (f32[64,2048]{1,0:T(8,128)S(1)}, f32[64,2048]{1,0:T(8,128)S(1)}, u32[]{:S(2)}, u32[]{:S(2)}) collective-permute-start(f32[64,2048]{1,0:T(8,128)S(1)} %copy-done.3), channel_id=1, source_target_pairs={{0,1},{1,0},{2,3},{3,2},{4,5},{5,4},{6,7},{7,6},{8,9},{9,8},{10,11... | collective-permute-start | bytes 1572872 | tf_op jit(solution)/shard_map/ppermute | solution.py:585
  13.1 9.5 %collective-permute-done.6.refs_1_ = f32[64,2048]{1,0:T(8,128)S(1)} collective-permute-done((f32[64,2048]{1,0:T(8,128)S(1)}, f32[64,2048]{1,0:T(8,128)S(1)}, u32[]{:S(2)}, u32[]{:S(2)}) %collective-permute-start.6) | collective-permute-done | bytes 524320 | tf_op jit(solution)/shard_map/ppermute | solution.py:585
  24.0 5.6 %collective-permute-start = (f32[4,256,256]{2,1,0:T(8,128)}, f32[4,256,256]{2,1,0:T(8,128)S(1)}, u32[]{:S(2)}, u32[]{:S(2)}) collective-permute-start(f32[4,256,256]{2,1,0:T(8,128)} %copy-done.4), channel_id=1, source_target_pairs={{0,4},{4,0},{8,12},{12,8},{16,20},{20,16},{24,28},{28,24},{1,5},{5... | collective-permute-start | bytes 3145736 | tf_op jit(solution)/shard_map/ppermute | solution.py:704
  29.6 2.1 %collective-permute-start.3 = (f32[4,256,256]{2,1,0:T(8,128)}, f32[4,256,256]{2,1,0:T(8,128)S(1)}, u32[]{:S(2)}, u32[]{:S(2)}) collective-permute-start(f32[4,256,256]{2,1,0:T(8,128)} %collective-permute-done.2), channel_id=1, source_target_pairs={{28,16},{0,12},{29,17},{1,13},{30,18},{2,14},{31,19},{3,15}} | collective-permute-start | bytes 3145736 | tf_op jit(solution)/shard_map/ppermute | solution.py:702
  31.8 1.3 collective-permute-start.8
  33.1 1.3 collective-permute-start.10
  34.4 2.2 %copy-done.1 = f32[8,256,512]{2,1,0:T(8,128)S(1)} copy-done((f32[8,256,512]{2,1,0:T(8,128)S(1)}, f32[8,256,512]{2,1,0:T(8,128)}, u32[]{:S(2)}) %copy-start.1) | copy-done | bytes 4194328
  36.6 9.5 %diffuse.2 = (f32[8,256,512]{2,1,0:T(8,128)}, bf16[8,256,256]{2,1,0:T(8,128)(2,1)S(1)}, bf16[8,256,256]{2,1,0:T(8,128)(2,1)S(1)}) custom-call(s32[7]{0:T(128)S(1)} %stack.43.flags.scalars, f32[8,256,512]{2,1,0:T(8,128)S(1)} %copy-done.1, f32[4,256,256]{2,1,0:T(8,128)S(1)} %collective-permute-done.4.refs_1_, f32[4,256,256]{2,1,0:T(8,128)S(1)} %collective-permute-done.5.refs_2_), custom_call_target="tpu_custom_call" | custom-call | flops 104857600 | bytes 8388608 | tf_op jit(solution)/shard_map/diffuse/pallas_call | solution.py:223
  46.1 4.0 %collective-permute-done.8.refs_3_ = f32[64,2048]{1,0:T(8,128)S(1)} collective-permute-done((f32[64,2048]{1,0:T(8,128)S(1)}, f32[64,2048]{1,0:T(8,128)S(1)}, u32[]{:S(2)}, u32[]{:S(2)}) %collective-permute-start.8) | collective-permute-done | bytes 524320 | tf_op jit(solution)/shard_map/ppermute | solution.py:588
  50.1 6.6 %collective-permute-start.11 = (f32[1,32,512]{2,1,0:T(8,128)S(1)}, f32[1,32,512]{2,1,0:T(8,128)S(1)}, u32[]{:S(2)}, u32[]{:S(2)}) collective-permute-start(f32[1,32,512]{2,1,0:T(8,128)S(1)} %bitcast.30), channel_id=1, source_target_pairs={{0,16},{4,20},{8,24},{12,28},{16,0},{20,4},{24,8},{28,12},{1,17},{... | collective-permute-start | bytes 196616 | tf_op jit(solution)/shard_map/ppermute | solution.py:710
  56.8 4.6 %collective-permute-done.10.refs_5_ = f32[64,2048]{1,0:T(8,128)S(1)} collective-permute-done((f32[64,2048]{1,0:T(8,128)S(1)}, f32[64,2048]{1,0:T(8,128)S(1)}, u32[]{:S(2)}, u32[]{:S(2)}) %collective-permute-start.10) | collective-permute-done | bytes 524320 | tf_op jit(solution)/shard_map/ppermute | solution.py:589
  61.3 1.8 %footprints.1 = (bf16[512,2048]{1,0:T(8,128)(2,1)S(1)}, f32[256,256]{1,0:T(8,128)S(1)}) custom-call(s32[7]{0:T(128)S(1)} %stack.43.flags.scalars, f32[64,2048]{1,0:T(8,128)S(1)} %copy-done.3, f32[64,2048]{1,0:T(8,128)S(1)} %collective-permute-done.6.refs_1_, f32[64,2048]{1,0:T(8,128)S(1)} %collective-permute-done.7.refs_2_, ...), custom_call_target="tpu_custom_call" | custom-call | flops 536870912 | bytes 4194304 | tf_op jit(solution)/shard_map/footprints/pallas_call | solution.py:288
  63.2 9.5 %diffuse.3 = (f32[8,256,512]{2,1,0:T(8,128)}, bf16[8,256,256]{2,1,0:T(8,128)(2,1)S(1)}, bf16[8,256,256]{2,1,0:T(8,128)(2,1)S(1)}) custom-call(s32[7]{0:T(128)S(1)} %stack.43.flags.scalars, f32[8,256,512]{2,1,0:T(8,128)S(1)} %copy-done.2, f32[4,256,256]{2,1,0:T(8,128)S(1)} %collective-permute-done.refs_1_, ...), custom_call_target="tpu_custom_call", output_to_operand_aliasing={{0}: (5, {})} | custom-call | flops 104857600 | bytes 8388608 | tf_op jit(solution)/shard_map/diffuse/pallas_call | solution.py:223
  72.7 2.4 %numerator.1 = (f32[4,32,768]{2,1,0:T(8,128)S(1)}, f32[4,32,768]{2,1,0:T(8,128)S(1)}) custom-call(s32[7]{0:T(128)S(1)} %stack.43.flags.scalars, bf16[512,2048]{1,0:T(8,128)(2,1)S(1)} %get-tuple-element.33.foot_ref.later_ref, f32[256,256]{1,0:T(8,128)S(1)} %get-tuple-element.34.gram_ref, bf16[2048,256]{1,0:T(8,128)(2,1)S(1)} %bitcast.18, ...), custom_call_target="tpu_custom_call" | custom-call | flops 3221225472 | bytes 8388608 | tf_op jit(solution)/shard_map/numerator/pallas_call | solution.py:343
  75.7 1.4 collective-permute-done.12
  77.2 2.5 %collective-permute-start.13 = (f32[4,32,512]{2,1,0:T(8,128)S(1)}, f32[4,32,512]{2,1,0:T(8,128)S(1)}, u32[]{:S(2)}, u32[]{:S(2)}) collective-permute-start(f32[4,32,512]{2,1,0:T(8,128)S(1)} %pad_maximum_fusion.refs_0_), channel_id=1, source_target_pairs={{0,8},{4,12},{8,0},{12,4},{16,24},{20,28},{24,16},{28,20},{1,9},{5... | collective-permute-start | bytes 786440 | tf_op jit(solution)/shard_map/ppermute | solution.py:714
  79.8 1.5 collective-permute-start.16
  81.3 2.0 %collective-permute-start.17 = (f32[32,768]{1,0:T(8,128)S(1)}, f32[32,768]{1,0:T(8,128)S(1)}, u32[]{:S(2)}, u32[]{:S(2)}) collective-permute-start(f32[32,768]{1,0:T(8,128)S(1)} %get-tuple-element.53), channel_id=1, source_target_pairs={{0,24},{4,28},{8,16},{12,20},{16,8},{20,12},{24,0},{28,4},{1,25},{... | collective-permute-start | bytes 294920 | tf_op jit(solution)/shard_map/ppermute | solution.py:735
  83.3 3.6 %collective-permute-done.13.refs_1_ = f32[4,32,512]{2,1,0:T(8,128)S(1)} collective-permute-done((f32[4,32,512]{2,1,0:T(8,128)S(1)}, f32[4,32,512]{2,1,0:T(8,128)S(1)}, u32[]{:S(2)}, u32[]{:S(2)}) %collective-permute-start.13) | collective-permute-done | bytes 262176 | tf_op jit(solution)/shard_map/ppermute | solution.py:714
  86.8 2.1 %collective-permute-done.15.refs_4_ = f32[32,768]{1,0:T(8,128)S(1)} collective-permute-done((f32[32,768]{1,0:T(8,128)S(1)}, f32[32,768]{1,0:T(8,128)S(1)}, u32[]{:S(2)}, u32[]{:S(2)}) %collective-permute-start.15) | collective-permute-done | bytes 98336 | tf_op jit(solution)/shard_map/ppermute | solution.py:735
  88.9 2.4 %collective-permute-done.17.refs_6_ = f32[32,768]{1,0:T(8,128)S(1)} collective-permute-done((f32[32,768]{1,0:T(8,128)S(1)}, f32[32,768]{1,0:T(8,128)S(1)}, u32[]{:S(2)}, u32[]{:S(2)}) %collective-permute-start.17) | collective-permute-done | bytes 98336 | tf_op jit(solution)/shard_map/ppermute | solution.py:735
  91.3 1.4 traces.1
  92.8 1.7 %collective-permute-start.18 = (f32[32,512]{1,0:T(8,128)S(1)}, f32[32,512]{1,0:T(8,128)S(1)}, u32[]{:S(2)}, u32[]{:S(2)}) collective-permute-start(f32[32,512]{1,0:T(8,128)S(1)} %get-tuple-element.41.refs_0_), channel_id=1, source_target_pairs={{0,8},{4,12},{8,0},{12,4},{16,24},{20,28},{24,16},{28,20},{1,9},{5... | collective-permute-start | bytes 196616 | tf_op jit(solution)/shard_map/ppermute | solution.py:739
  94.5 0.9 collective-permute-start.19
  95.4 0.9 collective-permute-start.20
  96.3 0.8 collective-permute-done.18.refs_1_
  97.0 2.2 %collective-permute-done.19.refs_2_ = f32[32,512]{1,0:T(8,128)S(1)} collective-permute-done((f32[32,512]{1,0:T(8,128)S(1)}, f32[32,512]{1,0:T(8,128)S(1)}, u32[]{:S(2)}, u32[]{:S(2)}) %collective-permute-start.19) | collective-permute-done | bytes 65568 | tf_op jit(solution)/shard_map/ppermute | solution.py:739
  99.2 1.3 collective-permute-done.20.refs_3_
  100.5 1.2 collective-permute-done.24.refs_7_
  101.8 1.9 %products.2 = (f32[64,1152]{1,0:T(8,128)S(1)}, f32[64,1152]{1,0:T(8,128)S(1)}, f32[64,1152]{1,0:T(8,128)S(1)}, f32[64,1152]{1,0:T(8,128)S(1)}) custom-call(s32[7]{0:T(128)S(1)} %stack.43.flags.scalars, f32[32,512]{1,0:T(8,128)S(1)} %get-tuple-element.41.refs_0_, f32[32,512]{1,0:T(8,128)S(1)} %collective-permute-done.18.refs_1_, ...), custom_call_target="tpu_custom_call" | custom-call | flops 1073741824 | bytes 3145728 | tf_op jit(solution)/shard_map/products/pallas_call | solution.py:462
  103.7 1.8 %collective-permute-start.25 = (f32[64,1152]{1,0:T(8,128)S(1)}, f32[64,1152]{1,0:T(8,128)S(1)}, u32[]{:S(2)}, u32[]{:S(2)}) collective-permute-start(f32[64,1152]{1,0:T(8,128)S(1)} %get-tuple-element.45), channel_id=1, source_target_pairs={{0,1},{3,2},{4,5},{7,6},{8,9},{11,10},{12,13},{15,14},{16,17},{19,... | collective-permute-start | bytes 884744 | tf_op jit(solution)/shard_map/ppermute | solution.py:634
  105.4 1.3 collective-permute-start.28
  106.8 6.0 %collective-permute-done.25 = f32[64,1152]{1,0:T(8,128)S(1)} collective-permute-done((f32[64,1152]{1,0:T(8,128)S(1)}, f32[64,1152]{1,0:T(8,128)S(1)}, u32[]{:S(2)}, u32[]{:S(2)}) %collective-permute-start.25) | collective-permute-done | bytes 294944 | tf_op jit(solution)/shard_map/ppermute | solution.py:634
  113.5 1.6 %products.3 = (f32[64,1024]{1,0:T(8,128)S(1)}, f32[64,1024]{1,0:T(8,128)S(1)}, f32[64,1024]{1,0:T(8,128)S(1)}, f32[64,1024]{1,0:T(8,128)S(1)}) custom-call(s32[7]{0:T(128)S(1)} %stack.43.flags.scalars, f32[32,512]{1,0:T(8,128)S(1)} %get-tuple-element.41.refs_0_, f32[32,512]{1,0:T(8,128)S(1)} %collective-permute-done.18.refs_1_, ...), custom_call_target="tpu_custom_call" | custom-call | flops 1073741824 | bytes 3145728 | tf_op jit(solution)/shard_map/products/pallas_call | solution.py:462
  115.2 7.8 %collective-permute-start.31 = (f32[64,1024]{1,0:T(8,128)S(1)}, f32[64,1024]{1,0:T(8,128)S(1)}, u32[]{:S(2)}, u32[]{:S(2)}) collective-permute-start(f32[64,1024]{1,0:T(8,128)S(1)} %get-tuple-element.50), channel_id=1, source_target_pairs={{0,1},{3,2},{4,5},{7,6},{8,9},{11,10},{12,13},{15,14},{16,17},{19,... | collective-permute-start | bytes 786440 | tf_op jit(solution)/shard_map/ppermute | solution.py:634
  123.7 1.4 collective-permute-start.27
  125.1 2.6 %collective-permute-start.34 = (f32[64,1024]{1,0:T(8,128)S(1)}, f32[64,1024]{1,0:T(8,128)S(1)}, u32[]{:S(2)}, u32[]{:S(2)}) collective-permute-start(f32[64,1024]{1,0:T(8,128)S(1)} %get-tuple-element.49), channel_id=1, source_target_pairs={{0,1},{3,2},{4,5},{7,6},{8,9},{11,10},{12,13},{15,14},{16,17},{19,... | collective-permute-start | bytes 786440 | tf_op jit(solution)/shard_map/ppermute | solution.py:635
  127.7 1.8 %collective-permute-done.31 = f32[64,1024]{1,0:T(8,128)S(1)} collective-permute-done((f32[64,1024]{1,0:T(8,128)S(1)}, f32[64,1024]{1,0:T(8,128)S(1)}, u32[]{:S(2)}, u32[]{:S(2)}) %collective-permute-start.31) | collective-permute-done | bytes 262176 | tf_op jit(solution)/shard_map/ppermute | solution.py:634
  130.3 8.5 %collective-permute-done.34 = f32[64,1024]{1,0:T(8,128)S(1)} collective-permute-done((f32[64,1024]{1,0:T(8,128)S(1)}, f32[64,1024]{1,0:T(8,128)S(1)}, u32[]{:S(2)}, u32[]{:S(2)}) %collective-permute-start.34) | collective-permute-done | bytes 262176 | tf_op jit(solution)/shard_map/ppermute | solution.py:635
  139.5 4.1 %collective-permute-start.33 = (f32[64,1024]{1,0:T(8,128)S(1)}, f32[64,1024]{1,0:T(8,128)S(1)}, u32[]{:S(2)}, u32[]{:S(2)}) collective-permute-start(f32[64,1024]{1,0:T(8,128)S(1)} %add.62), channel_id=1, source_target_pairs={{0,1},{1,0},{2,3},{3,2},{4,5},{5,4},{6,7},{7,6},{8,9},{9,8},{10,11... | collective-permute-start | bytes 786440 | tf_op jit(solution)/shard_map/ppermute | solution.py:637
  143.7 1.2 collective-permute-done.30.refs_4_
  144.9 1.6 %final.2 = (f32[64,2048]{1,0:T(8,128)}, f32[64,1024]{1,0:T(8,128)S(1)}) custom-call(s32[7]{0:T(128)S(1)} %stack.43.flags.scalars, f32[64,2048]{1,0:T(8,128)S(1)} %copy-done.3, bf16[512,2048]{1,0:T(8,128)(2,1)S(1)} %get-tuple-element.33.foot_ref.later_ref, bf16[512,2048]{1,0:T(8,128)(2,1)S(1)} %get-tuple-element.33.foot_ref.later_ref, ...), custom_call_target="tpu_custom_call" | custom-call | flops 201326592 | bytes 3407872 | tf_op jit(solution)/shard_map/final/pallas_call | solution.py:518
  146.5 1.5 collective-permute-done.33.refs_1_
  (58 shorter events, 8.0 us)
Async XLA Ops:
  0.7 2.2 %copy-start = (f32[8,256,512]{2,1,0:T(8,128)S(1)}, f32[8,256,512]{2,1,0:T(8,128)}, u32[]{:S(2)}) copy-start(f32[8,256,512]{2,1,0:T(8,128)} %refs_0_.4) | copy-start | bytes 12582916
  2.9 6.8 %copy-start.3 = (f32[64,2048]{1,0:T(8,128)S(1)}, f32[64,2048]{1,0:T(8,128)}, u32[]{:S(2)}) copy-start(f32[64,2048]{1,0:T(8,128)} %own_ref.3) | copy-start | bytes 1572868
  4.9 1.0 copy-start.4
  5.9 18.1 %collective-permute-start.4 = (f32[4,256,256]{2,1,0:T(8,128)}, f32[4,256,256]{2,1,0:T(8,128)S(1)}, u32[]{:S(2)}, u32[]{:S(2)}) collective-permute-start(f32[4,256,256]{2,1,0:T(8,128)} %get-tuple-element.30), channel_id=1, source_target_pairs={{0,4},{4,0},{8,12},{12,8},{16,20},{20,16},{24,28},{28,24},{1,5},{5... | collective-permute-start | bytes 3145736 | tf_op jit(solution)/shard_map/ppermute | solution.py:704
  6.4 23.3 %collective-permute-start.2 = (f32[4,256,256]{2,1,0:T(8,128)S(1)}, f32[4,256,256]{2,1,0:T(8,128)}, u32[]{:S(2)}, u32[]{:S(2)}) collective-permute-start(f32[4,256,256]{2,1,0:T(8,128)S(1)} %get-tuple-element.29), channel_id=1, source_target_pairs={{12,28},{16,0},{13,29},{17,1},{14,30},{18,2},{15,31},{19,3}} | collective-permute-start | bytes 3145736 | tf_op jit(solution)/shard_map/ppermute | solution.py:701
  7.7 42.4 %copy-start.5 = (f32[32,512]{1,0:T(8,128)S(1)}, f32[32,512]{1,0:T(8,128)}, u32[]{:S(2)}) copy-start(f32[32,512]{1,0:T(8,128)} %param.5) | copy-start | bytes 196612
  9.0 22.7 %collective-permute-start.5 = (f32[4,256,256]{2,1,0:T(8,128)S(1)}, f32[4,256,256]{2,1,0:T(8,128)S(1)}, u32[]{:S(2)}, u32[]{:S(2)}) collective-permute-start(f32[4,256,256]{2,1,0:T(8,128)S(1)} %constant_dynamic-slice_fusion), channel_id=1, source_target_pairs={{4,8},{12,16},{20,24},{8,4},{16,12},{24,20},{5,9},{13,17},{21,25},... | collective-permute-start | bytes 3145736 | tf_op jit(solution)/shard_map/ppermute | solution.py:703
  9.8 12.8 %collective-permute-start.6 = (f32[64,2048]{1,0:T(8,128)S(1)}, f32[64,2048]{1,0:T(8,128)S(1)}, u32[]{:S(2)}, u32[]{:S(2)}) collective-permute-start(f32[64,2048]{1,0:T(8,128)S(1)} %copy-done.3), channel_id=1, source_target_pairs={{0,1},{1,0},{2,3},{3,2},{4,5},{5,4},{6,7},{7,6},{8,9},{9,8},{10,11... | collective-permute-start | bytes 1572872 | tf_op jit(solution)/shard_map/ppermute | solution.py:585
  12.4 10.9 %collective-permute-start.7 = (f32[64,2048]{1,0:T(8,128)S(1)}, f32[64,2048]{1,0:T(8,128)S(1)}, u32[]{:S(2)}, u32[]{:S(2)}) collective-permute-start(f32[64,2048]{1,0:T(8,128)S(1)} %copy-done.3), channel_id=1, source_target_pairs={{1,2},{2,1},{5,6},{6,5},{9,10},{10,9},{13,14},{14,13},{17,18},{18,... | collective-permute-start | bytes 1572872 | tf_op jit(solution)/shard_map/ppermute | solution.py:586
  22.6 10.5 %collective-permute-start.9 = (f32[64,2048]{1,0:T(8,128)S(1)}, f32[64,2048]{1,0:T(8,128)S(1)}, u32[]{:S(2)}, u32[]{:S(2)}) collective-permute-start(f32[64,2048]{1,0:T(8,128)S(1)} %collective-permute-done.6.refs_1_), channel_id=1, source_target_pairs={{1,2},{2,1},{5,6},{6,5},{9,10},{10,9},{13,14},{14,13},{17,18},{18,... | collective-permute-start | bytes 1572872 | tf_op jit(solution)/shard_map/ppermute | solution.py:587
  23.3 39.9 %collective-permute-start.1 = (f32[4,256,256]{2,1,0:T(8,128)S(1)}, f32[4,256,256]{2,1,0:T(8,128)S(1)}, u32[]{:S(2)}, u32[]{:S(2)}) collective-permute-start(f32[4,256,256]{2,1,0:T(8,128)S(1)} %get-tuple-element.29), channel_id=1, source_target_pairs={{4,8},{20,24},{8,4},{24,20},{5,9},{21,25},{9,5},{25,21},{6,10},{22... | collective-permute-start | bytes 3145736 | tf_op jit(solution)/shard_map/ppermute | solution.py:703
  24.0 39.1 %collective-permute-start = (f32[4,256,256]{2,1,0:T(8,128)}, f32[4,256,256]{2,1,0:T(8,128)S(1)}, u32[]{:S(2)}, u32[]{:S(2)}) collective-permute-start(f32[4,256,256]{2,1,0:T(8,128)} %copy-done.4), channel_id=1, source_target_pairs={{0,4},{4,0},{8,12},{12,8},{16,20},{20,16},{24,28},{28,24},{1,5},{5... | collective-permute-start | bytes 3145736 | tf_op jit(solution)/shard_map/ppermute | solution.py:704
  29.6 33.5 %collective-permute-start.3 = (f32[4,256,256]{2,1,0:T(8,128)}, f32[4,256,256]{2,1,0:T(8,128)S(1)}, u32[]{:S(2)}, u32[]{:S(2)}) collective-permute-start(f32[4,256,256]{2,1,0:T(8,128)} %collective-permute-done.2), channel_id=1, source_target_pairs={{28,16},{0,12},{29,17},{1,13},{30,18},{2,14},{31,19},{3,15}} | collective-permute-start | bytes 3145736 | tf_op jit(solution)/shard_map/ppermute | solution.py:702
  31.8 18.3 %collective-permute-start.8 = (f32[64,2048]{1,0:T(8,128)S(1)}, f32[64,2048]{1,0:T(8,128)S(1)}, u32[]{:S(2)}, u32[]{:S(2)}) collective-permute-start(f32[64,2048]{1,0:T(8,128)S(1)} %collective-permute-done.7.refs_2_), channel_id=1, source_target_pairs={{1,0},{2,3},{5,4},{6,7},{9,8},{10,11},{13,12},{14,15},{17,16},{18,... | collective-permute-start | bytes 1572872 | tf_op jit(solution)/shard_map/ppermute | solution.py:588
  33.1 28.2 %collective-permute-start.10 = (f32[64,2048]{1,0:T(8,128)S(1)}, f32[64,2048]{1,0:T(8,128)S(1)}, u32[]{:S(2)}, u32[]{:S(2)}) collective-permute-start(f32[64,2048]{1,0:T(8,128)S(1)} %collective-permute-done.9.refs_4_), channel_id=1, source_target_pairs={{1,0},{2,3},{5,4},{6,7},{9,8},{10,11},{13,12},{14,15},{17,16},{18,... | collective-permute-start | bytes 1572872 | tf_op jit(solution)/shard_map/ppermute | solution.py:589
  34.4 2.2 %copy-start.1 = (f32[8,256,512]{2,1,0:T(8,128)S(1)}, f32[8,256,512]{2,1,0:T(8,128)}, u32[]{:S(2)}) copy-start(f32[8,256,512]{2,1,0:T(8,128)} %refs_0_.4) | copy-start | bytes 12582916
  36.6 26.6 %copy-start.2 = (f32[8,256,512]{2,1,0:T(8,128)S(1)}, f32[8,256,512]{2,1,0:T(8,128)}, u32[]{:S(2)}) copy-start(f32[8,256,512]{2,1,0:T(8,128)} %refs_0_.4) | copy-start | bytes 12582916
  50.1 25.5 %collective-permute-start.11 = (f32[1,32,512]{2,1,0:T(8,128)S(1)}, f32[1,32,512]{2,1,0:T(8,128)S(1)}, u32[]{:S(2)}, u32[]{:S(2)}) collective-permute-start(f32[1,32,512]{2,1,0:T(8,128)S(1)} %bitcast.30), channel_id=1, source_target_pairs={{0,16},{4,20},{8,24},{12,28},{16,0},{20,4},{24,8},{28,12},{1,17},{... | collective-permute-start | bytes 196616 | tf_op jit(solution)/shard_map/ppermute | solution.py:710
  75.1 4.6 %collective-permute-start.14 = (f32[4,32,768]{2,1,0:T(8,128)S(1)}, f32[4,32,768]{2,1,0:T(8,128)S(1)}, u32[]{:S(2)}, u32[]{:S(2)}) collective-permute-start(f32[4,32,768]{2,1,0:T(8,128)S(1)} %get-tuple-element.40), channel_id=1, source_target_pairs={{0,4},{4,0},{8,12},{12,8},{16,20},{20,16},{24,28},{28,24},{1,5},{5... | collective-permute-start | bytes 1179656 | tf_op jit(solution)/shard_map/ppermute | solution.py:732
  75.6 1.5 %collective-permute-start.12 = (f32[2,32,512]{2,1,0:T(8,128)S(1)}, f32[2,32,512]{2,1,0:T(8,128)S(1)}, u32[]{:S(2)}, u32[]{:S(2)}) collective-permute-start(f32[2,32,512]{2,1,0:T(8,128)S(1)} %pad_maximum_fusion.1), channel_id=1, source_target_pairs={{0,4},{4,0},{8,12},{12,8},{16,20},{20,16},{24,28},{28,24},{1,5},{5... | collective-permute-start | bytes 393224 | tf_op jit(solution)/shard_map/ppermute | solution.py:710
  77.2 9.6 %collective-permute-start.13 = (f32[4,32,512]{2,1,0:T(8,128)S(1)}, f32[4,32,512]{2,1,0:T(8,128)S(1)}, u32[]{:S(2)}, u32[]{:S(2)}) collective-permute-start(f32[4,32,512]{2,1,0:T(8,128)S(1)} %pad_maximum_fusion.refs_0_), channel_id=1, source_target_pairs={{0,8},{4,12},{8,0},{12,4},{16,24},{20,28},{24,16},{28,20},{1,9},{5... | collective-permute-start | bytes 786440 | tf_op jit(solution)/shard_map/ppermute | solution.py:714
  79.7 9.2 %collective-permute-start.15 = (f32[32,768]{1,0:T(8,128)S(1)}, f32[32,768]{1,0:T(8,128)S(1)}, u32[]{:S(2)}, u32[]{:S(2)}) collective-permute-start(f32[32,768]{1,0:T(8,128)S(1)} %get-tuple-element.55), channel_id=1, source_target_pairs={{0,8},{4,12},{8,0},{12,4},{16,24},{20,28},{24,16},{28,20},{1,9},{5... | collective-permute-start | bytes 294920 | tf_op jit(solution)/shard_map/ppermute | solution.py:735
  79.8 9.1 %collective-permute-start.16 = (f32[32,768]{1,0:T(8,128)S(1)}, f32[32,768]{1,0:T(8,128)S(1)}, u32[]{:S(2)}, u32[]{:S(2)}) collective-permute-start(f32[32,768]{1,0:T(8,128)S(1)} %get-tuple-element.54), channel_id=1, source_target_pairs={{0,16},{4,20},{8,24},{12,28},{16,0},{20,4},{24,8},{28,12},{1,17},{... | collective-permute-start | bytes 294920 | tf_op jit(solution)/shard_map/ppermute | solution.py:735
  81.3 10.1 %collective-permute-start.17 = (f32[32,768]{1,0:T(8,128)S(1)}, f32[32,768]{1,0:T(8,128)S(1)}, u32[]{:S(2)}, u32[]{:S(2)}) collective-permute-start(f32[32,768]{1,0:T(8,128)S(1)} %get-tuple-element.53), channel_id=1, source_target_pairs={{0,24},{4,28},{8,16},{12,20},{16,8},{20,12},{24,0},{28,4},{1,25},{... | collective-permute-start | bytes 294920 | tf_op jit(solution)/shard_map/ppermute | solution.py:735
  92.8 4.3 %collective-permute-start.18 = (f32[32,512]{1,0:T(8,128)S(1)}, f32[32,512]{1,0:T(8,128)S(1)}, u32[]{:S(2)}, u32[]{:S(2)}) collective-permute-start(f32[32,512]{1,0:T(8,128)S(1)} %get-tuple-element.41.refs_0_), channel_id=1, source_target_pairs={{0,8},{4,12},{8,0},{12,4},{16,24},{20,28},{24,16},{28,20},{1,9},{5... | collective-permute-start | bytes 196616 | tf_op jit(solution)/shard_map/ppermute | solution.py:739
  94.5 4.7 %collective-permute-start.19 = (f32[32,512]{1,0:T(8,128)S(1)}, f32[32,512]{1,0:T(8,128)S(1)}, u32[]{:S(2)}, u32[]{:S(2)}) collective-permute-start(f32[32,512]{1,0:T(8,128)S(1)} %get-tuple-element.41.refs_0_), channel_id=1, source_target_pairs={{0,16},{4,20},{8,24},{12,28},{16,0},{20,4},{24,8},{28,12},{1,17},{... | collective-permute-start | bytes 196616 | tf_op jit(solution)/shard_map/ppermute | solution.py:739
  95.4 5.2 %collective-permute-start.20 = (f32[32,512]{1,0:T(8,128)S(1)}, f32[32,512]{1,0:T(8,128)S(1)}, u32[]{:S(2)}, u32[]{:S(2)}) collective-permute-start(f32[32,512]{1,0:T(8,128)S(1)} %get-tuple-element.41.refs_0_), channel_id=1, source_target_pairs={{0,24},{4,28},{8,16},{12,20},{16,8},{20,12},{24,0},{28,4},{1,25},{... | collective-permute-start | bytes 196616 | tf_op jit(solution)/shard_map/ppermute | solution.py:739
  96.2 4.3 %collective-permute-start.21 = (f32[32,512]{1,0:T(8,128)S(1)}, f32[32,512]{1,0:T(8,128)S(1)}, u32[]{:S(2)}, u32[]{:S(2)}) collective-permute-start(f32[32,512]{1,0:T(8,128)S(1)} %get-tuple-element.41.refs_0_), channel_id=1, source_target_pairs={{0,4},{4,0},{8,12},{12,8},{16,20},{20,16},{24,28},{28,24},{1,5},{5... | collective-permute-start | bytes 196616 | tf_op jit(solution)/shard_map/ppermute | solution.py:742
  97.0 3.5 %collective-permute-start.22 = (f32[32,512]{1,0:T(8,128)S(1)}, f32[32,512]{1,0:T(8,128)S(1)}, u32[]{:S(2)}, u32[]{:S(2)}) collective-permute-start(f32[32,512]{1,0:T(8,128)S(1)} %collective-permute-done.18.refs_1_), channel_id=1, source_target_pairs={{0,4},{4,0},{8,12},{12,8},{16,20},{20,16},{24,28},{28,24},{1,5},{5... | collective-permute-start | bytes 196616 | tf_op jit(solution)/shard_map/ppermute | solution.py:742
  99.2 1.3 collective-permute-start.23
  100.5 1.3 collective-permute-start.24
  103.7 9.1 %collective-permute-start.25 = (f32[64,1152]{1,0:T(8,128)S(1)}, f32[64,1152]{1,0:T(8,128)S(1)}, u32[]{:S(2)}, u32[]{:S(2)}) collective-permute-start(f32[64,1152]{1,0:T(8,128)S(1)} %get-tuple-element.45), channel_id=1, source_target_pairs={{0,1},{3,2},{4,5},{7,6},{8,9},{11,10},{12,13},{15,14},{16,17},{19,... | collective-permute-start | bytes 884744 | tf_op jit(solution)/shard_map/ppermute | solution.py:634
  105.4 17.5 %collective-permute-start.28 = (f32[64,1152]{1,0:T(8,128)S(1)}, f32[64,1152]{1,0:T(8,128)S(1)}, u32[]{:S(2)}, u32[]{:S(2)}) collective-permute-start(f32[64,1152]{1,0:T(8,128)S(1)} %get-tuple-element.44), channel_id=1, source_target_pairs={{0,1},{3,2},{4,5},{7,6},{8,9},{11,10},{12,13},{15,14},{16,17},{19,... | collective-permute-start | bytes 884744 | tf_op jit(solution)/shard_map/ppermute | solution.py:635
  112.8 10.8 %collective-permute-start.26 = (f32[64,1152]{1,0:T(8,128)S(1)}, f32[64,1152]{1,0:T(8,128)S(1)}, u32[]{:S(2)}, u32[]{:S(2)}) collective-permute-start(f32[64,1152]{1,0:T(8,128)S(1)} %add.56), channel_id=1, source_target_pairs={{1,2},{2,1},{5,6},{6,5},{9,10},{10,9},{13,14},{14,13},{17,18},{18,... | collective-permute-start | bytes 884744 | tf_op jit(solution)/shard_map/ppermute | solution.py:636
  115.2 14.4 %collective-permute-start.31 = (f32[64,1024]{1,0:T(8,128)S(1)}, f32[64,1024]{1,0:T(8,128)S(1)}, u32[]{:S(2)}, u32[]{:S(2)}) collective-permute-start(f32[64,1024]{1,0:T(8,128)S(1)} %get-tuple-element.50), channel_id=1, source_target_pairs={{0,1},{3,2},{4,5},{7,6},{8,9},{11,10},{12,13},{15,14},{16,17},{19,... | collective-permute-start | bytes 786440 | tf_op jit(solution)/shard_map/ppermute | solution.py:634
  123.0 20.6 %collective-permute-start.29 = (f32[64,1152]{1,0:T(8,128)S(1)}, f32[64,1152]{1,0:T(8,128)S(1)}, u32[]{:S(2)}, u32[]{:S(2)}) collective-permute-start(f32[64,1152]{1,0:T(8,128)S(1)} %add.58), channel_id=1, source_target_pairs={{1,2},{2,1},{5,6},{6,5},{9,10},{10,9},{13,14},{14,13},{17,18},{18,... | collective-permute-start | bytes 884744 | tf_op jit(solution)/shard_map/ppermute | solution.py:638
  123.7 19.9 %collective-permute-start.27 = (f32[64,1152]{1,0:T(8,128)S(1)}, f32[64,1152]{1,0:T(8,128)S(1)}, u32[]{:S(2)}, u32[]{:S(2)}) collective-permute-start(f32[64,1152]{1,0:T(8,128)S(1)} %add.57), channel_id=1, source_target_pairs={{0,1},{1,0},{2,3},{3,2},{4,5},{5,4},{6,7},{7,6},{8,9},{9,8},{10,11... | collective-permute-start | bytes 884744 | tf_op jit(solution)/shard_map/ppermute | solution.py:637
  125.1 13.7 %collective-permute-start.34 = (f32[64,1024]{1,0:T(8,128)S(1)}, f32[64,1024]{1,0:T(8,128)S(1)}, u32[]{:S(2)}, u32[]{:S(2)}) collective-permute-start(f32[64,1024]{1,0:T(8,128)S(1)} %get-tuple-element.49), channel_id=1, source_target_pairs={{0,1},{3,2},{4,5},{7,6},{8,9},{11,10},{12,13},{15,14},{16,17},{19,... | collective-permute-start | bytes 786440 | tf_op jit(solution)/shard_map/ppermute | solution.py:635
  129.6 9.9 %collective-permute-start.32 = (f32[64,1024]{1,0:T(8,128)S(1)}, f32[64,1024]{1,0:T(8,128)S(1)}, u32[]{:S(2)}, u32[]{:S(2)}) collective-permute-start(f32[64,1024]{1,0:T(8,128)S(1)} %add.61), channel_id=1, source_target_pairs={{1,2},{2,1},{5,6},{6,5},{9,10},{10,9},{13,14},{14,13},{17,18},{18,... | collective-permute-start | bytes 786440 | tf_op jit(solution)/shard_map/ppermute | solution.py:636
  138.8 7.7 %collective-permute-start.35 = (f32[64,1024]{1,0:T(8,128)S(1)}, f32[64,1024]{1,0:T(8,128)S(1)}, u32[]{:S(2)}, u32[]{:S(2)}) collective-permute-start(f32[64,1024]{1,0:T(8,128)S(1)} %add.63), channel_id=1, source_target_pairs={{1,2},{2,1},{5,6},{6,5},{9,10},{10,9},{13,14},{14,13},{17,18},{18,... | collective-permute-start | bytes 786440 | tf_op jit(solution)/shard_map/ppermute | solution.py:638
  139.5 8.4 %collective-permute-start.33 = (f32[64,1024]{1,0:T(8,128)S(1)}, f32[64,1024]{1,0:T(8,128)S(1)}, u32[]{:S(2)}, u32[]{:S(2)}) collective-permute-start(f32[64,1024]{1,0:T(8,128)S(1)} %add.62), channel_id=1, source_target_pairs={{0,1},{1,0},{2,3},{3,2},{4,5},{5,4},{6,7},{7,6},{8,9},{9,8},{10,11... | collective-permute-start | bytes 786440 | tf_op jit(solution)/shard_map/ppermute | solution.py:637
  143.6 1.3 collective-permute-start.30
